TPU v7x, 32 devices: a whole 2x2x4 slice. The times are simulated.
32 devices in a mesh: groups: 2 (over x), ctx: 16 (over z, y, core).
Axes of the slice: x: 2, y: 2, z: 4, core: 2. Of those that a mesh axis runs over, the one named last changes fastest.
Arguments:
- queries: bfloat16 [256, 2048], P(('groups', 'ctx')), parts along dimension 0, may hold values from -8 to 8, as said below
- keys: bfloat16 [2, 8192, 256], P('groups', 'ctx'), parts along dimension 0, may hold values from -8 to 8
- values: bfloat16 [2, 8192, 256], P('groups', 'ctx'), parts along dimension 0, may hold values from -16 to 16
- lengths: int32 [2], P('groups'), parts along dimension 0, may hold values from 4096 to 8192, as said below
- owner_counts: int32 [32], P('groups'), parts along dimension 0, may hold values from 1 to 16, 128 in all
- row_order: int32 [256], P('groups'), parts along dimension 0, may hold values from 0 to 127, each once
- residual: bfloat16 [512, 2048], P(('groups', 'ctx')), parts along dimension 0, may hold values from -40 to 40, as said below
- out_weight: bfloat16 [2048, 2048], P('ctx'), may hold values from -0.125 to 0.125
- norm_gain: float32 [2048], replicated, may hold values from 0.1 to 1.9
- expert_ids: int32 [512, 8], P(('groups', 'ctx')), parts along dimension 0, may hold values from 0 to 15, all different within a row; in each aligned block of 16 rows (0 to 15, 16 to 31, ...) at most 16 rows name the same one
- route_weights: float32 [512, 8], P(('groups', 'ctx')), parts along dimension 0, may hold values from 0.1 to 1
- gate_up: bfloat16 [16, 2048, 1536], P('ctx'), may hold values from -0.125 to 0.125
- expert_down: bfloat16 [16, 768, 2048], P('ctx'), may hold values from -0.21875 to 0.21875
Outputs:
- attn_slots: bfloat16 [512, 2048], P(('groups', 'ctx')), parts along dimension 0
- layer_out: bfloat16 [512, 2048], P(('groups', 'ctx')), parts along dimension 0
There are 2 independent parts, one for each index of `groups`. A program takes and returns all parts, laid end to end along the dimension named above; an argument that names none is the same for every part. Nothing has to cross between parts.
Inputs may be any that keep to these rules, and one draw needn't show every extreme that they name: Large entries of queries and keys may line up. `lengths`: at least 4096; one request has exactly 8192. `owner_counts`: sum to 128; the largest is exactly 16. `row_order`: each row once. `residual`: entries may be any real values in the range. `expert_ids`: each slot names 8 different experts; within the 16 slots of one owner no expert is named more than 16 times, and some expert exactly that many times.
All inputs are finite; a program needn't handle non-finite values.
Results may differ from a plain program's by a relative error of at most 0.009.
Values may be sent and summed in bfloat16 or wider, within the bound.
No kernel may reach another device: no remote copies, remote signals or barrier semaphores. Data moves between devices by JAX's collectives and lax.ppermute only.
A program may use at most 128 MiB of HBM per device.

v0:
```python
import functools

import jax
import jax.numpy as jnp
from jax import lax
from jax.experimental import pallas as pl
from jax.experimental.pallas import tpu as pltpu
from jax.sharding import PartitionSpec as P


D = 2048
HQ = 16
KVH = 2
HD = 128
EFF = 768
TOPK = 8
STRETCH = 128
BF = jnp.bfloat16
F32 = jnp.float32
MIB = 1 << 20
STAT = 8


NT = (((1,), (1,)), ((), ()))
NN = (((1,), (0,)), ((), ()))


def dot(a, b, dims):
    return lax.dot_general(a, b, dims, preferred_element_type=F32)


def place():
    device = lax.axis_index("ctx")
    return device, device & 1, device >> 1, device >> 2


def hop(x, mask, width):
    return lax.ppermute(x, "ctx", [(i, i ^ mask) for i in range(width)])


def split3(x):
    hi = x.astype(BF)
    rest = x - hi.astype(F32)
    mid = rest.astype(BF)
    return hi, mid, (rest - mid.astype(F32)).astype(BF)


def row_ids(per, core, axis, shape):
    i = lax.broadcasted_iota(jnp.int32, shape, axis)
    return (i // per) * (2 * per) + core * per + i % per


def fetch_kernel(count, *refs):
    sems = refs[2 * count]
    copies = [
        pltpu.make_async_copy(refs[i], refs[count + i], sems.at[i]) for i in range(count)
    ]
    for copy in copies:
        copy.start()
    for copy in copies:
        copy.wait()


def in_hbm(x):
    return pltpu.with_memory_space_constraint(x, pltpu.HBM)


def fetch(*arrays):
    count = len(arrays)
    size = sum(a.size * a.dtype.itemsize for a in arrays)
    return pl.pallas_call(
        functools.partial(fetch_kernel, count),
        out_shape=[pltpu.VMEM(a.shape, a.dtype) for a in arrays],
        in_specs=[pl.BlockSpec(memory_space=pltpu.HBM)] * count,
        out_specs=[pl.BlockSpec(memory_space=pltpu.VMEM)] * count,
        scratch_shapes=[pltpu.SemaphoreType.DMA((count,))],
        cost_estimate=pl.CostEstimate(flops=0, bytes_accessed=2 * size, transcendentals=0),
        compiler_params=pltpu.CompilerParams(vmem_limit_bytes=16 * MIB),
        name="fetch",
    )(*[in_hbm(a) for a in arrays])


def prepare_kernel(per, width, counts, order, ids, weights, residual, res, home, fill, turn, picks, table, own):
    device, core, _, _ = place()
    cap, rows = residual.shape[0], order.shape[1]
    half = home.shape[0]
    p = lax.broadcasted_iota(jnp.int32, (cap, rows), 1)
    j = lax.broadcasted_iota(jnp.int32, (cap, rows), 0)
    start = jnp.int32(0)
    for o in range(width):
        hit = (p - start == j) & (j < counts[o])
        picks[o * cap : (o + 1) * cap, :] = hit.astype(F32).astype(BF)
        start = start + counts[o]
    seats = [
        (order[...] == row_ids(per, c, 0, (half, rows))).astype(F32).astype(BF)
        for c in range(2)
    ]
    mine = (order[...] == row_ids(per, core, 0, (half, rows))).astype(F32).astype(BF)
    own[...] = dot(picks[...], mine, NT).astype(BF)
    table[...] = dot(picks[...], jnp.concatenate(seats, axis=0), NT).astype(BF)
    for kc in range(2):
        for ky in range(2):
            for kz in range(width // 4):
                owner = device ^ (kc + 2 * ky + 4 * kz)
                to = (kc * 2 + ky) * (width // 4) + kz
                there = pl.ds(pl.multiple_of(owner * cap, cap), cap)
                turn[to * cap : (to + 1) * cap, :] = table[there, :]
                fill[to * cap : (to + 1) * cap, :] = own[there, :]
    chip_picks = [
        picks[pl.ds(pl.multiple_of(o * cap, cap), cap), :] for o in (device, device ^ 1)
    ]
    home[...] = dot(mine, jnp.concatenate(chip_picks, axis=0), NT).astype(BF)
    lanes = res.shape[1] - D
    lane = lax.broadcasted_iota(jnp.int32, (cap, lanes), 1)
    norm = weights[...] / jnp.sum(weights[...], axis=-1, keepdims=True)
    dense = jnp.zeros((cap, lanes), F32)
    for k in range(TOPK):
        hit = ids[:, k : k + 1] == lane % width
        dense = dense + jnp.where(hit, norm[:, k : k + 1], 0.0)
    high = dense.astype(BF).astype(F32)
    low = jnp.where(lane < 2 * width, dense - high, 0.0)
    res[:, :D] = residual[...]
    res[:, D:] = jnp.where(lane < width, high, low).astype(BF)


def prepare(counts, order, ids, weights, residual, per, width):
    cap, rows = residual.shape[0], order.shape[1]
    half = width // 2 * per
    lanes = -(-2 * width // 128) * 128
    slots = width * cap
    return pl.pallas_call(
        functools.partial(prepare_kernel, per, width),
        out_shape=[
            jax.ShapeDtypeStruct((cap, D + lanes), BF),
            jax.ShapeDtypeStruct((half, 2 * cap), BF),
            jax.ShapeDtypeStruct((slots, half), BF),
            jax.ShapeDtypeStruct((slots, 2 * half), BF),
        ],
        in_specs=[pl.BlockSpec(memory_space=pltpu.SMEM)]
        + [pl.BlockSpec(memory_space=pltpu.VMEM)] * 4,
        out_specs=[pl.BlockSpec(memory_space=pltpu.VMEM)] * 4,
        scratch_shapes=[
            pltpu.VMEM((slots, rows), BF),
            pltpu.VMEM((slots, 2 * half), BF),
            pltpu.VMEM((slots, half), BF),
        ],
        cost_estimate=pl.CostEstimate(
            flops=6 * slots * rows * half, bytes_accessed=8 * slots * half, transcendentals=0
        ),
        compiler_params=pltpu.CompilerParams(vmem_limit_bytes=8 * MIB),
        name="prepare",
    )(counts, in_hbm(order), ids, weights, in_hbm(residual))


def attention_kernel(nz, lengths, *refs):
    pieces, (k_own, v_own, k_oth, v_oth, out, rows) = refs[:nz], refs[nz:]
    device, core, chip, _ = place()
    per = pieces[0].shape[1]
    requests, span = k_own.shape[0], k_own.shape[1]
    count = rows.shape[0]
    seat = count // requests
    chips, depth = out.shape[0], out.shape[1] - STAT
    cols = HQ * HD // chips
    heads = max(1, cols // HD)
    for kz in range(nz):
        both = pieces[kz][...].astype(F32)
        for ky in range(2):
            spot = (chip ^ (2 * kz + ky)) * per
            rows[pl.ds(pl.multiple_of(spot, per), per), :] = both[ky]
    key = lax.broadcasted_iota(jnp.int32, (span, 2 * seat), 0)
    lane = lax.broadcasted_iota(jnp.int32, (1, 2 * seat), 1) % seat
    ahead = (lane // per) * (2 * per) + core * per + lane % per - STRETCH
    first_own, first_oth = device * span, (device ^ 1) * span
    for q in range(requests):
        last = lengths[q] + ahead
        see_own, see_oth = key <= last - first_own, key <= last - first_oth
        for j in range(HQ // 2):
            v = 2 * j // (HQ // KVH)
            kv = slice(v * HD, (v + 1) * HD)
            if 2 * j % (HQ // KVH) == 0:
                vt_own, vt_oth = v_own[q, :, kv].T, v_oth[q, :, kv].T
            pair = jnp.concatenate(
                [
                    rows[q * seat : (q + 1) * seat, (2 * j + e) * HD : (2 * j + e + 1) * HD]
                    for e in range(2)
                ],
                axis=0,
            ).astype(BF)
            s_own = dot(k_own[q, :, kv], pair, NT) * HD ** (-0.5)
            s_oth = dot(k_oth[q, :, kv], pair, NT) * HD ** (-0.5)
            s_own = jnp.where(see_own, s_own, -1e30)
            s_oth = jnp.where(see_oth, s_oth, -1e30)
            top = jnp.maximum(
                jnp.max(s_own, axis=0, keepdims=True), jnp.max(s_oth, axis=0, keepdims=True)
            )
            w_own = jnp.where(see_own, jnp.exp(s_own - top), 0.0)
            w_oth = jnp.where(see_oth, jnp.exp(s_oth - top), 0.0)
            total = jnp.sum(w_own, axis=0, keepdims=True) + jnp.sum(w_oth, axis=0, keepdims=True)
            mixed = dot(vt_own, w_own.astype(BF), NN) + dot(vt_oth, w_oth.astype(BF), NN)
            some = total > 0.0
            safe = jnp.where(some, total, 1.0)
            mixed = (mixed / safe).astype(BF)
            lse = jnp.where(some, top + jnp.log(safe), -1e30)
            hi, mid, low = split3(lse)
            stat = jnp.concatenate(
                [hi.astype(F32), mid.astype(F32), low.astype(F32)]
                + [jnp.zeros((STAT - 3, 2 * seat), F32)],
                axis=0,
            ).astype(BF)
            if heads == 2 and requests == 1:
                out[j, :depth, :] = mixed
                out[j, depth:, :] = stat
            else:
                for e in range(2):
                    mine = slice(e * seat, (e + 1) * seat)
                    head = 2 * j + e
                    lo = (head % heads) * count + q * seat
                    for part in range(HD // depth):
                        dest = (head * HD + part * depth) // cols
                        out[dest, :depth, lo : lo + seat] = mixed[
                            part * depth : (part + 1) * depth, mine
                        ]
                        out[dest, depth:, lo : lo + seat] = stat[:, mine]


def attention(pieces, k_own, v_own, k_oth, v_oth, lengths, chips):
    nz = len(pieces)
    per = pieces[0].shape[1]
    count = chips * per
    cols = HQ * HD // chips
    heads = max(1, cols // HD)
    shape = (chips, min(cols, HD) + STAT, heads * count)
    work = 4 * k_own.size * (HQ // KVH) * 2 * count
    return pl.pallas_call(
        functools.partial(attention_kernel, nz),
        out_shape=jax.ShapeDtypeStruct(shape, BF),
        in_specs=[pl.BlockSpec(memory_space=pltpu.SMEM)]
        + [pl.BlockSpec(memory_space=pltpu.VMEM)] * (nz + 4),
        out_specs=pl.BlockSpec(memory_space=pltpu.VMEM),
        scratch_shapes=[pltpu.VMEM((count, HQ * HD), F32)],
        cost_estimate=pl.CostEstimate(
            flops=work, bytes_accessed=8 * k_own.size, transcendentals=work // (4 * HD)
        ),
        compiler_params=pltpu.CompilerParams(vmem_limit_bytes=16 * MIB),
        name="attention",
    )(lengths, *pieces, k_own, v_own, k_oth, v_oth)


def project_kernel(nz, got, w_own, w_oth, res_own, res_oth, home, *refs):
    outs, attn, part = refs[:nz], refs[nz], refs[nz + 1]
    _, core, _, z = place()
    chips, depth = got.shape[0], got.shape[1] - STAT
    count = part.shape[0]
    heads = got.shape[2] // count
    lse = [
        jnp.sum(got[i, depth:, :].astype(F32), axis=0, keepdims=True) for i in range(chips)
    ]
    best = functools.reduce(jnp.maximum, lse)
    factor = [jnp.exp(x - best) for x in lse]
    denom = functools.reduce(lambda a, b: a + b, factor)
    merged = functools.reduce(
        lambda a, b: a + b, [got[i, :depth, :].astype(F32) * factor[i] for i in range(chips)]
    )
    merged = (merged / denom).T.astype(BF)
    if heads == 2:
        first, second = merged[:count], merged[count:]
        attn[...] = jnp.concatenate([first, second], axis=1)
    else:
        first, second = merged[:, : depth // 2], merged[:, depth // 2 :]
        attn[...] = merged
    low = (core == 0).astype(F32)
    first, second = first.astype(F32), second.astype(F32)
    own = (first * low + second * (1.0 - low)).astype(BF)
    oth = (second * low + first * (1.0 - low)).astype(BF)
    res = jnp.concatenate([res_own[...], res_oth[...]], axis=0)
    part[:, :D] = (
        dot(home[...], res[:, :D], NN) + dot(own, w_own[...], NN) + dot(oth, w_oth[...], NN)
    )
    part[:, D:] = dot(home[...], res[:, D:], NN)
    block = outs[0].shape[0]
    for kz in range(nz):
        spot = pl.multiple_of((z ^ kz) * block, block)
        outs[kz][...] = part[pl.ds(spot, block), :].astype(BF)


def project(got, w_own, w_oth, res_own, res_oth, home, nz):
    chips = got.shape[0]
    count = home.shape[0]
    cols = D // chips
    wide = res_own.shape[1]
    return pl.pallas_call(
        functools.partial(project_kernel, nz),
        out_shape=[jax.ShapeDtypeStruct((count // nz, wide), BF)] * nz
        + [jax.ShapeDtypeStruct((count, cols), BF)],
        in_specs=[pl.BlockSpec(memory_space=pltpu.VMEM)] * 6,
        out_specs=[pl.BlockSpec(memory_space=pltpu.VMEM)] * (nz + 1),
        scratch_shapes=[pltpu.VMEM((count, wide), F32)],
        cost_estimate=pl.CostEstimate(
            flops=2 * count * cols * D, bytes_accessed=4 * cols * D, transcendentals=0
        ),
        compiler_params=pltpu.CompilerParams(vmem_limit_bytes=12 * MIB),
        name="project",
    )(got, w_own, w_oth, res_own, res_oth, home)


def expert_kernel(nz, width, *refs):
    mine, theirs = refs[:nz], refs[nz : 2 * nz]
    (gain, gate_up, down, turn, fill, mixed, keep0, keep1, send0, send1, stream_own) = refs[
        2 * nz : 2 * nz + 11
    ]
    x, normed, hidden, scaled = refs[2 * nz + 11 :]
    device, core, _, z = place()
    block = mine[0].shape[0]
    half = block * nz
    cap = stream_own.shape[0]
    for kz in range(nz):
        spot = (z ^ kz) * block
        x[pl.ds(pl.multiple_of(core * half + spot, block), block), :] = mine[kz][...]
        x[pl.ds(pl.multiple_of((1 - core) * half + spot, block), block), :] = theirs[kz][...]
    stream = x[:, :D].astype(F32)
    scale = lax.rsqrt(jnp.mean(stream * stream, axis=-1, keepdims=True) + 1e-06)
    normed[...] = (stream * scale * gain[...]).astype(BF)
    extra = x[:, D:].astype(F32)
    lane = lax.broadcasted_iota(jnp.int32, extra.shape, 1)
    pick = (lane == device) | (lane == device + width)
    weight = jnp.sum(jnp.where(pick, extra, 0.0), axis=-1, keepdims=True)
    tile = 256
    for lo in range(0, EFF, tile):
        g = dot(normed[...], gate_up[0, :, lo : lo + tile], NN)
        u = dot(normed[...], gate_up[0, :, EFF + lo : EFF + lo + tile], NN)
        hidden[:, lo : lo + tile] = (g / (1.0 + jnp.exp(-g)) * u).astype(BF)
    for lo in range(0, D, tile):
        y = dot(hidden[...], down[0, :, lo : lo + tile], NN).astype(BF)
        scaled[:, lo : lo + tile] = (y.astype(F32) * weight).astype(BF)
    for k, target in enumerate((keep0, keep1, send0, send1)):
        size = target.shape[0]
        some = slice(k * size, (k + 1) * size)
        target[:, :D] = dot(turn[some, :], scaled[...], NN).astype(BF)
        target[:, D:] = dot(fill[some, :], mixed[...], NN).astype(BF)
    stream_own[...] = dot(turn[:cap, :], x[:, :D], NN).astype(BF)


def experts(mine, theirs, gain, gate_up, down, turn, fill, mixed, width, cap):
    nz = len(mine)
    block, wide = mine[0].shape
    total = 2 * nz * block
    wide_out = jax.ShapeDtypeStruct((nz * cap, D + mixed.shape[1]), BF)
    return pl.pallas_call(
        functools.partial(expert_kernel, nz, width),
        out_shape=[wide_out] * 4 + [jax.ShapeDtypeStruct((cap, D), BF)],
        in_specs=[pl.BlockSpec(memory_space=pltpu.VMEM)] * (2 * nz + 6),
        out_specs=[pl.BlockSpec(memory_space=pltpu.VMEM)] * 5,
        scratch_shapes=[
            pltpu.VMEM((total, wide), BF),
            pltpu.VMEM((total, D), BF),
            pltpu.VMEM((total, EFF), BF),
            pltpu.VMEM((total, D), BF),
        ],
        cost_estimate=pl.CostEstimate(
            flops=6 * total * D * EFF, bytes_accessed=6 * D * EFF, transcendentals=total * EFF
        ),
        compiler_params=pltpu.CompilerParams(vmem_limit_bytes=32 * MIB),
        name="experts",
    )(*mine, *theirs, gain, gate_up, down, turn, fill, mixed)


def mix_kernel(keep, near, far, *outs):
    cap = outs[0].shape[0]
    for kz, out in enumerate(outs):
        some = slice(kz * cap, (kz + 1) * cap)
        own = keep[some, :].astype(F32) + near[some, :].astype(F32)
        other = far[some, :].astype(F32)
        out[:, :D] = (own[:, :D] + other[:, :D]).astype(BF)
        out[:, D:] = jnp.concatenate([own[:, D:], other[:, D:]], axis=1).astype(BF)


def mix(keep, near, far, nz):
    cap = keep.shape[0] // nz
    cols = keep.shape[1] - D
    return pl.pallas_call(
        mix_kernel,
        out_shape=[jax.ShapeDtypeStruct((cap, D + 2 * cols), BF)] * nz,
        in_specs=[pl.BlockSpec(memory_space=pltpu.VMEM)] * 3,
        out_specs=[pl.BlockSpec(memory_space=pltpu.VMEM)] * nz,
        cost_estimate=pl.CostEstimate(
            flops=3 * keep.size, bytes_accessed=8 * keep.size, transcendentals=0
        ),
        compiler_params=pltpu.CompilerParams(vmem_limit_bytes=16 * MIB),
        name="mix",
    )(keep, near, far)


def finish_kernel(nz, stream, *refs):
    pieces, (attn, out) = refs[:nz], refs[nz:]
    _, _, chip, _ = place()
    cols = (pieces[0].shape[1] - D) // 2
    total = stream[...].astype(F32)
    for kz in range(nz):
        total = total + pieces[kz][:, :D].astype(F32)
    out[...] = total.astype(BF)
    if cols % 128 == 0:
        for kz in range(nz):
            for ky in range(2):
                spot = pl.multiple_of((chip ^ (2 * kz + ky)) * cols, cols)
                attn[:, pl.ds(spot, cols)] = pieces[kz][:, D + ky * cols : D + (ky + 1) * cols]
    else:
        whole = jnp.zeros(attn.shape, F32)
        lane = lax.broadcasted_iota(jnp.int32, (cols, D), 1)
        line = lax.broadcasted_iota(jnp.int32, (cols, D), 0)
        for kz in range(nz):
            for ky in range(2):
                spot = (chip ^ (2 * kz + ky)) * cols
                put = (lane == line + spot).astype(F32).astype(BF)
                part = pieces[kz][:, D + ky * cols : D + (ky + 1) * cols]
                whole = whole + dot(part, put, NN)
        attn[...] = whole.astype(BF)


def finish(stream, pieces):
    shape = jax.ShapeDtypeStruct(stream.shape, BF)
    nz = len(pieces)
    return pl.pallas_call(
        functools.partial(finish_kernel, nz),
        out_shape=[shape, shape],
        in_specs=[pl.BlockSpec(memory_space=pltpu.VMEM)] * (nz + 1),
        out_specs=[pl.BlockSpec(memory_space=pltpu.VMEM)] * 2,
        cost_estimate=pl.CostEstimate(
            flops=nz * stream.size, bytes_accessed=4 * nz * stream.size, transcendentals=0
        ),
        compiler_params=pltpu.CompilerParams(vmem_limit_bytes=16 * MIB),
        name="finish",
    )(stream, *pieces)


def body(
    queries,
    keys,
    values,
    lengths,
    owner_counts,
    row_order,
    residual,
    out_weight,
    norm_gain,
    expert_ids,
    route_weights,
    gate_up,
    expert_down,
):
    width = lax.axis_size("ctx")
    chips, nz = width // 2, width // 4
    per = queries.shape[0]
    cap = residual.shape[0]
    order = row_order.reshape(1, -1)
    same_core = [[2 * i + c for i in range(chips)] for c in range(2)]

    def along_z(terms):
        out = [terms[0]]
        for kz in range(1, nz):
            out.append(hop(terms[kz], 4 * kz, width))
        return out

    def add(*terms):
        return functools.reduce(lambda a, b: a + b, [t.astype(F32) for t in terms]).astype(BF)

    near = hop(queries, 2, width)
    k_oth, v_oth = hop(keys, 1, width), hop(values, 1, width)
    column = jnp.stack([queries, near])
    pieces = along_z([column] * nz)
    k_own, v_own = fetch(keys, values)
    w_oth = hop(out_weight, 1, width)
    res_own, home, fill, turn = prepare(
        owner_counts, order, expert_ids, route_weights, residual, per, width
    )
    res_oth = hop(res_own, 1, width)

    partial = attention(pieces, k_own, v_own, k_oth, v_oth, lengths, chips)
    got = lax.all_to_all(
        partial, "ctx", split_axis=0, concat_axis=0, tiled=True, axis_index_groups=same_core
    )
    w_own, gain = fetch(out_weight, norm_gain.reshape(1, -1))
    *parts, mixed = project(got, w_own, w_oth, res_own, res_oth, home, nz)
    chunk = add(*along_z(parts))
    chunk = add(chunk, hop(chunk, 2, width))
    mine = along_z([chunk] * nz)
    theirs = [hop(x, 1, width) for x in mine]
    up, down = fetch(gate_up, lax.optimization_barrier((expert_down, chunk))[0])
    keep0, keep1, send0, send1, stream = experts(
        mine, theirs, gain, up, down, turn, fill, mixed, width, cap
    )
    far = hop(add(keep1, hop(send1, 1, width)), 2, width)
    sums = mix(keep0, hop(send0, 1, width), far, nz)
    attn, layer_out = finish(stream, along_z(sums))
    return (attn, layer_out)


def solution(mesh):
    placed = (
        P(("groups", "ctx"), None),
        P("groups", "ctx", None),
        P("groups", "ctx", None),
        P("groups"),
        P("groups"),
        P("groups"),
        P(("groups", "ctx"), None),
        P("ctx", None),
        P(),
        P(("groups", "ctx"), None),
        P(("groups", "ctx"), None),
        P("ctx", None, None),
        P("ctx", None, None),
    )

    return jax.shard_map(
        body,
        mesh=mesh,
        in_specs=placed,
        out_specs=(P(("groups", "ctx"), None), P(("groups", "ctx"), None)),
        check_vma=False,
    )
```

profile of v0, /device:TPU:0, one launch (start us, length us, event | category | flops | bytes accessed | tf_op | source)
XLA Modules:
  0.0 81.6 jit_solution(9820537767609987363)
XLA Ops:
  0.6 3.1 %collective-permute-start = (bf16[8,2048]{1,0:T(8,128)(2,1)}, bf16[8,2048]{1,0:T(8,128)(2,1)S(1)}, u32[]{:S(2)}, u32[]{:S(2)}) collective-permute-start(bf16[8,2048]{1,0:T(8,128)(2,1)} %param.13), channel_id=1, source_target_pairs={{0,2},{1,3},{2,0},{3,1},{4,6},{5,7},{6,4},{7,5},{8,10},{9,11},{10,... | collective-permute-start | bytes 98312 | tf_op jit(solution)/shard_map/ppermute | solution.py:38
  4.2 1.6 %collective-permute-done = bf16[8,2048]{1,0:T(8,128)(2,1)S(1)} collective-permute-done((bf16[8,2048]{1,0:T(8,128)(2,1)}, bf16[8,2048]{1,0:T(8,128)(2,1)S(1)}, u32[]{:S(2)}, u32[]{:S(2)}) %collective-permute-start) | collective-permute-done | bytes 32800 | tf_op jit(solution)/shard_map/ppermute | solution.py:38
  5.8 0.8 pad_maximum_fusion.refs_0_
  6.6 4.1 %collective-permute-start.3 = (bf16[2,8,2048]{2,1,0:T(8,128)(2,1)S(1)}, bf16[2,8,2048]{2,1,0:T(8,128)(2,1)S(1)}, u32[]{:S(2)}, u32[]{:S(2)}) collective-permute-start(bf16[2,8,2048]{2,1,0:T(8,128)(2,1)S(1)} %pad_maximum_fusion.refs_0_), channel_id=1, source_target_pairs={{0,12},{1,13},{2,14},{3,15},{4,8},{5,9},{6,10},{7,11},{8,4},{9,5},... | collective-permute-start | bytes 196616 | tf_op jit(solution)/shard_map/ppermute | solution.py:38
  11.3 1.0 %fetch.3 = (bf16[1,512,256]{2,1,0:T(8,128)(2,1)S(1)}, bf16[1,512,256]{2,1,0:T(8,128)(2,1)S(1)}) custom-call(bf16[1,512,256]{2,1,0:T(8,128)(2,1)} %refs_0_.3, bf16[1,512,256]{2,1,0:T(8,128)(2,1)} %refs_1_.1), custom_call_target="tpu_custom_call" | custom-call | bytes 1048576 | tf_op jit(solution)/shard_map/fetch/pallas_call | solution.py:71
  13.1 2.8 %collective-permute-done.2.refs_2_ = bf16[2,8,2048]{2,1,0:T(8,128)(2,1)S(1)} collective-permute-done((bf16[2,8,2048]{2,1,0:T(8,128)(2,1)S(1)}, bf16[2,8,2048]{2,1,0:T(8,128)(2,1)S(1)}, u32[]{:S(2)}, u32[]{:S(2)}) %collective-permute-start.2) | collective-permute-done | bytes 65568 | tf_op jit(solution)/shard_map/ppermute | solution.py:38
  15.9 4.0 %attention.1 = bf16[8,136,128]{2,1,0:T(8,128)(2,1)} custom-call(s32[1]{0:T(128)S(6)} %copy.17.lengths, bf16[2,8,2048]{2,1,0:T(8,128)(2,1)S(1)} %pad_maximum_fusion.refs_0_, bf16[2,8,2048]{2,1,0:T(8,128)(2,1)S(1)} %collective-permute-done.1.refs_1_, bf16[2,8,2048]{2,1,0:T(8,128)(2,1)S(1)} %collective-permute-done.2.refs_2_, ...), custom_call_target="tpu_custom_call" | custom-call | flops 536870912 | bytes 1048576 | tf_op jit(solution)/shard_map/attention/pallas_call | solution.py:234
  19.8 4.3 %all-to-all-start = ((bf16[8,136,128]{2,1,0:T(8,128)(2,1)}), bf16[8,136,128]{2,1,0:T(8,128)(2,1)S(1)}, u32[]{:S(2)}, u32[]{:S(2)}) async-start(bf16[8,136,128]{2,1,0:T(8,128)(2,1)} %attention.1), calls=%async_computation | async-start | bytes 557056 | tf_op jit(solution)/shard_map/all_to_all | solution.py:478
  24.1 0.8 copy.15.ids
  24.9 0.8 copy.16.weights
  26.3 1.1 %prepare.1 = (bf16[16,2176]{1,0:T(8,128)(2,1)S(1)}, bf16[64,32]{1,0:T(8,128)(2,1)S(1)}, bf16[256,64]{1,0:T(8,128)(2,1)S(1)}, bf16[256,128]{1,0:T(8,128)(2,1)S(1)}) custom-call(s32[16]{0:T(128)S(1)} %copy-done, s32[1,128]{1,0:T(1,128)} %bitcast.7, s32[16,8]{1,0:T(8,128)S(1)} %copy.15.ids, f32[16,8]{1,0:T(8,128)S(1)} %copy.16.weights, bf16[16,2048]{1,0:T(8,128)(2,1)} %residual.1), custom_call_target="tpu_custom_call" | custom-call | flops 12582912 | bytes 131072 | tf_op jit(solution)/shard_map/prepare/pallas_call | solution.py:131
  27.5 1.1 %fetch.4 = (bf16[128,2048]{1,0:T(8,128)(2,1)S(1)}, f32[1,2048]{1,0:T(1,128)S(1)}) custom-call(bf16[128,2048]{1,0:T(8,128)(2,1)} %refs_0_.4, f32[1,2048]{1,0:T(1,128)} %bitcast.6), custom_call_target="tpu_custom_call" | custom-call | bytes 1064960 | tf_op jit(solution)/shard_map/fetch/pallas_call | solution.py:71
  28.7 4.2 %all-to-all-done.got = bf16[8,136,128]{2,1,0:T(8,128)(2,1)S(1)} async-done(((bf16[8,136,128]{2,1,0:T(8,128)(2,1)}), bf16[8,136,128]{2,1,0:T(8,128)(2,1)S(1)}, u32[]{:S(2)}, u32[]{:S(2)}) %all-to-all-start) | async-done | bytes 278560 | tf_op jit(solution)/shard_map/all_to_all | solution.py:478
  33.5 1.2 %collective-permute-start.8 = (bf16[16,2176]{1,0:T(8,128)(2,1)S(1)}, bf16[16,2176]{1,0:T(8,128)(2,1)S(1)}, u32[]{:S(2)}, u32[]{:S(2)}) collective-permute-start(bf16[16,2176]{1,0:T(8,128)(2,1)S(1)} %get-tuple-element.33), channel_id=1, source_target_pairs={{0,4},{1,5},{2,6},{3,7},{4,0},{5,1},{6,2},{7,3},{8,12},{9,13},{10,... | collective-permute-start | bytes 208904 | tf_op jit(solution)/shard_map/ppermute | solution.py:38
  35.3 2.6 %collective-permute-start.10 = (bf16[16,2176]{1,0:T(8,128)(2,1)S(1)}, bf16[16,2176]{1,0:T(8,128)(2,1)S(1)}, u32[]{:S(2)}, u32[]{:S(2)}) collective-permute-start(bf16[16,2176]{1,0:T(8,128)(2,1)S(1)} %get-tuple-element.35), channel_id=1, source_target_pairs={{0,12},{1,13},{2,14},{3,15},{4,8},{5,9},{6,10},{7,11},{8,4},{9,5},... | collective-permute-start | bytes 208904 | tf_op jit(solution)/shard_map/ppermute | solution.py:38
  37.9 2.8 %collective-permute-done.9 = bf16[16,2176]{1,0:T(8,128)(2,1)S(1)} collective-permute-done((bf16[16,2176]{1,0:T(8,128)(2,1)S(1)}, bf16[16,2176]{1,0:T(8,128)(2,1)S(1)}, u32[]{:S(2)}, u32[]{:S(2)}) %collective-permute-start.9) | collective-permute-done | bytes 69664 | tf_op jit(solution)/shard_map/ppermute | solution.py:38
  41.6 1.8 %collective-permute-start.11 = (bf16[16,2176]{1,0:T(8,128)(2,1)S(1)}, bf16[16,2176]{1,0:T(8,128)(2,1)S(1)}, u32[]{:S(2)}, u32[]{:S(2)}) collective-permute-start(bf16[16,2176]{1,0:T(8,128)(2,1)S(1)} %add_convert_fusion.2), channel_id=1, source_target_pairs={{0,2},{1,3},{2,0},{3,1},{4,6},{5,7},{6,4},{7,5},{8,10},{9,11},{10,... | collective-permute-start | bytes 208904 | tf_op jit(solution)/shard_map/ppermute | solution.py:38
  43.4 2.6 %collective-permute-done.11 = bf16[16,2176]{1,0:T(8,128)(2,1)S(1)} collective-permute-done((bf16[16,2176]{1,0:T(8,128)(2,1)S(1)}, bf16[16,2176]{1,0:T(8,128)(2,1)S(1)}, u32[]{:S(2)}, u32[]{:S(2)}) %collective-permute-start.11) | collective-permute-done | bytes 69664 | tf_op jit(solution)/shard_map/ppermute | solution.py:38
  46.0 2.7 %collective-permute-start.14 = (bf16[16,2176]{1,0:T(8,128)(2,1)S(1)}, bf16[16,2176]{1,0:T(8,128)(2,1)S(1)}, u32[]{:S(2)}, u32[]{:S(2)}) collective-permute-start(bf16[16,2176]{1,0:T(8,128)(2,1)S(1)} %add_convert_fusion.1.refs_0_), channel_id=1, source_target_pairs={{0,12},{1,13},{2,14},{3,15},{4,8},{5,9},{6,10},{7,11},{8,4},{9,5},... | collective-permute-start | bytes 208904 | tf_op jit(solution)/shard_map/ppermute | solution.py:38
  48.8 1.6 %collective-permute-start.12 = (bf16[16,2176]{1,0:T(8,128)(2,1)S(1)}, bf16[16,2176]{1,0:T(8,128)(2,1)S(1)}, u32[]{:S(2)}, u32[]{:S(2)}) collective-permute-start(bf16[16,2176]{1,0:T(8,128)(2,1)S(1)} %add_convert_fusion.1.refs_0_), channel_id=1, source_target_pairs={{0,4},{1,5},{2,6},{3,7},{4,0},{5,1},{6,2},{7,3},{8,12},{9,13},{10,... | collective-permute-start | bytes 208904 | tf_op jit(solution)/shard_map/ppermute | solution.py:38
  50.4 1.7 %collective-permute-done.14.refs_3_ = bf16[16,2176]{1,0:T(8,128)(2,1)S(1)} collective-permute-done((bf16[16,2176]{1,0:T(8,128)(2,1)S(1)}, bf16[16,2176]{1,0:T(8,128)(2,1)S(1)}, u32[]{:S(2)}, u32[]{:S(2)}) %collective-permute-start.14) | collective-permute-done | bytes 69664 | tf_op jit(solution)/shard_map/ppermute | solution.py:38
  52.1 1.7 %collective-permute-done.13.refs_2_ = bf16[16,2176]{1,0:T(8,128)(2,1)S(1)} collective-permute-done((bf16[16,2176]{1,0:T(8,128)(2,1)S(1)}, bf16[16,2176]{1,0:T(8,128)(2,1)S(1)}, u32[]{:S(2)}, u32[]{:S(2)}) %collective-permute-start.13) | collective-permute-done | bytes 69664 | tf_op jit(solution)/shard_map/ppermute | solution.py:38
  54.4 3.7 %fetch.5 = (bf16[1,2048,1536]{2,1,0:T(8,128)(2,1)S(1)}, bf16[1,768,2048]{2,1,0:T(8,128)(2,1)S(1)}) custom-call(bf16[1,2048,1536]{2,1,0:T(8,128)(2,1)} %refs_0_.5, bf16[1,768,2048]{2,1,0:T(8,128)(2,1)} %refs_1_.2), custom_call_target="tpu_custom_call" | custom-call | bytes 18874368 | tf_op jit(solution)/shard_map/fetch/pallas_call | solution.py:71
  58.2 2.1 %experts.1 = (bf16[64,2304]{1,0:T(8,128)(2,1)S(1)}, bf16[64,2304]{1,0:T(8,128)(2,1)S(1)}, bf16[64,2304]{1,0:T(8,128)(2,1)S(1)}, bf16[64,2304]{1,0:T(8,128)(2,1)S(1)}, bf16[16,2048]{1,0:T(8,128)(2,1)S(1)}) custom-call(bf16[16,2176]{1,0:T(8,128)(2,1)S(1)} %add_convert_fusion.1.refs_0_, bf16[16,2176]{1,0:T(8,128)(2,1)S(1)} %collective-permute-done.12.refs_1_, ...), custom_call_target="tpu_custom_call" | custom-call | flops 1207959552 | bytes 9437184 | tf_op jit(solution)/shard_map/experts/pallas_call | solution.py:348
  60.9 1.1 %collective-permute-done.20 = bf16[64,2304]{1,0:T(8,128)(2,1)S(1)} collective-permute-done((bf16[64,2304]{1,0:T(8,128)(2,1)S(1)}, bf16[64,2304]{1,0:T(8,128)(2,1)S(1)}, u32[]{:S(2)}, u32[]{:S(2)}) %collective-permute-start.20) | collective-permute-done | bytes 294944 | tf_op jit(solution)/shard_map/ppermute | solution.py:38
  62.0 1.6 %collective-permute-start.21 = (bf16[64,2304]{1,0:T(8,128)(2,1)S(1)}, bf16[64,2304]{1,0:T(8,128)(2,1)S(1)}, u32[]{:S(2)}, u32[]{:S(2)}) collective-permute-start(bf16[64,2304]{1,0:T(8,128)(2,1)S(1)} %add_convert_fusion), channel_id=1, source_target_pairs={{0,2},{1,3},{2,0},{3,1},{4,6},{5,7},{6,4},{7,5},{8,10},{9,11},{10,... | collective-permute-start | bytes 884744 | tf_op jit(solution)/shard_map/ppermute | solution.py:38
  63.6 7.6 %collective-permute-done.21.far = bf16[64,2304]{1,0:T(8,128)(2,1)S(1)} collective-permute-done((bf16[64,2304]{1,0:T(8,128)(2,1)S(1)}, bf16[64,2304]{1,0:T(8,128)(2,1)S(1)}, u32[]{:S(2)}, u32[]{:S(2)}) %collective-permute-start.21) | collective-permute-done | bytes 294944 | tf_op jit(solution)/shard_map/ppermute | solution.py:38
  71.2 0.8 collective-permute-start.22
  72.0 2.2 %collective-permute-start.23 = (bf16[16,2560]{1,0:T(8,128)(2,1)S(1)}, bf16[16,2560]{1,0:T(8,128)(2,1)S(1)}, u32[]{:S(2)}, u32[]{:S(2)}) collective-permute-start(bf16[16,2560]{1,0:T(8,128)(2,1)S(1)} %get-tuple-element.50), channel_id=1, source_target_pairs={{0,8},{1,9},{2,10},{3,11},{4,12},{5,13},{6,14},{7,15},{8,0},{9,1},... | collective-permute-start | bytes 245768 | tf_op jit(solution)/shard_map/ppermute | solution.py:38
  74.2 1.4 %collective-permute-start.24 = (bf16[16,2560]{1,0:T(8,128)(2,1)S(1)}, bf16[16,2560]{1,0:T(8,128)(2,1)S(1)}, u32[]{:S(2)}, u32[]{:S(2)}) collective-permute-start(bf16[16,2560]{1,0:T(8,128)(2,1)S(1)} %get-tuple-element.51), channel_id=1, source_target_pairs={{0,12},{1,13},{2,14},{3,15},{4,8},{5,9},{6,10},{7,11},{8,4},{9,5},... | collective-permute-start | bytes 245768 | tf_op jit(solution)/shard_map/ppermute | solution.py:38
  75.7 0.8 %collective-permute-done.22.refs_1_ = bf16[16,2560]{1,0:T(8,128)(2,1)S(1)} collective-permute-done((bf16[16,2560]{1,0:T(8,128)(2,1)S(1)}, bf16[16,2560]{1,0:T(8,128)(2,1)S(1)}, u32[]{:S(2)}, u32[]{:S(2)}) %collective-permute-start.22) | collective-permute-done | bytes 81952 | tf_op jit(solution)/shard_map/ppermute | solution.py:38
  76.5 4.4 %collective-permute-done.23.refs_2_ = bf16[16,2560]{1,0:T(8,128)(2,1)S(1)} collective-permute-done((bf16[16,2560]{1,0:T(8,128)(2,1)S(1)}, bf16[16,2560]{1,0:T(8,128)(2,1)S(1)}, u32[]{:S(2)}, u32[]{:S(2)}) %collective-permute-start.23) | collective-permute-done | bytes 81952 | tf_op jit(solution)/shard_map/ppermute | solution.py:38
  (37 shorter events, 6.2 us)
Async XLA Ops:
  0.6 5.2 %collective-permute-start = (bf16[8,2048]{1,0:T(8,128)(2,1)}, bf16[8,2048]{1,0:T(8,128)(2,1)S(1)}, u32[]{:S(2)}, u32[]{:S(2)}) collective-permute-start(bf16[8,2048]{1,0:T(8,128)(2,1)} %param.13), channel_id=1, source_target_pairs={{0,2},{1,3},{2,0},{3,1},{4,6},{5,7},{6,4},{7,5},{8,10},{9,11},{10,... | collective-permute-start | bytes 98312 | tf_op jit(solution)/shard_map/ppermute | solution.py:38
  3.7 12.2 %collective-permute-start.4 = (bf16[1,512,256]{2,1,0:T(8,128)(2,1)}, bf16[1,512,256]{2,1,0:T(8,128)(2,1)S(1)}, u32[]{:S(2)}, u32[]{:S(2)}) collective-permute-start(bf16[1,512,256]{2,1,0:T(8,128)(2,1)} %refs_0_.3), channel_id=1, source_target_pairs={{0,1},{1,0},{2,3},{3,2},{4,5},{5,4},{6,7},{7,6},{8,9},{9,8},{10,11... | collective-permute-start | bytes 786440 | tf_op jit(solution)/shard_map/ppermute | solution.py:38
  3.7 12.2 %collective-permute-start.5 = (bf16[1,512,256]{2,1,0:T(8,128)(2,1)}, bf16[1,512,256]{2,1,0:T(8,128)(2,1)S(1)}, u32[]{:S(2)}, u32[]{:S(2)}) collective-permute-start(bf16[1,512,256]{2,1,0:T(8,128)(2,1)} %refs_1_.1), channel_id=1, source_target_pairs={{0,1},{1,0},{2,3},{3,2},{4,5},{5,4},{6,7},{7,6},{8,9},{9,8},{10,11... | collective-permute-start | bytes 786440 | tf_op jit(solution)/shard_map/ppermute | solution.py:38
  6.6 6.5 %collective-permute-start.3 = (bf16[2,8,2048]{2,1,0:T(8,128)(2,1)S(1)}, bf16[2,8,2048]{2,1,0:T(8,128)(2,1)S(1)}, u32[]{:S(2)}, u32[]{:S(2)}) collective-permute-start(bf16[2,8,2048]{2,1,0:T(8,128)(2,1)S(1)} %pad_maximum_fusion.refs_0_), channel_id=1, source_target_pairs={{0,12},{1,13},{2,14},{3,15},{4,8},{5,9},{6,10},{7,11},{8,4},{9,5},... | collective-permute-start | bytes 196616 | tf_op jit(solution)/shard_map/ppermute | solution.py:38
  10.7 5.2 %collective-permute-start.2 = (bf16[2,8,2048]{2,1,0:T(8,128)(2,1)S(1)}, bf16[2,8,2048]{2,1,0:T(8,128)(2,1)S(1)}, u32[]{:S(2)}, u32[]{:S(2)}) collective-permute-start(bf16[2,8,2048]{2,1,0:T(8,128)(2,1)S(1)} %pad_maximum_fusion.refs_0_), channel_id=1, source_target_pairs={{0,8},{1,9},{2,10},{3,11},{4,12},{5,13},{6,14},{7,15},{8,0},{9,1},... | collective-permute-start | bytes 196616 | tf_op jit(solution)/shard_map/ppermute | solution.py:38
  10.7 5.2 %collective-permute-start.1 = (bf16[2,8,2048]{2,1,0:T(8,128)(2,1)S(1)}, bf16[2,8,2048]{2,1,0:T(8,128)(2,1)S(1)}, u32[]{:S(2)}, u32[]{:S(2)}) collective-permute-start(bf16[2,8,2048]{2,1,0:T(8,128)(2,1)S(1)} %pad_maximum_fusion.refs_0_), channel_id=1, source_target_pairs={{0,4},{1,5},{2,6},{3,7},{4,0},{5,1},{6,2},{7,3},{8,12},{9,13},{10,... | collective-permute-start | bytes 196616 | tf_op jit(solution)/shard_map/ppermute | solution.py:38
  13.1 15.7 %collective-permute-start.6 = (bf16[128,2048]{1,0:T(8,128)(2,1)}, bf16[128,2048]{1,0:T(8,128)(2,1)S(1)}, u32[]{:S(2)}, u32[]{:S(2)}) collective-permute-start(bf16[128,2048]{1,0:T(8,128)(2,1)} %refs_0_.4), channel_id=1, source_target_pairs={{0,1},{1,0},{2,3},{3,2},{4,5},{5,4},{6,7},{7,6},{8,9},{9,8},{10,11... | collective-permute-start | bytes 1572872 | tf_op jit(solution)/shard_map/ppermute | solution.py:38
  19.8 13.1 %all-to-all-start = ((bf16[8,136,128]{2,1,0:T(8,128)(2,1)}), bf16[8,136,128]{2,1,0:T(8,128)(2,1)S(1)}, u32[]{:S(2)}, u32[]{:S(2)}) async-start(bf16[8,136,128]{2,1,0:T(8,128)(2,1)} %attention.1), calls=%async_computation | async-start | bytes 557056 | tf_op jit(solution)/shard_map/all_to_all | solution.py:478
  25.7 0.7 copy-start
  27.4 1.3 %collective-permute-start.7 = (bf16[16,2176]{1,0:T(8,128)(2,1)S(1)}, bf16[16,2176]{1,0:T(8,128)(2,1)S(1)}, u32[]{:S(2)}, u32[]{:S(2)}) collective-permute-start(bf16[16,2176]{1,0:T(8,128)(2,1)S(1)} %get-tuple-element.30.res_own), channel_id=1, source_target_pairs={{0,1},{1,0},{2,3},{3,2},{4,5},{5,4},{6,7},{7,6},{8,9},{9,8},{10,11... | collective-permute-start | bytes 208904 | tf_op jit(solution)/shard_map/ppermute | solution.py:38
  33.5 4.5 %collective-permute-start.8 = (bf16[16,2176]{1,0:T(8,128)(2,1)S(1)}, bf16[16,2176]{1,0:T(8,128)(2,1)S(1)}, u32[]{:S(2)}, u32[]{:S(2)}) collective-permute-start(bf16[16,2176]{1,0:T(8,128)(2,1)S(1)} %get-tuple-element.33), channel_id=1, source_target_pairs={{0,4},{1,5},{2,6},{3,7},{4,0},{5,1},{6,2},{7,3},{8,12},{9,13},{10,... | collective-permute-start | bytes 208904 | tf_op jit(solution)/shard_map/ppermute | solution.py:38
  34.7 6.1 %collective-permute-start.9 = (bf16[16,2176]{1,0:T(8,128)(2,1)S(1)}, bf16[16,2176]{1,0:T(8,128)(2,1)S(1)}, u32[]{:S(2)}, u32[]{:S(2)}) collective-permute-start(bf16[16,2176]{1,0:T(8,128)(2,1)S(1)} %get-tuple-element.34), channel_id=1, source_target_pairs={{0,8},{1,9},{2,10},{3,11},{4,12},{5,13},{6,14},{7,15},{8,0},{9,1},... | collective-permute-start | bytes 208904 | tf_op jit(solution)/shard_map/ppermute | solution.py:38
  35.3 6.2 %collective-permute-start.10 = (bf16[16,2176]{1,0:T(8,128)(2,1)S(1)}, bf16[16,2176]{1,0:T(8,128)(2,1)S(1)}, u32[]{:S(2)}, u32[]{:S(2)}) collective-permute-start(bf16[16,2176]{1,0:T(8,128)(2,1)S(1)} %get-tuple-element.35), channel_id=1, source_target_pairs={{0,12},{1,13},{2,14},{3,15},{4,8},{5,9},{6,10},{7,11},{8,4},{9,5},... | collective-permute-start | bytes 208904 | tf_op jit(solution)/shard_map/ppermute | solution.py:38
  41.6 4.4 %collective-permute-start.11 = (bf16[16,2176]{1,0:T(8,128)(2,1)S(1)}, bf16[16,2176]{1,0:T(8,128)(2,1)S(1)}, u32[]{:S(2)}, u32[]{:S(2)}) collective-permute-start(bf16[16,2176]{1,0:T(8,128)(2,1)S(1)} %add_convert_fusion.2), channel_id=1, source_target_pairs={{0,2},{1,3},{2,0},{3,1},{4,6},{5,7},{6,4},{7,5},{8,10},{9,11},{10,... | collective-permute-start | bytes 208904 | tf_op jit(solution)/shard_map/ppermute | solution.py:38
  46.0 6.2 %collective-permute-start.14 = (bf16[16,2176]{1,0:T(8,128)(2,1)S(1)}, bf16[16,2176]{1,0:T(8,128)(2,1)S(1)}, u32[]{:S(2)}, u32[]{:S(2)}) collective-permute-start(bf16[16,2176]{1,0:T(8,128)(2,1)S(1)} %add_convert_fusion.1.refs_0_), channel_id=1, source_target_pairs={{0,12},{1,13},{2,14},{3,15},{4,8},{5,9},{6,10},{7,11},{8,4},{9,5},... | collective-permute-start | bytes 208904 | tf_op jit(solution)/shard_map/ppermute | solution.py:38
  48.7 5.2 %collective-permute-start.13 = (bf16[16,2176]{1,0:T(8,128)(2,1)S(1)}, bf16[16,2176]{1,0:T(8,128)(2,1)S(1)}, u32[]{:S(2)}, u32[]{:S(2)}) collective-permute-start(bf16[16,2176]{1,0:T(8,128)(2,1)S(1)} %add_convert_fusion.1.refs_0_), channel_id=1, source_target_pairs={{0,8},{1,9},{2,10},{3,11},{4,12},{5,13},{6,14},{7,15},{8,0},{9,1},... | collective-permute-start | bytes 208904 | tf_op jit(solution)/shard_map/ppermute | solution.py:38
  48.8 5.1 %collective-permute-start.12 = (bf16[16,2176]{1,0:T(8,128)(2,1)S(1)}, bf16[16,2176]{1,0:T(8,128)(2,1)S(1)}, u32[]{:S(2)}, u32[]{:S(2)}) collective-permute-start(bf16[16,2176]{1,0:T(8,128)(2,1)S(1)} %add_convert_fusion.1.refs_0_), channel_id=1, source_target_pairs={{0,4},{1,5},{2,6},{3,7},{4,0},{5,1},{6,2},{7,3},{8,12},{9,13},{10,... | collective-permute-start | bytes 208904 | tf_op jit(solution)/shard_map/ppermute | solution.py:38
  50.4 7.7 %collective-permute-start.15 = (bf16[16,2176]{1,0:T(8,128)(2,1)S(1)}, bf16[16,2176]{1,0:T(8,128)(2,1)S(1)}, u32[]{:S(2)}, u32[]{:S(2)}) collective-permute-start(bf16[16,2176]{1,0:T(8,128)(2,1)S(1)} %add_convert_fusion.1.refs_0_), channel_id=1, source_target_pairs={{0,1},{1,0},{2,3},{3,2},{4,5},{5,4},{6,7},{7,6},{8,9},{9,8},{10,11... | collective-permute-start | bytes 208904 | tf_op jit(solution)/shard_map/ppermute | solution.py:38
  52.1 6.0 %collective-permute-start.18 = (bf16[16,2176]{1,0:T(8,128)(2,1)S(1)}, bf16[16,2176]{1,0:T(8,128)(2,1)S(1)}, u32[]{:S(2)}, u32[]{:S(2)}) collective-permute-start(bf16[16,2176]{1,0:T(8,128)(2,1)S(1)} %collective-permute-done.14.refs_3_), channel_id=1, source_target_pairs={{0,1},{1,0},{2,3},{3,2},{4,5},{5,4},{6,7},{7,6},{8,9},{9,8},{10,11... | collective-permute-start | bytes 208904 | tf_op jit(solution)/shard_map/ppermute | solution.py:38
  53.9 4.3 %collective-permute-start.17 = (bf16[16,2176]{1,0:T(8,128)(2,1)S(1)}, bf16[16,2176]{1,0:T(8,128)(2,1)S(1)}, u32[]{:S(2)}, u32[]{:S(2)}) collective-permute-start(bf16[16,2176]{1,0:T(8,128)(2,1)S(1)} %collective-permute-done.13.refs_2_), channel_id=1, source_target_pairs={{0,1},{1,0},{2,3},{3,2},{4,5},{5,4},{6,7},{7,6},{8,9},{9,8},{10,11... | collective-permute-start | bytes 208904 | tf_op jit(solution)/shard_map/ppermute | solution.py:38
  53.9 4.3 %collective-permute-start.16 = (bf16[16,2176]{1,0:T(8,128)(2,1)S(1)}, bf16[16,2176]{1,0:T(8,128)(2,1)S(1)}, u32[]{:S(2)}, u32[]{:S(2)}) collective-permute-start(bf16[16,2176]{1,0:T(8,128)(2,1)S(1)} %collective-permute-done.12.refs_1_), channel_id=1, source_target_pairs={{0,1},{1,0},{2,3},{3,2},{4,5},{5,4},{6,7},{7,6},{8,9},{9,8},{10,11... | collective-permute-start | bytes 208904 | tf_op jit(solution)/shard_map/ppermute | solution.py:38
  60.3 1.6 %collective-permute-start.20 = (bf16[64,2304]{1,0:T(8,128)(2,1)S(1)}, bf16[64,2304]{1,0:T(8,128)(2,1)S(1)}, u32[]{:S(2)}, u32[]{:S(2)}) collective-permute-start(bf16[64,2304]{1,0:T(8,128)(2,1)S(1)} %get-tuple-element.47), channel_id=1, source_target_pairs={{0,1},{1,0},{2,3},{3,2},{4,5},{5,4},{6,7},{7,6},{8,9},{9,8},{10,11... | collective-permute-start | bytes 884744 | tf_op jit(solution)/shard_map/ppermute | solution.py:38
  60.4 3.2 %collective-permute-start.19 = (bf16[64,2304]{1,0:T(8,128)(2,1)S(1)}, bf16[64,2304]{1,0:T(8,128)(2,1)S(1)}, u32[]{:S(2)}, u32[]{:S(2)}) collective-permute-start(bf16[64,2304]{1,0:T(8,128)(2,1)S(1)} %get-tuple-element.45), channel_id=1, source_target_pairs={{0,1},{1,0},{2,3},{3,2},{4,5},{5,4},{6,7},{7,6},{8,9},{9,8},{10,11... | collective-permute-start | bytes 884744 | tf_op jit(solution)/shard_map/ppermute | solution.py:38
  62.0 9.1 %collective-permute-start.21 = (bf16[64,2304]{1,0:T(8,128)(2,1)S(1)}, bf16[64,2304]{1,0:T(8,128)(2,1)S(1)}, u32[]{:S(2)}, u32[]{:S(2)}) collective-permute-start(bf16[64,2304]{1,0:T(8,128)(2,1)S(1)} %add_convert_fusion), channel_id=1, source_target_pairs={{0,2},{1,3},{2,0},{3,1},{4,6},{5,7},{6,4},{7,5},{8,10},{9,11},{10,... | collective-permute-start | bytes 884744 | tf_op jit(solution)/shard_map/ppermute | solution.py:38
  71.2 5.3 %collective-permute-start.22 = (bf16[16,2560]{1,0:T(8,128)(2,1)S(1)}, bf16[16,2560]{1,0:T(8,128)(2,1)S(1)}, u32[]{:S(2)}, u32[]{:S(2)}) collective-permute-start(bf16[16,2560]{1,0:T(8,128)(2,1)S(1)} %get-tuple-element.49), channel_id=1, source_target_pairs={{0,4},{1,5},{2,6},{3,7},{4,0},{5,1},{6,2},{7,3},{8,12},{9,13},{10,... | collective-permute-start | bytes 245768 | tf_op jit(solution)/shard_map/ppermute | solution.py:38
  72.0 8.9 %collective-permute-start.23 = (bf16[16,2560]{1,0:T(8,128)(2,1)S(1)}, bf16[16,2560]{1,0:T(8,128)(2,1)S(1)}, u32[]{:S(2)}, u32[]{:S(2)}) collective-permute-start(bf16[16,2560]{1,0:T(8,128)(2,1)S(1)} %get-tuple-element.50), channel_id=1, source_target_pairs={{0,8},{1,9},{2,10},{3,11},{4,12},{5,13},{6,14},{7,15},{8,0},{9,1},... | collective-permute-start | bytes 245768 | tf_op jit(solution)/shard_map/ppermute | solution.py:38
  74.2 6.7 %collective-permute-start.24 = (bf16[16,2560]{1,0:T(8,128)(2,1)S(1)}, bf16[16,2560]{1,0:T(8,128)(2,1)S(1)}, u32[]{:S(2)}, u32[]{:S(2)}) collective-permute-start(bf16[16,2560]{1,0:T(8,128)(2,1)S(1)} %get-tuple-element.51), channel_id=1, source_target_pairs={{0,12},{1,13},{2,14},{3,15},{4,8},{5,9},{6,10},{7,11},{8,4},{9,5},... | collective-permute-start | bytes 245768 | tf_op jit(solution)/shard_map/ppermute | solution.py:38
where the time goes:
time: 82 us; the launch traced here: 81.6 us
  waiting for transfers between devices  32.3 us (39%)
  starting transfers between devices  30.5 us (37%)
  Pallas kernels  14.3 us (17%)
  local copies, waits for them, and re-layouts  2.17 us (3%)
  between operations  1.41 us (2%)
  other arithmetic  0.89 us (1%)
    ppermute x25, waiting for transfers between devices, hop(): return lax.ppermute(x, 'ctx', [(i, i ^ mask) for i in range(width)])  28.1 us
    ppermute x25, starting transfers between devices, hop(): return lax.ppermute(x, 'ctx', [(i, i ^ mask) for i in range(width)])  26.2 us
    pallas_call x3, Pallas kernels, fetch(): pl.pallas_call(functools.partial(fetch_kernel, count), out_shape=[pltpu.V...  5.83 us
    all_to_all x1, starting transfers between devices, body(): lax.all_to_all(partial, 'ctx', split_axis=0, concat_axis=0, tiled=True, a...  4.33 us
    all_to_all x1, waiting for transfers between devices, body(): lax.all_to_all(partial, 'ctx', split_axis=0, concat_axis=0, tiled=True, a...  4.22 us
    pallas_call x1, Pallas kernels, attention(): pl.pallas_call(functools.partial(attention_kernel, nz), out_shape=jax.Sha...  3.96 us
    unnamed x4, local copies, waits for them, and re-layouts  2.17 us
    pallas_call x1, Pallas kernels, experts(): pl.pallas_call(functools.partial(expert_kernel, nz, width), out_shape=[wi...  2.12 us
  transfers between devices with their start and end apart: 26, of which 14 were waited for; matrix products, arithmetic and copies ran while one was open for 3% of the time, Pallas kernels for 13%

commit v1 on v0

--- a/solution.py
+++ b/solution.py
@@ -18,6 +18,7 @@
 BF = jnp.bfloat16
 F32 = jnp.float32
 MIB = 1 << 20
+LOG2E = 1.4426950408889634
 STAT = 8
 
 
@@ -80,17 +81,32 @@
     )(*[in_hbm(a) for a in arrays])
 
 
-def prepare_kernel(per, width, counts, order, ids, weights, residual, res, home, fill, turn, picks, table, own):
+def prepare_kernel(per, width, *refs):
+    (counts, order, ids, weights, residual, weight_in, gain_in) = refs[:7]
+    (res, home, fill, turn, weight_out, gain_out) = refs[7:13]
+    picks, table, own, sems = refs[13:]
+    copies = [
+        pltpu.make_async_copy(weight_in, weight_out, sems.at[0]),
+        pltpu.make_async_copy(gain_in, gain_out, sems.at[1]),
+    ]
+    for copy in copies:
+        copy.start()
     device, core, _, _ = place()
     cap, rows = residual.shape[0], order.shape[1]
     half = home.shape[0]
-    p = lax.broadcasted_iota(jnp.int32, (cap, rows), 1)
-    j = lax.broadcasted_iota(jnp.int32, (cap, rows), 0)
-    start = jnp.int32(0)
-    for o in range(width):
-        hit = (p - start == j) & (j < counts[o])
-        picks[o * cap : (o + 1) * cap, :] = hit.astype(F32).astype(BF)
-        start = start + counts[o]
+    slots = picks.shape[0]
+    lane = lax.broadcasted_iota(jnp.int32, (width, width), 1)
+    line = lax.broadcasted_iota(jnp.int32, (width, width), 0)
+    many = counts[...].astype(F32)
+    end = jnp.sum(jnp.where(lane <= line, many, 0.0), axis=1, keepdims=True)
+    size = jnp.sum(jnp.where(lane == line, many, 0.0), axis=1, keepdims=True)
+    p = lax.broadcasted_iota(jnp.int32, (width, rows), 1).astype(F32)
+    past = (p >= end).astype(F32)
+    owner = jnp.sum(past, axis=0, keepdims=True)
+    start = jnp.sum(past * size, axis=0, keepdims=True)
+    slot = owner * cap + p[:1] - start
+    at = lax.broadcasted_iota(jnp.int32, (slots, rows), 0).astype(F32)
+    picks[...] = (at == slot).astype(F32).astype(BF)
     seats = [
         (order[...] == row_ids(per, c, 0, (half, rows))).astype(F32).astype(BF)
         for c in range(2)
@@ -101,9 +117,9 @@
     for kc in range(2):
         for ky in range(2):
             for kz in range(width // 4):
-                owner = device ^ (kc + 2 * ky + 4 * kz)
+                there = device ^ (kc + 2 * ky + 4 * kz)
+                there = pl.ds(pl.multiple_of(there * cap, cap), cap)
                 to = (kc * 2 + ky) * (width // 4) + kz
-                there = pl.ds(pl.multiple_of(owner * cap, cap), cap)
                 turn[to * cap : (to + 1) * cap, :] = table[there, :]
                 fill[to * cap : (to + 1) * cap, :] = own[there, :]
     chip_picks = [
@@ -111,23 +127,28 @@
     ]
     home[...] = dot(mine, jnp.concatenate(chip_picks, axis=0), NT).astype(BF)
     lanes = res.shape[1] - D
-    lane = lax.broadcasted_iota(jnp.int32, (cap, lanes), 1)
-    norm = weights[...] / jnp.sum(weights[...], axis=-1, keepdims=True)
-    dense = jnp.zeros((cap, lanes), F32)
+    kind = lax.broadcasted_iota(jnp.int32, (lanes, cap), 0)
+    norm = weights[...] / jnp.sum(weights[...], axis=0, keepdims=True)
+    dense = jnp.zeros((lanes, cap), F32)
     for k in range(TOPK):
-        hit = ids[:, k : k + 1] == lane % width
-        dense = dense + jnp.where(hit, norm[:, k : k + 1], 0.0)
+        dense = dense + jnp.where(ids[k : k + 1, :] == kind % width, norm[k : k + 1, :], 0.0)
     high = dense.astype(BF).astype(F32)
-    low = jnp.where(lane < 2 * width, dense - high, 0.0)
+    low = jnp.where(kind < 2 * width, dense - high, 0.0)
+    both = jnp.where(kind < width, high, low).astype(BF)
+    i = lax.broadcasted_iota(jnp.int32, (cap, cap), 0)
+    j = lax.broadcasted_iota(jnp.int32, (cap, cap), 1)
     res[:, :D] = residual[...]
-    res[:, D:] = jnp.where(lane < width, high, low).astype(BF)
-
-
-def prepare(counts, order, ids, weights, residual, per, width):
+    res[:, D:] = dot((i == j).astype(F32).astype(BF), both, NT).astype(BF)
+    for copy in copies:
+        copy.wait()
+
+
+def prepare(counts, order, ids, weights, residual, out_weight, gain, per, width):
     cap, rows = residual.shape[0], order.shape[1]
     half = width // 2 * per
     lanes = -(-2 * width // 128) * 128
     slots = width * cap
+    given = (counts, order, ids, weights, residual, out_weight, gain)
     return pl.pallas_call(
         functools.partial(prepare_kernel, per, width),
         out_shape=[
@@ -135,21 +156,49 @@
             jax.ShapeDtypeStruct((half, 2 * cap), BF),
             jax.ShapeDtypeStruct((slots, half), BF),
             jax.ShapeDtypeStruct((slots, 2 * half), BF),
+            pltpu.VMEM(out_weight.shape, out_weight.dtype),
+            pltpu.VMEM(gain.shape, gain.dtype),
         ],
-        in_specs=[pl.BlockSpec(memory_space=pltpu.SMEM)]
-        + [pl.BlockSpec(memory_space=pltpu.VMEM)] * 4,
-        out_specs=[pl.BlockSpec(memory_space=pltpu.VMEM)] * 4,
+        in_specs=[pl.BlockSpec(memory_space=pltpu.VMEM)] * 5
+        + [pl.BlockSpec(memory_space=pltpu.HBM)] * 2,
+        out_specs=[pl.BlockSpec(memory_space=pltpu.VMEM)] * 6,
         scratch_shapes=[
             pltpu.VMEM((slots, rows), BF),
             pltpu.VMEM((slots, 2 * half), BF),
             pltpu.VMEM((slots, half), BF),
+            pltpu.SemaphoreType.DMA((2,)),
         ],
         cost_estimate=pl.CostEstimate(
             flops=6 * slots * rows * half, bytes_accessed=8 * slots * half, transcendentals=0
         ),
-        compiler_params=pltpu.CompilerParams(vmem_limit_bytes=8 * MIB),
+        compiler_params=pltpu.CompilerParams(vmem_limit_bytes=12 * MIB),
         name="prepare",
-    )(counts, in_hbm(order), ids, weights, in_hbm(residual))
+    )(*[in_hbm(a) for a in given])
+
+
+def total_kernel(*refs):
+    terms, out = refs[:-1], refs[-1]
+    out[...] = functools.reduce(lambda a, b: a + b, [t[...].astype(F32) for t in terms]).astype(BF)
+
+
+def pair_kernel(first, second, out):
+    out[0] = first[...]
+    out[1] = second[...]
+
+
+def small(kernel, shape, *terms):
+    return pl.pallas_call(
+        kernel,
+        out_shape=jax.ShapeDtypeStruct(shape, BF),
+        in_specs=[pl.BlockSpec(memory_space=pltpu.VMEM)] * len(terms),
+        out_specs=pl.BlockSpec(memory_space=pltpu.VMEM),
+        cost_estimate=pl.CostEstimate(
+            flops=len(terms) * terms[0].size,
+            bytes_accessed=2 * (len(terms) + 1) * terms[0].size,
+            transcendentals=0,
+        ),
+        compiler_params=pltpu.CompilerParams(vmem_limit_bytes=16 * MIB),
+    )(*terms)
 
 
 def attention_kernel(nz, lengths, *refs):
@@ -186,21 +235,22 @@
                 ],
                 axis=0,
             ).astype(BF)
-            s_own = dot(k_own[q, :, kv], pair, NT) * HD ** (-0.5)
-            s_oth = dot(k_oth[q, :, kv], pair, NT) * HD ** (-0.5)
+            s_own = dot(k_own[q, :, kv], pair, NT) * (HD ** (-0.5) * LOG2E)
+            s_oth = dot(k_oth[q, :, kv], pair, NT) * (HD ** (-0.5) * LOG2E)
             s_own = jnp.where(see_own, s_own, -1e30)
             s_oth = jnp.where(see_oth, s_oth, -1e30)
             top = jnp.maximum(
                 jnp.max(s_own, axis=0, keepdims=True), jnp.max(s_oth, axis=0, keepdims=True)
             )
-            w_own = jnp.where(see_own, jnp.exp(s_own - top), 0.0)
-            w_oth = jnp.where(see_oth, jnp.exp(s_oth - top), 0.0)
+            top = jnp.maximum(top, -1e29)
+            w_own = jnp.exp2(s_own - top)
+            w_oth = jnp.exp2(s_oth - top)
             total = jnp.sum(w_own, axis=0, keepdims=True) + jnp.sum(w_oth, axis=0, keepdims=True)
             mixed = dot(vt_own, w_own.astype(BF), NN) + dot(vt_oth, w_oth.astype(BF), NN)
             some = total > 0.0
             safe = jnp.where(some, total, 1.0)
             mixed = (mixed / safe).astype(BF)
-            lse = jnp.where(some, top + jnp.log(safe), -1e30)
+            lse = jnp.where(some, top * (1.0 / LOG2E) + jnp.log(safe), -1e30)
             hi, mid, low = split3(lse)
             stat = jnp.concatenate(
                 [hi.astype(F32), mid.astype(F32), low.astype(F32)]
@@ -461,16 +511,25 @@
         return out
 
     def add(*terms):
-        return functools.reduce(lambda a, b: a + b, [t.astype(F32) for t in terms]).astype(BF)
+        return small(total_kernel, terms[0].shape, *terms)
 
     near = hop(queries, 2, width)
-    k_oth, v_oth = hop(keys, 1, width), hop(values, 1, width)
-    column = jnp.stack([queries, near])
+    k_oth = hop(keys, 1, width)
+    v_oth = hop(values, 1, width)
+    q_own, k_own, v_own = fetch(queries, keys, values)
+    column = small(pair_kernel, (2,) + queries.shape, q_own, near)
     pieces = along_z([column] * nz)
-    k_own, v_own = fetch(keys, values)
     w_oth = hop(out_weight, 1, width)
-    res_own, home, fill, turn = prepare(
-        owner_counts, order, expert_ids, route_weights, residual, per, width
+    res_own, home, fill, turn, w_own, gain = prepare(
+        owner_counts.reshape(1, -1),
+        order,
+        expert_ids.T,
+        route_weights.T,
+        residual,
+        out_weight,
+        norm_gain.reshape(1, -1),
+        per,
+        width,
     )
     res_oth = hop(res_own, 1, width)
 
@@ -478,13 +537,14 @@
     got = lax.all_to_all(
         partial, "ctx", split_axis=0, concat_axis=0, tiled=True, axis_index_groups=same_core
     )
-    w_own, gain = fetch(out_weight, norm_gain.reshape(1, -1))
     *parts, mixed = project(got, w_own, w_oth, res_own, res_oth, home, nz)
     chunk = add(*along_z(parts))
-    chunk = add(chunk, hop(chunk, 2, width))
+    (up,) = fetch(gate_up)
+    other = hop(chunk, 2, width)
+    chunk = add(chunk, other)
     mine = along_z([chunk] * nz)
     theirs = [hop(x, 1, width) for x in mine]
-    up, down = fetch(gate_up, lax.optimization_barrier((expert_down, chunk))[0])
+    (down,) = fetch(expert_down)
     keep0, keep1, send0, send1, stream = experts(
         mine, theirs, gain, up, down, turn, fill, mixed, width, cap
     )

time: 82 us -> 82.8 us (level)
  waiting for transfers between devices: 32.3 us -> 35.1 us
  local copies, waits for them, and re-layouts: 2.17 us -> 0 us
  Pallas kernels: 14.3 us -> 15.3 us
  other arithmetic: 0.89 us -> 0 us
    unnamed x4 -> x0, local copies, waits for them, and re-layouts: 2.17 us -> none
    ppermute x25, waiting for transfers between devices: 28.1 us -> 29.7 us  [hop(): return lax.ppermute(x, 'ctx', [(i, i ^ mask) for i in range(width)])]
    all_to_all x1, waiting for transfers between devices: 4.22 us -> 5.46 us  [body(): lax.all_to_all(partial, 'ctx', split_axis=0, concat_axis=0, tiled=True, a...]
    pallas_call x1, Pallas kernels: 1.08 us -> 1.98 us  [prepare(): pl.pallas_call(functools.partial(prepare_kernel, per, width), out_shape=[...]
  transfers between devices with their start and end apart: 26 -> 26, of which waited for: 14 -> 13; matrix products, arithmetic and copies ran while one was open for 3% -> 0% of each run, Pallas kernels for 13% -> 14%
where the time goes in v1:
time: 82.8 us; the launch traced here: 82.4 us
  waiting for transfers between devices  35.1 us (42%)
  starting transfers between devices  30.6 us (37%)
  Pallas kernels  15.3 us (18%)
  between operations  1.41 us (2%)
    ppermute x25, waiting for transfers between devices, hop(): return lax.ppermute(x, 'ctx', [(i, i ^ mask) for i in range(width)])  29.7 us
    ppermute x25, starting transfers between devices, hop(): return lax.ppermute(x, 'ctx', [(i, i ^ mask) for i in range(width)])  26.2 us
    pallas_call x3, Pallas kernels, fetch(): pl.pallas_call(functools.partial(fetch_kernel, count), out_shape=[pltpu.V...  5.77 us
    all_to_all x1, waiting for transfers between devices, body(): lax.all_to_all(partial, 'ctx', split_axis=0, concat_axis=0, tiled=True, a...  5.46 us
    all_to_all x1, starting transfers between devices, body(): lax.all_to_all(partial, 'ctx', split_axis=0, concat_axis=0, tiled=True, a...  4.4 us
    pallas_call x1, Pallas kernels, attention(): pl.pallas_call(functools.partial(attention_kernel, nz), out_shape=jax.Sha...  3.91 us
    pallas_call x1, Pallas kernels, experts(): pl.pallas_call(functools.partial(expert_kernel, nz, width), out_shape=[wi...  2.19 us
    pallas_call x1, Pallas kernels, prepare(): pl.pallas_call(functools.partial(prepare_kernel, per, width), out_shape=[...  1.98 us
  transfers between devices with their start and end apart: 26, of which 13 were waited for; matrix products, arithmetic and copies ran while one was open for 0% of the time, Pallas kernels for 14%

profile of v1, /device:TPU:0, one launch (start us, length us, event | category | flops | bytes accessed | tf_op | source)
XLA Modules:
  0.0 82.4 jit_solution(3084983092756763924)
XLA Ops:
  1.3 2.9 %collective-permute-start = (bf16[8,2048]{1,0:T(8,128)(2,1)}, bf16[8,2048]{1,0:T(8,128)(2,1)S(1)}, u32[]{:S(2)}, u32[]{:S(2)}) collective-permute-start(bf16[8,2048]{1,0:T(8,128)(2,1)} %refs_0_.3), channel_id=1, source_target_pairs={{0,2},{1,3},{2,0},{3,1},{4,6},{5,7},{6,4},{7,5},{8,10},{9,11},{10,... | collective-permute-start | bytes 98312 | tf_op jit(solution)/shard_map/ppermute | solution.py:39
  4.2 1.1 %fetch.3 = (bf16[8,2048]{1,0:T(8,128)(2,1)S(1)}, bf16[1,512,256]{2,1,0:T(8,128)(2,1)S(1)}, bf16[1,512,256]{2,1,0:T(8,128)(2,1)S(1)}) custom-call(bf16[8,2048]{1,0:T(8,128)(2,1)} %refs_0_.3, bf16[1,512,256]{2,1,0:T(8,128)(2,1)} %refs_1_.1, bf16[1,512,256]{2,1,0:T(8,128)(2,1)} %refs_2_.1), custom_call_target="tpu_custom_call" | custom-call | bytes 1114112 | tf_op jit(solution)/shard_map/fetch/pallas_call | solution.py:72
  5.3 1.0 %collective-permute-done.second = bf16[8,2048]{1,0:T(8,128)(2,1)S(1)} collective-permute-done((bf16[8,2048]{1,0:T(8,128)(2,1)}, bf16[8,2048]{1,0:T(8,128)(2,1)S(1)}, u32[]{:S(2)}, u32[]{:S(2)}) %collective-permute-start) | collective-permute-done | bytes 32800 | tf_op jit(solution)/shard_map/ppermute | solution.py:39
  6.3 4.1 %collective-permute-start.3 = (bf16[2,8,2048]{2,1,0:T(8,128)(2,1)S(1)}, bf16[2,8,2048]{2,1,0:T(8,128)(2,1)S(1)}, u32[]{:S(2)}, u32[]{:S(2)}) collective-permute-start(bf16[2,8,2048]{2,1,0:T(8,128)(2,1)S(1)} %shard_map.140.refs_0_), channel_id=1, source_target_pairs={{0,12},{1,13},{2,14},{3,15},{4,8},{5,9},{6,10},{7,11},{8,4},{9,5},... | collective-permute-start | bytes 196616 | tf_op jit(solution)/shard_map/ppermute | solution.py:39
  11.7 1.4 %collective-permute-done.3.refs_3_ = bf16[2,8,2048]{2,1,0:T(8,128)(2,1)S(1)} collective-permute-done((bf16[2,8,2048]{2,1,0:T(8,128)(2,1)S(1)}, bf16[2,8,2048]{2,1,0:T(8,128)(2,1)S(1)}, u32[]{:S(2)}, u32[]{:S(2)}) %collective-permute-start.3) | collective-permute-done | bytes 65568 | tf_op jit(solution)/shard_map/ppermute | solution.py:39
  13.1 2.7 %collective-permute-done.2.refs_2_ = bf16[2,8,2048]{2,1,0:T(8,128)(2,1)S(1)} collective-permute-done((bf16[2,8,2048]{2,1,0:T(8,128)(2,1)S(1)}, bf16[2,8,2048]{2,1,0:T(8,128)(2,1)S(1)}, u32[]{:S(2)}, u32[]{:S(2)}) %collective-permute-start.2) | collective-permute-done | bytes 65568 | tf_op jit(solution)/shard_map/ppermute | solution.py:39
  15.8 3.9 %attention.1 = bf16[8,136,128]{2,1,0:T(8,128)(2,1)} custom-call(s32[1]{0:T(128)S(6)} %copy.15.lengths, bf16[2,8,2048]{2,1,0:T(8,128)(2,1)S(1)} %shard_map.140.refs_0_, bf16[2,8,2048]{2,1,0:T(8,128)(2,1)S(1)} %collective-permute-done.1.refs_1_, bf16[2,8,2048]{2,1,0:T(8,128)(2,1)S(1)} %collective-permute-done.2.refs_2_, ...), custom_call_target="tpu_custom_call" | custom-call | flops 536870912 | bytes 1048576 | tf_op jit(solution)/shard_map/attention/pallas_call | solution.py:284
  19.7 4.4 %all-to-all-start = ((bf16[8,136,128]{2,1,0:T(8,128)(2,1)}), bf16[8,136,128]{2,1,0:T(8,128)(2,1)S(1)}, u32[]{:S(2)}, u32[]{:S(2)}) async-start(bf16[8,136,128]{2,1,0:T(8,128)(2,1)} %attention.1), calls=%async_computation | async-start | bytes 557056 | tf_op jit(solution)/shard_map/all_to_all | solution.py:537
  24.1 2.0 %prepare.1 = (bf16[16,2176]{1,0:T(8,128)(2,1)S(1)}, bf16[64,32]{1,0:T(8,128)(2,1)S(1)}, bf16[256,64]{1,0:T(8,128)(2,1)S(1)}, bf16[256,128]{1,0:T(8,128)(2,1)S(1)...) custom-call(s32[1,16]{1,0:T(1,128)} %bitcast.8, s32[1,128]{1,0:T(1,128)} %bitcast.9, s32[8,16]{1,0:T(8,128)} %bitcast.6, ...), custom_call_target="tpu_custom_call" | custom-call | flops 12582912 | bytes 131072 | tf_op jit(solution)/shard_map/prepare/pallas_call | solution.py:152
  26.2 1.2 %collective-permute-done.7.res_oth = bf16[16,2176]{1,0:T(8,128)(2,1)S(1)} collective-permute-done((bf16[16,2176]{1,0:T(8,128)(2,1)S(1)}, bf16[16,2176]{1,0:T(8,128)(2,1)S(1)}, u32[]{:S(2)}, u32[]{:S(2)}) %collective-permute-start.7) | collective-permute-done | bytes 69664 | tf_op jit(solution)/shard_map/ppermute | solution.py:39
  27.4 5.5 %all-to-all-done.got = bf16[8,136,128]{2,1,0:T(8,128)(2,1)S(1)} async-done(((bf16[8,136,128]{2,1,0:T(8,128)(2,1)}), bf16[8,136,128]{2,1,0:T(8,128)(2,1)S(1)}, u32[]{:S(2)}, u32[]{:S(2)}) %all-to-all-start) | async-done | bytes 278560 | tf_op jit(solution)/shard_map/all_to_all | solution.py:537
  33.4 1.1 %collective-permute-start.8 = (bf16[16,2176]{1,0:T(8,128)(2,1)S(1)}, bf16[16,2176]{1,0:T(8,128)(2,1)S(1)}, u32[]{:S(2)}, u32[]{:S(2)}) collective-permute-start(bf16[16,2176]{1,0:T(8,128)(2,1)S(1)} %get-tuple-element.32), channel_id=1, source_target_pairs={{0,4},{1,5},{2,6},{3,7},{4,0},{5,1},{6,2},{7,3},{8,12},{9,13},{10,... | collective-permute-start | bytes 208904 | tf_op jit(solution)/shard_map/ppermute | solution.py:39
  35.1 2.8 %collective-permute-start.10 = (bf16[16,2176]{1,0:T(8,128)(2,1)S(1)}, bf16[16,2176]{1,0:T(8,128)(2,1)S(1)}, u32[]{:S(2)}, u32[]{:S(2)}) collective-permute-start(bf16[16,2176]{1,0:T(8,128)(2,1)S(1)} %get-tuple-element.34), channel_id=1, source_target_pairs={{0,12},{1,13},{2,14},{3,15},{4,8},{5,9},{6,10},{7,11},{8,4},{9,5},... | collective-permute-start | bytes 208904 | tf_op jit(solution)/shard_map/ppermute | solution.py:39
  37.9 3.4 %collective-permute-done.9.refs_2_ = bf16[16,2176]{1,0:T(8,128)(2,1)S(1)} collective-permute-done((bf16[16,2176]{1,0:T(8,128)(2,1)S(1)}, bf16[16,2176]{1,0:T(8,128)(2,1)S(1)}, u32[]{:S(2)}, u32[]{:S(2)}) %collective-permute-start.9) | collective-permute-done | bytes 69664 | tf_op jit(solution)/shard_map/ppermute | solution.py:39
  41.3 1.8 %collective-permute-start.11 = (bf16[16,2176]{1,0:T(8,128)(2,1)S(1)}, bf16[16,2176]{1,0:T(8,128)(2,1)S(1)}, u32[]{:S(2)}, u32[]{:S(2)}) collective-permute-start(bf16[16,2176]{1,0:T(8,128)(2,1)S(1)} %shard_map.141.refs_0_), channel_id=1, source_target_pairs={{0,2},{1,3},{2,0},{3,1},{4,6},{5,7},{6,4},{7,5},{8,10},{9,11},{10,... | collective-permute-start | bytes 208904 | tf_op jit(solution)/shard_map/ppermute | solution.py:39
  43.2 2.5 %collective-permute-done.11.refs_1_ = bf16[16,2176]{1,0:T(8,128)(2,1)S(1)} collective-permute-done((bf16[16,2176]{1,0:T(8,128)(2,1)S(1)}, bf16[16,2176]{1,0:T(8,128)(2,1)S(1)}, u32[]{:S(2)}, u32[]{:S(2)}) %collective-permute-start.11) | collective-permute-done | bytes 69664 | tf_op jit(solution)/shard_map/ppermute | solution.py:39
  45.7 2.8 %collective-permute-start.14 = (bf16[16,2176]{1,0:T(8,128)(2,1)S(1)}, bf16[16,2176]{1,0:T(8,128)(2,1)S(1)}, u32[]{:S(2)}, u32[]{:S(2)}) collective-permute-start(bf16[16,2176]{1,0:T(8,128)(2,1)S(1)} %shard_map.142.refs_0_), channel_id=1, source_target_pairs={{0,12},{1,13},{2,14},{3,15},{4,8},{5,9},{6,10},{7,11},{8,4},{9,5},... | collective-permute-start | bytes 208904 | tf_op jit(solution)/shard_map/ppermute | solution.py:39
  48.6 1.6 %collective-permute-start.12 = (bf16[16,2176]{1,0:T(8,128)(2,1)S(1)}, bf16[16,2176]{1,0:T(8,128)(2,1)S(1)}, u32[]{:S(2)}, u32[]{:S(2)}) collective-permute-start(bf16[16,2176]{1,0:T(8,128)(2,1)S(1)} %shard_map.142.refs_0_), channel_id=1, source_target_pairs={{0,4},{1,5},{2,6},{3,7},{4,0},{5,1},{6,2},{7,3},{8,12},{9,13},{10,... | collective-permute-start | bytes 208904 | tf_op jit(solution)/shard_map/ppermute | solution.py:39
  50.2 1.7 %collective-permute-done.14.refs_3_ = bf16[16,2176]{1,0:T(8,128)(2,1)S(1)} collective-permute-done((bf16[16,2176]{1,0:T(8,128)(2,1)S(1)}, bf16[16,2176]{1,0:T(8,128)(2,1)S(1)}, u32[]{:S(2)}, u32[]{:S(2)}) %collective-permute-start.14) | collective-permute-done | bytes 69664 | tf_op jit(solution)/shard_map/ppermute | solution.py:39
  51.9 1.8 %collective-permute-done.13.refs_2_ = bf16[16,2176]{1,0:T(8,128)(2,1)S(1)} collective-permute-done((bf16[16,2176]{1,0:T(8,128)(2,1)S(1)}, bf16[16,2176]{1,0:T(8,128)(2,1)S(1)}, u32[]{:S(2)}, u32[]{:S(2)}) %collective-permute-start.13) | collective-permute-done | bytes 69664 | tf_op jit(solution)/shard_map/ppermute | solution.py:39
  54.2 1.9 %fetch.5.refs_10_ = bf16[1,768,2048]{2,1,0:T(8,128)(2,1)S(1)} custom-call(bf16[1,768,2048]{2,1,0:T(8,128)(2,1)} %refs_0_.5), custom_call_target="tpu_custom_call" | custom-call | bytes 6291456 | tf_op jit(solution)/shard_map/fetch/pallas_call | solution.py:72
  56.1 2.8 %fetch.4.refs_9_ = bf16[1,2048,1536]{2,1,0:T(8,128)(2,1)S(1)} custom-call(bf16[1,2048,1536]{2,1,0:T(8,128)(2,1)} %refs_0_.4), custom_call_target="tpu_custom_call" | custom-call | bytes 12582912 | tf_op jit(solution)/shard_map/fetch/pallas_call | solution.py:72
  59.0 2.2 %experts.1 = (bf16[64,2304]{1,0:T(8,128)(2,1)S(1)}, bf16[64,2304]{1,0:T(8,128)(2,1)S(1)}, bf16[64,2304]{1,0:T(8,128)(2,1)S(1)}, bf16[64,2304]{1,0:T(8,128)(2,1)S(1)}, bf16[16,2048]{1,0:T(8,128)(2,1)S(1)}) custom-call(bf16[16,2176]{1,0:T(8,128)(2,1)S(1)} %shard_map.142.refs_0_, bf16[16,2176]{1,0:T(8,128)(2,1)S(1)} %collective-permute-done.12.refs_1_, ...), custom_call_target="tpu_custom_call" | custom-call | flops 1207959552 | bytes 9437184 | tf_op jit(solution)/shard_map/experts/pallas_call | solution.py:398
  61.7 1.1 %collective-permute-done.20.refs_1_ = bf16[64,2304]{1,0:T(8,128)(2,1)S(1)} collective-permute-done((bf16[64,2304]{1,0:T(8,128)(2,1)S(1)}, bf16[64,2304]{1,0:T(8,128)(2,1)S(1)}, u32[]{:S(2)}, u32[]{:S(2)}) %collective-permute-start.20) | collective-permute-done | bytes 294944 | tf_op jit(solution)/shard_map/ppermute | solution.py:39
  62.8 1.5 %collective-permute-start.21 = (bf16[64,2304]{1,0:T(8,128)(2,1)S(1)}, bf16[64,2304]{1,0:T(8,128)(2,1)S(1)}, u32[]{:S(2)}, u32[]{:S(2)}) collective-permute-start(bf16[64,2304]{1,0:T(8,128)(2,1)S(1)} %shard_map.143), channel_id=1, source_target_pairs={{0,2},{1,3},{2,0},{3,1},{4,6},{5,7},{6,4},{7,5},{8,10},{9,11},{10,... | collective-permute-start | bytes 884744 | tf_op jit(solution)/shard_map/ppermute | solution.py:39
  64.4 7.6 %collective-permute-done.21.far = bf16[64,2304]{1,0:T(8,128)(2,1)S(1)} collective-permute-done((bf16[64,2304]{1,0:T(8,128)(2,1)S(1)}, bf16[64,2304]{1,0:T(8,128)(2,1)S(1)}, u32[]{:S(2)}, u32[]{:S(2)}) %collective-permute-start.21) | collective-permute-done | bytes 294944 | tf_op jit(solution)/shard_map/ppermute | solution.py:39
  72.1 0.8 collective-permute-start.22
  72.8 2.3 %collective-permute-start.23 = (bf16[16,2560]{1,0:T(8,128)(2,1)S(1)}, bf16[16,2560]{1,0:T(8,128)(2,1)S(1)}, u32[]{:S(2)}, u32[]{:S(2)}) collective-permute-start(bf16[16,2560]{1,0:T(8,128)(2,1)S(1)} %get-tuple-element.46), channel_id=1, source_target_pairs={{0,8},{1,9},{2,10},{3,11},{4,12},{5,13},{6,14},{7,15},{8,0},{9,1},... | collective-permute-start | bytes 245768 | tf_op jit(solution)/shard_map/ppermute | solution.py:39
  75.1 1.4 %collective-permute-start.24 = (bf16[16,2560]{1,0:T(8,128)(2,1)S(1)}, bf16[16,2560]{1,0:T(8,128)(2,1)S(1)}, u32[]{:S(2)}, u32[]{:S(2)}) collective-permute-start(bf16[16,2560]{1,0:T(8,128)(2,1)S(1)} %get-tuple-element.47), channel_id=1, source_target_pairs={{0,12},{1,13},{2,14},{3,15},{4,8},{5,9},{6,10},{7,11},{8,4},{9,5},... | collective-permute-start | bytes 245768 | tf_op jit(solution)/shard_map/ppermute | solution.py:39
  76.5 0.8 %collective-permute-done.22.refs_1_ = bf16[16,2560]{1,0:T(8,128)(2,1)S(1)} collective-permute-done((bf16[16,2560]{1,0:T(8,128)(2,1)S(1)}, bf16[16,2560]{1,0:T(8,128)(2,1)S(1)}, u32[]{:S(2)}, u32[]{:S(2)}) %collective-permute-start.22) | collective-permute-done | bytes 81952 | tf_op jit(solution)/shard_map/ppermute | solution.py:39
  77.4 4.4 %collective-permute-done.23.refs_2_ = bf16[16,2560]{1,0:T(8,128)(2,1)S(1)} collective-permute-done((bf16[16,2560]{1,0:T(8,128)(2,1)S(1)}, bf16[16,2560]{1,0:T(8,128)(2,1)S(1)}, u32[]{:S(2)}, u32[]{:S(2)}) %collective-permute-start.23) | collective-permute-done | bytes 81952 | tf_op jit(solution)/shard_map/ppermute | solution.py:39
  81.7 0.7 finish.1
  (33 shorter events, 3.9 us)
Async XLA Ops:
  0.6 15.2 %collective-permute-start.4 = (bf16[1,512,256]{2,1,0:T(8,128)(2,1)}, bf16[1,512,256]{2,1,0:T(8,128)(2,1)S(1)}, u32[]{:S(2)}, u32[]{:S(2)}) collective-permute-start(bf16[1,512,256]{2,1,0:T(8,128)(2,1)} %refs_1_.1), channel_id=1, source_target_pairs={{0,1},{1,0},{2,3},{3,2},{4,5},{5,4},{6,7},{7,6},{8,9},{9,8},{10,11... | collective-permute-start | bytes 786440 | tf_op jit(solution)/shard_map/ppermute | solution.py:39
  1.2 14.6 %collective-permute-start.5 = (bf16[1,512,256]{2,1,0:T(8,128)(2,1)}, bf16[1,512,256]{2,1,0:T(8,128)(2,1)S(1)}, u32[]{:S(2)}, u32[]{:S(2)}) collective-permute-start(bf16[1,512,256]{2,1,0:T(8,128)(2,1)} %refs_2_.1), channel_id=1, source_target_pairs={{0,1},{1,0},{2,3},{3,2},{4,5},{5,4},{6,7},{7,6},{8,9},{9,8},{10,11... | collective-permute-start | bytes 786440 | tf_op jit(solution)/shard_map/ppermute | solution.py:39
  1.3 5.0 %collective-permute-start = (bf16[8,2048]{1,0:T(8,128)(2,1)}, bf16[8,2048]{1,0:T(8,128)(2,1)S(1)}, u32[]{:S(2)}, u32[]{:S(2)}) collective-permute-start(bf16[8,2048]{1,0:T(8,128)(2,1)} %refs_0_.3), channel_id=1, source_target_pairs={{0,2},{1,3},{2,0},{3,1},{4,6},{5,7},{6,4},{7,5},{8,10},{9,11},{10,... | collective-permute-start | bytes 98312 | tf_op jit(solution)/shard_map/ppermute | solution.py:39
  6.3 6.8 %collective-permute-start.3 = (bf16[2,8,2048]{2,1,0:T(8,128)(2,1)S(1)}, bf16[2,8,2048]{2,1,0:T(8,128)(2,1)S(1)}, u32[]{:S(2)}, u32[]{:S(2)}) collective-permute-start(bf16[2,8,2048]{2,1,0:T(8,128)(2,1)S(1)} %shard_map.140.refs_0_), channel_id=1, source_target_pairs={{0,12},{1,13},{2,14},{3,15},{4,8},{5,9},{6,10},{7,11},{8,4},{9,5},... | collective-permute-start | bytes 196616 | tf_op jit(solution)/shard_map/ppermute | solution.py:39
  10.4 5.4 %collective-permute-start.2 = (bf16[2,8,2048]{2,1,0:T(8,128)(2,1)S(1)}, bf16[2,8,2048]{2,1,0:T(8,128)(2,1)S(1)}, u32[]{:S(2)}, u32[]{:S(2)}) collective-permute-start(bf16[2,8,2048]{2,1,0:T(8,128)(2,1)S(1)} %shard_map.140.refs_0_), channel_id=1, source_target_pairs={{0,8},{1,9},{2,10},{3,11},{4,12},{5,13},{6,14},{7,15},{8,0},{9,1},... | collective-permute-start | bytes 196616 | tf_op jit(solution)/shard_map/ppermute | solution.py:39
  10.4 5.4 %collective-permute-start.1 = (bf16[2,8,2048]{2,1,0:T(8,128)(2,1)S(1)}, bf16[2,8,2048]{2,1,0:T(8,128)(2,1)S(1)}, u32[]{:S(2)}, u32[]{:S(2)}) collective-permute-start(bf16[2,8,2048]{2,1,0:T(8,128)(2,1)S(1)} %shard_map.140.refs_0_), channel_id=1, source_target_pairs={{0,4},{1,5},{2,6},{3,7},{4,0},{5,1},{6,2},{7,3},{8,12},{9,13},{10,... | collective-permute-start | bytes 196616 | tf_op jit(solution)/shard_map/ppermute | solution.py:39
  13.1 14.4 %collective-permute-start.6 = (bf16[128,2048]{1,0:T(8,128)(2,1)}, bf16[128,2048]{1,0:T(8,128)(2,1)S(1)}, u32[]{:S(2)}, u32[]{:S(2)}) collective-permute-start(bf16[128,2048]{1,0:T(8,128)(2,1)} %refs_5_.1), channel_id=1, source_target_pairs={{0,1},{1,0},{2,3},{3,2},{4,5},{5,4},{6,7},{7,6},{8,9},{9,8},{10,11... | collective-permute-start | bytes 1572872 | tf_op jit(solution)/shard_map/ppermute | solution.py:39
  19.7 13.2 %all-to-all-start = ((bf16[8,136,128]{2,1,0:T(8,128)(2,1)}), bf16[8,136,128]{2,1,0:T(8,128)(2,1)S(1)}, u32[]{:S(2)}, u32[]{:S(2)}) async-start(bf16[8,136,128]{2,1,0:T(8,128)(2,1)} %attention.1), calls=%async_computation | async-start | bytes 557056 | tf_op jit(solution)/shard_map/all_to_all | solution.py:537
  26.1 1.3 %collective-permute-start.7 = (bf16[16,2176]{1,0:T(8,128)(2,1)S(1)}, bf16[16,2176]{1,0:T(8,128)(2,1)S(1)}, u32[]{:S(2)}, u32[]{:S(2)}) collective-permute-start(bf16[16,2176]{1,0:T(8,128)(2,1)S(1)} %get-tuple-element.29.res_own), channel_id=1, source_target_pairs={{0,1},{1,0},{2,3},{3,2},{4,5},{5,4},{6,7},{7,6},{8,9},{9,8},{10,11... | collective-permute-start | bytes 208904 | tf_op jit(solution)/shard_map/ppermute | solution.py:39
  33.4 4.5 %collective-permute-start.8 = (bf16[16,2176]{1,0:T(8,128)(2,1)S(1)}, bf16[16,2176]{1,0:T(8,128)(2,1)S(1)}, u32[]{:S(2)}, u32[]{:S(2)}) collective-permute-start(bf16[16,2176]{1,0:T(8,128)(2,1)S(1)} %get-tuple-element.32), channel_id=1, source_target_pairs={{0,4},{1,5},{2,6},{3,7},{4,0},{5,1},{6,2},{7,3},{8,12},{9,13},{10,... | collective-permute-start | bytes 208904 | tf_op jit(solution)/shard_map/ppermute | solution.py:39
  34.5 6.8 %collective-permute-start.9 = (bf16[16,2176]{1,0:T(8,128)(2,1)S(1)}, bf16[16,2176]{1,0:T(8,128)(2,1)S(1)}, u32[]{:S(2)}, u32[]{:S(2)}) collective-permute-start(bf16[16,2176]{1,0:T(8,128)(2,1)S(1)} %get-tuple-element.33), channel_id=1, source_target_pairs={{0,8},{1,9},{2,10},{3,11},{4,12},{5,13},{6,14},{7,15},{8,0},{9,1},... | collective-permute-start | bytes 208904 | tf_op jit(solution)/shard_map/ppermute | solution.py:39
  35.1 6.2 %collective-permute-start.10 = (bf16[16,2176]{1,0:T(8,128)(2,1)S(1)}, bf16[16,2176]{1,0:T(8,128)(2,1)S(1)}, u32[]{:S(2)}, u32[]{:S(2)}) collective-permute-start(bf16[16,2176]{1,0:T(8,128)(2,1)S(1)} %get-tuple-element.34), channel_id=1, source_target_pairs={{0,12},{1,13},{2,14},{3,15},{4,8},{5,9},{6,10},{7,11},{8,4},{9,5},... | collective-permute-start | bytes 208904 | tf_op jit(solution)/shard_map/ppermute | solution.py:39
  41.3 4.4 %collective-permute-start.11 = (bf16[16,2176]{1,0:T(8,128)(2,1)S(1)}, bf16[16,2176]{1,0:T(8,128)(2,1)S(1)}, u32[]{:S(2)}, u32[]{:S(2)}) collective-permute-start(bf16[16,2176]{1,0:T(8,128)(2,1)S(1)} %shard_map.141.refs_0_), channel_id=1, source_target_pairs={{0,2},{1,3},{2,0},{3,1},{4,6},{5,7},{6,4},{7,5},{8,10},{9,11},{10,... | collective-permute-start | bytes 208904 | tf_op jit(solution)/shard_map/ppermute | solution.py:39
  45.7 6.2 %collective-permute-start.14 = (bf16[16,2176]{1,0:T(8,128)(2,1)S(1)}, bf16[16,2176]{1,0:T(8,128)(2,1)S(1)}, u32[]{:S(2)}, u32[]{:S(2)}) collective-permute-start(bf16[16,2176]{1,0:T(8,128)(2,1)S(1)} %shard_map.142.refs_0_), channel_id=1, source_target_pairs={{0,12},{1,13},{2,14},{3,15},{4,8},{5,9},{6,10},{7,11},{8,4},{9,5},... | collective-permute-start | bytes 208904 | tf_op jit(solution)/shard_map/ppermute | solution.py:39
  48.5 5.2 %collective-permute-start.13 = (bf16[16,2176]{1,0:T(8,128)(2,1)S(1)}, bf16[16,2176]{1,0:T(8,128)(2,1)S(1)}, u32[]{:S(2)}, u32[]{:S(2)}) collective-permute-start(bf16[16,2176]{1,0:T(8,128)(2,1)S(1)} %shard_map.142.refs_0_), channel_id=1, source_target_pairs={{0,8},{1,9},{2,10},{3,11},{4,12},{5,13},{6,14},{7,15},{8,0},{9,1},... | collective-permute-start | bytes 208904 | tf_op jit(solution)/shard_map/ppermute | solution.py:39
  48.6 5.1 %collective-permute-start.12 = (bf16[16,2176]{1,0:T(8,128)(2,1)S(1)}, bf16[16,2176]{1,0:T(8,128)(2,1)S(1)}, u32[]{:S(2)}, u32[]{:S(2)}) collective-permute-start(bf16[16,2176]{1,0:T(8,128)(2,1)S(1)} %shard_map.142.refs_0_), channel_id=1, source_target_pairs={{0,4},{1,5},{2,6},{3,7},{4,0},{5,1},{6,2},{7,3},{8,12},{9,13},{10,... | collective-permute-start | bytes 208904 | tf_op jit(solution)/shard_map/ppermute | solution.py:39
  50.2 8.7 %collective-permute-start.15 = (bf16[16,2176]{1,0:T(8,128)(2,1)S(1)}, bf16[16,2176]{1,0:T(8,128)(2,1)S(1)}, u32[]{:S(2)}, u32[]{:S(2)}) collective-permute-start(bf16[16,2176]{1,0:T(8,128)(2,1)S(1)} %shard_map.142.refs_0_), channel_id=1, source_target_pairs={{0,1},{1,0},{2,3},{3,2},{4,5},{5,4},{6,7},{7,6},{8,9},{9,8},{10,11... | collective-permute-start | bytes 208904 | tf_op jit(solution)/shard_map/ppermute | solution.py:39
  51.9 7.0 %collective-permute-start.18 = (bf16[16,2176]{1,0:T(8,128)(2,1)S(1)}, bf16[16,2176]{1,0:T(8,128)(2,1)S(1)}, u32[]{:S(2)}, u32[]{:S(2)}) collective-permute-start(bf16[16,2176]{1,0:T(8,128)(2,1)S(1)} %collective-permute-done.14.refs_3_), channel_id=1, source_target_pairs={{0,1},{1,0},{2,3},{3,2},{4,5},{5,4},{6,7},{7,6},{8,9},{9,8},{10,11... | collective-permute-start | bytes 208904 | tf_op jit(solution)/shard_map/ppermute | solution.py:39
  53.7 5.2 %collective-permute-start.17 = (bf16[16,2176]{1,0:T(8,128)(2,1)S(1)}, bf16[16,2176]{1,0:T(8,128)(2,1)S(1)}, u32[]{:S(2)}, u32[]{:S(2)}) collective-permute-start(bf16[16,2176]{1,0:T(8,128)(2,1)S(1)} %collective-permute-done.13.refs_2_), channel_id=1, source_target_pairs={{0,1},{1,0},{2,3},{3,2},{4,5},{5,4},{6,7},{7,6},{8,9},{9,8},{10,11... | collective-permute-start | bytes 208904 | tf_op jit(solution)/shard_map/ppermute | solution.py:39
  53.7 5.3 %collective-permute-start.16 = (bf16[16,2176]{1,0:T(8,128)(2,1)S(1)}, bf16[16,2176]{1,0:T(8,128)(2,1)S(1)}, u32[]{:S(2)}, u32[]{:S(2)}) collective-permute-start(bf16[16,2176]{1,0:T(8,128)(2,1)S(1)} %collective-permute-done.12.refs_1_), channel_id=1, source_target_pairs={{0,1},{1,0},{2,3},{3,2},{4,5},{5,4},{6,7},{7,6},{8,9},{9,8},{10,11... | collective-permute-start | bytes 208904 | tf_op jit(solution)/shard_map/ppermute | solution.py:39
  61.1 1.6 %collective-permute-start.20 = (bf16[64,2304]{1,0:T(8,128)(2,1)S(1)}, bf16[64,2304]{1,0:T(8,128)(2,1)S(1)}, u32[]{:S(2)}, u32[]{:S(2)}) collective-permute-start(bf16[64,2304]{1,0:T(8,128)(2,1)S(1)} %get-tuple-element.43), channel_id=1, source_target_pairs={{0,1},{1,0},{2,3},{3,2},{4,5},{5,4},{6,7},{7,6},{8,9},{9,8},{10,11... | collective-permute-start | bytes 884744 | tf_op jit(solution)/shard_map/ppermute | solution.py:39
  61.2 3.2 %collective-permute-start.19 = (bf16[64,2304]{1,0:T(8,128)(2,1)S(1)}, bf16[64,2304]{1,0:T(8,128)(2,1)S(1)}, u32[]{:S(2)}, u32[]{:S(2)}) collective-permute-start(bf16[64,2304]{1,0:T(8,128)(2,1)S(1)} %get-tuple-element.41), channel_id=1, source_target_pairs={{0,1},{1,0},{2,3},{3,2},{4,5},{5,4},{6,7},{7,6},{8,9},{9,8},{10,11... | collective-permute-start | bytes 884744 | tf_op jit(solution)/shard_map/ppermute | solution.py:39
  62.8 9.1 %collective-permute-start.21 = (bf16[64,2304]{1,0:T(8,128)(2,1)S(1)}, bf16[64,2304]{1,0:T(8,128)(2,1)S(1)}, u32[]{:S(2)}, u32[]{:S(2)}) collective-permute-start(bf16[64,2304]{1,0:T(8,128)(2,1)S(1)} %shard_map.143), channel_id=1, source_target_pairs={{0,2},{1,3},{2,0},{3,1},{4,6},{5,7},{6,4},{7,5},{8,10},{9,11},{10,... | collective-permute-start | bytes 884744 | tf_op jit(solution)/shard_map/ppermute | solution.py:39
  72.1 5.3 %collective-permute-start.22 = (bf16[16,2560]{1,0:T(8,128)(2,1)S(1)}, bf16[16,2560]{1,0:T(8,128)(2,1)S(1)}, u32[]{:S(2)}, u32[]{:S(2)}) collective-permute-start(bf16[16,2560]{1,0:T(8,128)(2,1)S(1)} %get-tuple-element.45), channel_id=1, source_target_pairs={{0,4},{1,5},{2,6},{3,7},{4,0},{5,1},{6,2},{7,3},{8,12},{9,13},{10,... | collective-permute-start | bytes 245768 | tf_op jit(solution)/shard_map/ppermute | solution.py:39
  72.8 8.9 %collective-permute-start.23 = (bf16[16,2560]{1,0:T(8,128)(2,1)S(1)}, bf16[16,2560]{1,0:T(8,128)(2,1)S(1)}, u32[]{:S(2)}, u32[]{:S(2)}) collective-permute-start(bf16[16,2560]{1,0:T(8,128)(2,1)S(1)} %get-tuple-element.46), channel_id=1, source_target_pairs={{0,8},{1,9},{2,10},{3,11},{4,12},{5,13},{6,14},{7,15},{8,0},{9,1},... | collective-permute-start | bytes 245768 | tf_op jit(solution)/shard_map/ppermute | solution.py:39
  75.1 6.7 %collective-permute-start.24 = (bf16[16,2560]{1,0:T(8,128)(2,1)S(1)}, bf16[16,2560]{1,0:T(8,128)(2,1)S(1)}, u32[]{:S(2)}, u32[]{:S(2)}) collective-permute-start(bf16[16,2560]{1,0:T(8,128)(2,1)S(1)} %get-tuple-element.47), channel_id=1, source_target_pairs={{0,12},{1,13},{2,14},{3,15},{4,8},{5,9},{6,10},{7,11},{8,4},{9,5},... | collective-permute-start | bytes 245768 | tf_op jit(solution)/shard_map/ppermute | solution.py:39

commit v2 on v1

--- a/solution.py
+++ b/solution.py
@@ -202,41 +202,41 @@
 
 
 def attention_kernel(nz, lengths, *refs):
-    pieces, (k_own, v_own, k_oth, v_oth, out, rows) = refs[:nz], refs[nz:]
+    pieces, (k_own, v_own, k_oth, v_oth) = refs[:nz], refs[nz : nz + 4]
+    outs, (rows, ready) = refs[nz + 4 : 2 * nz + 4], refs[2 * nz + 4 :]
     device, core, chip, _ = place()
     per = pieces[0].shape[1]
     requests, span = k_own.shape[0], k_own.shape[1]
     count = rows.shape[0]
     seat = count // requests
-    chips, depth = out.shape[0], out.shape[1] - STAT
+    chips, depth = ready.shape[0], ready.shape[1] - STAT
     cols = HQ * HD // chips
     heads = max(1, cols // HD)
+    group = HQ // KVH
     for kz in range(nz):
         both = pieces[kz][...].astype(F32)
         for ky in range(2):
             spot = (chip ^ (2 * kz + ky)) * per
             rows[pl.ds(pl.multiple_of(spot, per), per), :] = both[ky]
-    key = lax.broadcasted_iota(jnp.int32, (span, 2 * seat), 0)
-    lane = lax.broadcasted_iota(jnp.int32, (1, 2 * seat), 1) % seat
+    wide = group * seat
+    key = lax.broadcasted_iota(jnp.int32, (span, wide), 0)
+    lane = lax.broadcasted_iota(jnp.int32, (1, wide), 1) % seat
     ahead = (lane // per) * (2 * per) + core * per + lane % per - STRETCH
     first_own, first_oth = device * span, (device ^ 1) * span
     for q in range(requests):
         last = lengths[q] + ahead
         see_own, see_oth = key <= last - first_own, key <= last - first_oth
-        for j in range(HQ // 2):
-            v = 2 * j // (HQ // KVH)
+        for v in range(KVH):
             kv = slice(v * HD, (v + 1) * HD)
-            if 2 * j % (HQ // KVH) == 0:
-                vt_own, vt_oth = v_own[q, :, kv].T, v_oth[q, :, kv].T
-            pair = jnp.concatenate(
+            asked = jnp.concatenate(
                 [
-                    rows[q * seat : (q + 1) * seat, (2 * j + e) * HD : (2 * j + e + 1) * HD]
-                    for e in range(2)
+                    rows[q * seat : (q + 1) * seat, h * HD : (h + 1) * HD]
+                    for h in range(v * group, (v + 1) * group)
                 ],
                 axis=0,
             ).astype(BF)
-            s_own = dot(k_own[q, :, kv], pair, NT) * (HD ** (-0.5) * LOG2E)
-            s_oth = dot(k_oth[q, :, kv], pair, NT) * (HD ** (-0.5) * LOG2E)
+            s_own = dot(k_own[q, :, kv], asked, NT) * (HD ** (-0.5) * LOG2E)
+            s_oth = dot(k_oth[q, :, kv], asked, NT) * (HD ** (-0.5) * LOG2E)
             s_own = jnp.where(see_own, s_own, -1e30)
             s_oth = jnp.where(see_oth, s_oth, -1e30)
             top = jnp.maximum(
@@ -246,31 +246,37 @@
             w_own = jnp.exp2(s_own - top)
             w_oth = jnp.exp2(s_oth - top)
             total = jnp.sum(w_own, axis=0, keepdims=True) + jnp.sum(w_oth, axis=0, keepdims=True)
-            mixed = dot(vt_own, w_own.astype(BF), NN) + dot(vt_oth, w_oth.astype(BF), NN)
+            mixed = dot(v_own[q, :, kv].T, w_own.astype(BF), NN) + dot(
+                v_oth[q, :, kv].T, w_oth.astype(BF), NN
+            )
             some = total > 0.0
             safe = jnp.where(some, total, 1.0)
-            mixed = (mixed / safe).astype(BF)
+            mixed = (mixed * (1.0 / safe)).astype(BF)
             lse = jnp.where(some, top * (1.0 / LOG2E) + jnp.log(safe), -1e30)
-            hi, mid, low = split3(lse)
-            stat = jnp.concatenate(
-                [hi.astype(F32), mid.astype(F32), low.astype(F32)]
-                + [jnp.zeros((STAT - 3, 2 * seat), F32)],
-                axis=0,
-            ).astype(BF)
+            stat = with_lse(lse)
             if heads == 2 and requests == 1:
-                out[j, :depth, :] = mixed
-                out[j, depth:, :] = stat
+                for g in range(group // 2):
+                    dest = (v * group // 2 + g) ^ chip
+                    mine = slice(2 * g * seat, 2 * (g + 1) * seat)
+                    ready[dest, :depth, :] = mixed[:, mine]
+                    ready[dest, depth:, :] = stat[:, mine]
             else:
-                for e in range(2):
+                for e in range(group):
                     mine = slice(e * seat, (e + 1) * seat)
-                    head = 2 * j + e
+                    head = v * group + e
                     lo = (head % heads) * count + q * seat
                     for part in range(HD // depth):
-                        dest = (head * HD + part * depth) // cols
-                        out[dest, :depth, lo : lo + seat] = mixed[
-                            part * depth : (part + 1) * depth, mine
-                        ]
-                        out[dest, depth:, lo : lo + seat] = stat[:, mine]
+                        dest = ((head * HD + part * depth) // cols) ^ chip
+                        some_rows = slice(part * depth, (part + 1) * depth)
+                        ready[dest, :depth, lo : lo + seat] = mixed[some_rows, mine]
+                        ready[dest, depth:, lo : lo + seat] = stat[:, mine]
+    for kz in range(nz):
+        outs[kz][...] = ready[2 * kz : 2 * kz + 2]
+
+
+def with_lse(lse):
+    parts = [x.astype(F32) for x in split3(lse)]
+    return jnp.concatenate(parts + [jnp.zeros((STAT - 3, lse.shape[1]), F32)], axis=0).astype(BF)
 
 
 def attention(pieces, k_own, v_own, k_oth, v_oth, lengths, chips):
@@ -279,45 +285,77 @@
     count = chips * per
     cols = HQ * HD // chips
     heads = max(1, cols // HD)
-    shape = (chips, min(cols, HD) + STAT, heads * count)
+    shape = (2, min(cols, HD) + STAT, heads * count)
     work = 4 * k_own.size * (HQ // KVH) * 2 * count
     return pl.pallas_call(
         functools.partial(attention_kernel, nz),
-        out_shape=jax.ShapeDtypeStruct(shape, BF),
+        out_shape=[jax.ShapeDtypeStruct(shape, BF)] * nz,
         in_specs=[pl.BlockSpec(memory_space=pltpu.SMEM)]
         + [pl.BlockSpec(memory_space=pltpu.VMEM)] * (nz + 4),
-        out_specs=pl.BlockSpec(memory_space=pltpu.VMEM),
-        scratch_shapes=[pltpu.VMEM((count, HQ * HD), F32)],
+        out_specs=[pl.BlockSpec(memory_space=pltpu.VMEM)] * nz,
+        scratch_shapes=[
+            pltpu.VMEM((count, HQ * HD), F32),
+            pltpu.VMEM((chips,) + shape[1:], BF),
+        ],
         cost_estimate=pl.CostEstimate(
             flops=work, bytes_accessed=8 * k_own.size, transcendentals=work // (4 * HD)
         ),
-        compiler_params=pltpu.CompilerParams(vmem_limit_bytes=16 * MIB),
+        compiler_params=pltpu.CompilerParams(vmem_limit_bytes=24 * MIB),
         name="attention",
     )(lengths, *pieces, k_own, v_own, k_oth, v_oth)
 
 
-def project_kernel(nz, got, w_own, w_oth, res_own, res_oth, home, *refs):
-    outs, attn, part = refs[:nz], refs[nz], refs[nz + 1]
-    _, core, _, z = place()
-    chips, depth = got.shape[0], got.shape[1] - STAT
-    count = part.shape[0]
-    heads = got.shape[2] // count
-    lse = [
-        jnp.sum(got[i, depth:, :].astype(F32), axis=0, keepdims=True) for i in range(chips)
-    ]
+def merged(blocks):
+    depth = blocks[0].shape[0] - STAT
+    lse = [jnp.sum(x[depth:].astype(F32), axis=0, keepdims=True) for x in blocks]
     best = functools.reduce(jnp.maximum, lse)
     factor = [jnp.exp(x - best) for x in lse]
     denom = functools.reduce(lambda a, b: a + b, factor)
-    merged = functools.reduce(
-        lambda a, b: a + b, [got[i, :depth, :].astype(F32) * factor[i] for i in range(chips)]
+    mixed = functools.reduce(
+        lambda a, b: a + b, [x[:depth].astype(F32) * f for x, f in zip(blocks, factor)]
     )
-    merged = (merged / denom).T.astype(BF)
+    return mixed * (1.0 / denom), best + jnp.log(denom)
+
+
+def fold_kernel(nz, *refs):
+    pieces, outs = refs[:nz], refs[nz:]
+    depth = outs[0].shape[0] - STAT
+    for ky, out in enumerate(outs):
+        mixed, lse = merged([p[ky] for p in pieces])
+        out[:depth, :] = mixed.astype(BF)
+        out[depth:, :] = with_lse(lse)
+
+
+def fold(pieces):
+    nz = len(pieces)
+    shape = pieces[0].shape[1:]
+    return pl.pallas_call(
+        functools.partial(fold_kernel, nz),
+        out_shape=[jax.ShapeDtypeStruct(shape, BF)] * 2,
+        in_specs=[pl.BlockSpec(memory_space=pltpu.VMEM)] * nz,
+        out_specs=[pl.BlockSpec(memory_space=pltpu.VMEM)] * 2,
+        cost_estimate=pl.CostEstimate(
+            flops=4 * nz * pieces[0].size, bytes_accessed=4 * nz * pieces[0].size, transcendentals=0
+        ),
+        compiler_params=pltpu.CompilerParams(vmem_limit_bytes=16 * MIB),
+        name="fold",
+    )(*pieces)
+
+
+def project_kernel(nz, near, far, w_own, w_oth, res_own, res_oth, home, *refs):
+    outs, attn, part = refs[:nz], refs[nz], refs[nz + 1]
+    _, core, _, z = place()
+    depth = near.shape[0] - STAT
+    count = part.shape[0]
+    heads = near.shape[1] // count
+    mixed, _ = merged([near[...], far[...]])
+    mixed = mixed.T.astype(BF)
     if heads == 2:
-        first, second = merged[:count], merged[count:]
+        first, second = mixed[:count], mixed[count:]
         attn[...] = jnp.concatenate([first, second], axis=1)
     else:
-        first, second = merged[:, : depth // 2], merged[:, depth // 2 :]
-        attn[...] = merged
+        first, second = mixed[:, : depth // 2], mixed[:, depth // 2 :]
+        attn[...] = mixed
     low = (core == 0).astype(F32)
     first, second = first.astype(F32), second.astype(F32)
     own = (first * low + second * (1.0 - low)).astype(BF)
@@ -333,16 +371,15 @@
         outs[kz][...] = part[pl.ds(spot, block), :].astype(BF)
 
 
-def project(got, w_own, w_oth, res_own, res_oth, home, nz):
-    chips = got.shape[0]
+def project(near, far, w_own, w_oth, res_own, res_oth, home, nz):
     count = home.shape[0]
-    cols = D // chips
+    cols = D // (2 * nz)
     wide = res_own.shape[1]
     return pl.pallas_call(
         functools.partial(project_kernel, nz),
         out_shape=[jax.ShapeDtypeStruct((count // nz, wide), BF)] * nz
         + [jax.ShapeDtypeStruct((count, cols), BF)],
-        in_specs=[pl.BlockSpec(memory_space=pltpu.VMEM)] * 6,
+        in_specs=[pl.BlockSpec(memory_space=pltpu.VMEM)] * 7,
         out_specs=[pl.BlockSpec(memory_space=pltpu.VMEM)] * (nz + 1),
         scratch_shapes=[pltpu.VMEM((count, wide), F32)],
         cost_estimate=pl.CostEstimate(
@@ -350,7 +387,7 @@
         ),
         compiler_params=pltpu.CompilerParams(vmem_limit_bytes=12 * MIB),
         name="project",
-    )(got, w_own, w_oth, res_own, res_oth, home)
+    )(near, far, w_own, w_oth, res_own, res_oth, home)
 
 
 def expert_kernel(nz, width, *refs):
@@ -502,7 +539,6 @@
     per = queries.shape[0]
     cap = residual.shape[0]
     order = row_order.reshape(1, -1)
-    same_core = [[2 * i + c for i in range(chips)] for c in range(2)]
 
     def along_z(terms):
         out = [terms[0]]
@@ -533,11 +569,10 @@
     )
     res_oth = hop(res_own, 1, width)
 
-    partial = attention(pieces, k_own, v_own, k_oth, v_oth, lengths, chips)
-    got = lax.all_to_all(
-        partial, "ctx", split_axis=0, concat_axis=0, tiled=True, axis_index_groups=same_core
-    )
-    *parts, mixed = project(got, w_own, w_oth, res_own, res_oth, home, nz)
+    blocks = along_z(attention(pieces, k_own, v_own, k_oth, v_oth, lengths, chips))
+    mine, theirs = fold(blocks)
+    theirs = hop(theirs, 2, width)
+    *parts, mixed = project(mine, theirs, w_own, w_oth, res_own, res_oth, home, nz)
     chunk = add(*along_z(parts))
     (up,) = fetch(gate_up)
     other = hop(chunk, 2, width)

time: 82.8 us -> 84.3 us (1.018)
  Pallas kernels: 15.3 us -> 13.7 us
  starting transfers between devices: 30.6 us -> 32.2 us
  waiting for transfers between devices: 35.1 us -> 36.7 us
    ppermute x25 -> x29, waiting for transfers between devices: 29.7 us -> 36.7 us  [hop(): return lax.ppermute(x, 'ctx', [(i, i ^ mask) for i in range(width)])]
    ppermute x25 -> x29, starting transfers between devices: 26.2 us -> 32.2 us  [hop(): return lax.ppermute(x, 'ctx', [(i, i ^ mask) for i in range(width)])]
    all_to_all x1 -> x0, waiting for transfers between devices: 5.46 us -> none  [body(): lax.all_to_all(partial, 'ctx', split_axis=0, concat_axis=0, tiled=True, a...]
    all_to_all x1 -> x0, starting transfers between devices: 4.4 us -> none  [body(): lax.all_to_all(partial, 'ctx', split_axis=0, concat_axis=0, tiled=True, a...]
    pallas_call x1 -> x2, Pallas kernels: 3.91 us -> 2.3 us  [the longest x1 2.21 us: attention(): pl.pallas_call(functools.partial(attention_kernel, nz), out_shape=[jax.Sh...]
  transfers between devices with their start and end apart: 26 -> 29, of which waited for: 13 -> 16; matrix products, arithmetic and copies ran while one was open for 0% -> 0% of each run, Pallas kernels for 14% -> 12%
where the time goes in v2:
time: 84.3 us; the launch traced here: 84 us
  waiting for transfers between devices  36.7 us (44%)
  starting transfers between devices  32.2 us (38%)
  Pallas kernels  13.7 us (16%)
  between operations  1.43 us (2%)
    ppermute x29, waiting for transfers between devices, hop(): return lax.ppermute(x, 'ctx', [(i, i ^ mask) for i in range(width)])  36.7 us
    ppermute x29, starting transfers between devices, hop(): return lax.ppermute(x, 'ctx', [(i, i ^ mask) for i in range(width)])  32.2 us
    pallas_call x3, Pallas kernels, fetch(): pl.pallas_call(functools.partial(fetch_kernel, count), out_shape=[pltpu.V...  5.77 us
    pallas_call x1, Pallas kernels, attention(): pl.pallas_call(functools.partial(attention_kernel, nz), out_shape=[jax.Sh...  2.21 us
    pallas_call x1, Pallas kernels, experts(): pl.pallas_call(functools.partial(expert_kernel, nz, width), out_shape=[wi...  2.2 us
    pallas_call x1, Pallas kernels, prepare(): pl.pallas_call(functools.partial(prepare_kernel, per, width), out_shape=[...  1.98 us
  transfers between devices with their start and end apart: 29, of which 16 were waited for; matrix products, arithmetic and copies ran while one was open for 0% of the time, Pallas kernels for 12%

profile of v2, /device:TPU:0, one launch (start us, length us, event | category | flops | bytes accessed | tf_op | source)
XLA Modules:
  0.0 84.0 jit_solution(12633639731900552656)
XLA Ops:
  1.7 2.6 %collective-permute-start = (bf16[8,2048]{1,0:T(8,128)(2,1)}, bf16[8,2048]{1,0:T(8,128)(2,1)S(1)}, u32[]{:S(2)}, u32[]{:S(2)}) collective-permute-start(bf16[8,2048]{1,0:T(8,128)(2,1)} %refs_0_.3), channel_id=1, source_target_pairs={{0,2},{1,3},{2,0},{3,1},{4,6},{5,7},{6,4},{7,5},{8,10},{9,11},{10,... | collective-permute-start | bytes 98312 | tf_op jit(solution)/shard_map/ppermute | solution.py:39
  4.3 1.1 %fetch.3 = (bf16[8,2048]{1,0:T(8,128)(2,1)S(1)}, bf16[1,512,256]{2,1,0:T(8,128)(2,1)S(1)}, bf16[1,512,256]{2,1,0:T(8,128)(2,1)S(1)}) custom-call(bf16[8,2048]{1,0:T(8,128)(2,1)} %refs_0_.3, bf16[1,512,256]{2,1,0:T(8,128)(2,1)} %refs_1_.1, bf16[1,512,256]{2,1,0:T(8,128)(2,1)} %refs_2_.1), custom_call_target="tpu_custom_call" | custom-call | bytes 1114112 | tf_op jit(solution)/shard_map/fetch/pallas_call | solution.py:72
  5.4 1.1 %collective-permute-done.second = bf16[8,2048]{1,0:T(8,128)(2,1)S(1)} collective-permute-done((bf16[8,2048]{1,0:T(8,128)(2,1)}, bf16[8,2048]{1,0:T(8,128)(2,1)S(1)}, u32[]{:S(2)}, u32[]{:S(2)}) %collective-permute-start) | collective-permute-done | bytes 32800 | tf_op jit(solution)/shard_map/ppermute | solution.py:39
  6.5 4.0 %collective-permute-start.3 = (bf16[2,8,2048]{2,1,0:T(8,128)(2,1)S(1)}, bf16[2,8,2048]{2,1,0:T(8,128)(2,1)S(1)}, u32[]{:S(2)}, u32[]{:S(2)}) collective-permute-start(bf16[2,8,2048]{2,1,0:T(8,128)(2,1)S(1)} %shard_map.140.refs_0_), channel_id=1, source_target_pairs={{0,12},{1,13},{2,14},{3,15},{4,8},{5,9},{6,10},{7,11},{8,4},{9,5},... | collective-permute-start | bytes 196616 | tf_op jit(solution)/shard_map/ppermute | solution.py:39
  10.5 3.0 %collective-permute-done.3.refs_3_ = bf16[2,8,2048]{2,1,0:T(8,128)(2,1)S(1)} collective-permute-done((bf16[2,8,2048]{2,1,0:T(8,128)(2,1)S(1)}, bf16[2,8,2048]{2,1,0:T(8,128)(2,1)S(1)}, u32[]{:S(2)}, u32[]{:S(2)}) %collective-permute-start.3) | collective-permute-done | bytes 65568 | tf_op jit(solution)/shard_map/ppermute | solution.py:39
  15.7 2.1 %collective-permute-done.1.refs_1_ = bf16[2,8,2048]{2,1,0:T(8,128)(2,1)S(1)} collective-permute-done((bf16[2,8,2048]{2,1,0:T(8,128)(2,1)S(1)}, bf16[2,8,2048]{2,1,0:T(8,128)(2,1)S(1)}, u32[]{:S(2)}, u32[]{:S(2)}) %collective-permute-start.1) | collective-permute-done | bytes 65568 | tf_op jit(solution)/shard_map/ppermute | solution.py:39
  17.8 2.2 %attention.1 = (bf16[2,136,128]{2,1,0:T(8,128)(2,1)S(1)}, bf16[2,136,128]{2,1,0:T(8,128)(2,1)S(1)}, bf16[2,136,128]{2,1,0:T(8,128)(2,1)S(1)}, bf16[2,136,128]{2,1,0:T(8,128)(2,1)S(1)}) custom-call(s32[1]{0:T(128)S(6)} %copy.15.lengths, bf16[2,8,2048]{2,1,0:T(8,128)(2,1)S(1)} %shard_map.140.refs_0_, bf16[2,8,2048]{2,1,0:T(8,128)(2,1)S(1)} %collective-permute-done.1.refs_1_, ...), custom_call_target="tpu_custom_call" | custom-call | flops 536870912 | bytes 1048576 | tf_op jit(solution)/shard_map/attention/pallas_call | solution.py:290
  20.8 3.5 %collective-permute-start.7 = (bf16[2,136,128]{2,1,0:T(8,128)(2,1)S(1)}, bf16[2,136,128]{2,1,0:T(8,128)(2,1)S(1)}, u32[]{:S(2)}, u32[]{:S(2)}) collective-permute-start(bf16[2,136,128]{2,1,0:T(8,128)(2,1)S(1)} %get-tuple-element.36), channel_id=1, source_target_pairs={{0,8},{1,9},{2,10},{3,11},{4,12},{5,13},{6,14},{7,15},{8,0},{9,1},... | collective-permute-start | bytes 208904 | tf_op jit(solution)/shard_map/ppermute | solution.py:39
  24.4 2.0 %prepare.1 = (bf16[16,2176]{1,0:T(8,128)(2,1)S(1)}, bf16[64,32]{1,0:T(8,128)(2,1)S(1)}, bf16[256,64]{1,0:T(8,128)(2,1)S(1)}, bf16[256,128]{1,0:T(8,128)(2,1)S(1)...) custom-call(s32[1,16]{1,0:T(1,128)} %bitcast.8, s32[1,128]{1,0:T(1,128)} %bitcast.9, s32[8,16]{1,0:T(8,128)} %bitcast.6, ...), custom_call_target="tpu_custom_call" | custom-call | flops 12582912 | bytes 131072 | tf_op jit(solution)/shard_map/prepare/pallas_call | solution.py:152
  26.5 1.1 %collective-permute-done.7.refs_2_ = bf16[2,136,128]{2,1,0:T(8,128)(2,1)S(1)} collective-permute-done((bf16[2,136,128]{2,1,0:T(8,128)(2,1)S(1)}, bf16[2,136,128]{2,1,0:T(8,128)(2,1)S(1)}, u32[]{:S(2)}, u32[]{:S(2)}) %collective-permute-start.7) | collective-permute-done | bytes 69664 | tf_op jit(solution)/shard_map/ppermute | solution.py:39
  27.6 2.8 %collective-permute-done.8.refs_3_ = bf16[2,136,128]{2,1,0:T(8,128)(2,1)S(1)} collective-permute-done((bf16[2,136,128]{2,1,0:T(8,128)(2,1)S(1)}, bf16[2,136,128]{2,1,0:T(8,128)(2,1)S(1)}, u32[]{:S(2)}, u32[]{:S(2)}) %collective-permute-start.8) | collective-permute-done | bytes 69664 | tf_op jit(solution)/shard_map/ppermute | solution.py:39
  30.5 1.6 %collective-permute-start.9 = (bf16[136,128]{1,0:T(8,128)(2,1)S(1)}, bf16[136,128]{1,0:T(8,128)(2,1)S(1)}, u32[]{:S(2)}, u32[]{:S(2)}) collective-permute-start(bf16[136,128]{1,0:T(8,128)(2,1)S(1)} %get-tuple-element.39), channel_id=1, source_target_pairs={{0,2},{1,3},{2,0},{3,1},{4,6},{5,7},{6,4},{7,5},{8,10},{9,11},{10,... | collective-permute-start | bytes 104456 | tf_op jit(solution)/shard_map/ppermute | solution.py:39
  32.1 2.4 %collective-permute-done.9.far = bf16[136,128]{1,0:T(8,128)(2,1)S(1)} collective-permute-done((bf16[136,128]{1,0:T(8,128)(2,1)S(1)}, bf16[136,128]{1,0:T(8,128)(2,1)S(1)}, u32[]{:S(2)}, u32[]{:S(2)}) %collective-permute-start.9) | collective-permute-done | bytes 34848 | tf_op jit(solution)/shard_map/ppermute | solution.py:39
  35.1 1.4 %collective-permute-start.13 = (bf16[16,2176]{1,0:T(8,128)(2,1)S(1)}, bf16[16,2176]{1,0:T(8,128)(2,1)S(1)}, u32[]{:S(2)}, u32[]{:S(2)}) collective-permute-start(bf16[16,2176]{1,0:T(8,128)(2,1)S(1)} %get-tuple-element.45), channel_id=1, source_target_pairs={{0,8},{1,9},{2,10},{3,11},{4,12},{5,13},{6,14},{7,15},{8,0},{9,1},... | collective-permute-start | bytes 208904 | tf_op jit(solution)/shard_map/ppermute | solution.py:39
  36.5 3.0 %collective-permute-start.14 = (bf16[16,2176]{1,0:T(8,128)(2,1)S(1)}, bf16[16,2176]{1,0:T(8,128)(2,1)S(1)}, u32[]{:S(2)}, u32[]{:S(2)}) collective-permute-start(bf16[16,2176]{1,0:T(8,128)(2,1)S(1)} %get-tuple-element.46), channel_id=1, source_target_pairs={{0,12},{1,13},{2,14},{3,15},{4,8},{5,9},{6,10},{7,11},{8,4},{9,5},... | collective-permute-start | bytes 208904 | tf_op jit(solution)/shard_map/ppermute | solution.py:39
  39.5 1.4 %collective-permute-done.12.refs_1_ = bf16[16,2176]{1,0:T(8,128)(2,1)S(1)} collective-permute-done((bf16[16,2176]{1,0:T(8,128)(2,1)S(1)}, bf16[16,2176]{1,0:T(8,128)(2,1)S(1)}, u32[]{:S(2)}, u32[]{:S(2)}) %collective-permute-start.12) | collective-permute-done | bytes 69664 | tf_op jit(solution)/shard_map/ppermute | solution.py:39
  40.9 1.7 %collective-permute-done.14.refs_3_ = bf16[16,2176]{1,0:T(8,128)(2,1)S(1)} collective-permute-done((bf16[16,2176]{1,0:T(8,128)(2,1)S(1)}, bf16[16,2176]{1,0:T(8,128)(2,1)S(1)}, u32[]{:S(2)}, u32[]{:S(2)}) %collective-permute-start.14) | collective-permute-done | bytes 69664 | tf_op jit(solution)/shard_map/ppermute | solution.py:39
  42.7 1.6 %collective-permute-start.15 = (bf16[16,2176]{1,0:T(8,128)(2,1)S(1)}, bf16[16,2176]{1,0:T(8,128)(2,1)S(1)}, u32[]{:S(2)}, u32[]{:S(2)}) collective-permute-start(bf16[16,2176]{1,0:T(8,128)(2,1)S(1)} %shard_map.141.refs_0_), channel_id=1, source_target_pairs={{0,2},{1,3},{2,0},{3,1},{4,6},{5,7},{6,4},{7,5},{8,10},{9,11},{10,... | collective-permute-start | bytes 208904 | tf_op jit(solution)/shard_map/ppermute | solution.py:39
  44.3 2.8 %collective-permute-done.15.refs_1_ = bf16[16,2176]{1,0:T(8,128)(2,1)S(1)} collective-permute-done((bf16[16,2176]{1,0:T(8,128)(2,1)S(1)}, bf16[16,2176]{1,0:T(8,128)(2,1)S(1)}, u32[]{:S(2)}, u32[]{:S(2)}) %collective-permute-start.15) | collective-permute-done | bytes 69664 | tf_op jit(solution)/shard_map/ppermute | solution.py:39
  47.1 3.0 %collective-permute-start.18 = (bf16[16,2176]{1,0:T(8,128)(2,1)S(1)}, bf16[16,2176]{1,0:T(8,128)(2,1)S(1)}, u32[]{:S(2)}, u32[]{:S(2)}) collective-permute-start(bf16[16,2176]{1,0:T(8,128)(2,1)S(1)} %shard_map.142.refs_0_), channel_id=1, source_target_pairs={{0,12},{1,13},{2,14},{3,15},{4,8},{5,9},{6,10},{7,11},{8,4},{9,5},... | collective-permute-start | bytes 208904 | tf_op jit(solution)/shard_map/ppermute | solution.py:39
  50.1 1.4 %collective-permute-start.16 = (bf16[16,2176]{1,0:T(8,128)(2,1)S(1)}, bf16[16,2176]{1,0:T(8,128)(2,1)S(1)}, u32[]{:S(2)}, u32[]{:S(2)}) collective-permute-start(bf16[16,2176]{1,0:T(8,128)(2,1)S(1)} %shard_map.142.refs_0_), channel_id=1, source_target_pairs={{0,4},{1,5},{2,6},{3,7},{4,0},{5,1},{6,2},{7,3},{8,12},{9,13},{10,... | collective-permute-start | bytes 208904 | tf_op jit(solution)/shard_map/ppermute | solution.py:39
  51.5 1.7 %collective-permute-done.18.refs_3_ = bf16[16,2176]{1,0:T(8,128)(2,1)S(1)} collective-permute-done((bf16[16,2176]{1,0:T(8,128)(2,1)S(1)}, bf16[16,2176]{1,0:T(8,128)(2,1)S(1)}, u32[]{:S(2)}, u32[]{:S(2)}) %collective-permute-start.18) | collective-permute-done | bytes 69664 | tf_op jit(solution)/shard_map/ppermute | solution.py:39
  53.3 2.1 %collective-permute-done.17.refs_2_ = bf16[16,2176]{1,0:T(8,128)(2,1)S(1)} collective-permute-done((bf16[16,2176]{1,0:T(8,128)(2,1)S(1)}, bf16[16,2176]{1,0:T(8,128)(2,1)S(1)}, u32[]{:S(2)}, u32[]{:S(2)}) %collective-permute-start.17) | collective-permute-done | bytes 69664 | tf_op jit(solution)/shard_map/ppermute | solution.py:39
  55.8 1.9 %fetch.5.refs_10_ = bf16[1,768,2048]{2,1,0:T(8,128)(2,1)S(1)} custom-call(bf16[1,768,2048]{2,1,0:T(8,128)(2,1)} %refs_0_.5), custom_call_target="tpu_custom_call" | custom-call | bytes 6291456 | tf_op jit(solution)/shard_map/fetch/pallas_call | solution.py:72
  57.7 2.8 %fetch.4.refs_9_ = bf16[1,2048,1536]{2,1,0:T(8,128)(2,1)S(1)} custom-call(bf16[1,2048,1536]{2,1,0:T(8,128)(2,1)} %refs_0_.4), custom_call_target="tpu_custom_call" | custom-call | bytes 12582912 | tf_op jit(solution)/shard_map/fetch/pallas_call | solution.py:72
  60.6 2.2 %experts.1 = (bf16[64,2304]{1,0:T(8,128)(2,1)S(1)}, bf16[64,2304]{1,0:T(8,128)(2,1)S(1)}, bf16[64,2304]{1,0:T(8,128)(2,1)S(1)}, bf16[64,2304]{1,0:T(8,128)(2,1)S(1)}, bf16[16,2048]{1,0:T(8,128)(2,1)S(1)}) custom-call(bf16[16,2176]{1,0:T(8,128)(2,1)S(1)} %shard_map.142.refs_0_, bf16[16,2176]{1,0:T(8,128)(2,1)S(1)} %collective-permute-done.16.refs_1_, ...), custom_call_target="tpu_custom_call" | custom-call | flops 1207959552 | bytes 9437184 | tf_op jit(solution)/shard_map/experts/pallas_call | solution.py:435
  63.3 1.1 %collective-permute-done.24.refs_1_ = bf16[64,2304]{1,0:T(8,128)(2,1)S(1)} collective-permute-done((bf16[64,2304]{1,0:T(8,128)(2,1)S(1)}, bf16[64,2304]{1,0:T(8,128)(2,1)S(1)}, u32[]{:S(2)}, u32[]{:S(2)}) %collective-permute-start.24) | collective-permute-done | bytes 294944 | tf_op jit(solution)/shard_map/ppermute | solution.py:39
  64.5 1.6 %collective-permute-start.25 = (bf16[64,2304]{1,0:T(8,128)(2,1)S(1)}, bf16[64,2304]{1,0:T(8,128)(2,1)S(1)}, u32[]{:S(2)}, u32[]{:S(2)}) collective-permute-start(bf16[64,2304]{1,0:T(8,128)(2,1)S(1)} %shard_map.143), channel_id=1, source_target_pairs={{0,2},{1,3},{2,0},{3,1},{4,6},{5,7},{6,4},{7,5},{8,10},{9,11},{10,... | collective-permute-start | bytes 884744 | tf_op jit(solution)/shard_map/ppermute | solution.py:39
  66.1 7.5 %collective-permute-done.25.far = bf16[64,2304]{1,0:T(8,128)(2,1)S(1)} collective-permute-done((bf16[64,2304]{1,0:T(8,128)(2,1)S(1)}, bf16[64,2304]{1,0:T(8,128)(2,1)S(1)}, u32[]{:S(2)}, u32[]{:S(2)}) %collective-permute-start.25) | collective-permute-done | bytes 294944 | tf_op jit(solution)/shard_map/ppermute | solution.py:39
  74.2 2.4 %collective-permute-start.27 = (bf16[16,2560]{1,0:T(8,128)(2,1)S(1)}, bf16[16,2560]{1,0:T(8,128)(2,1)S(1)}, u32[]{:S(2)}, u32[]{:S(2)}) collective-permute-start(bf16[16,2560]{1,0:T(8,128)(2,1)S(1)} %get-tuple-element.58), channel_id=1, source_target_pairs={{0,8},{1,9},{2,10},{3,11},{4,12},{5,13},{6,14},{7,15},{8,0},{9,1},... | collective-permute-start | bytes 245768 | tf_op jit(solution)/shard_map/ppermute | solution.py:39
  76.7 1.5 %collective-permute-start.28 = (bf16[16,2560]{1,0:T(8,128)(2,1)S(1)}, bf16[16,2560]{1,0:T(8,128)(2,1)S(1)}, u32[]{:S(2)}, u32[]{:S(2)}) collective-permute-start(bf16[16,2560]{1,0:T(8,128)(2,1)S(1)} %get-tuple-element.59), channel_id=1, source_target_pairs={{0,12},{1,13},{2,14},{3,15},{4,8},{5,9},{6,10},{7,11},{8,4},{9,5},... | collective-permute-start | bytes 245768 | tf_op jit(solution)/shard_map/ppermute | solution.py:39
  78.7 4.6 %collective-permute-done.27.refs_2_ = bf16[16,2560]{1,0:T(8,128)(2,1)S(1)} collective-permute-done((bf16[16,2560]{1,0:T(8,128)(2,1)S(1)}, bf16[16,2560]{1,0:T(8,128)(2,1)S(1)}, u32[]{:S(2)}, u32[]{:S(2)}) %collective-permute-start.27) | collective-permute-done | bytes 81952 | tf_op jit(solution)/shard_map/ppermute | solution.py:39
  (40 shorter events, 7.4 us)
Async XLA Ops:
  0.6 33.9 %collective-permute-start.10 = (bf16[128,2048]{1,0:T(8,128)(2,1)}, bf16[128,2048]{1,0:T(8,128)(2,1)S(1)}, u32[]{:S(2)}, u32[]{:S(2)}) collective-permute-start(bf16[128,2048]{1,0:T(8,128)(2,1)} %refs_5_.1), channel_id=1, source_target_pairs={{0,1},{1,0},{2,3},{3,2},{4,5},{5,4},{6,7},{7,6},{8,9},{9,8},{10,11... | collective-permute-start | bytes 1572872 | tf_op jit(solution)/shard_map/ppermute | solution.py:39
  1.2 16.6 %collective-permute-start.4 = (bf16[1,512,256]{2,1,0:T(8,128)(2,1)}, bf16[1,512,256]{2,1,0:T(8,128)(2,1)S(1)}, u32[]{:S(2)}, u32[]{:S(2)}) collective-permute-start(bf16[1,512,256]{2,1,0:T(8,128)(2,1)} %refs_1_.1), channel_id=1, source_target_pairs={{0,1},{1,0},{2,3},{3,2},{4,5},{5,4},{6,7},{7,6},{8,9},{9,8},{10,11... | collective-permute-start | bytes 786440 | tf_op jit(solution)/shard_map/ppermute | solution.py:39
  1.3 16.5 %collective-permute-start.5 = (bf16[1,512,256]{2,1,0:T(8,128)(2,1)}, bf16[1,512,256]{2,1,0:T(8,128)(2,1)S(1)}, u32[]{:S(2)}, u32[]{:S(2)}) collective-permute-start(bf16[1,512,256]{2,1,0:T(8,128)(2,1)} %refs_2_.1), channel_id=1, source_target_pairs={{0,1},{1,0},{2,3},{3,2},{4,5},{5,4},{6,7},{7,6},{8,9},{9,8},{10,11... | collective-permute-start | bytes 786440 | tf_op jit(solution)/shard_map/ppermute | solution.py:39
  1.7 4.8 %collective-permute-start = (bf16[8,2048]{1,0:T(8,128)(2,1)}, bf16[8,2048]{1,0:T(8,128)(2,1)S(1)}, u32[]{:S(2)}, u32[]{:S(2)}) collective-permute-start(bf16[8,2048]{1,0:T(8,128)(2,1)} %refs_0_.3), channel_id=1, source_target_pairs={{0,2},{1,3},{2,0},{3,1},{4,6},{5,7},{6,4},{7,5},{8,10},{9,11},{10,... | collective-permute-start | bytes 98312 | tf_op jit(solution)/shard_map/ppermute | solution.py:39
  6.5 7.0 %collective-permute-start.3 = (bf16[2,8,2048]{2,1,0:T(8,128)(2,1)S(1)}, bf16[2,8,2048]{2,1,0:T(8,128)(2,1)S(1)}, u32[]{:S(2)}, u32[]{:S(2)}) collective-permute-start(bf16[2,8,2048]{2,1,0:T(8,128)(2,1)S(1)} %shard_map.140.refs_0_), channel_id=1, source_target_pairs={{0,12},{1,13},{2,14},{3,15},{4,8},{5,9},{6,10},{7,11},{8,4},{9,5},... | collective-permute-start | bytes 196616 | tf_op jit(solution)/shard_map/ppermute | solution.py:39
  10.5 5.2 %collective-permute-start.2 = (bf16[2,8,2048]{2,1,0:T(8,128)(2,1)S(1)}, bf16[2,8,2048]{2,1,0:T(8,128)(2,1)S(1)}, u32[]{:S(2)}, u32[]{:S(2)}) collective-permute-start(bf16[2,8,2048]{2,1,0:T(8,128)(2,1)S(1)} %shard_map.140.refs_0_), channel_id=1, source_target_pairs={{0,8},{1,9},{2,10},{3,11},{4,12},{5,13},{6,14},{7,15},{8,0},{9,1},... | collective-permute-start | bytes 196616 | tf_op jit(solution)/shard_map/ppermute | solution.py:39
  13.5 4.3 %collective-permute-start.1 = (bf16[2,8,2048]{2,1,0:T(8,128)(2,1)S(1)}, bf16[2,8,2048]{2,1,0:T(8,128)(2,1)S(1)}, u32[]{:S(2)}, u32[]{:S(2)}) collective-permute-start(bf16[2,8,2048]{2,1,0:T(8,128)(2,1)S(1)} %shard_map.140.refs_0_), channel_id=1, source_target_pairs={{0,4},{1,5},{2,6},{3,7},{4,0},{5,1},{6,2},{7,3},{8,12},{9,13},{10,... | collective-permute-start | bytes 196616 | tf_op jit(solution)/shard_map/ppermute | solution.py:39
  20.0 6.5 %collective-permute-start.6 = (bf16[2,136,128]{2,1,0:T(8,128)(2,1)S(1)}, bf16[2,136,128]{2,1,0:T(8,128)(2,1)S(1)}, u32[]{:S(2)}, u32[]{:S(2)}) collective-permute-start(bf16[2,136,128]{2,1,0:T(8,128)(2,1)S(1)} %get-tuple-element.35), channel_id=1, source_target_pairs={{0,4},{1,5},{2,6},{3,7},{4,0},{5,1},{6,2},{7,3},{8,12},{9,13},{10,... | collective-permute-start | bytes 208904 | tf_op jit(solution)/shard_map/ppermute | solution.py:39
  20.8 6.8 %collective-permute-start.7 = (bf16[2,136,128]{2,1,0:T(8,128)(2,1)S(1)}, bf16[2,136,128]{2,1,0:T(8,128)(2,1)S(1)}, u32[]{:S(2)}, u32[]{:S(2)}) collective-permute-start(bf16[2,136,128]{2,1,0:T(8,128)(2,1)S(1)} %get-tuple-element.36), channel_id=1, source_target_pairs={{0,8},{1,9},{2,10},{3,11},{4,12},{5,13},{6,14},{7,15},{8,0},{9,1},... | collective-permute-start | bytes 208904 | tf_op jit(solution)/shard_map/ppermute | solution.py:39
  24.3 6.1 %collective-permute-start.8 = (bf16[2,136,128]{2,1,0:T(8,128)(2,1)S(1)}, bf16[2,136,128]{2,1,0:T(8,128)(2,1)S(1)}, u32[]{:S(2)}, u32[]{:S(2)}) collective-permute-start(bf16[2,136,128]{2,1,0:T(8,128)(2,1)S(1)} %get-tuple-element.37), channel_id=1, source_target_pairs={{0,12},{1,13},{2,14},{3,15},{4,8},{5,9},{6,10},{7,11},{8,4},{9,5},... | collective-permute-start | bytes 208904 | tf_op jit(solution)/shard_map/ppermute | solution.py:39
  26.4 5.7 %collective-permute-start.11 = (bf16[16,2176]{1,0:T(8,128)(2,1)S(1)}, bf16[16,2176]{1,0:T(8,128)(2,1)S(1)}, u32[]{:S(2)}, u32[]{:S(2)}) collective-permute-start(bf16[16,2176]{1,0:T(8,128)(2,1)S(1)} %get-tuple-element.41.res_own), channel_id=1, source_target_pairs={{0,1},{1,0},{2,3},{3,2},{4,5},{5,4},{6,7},{7,6},{8,9},{9,8},{10,11... | collective-permute-start | bytes 208904 | tf_op jit(solution)/shard_map/ppermute | solution.py:39
  30.5 4.0 %collective-permute-start.9 = (bf16[136,128]{1,0:T(8,128)(2,1)S(1)}, bf16[136,128]{1,0:T(8,128)(2,1)S(1)}, u32[]{:S(2)}, u32[]{:S(2)}) collective-permute-start(bf16[136,128]{1,0:T(8,128)(2,1)S(1)} %get-tuple-element.39), channel_id=1, source_target_pairs={{0,2},{1,3},{2,0},{3,1},{4,6},{5,7},{6,4},{7,5},{8,10},{9,11},{10,... | collective-permute-start | bytes 104456 | tf_op jit(solution)/shard_map/ppermute | solution.py:39
  35.0 5.9 %collective-permute-start.12 = (bf16[16,2176]{1,0:T(8,128)(2,1)S(1)}, bf16[16,2176]{1,0:T(8,128)(2,1)S(1)}, u32[]{:S(2)}, u32[]{:S(2)}) collective-permute-start(bf16[16,2176]{1,0:T(8,128)(2,1)S(1)} %get-tuple-element.44), channel_id=1, source_target_pairs={{0,4},{1,5},{2,6},{3,7},{4,0},{5,1},{6,2},{7,3},{8,12},{9,13},{10,... | collective-permute-start | bytes 208904 | tf_op jit(solution)/shard_map/ppermute | solution.py:39
  35.1 5.8 %collective-permute-start.13 = (bf16[16,2176]{1,0:T(8,128)(2,1)S(1)}, bf16[16,2176]{1,0:T(8,128)(2,1)S(1)}, u32[]{:S(2)}, u32[]{:S(2)}) collective-permute-start(bf16[16,2176]{1,0:T(8,128)(2,1)S(1)} %get-tuple-element.45), channel_id=1, source_target_pairs={{0,8},{1,9},{2,10},{3,11},{4,12},{5,13},{6,14},{7,15},{8,0},{9,1},... | collective-permute-start | bytes 208904 | tf_op jit(solution)/shard_map/ppermute | solution.py:39
  36.5 6.1 %collective-permute-start.14 = (bf16[16,2176]{1,0:T(8,128)(2,1)S(1)}, bf16[16,2176]{1,0:T(8,128)(2,1)S(1)}, u32[]{:S(2)}, u32[]{:S(2)}) collective-permute-start(bf16[16,2176]{1,0:T(8,128)(2,1)S(1)} %get-tuple-element.46), channel_id=1, source_target_pairs={{0,12},{1,13},{2,14},{3,15},{4,8},{5,9},{6,10},{7,11},{8,4},{9,5},... | collective-permute-start | bytes 208904 | tf_op jit(solution)/shard_map/ppermute | solution.py:39
  42.7 4.4 %collective-permute-start.15 = (bf16[16,2176]{1,0:T(8,128)(2,1)S(1)}, bf16[16,2176]{1,0:T(8,128)(2,1)S(1)}, u32[]{:S(2)}, u32[]{:S(2)}) collective-permute-start(bf16[16,2176]{1,0:T(8,128)(2,1)S(1)} %shard_map.141.refs_0_), channel_id=1, source_target_pairs={{0,2},{1,3},{2,0},{3,1},{4,6},{5,7},{6,4},{7,5},{8,10},{9,11},{10,... | collective-permute-start | bytes 208904 | tf_op jit(solution)/shard_map/ppermute | solution.py:39
  47.1 6.2 %collective-permute-start.18 = (bf16[16,2176]{1,0:T(8,128)(2,1)S(1)}, bf16[16,2176]{1,0:T(8,128)(2,1)S(1)}, u32[]{:S(2)}, u32[]{:S(2)}) collective-permute-start(bf16[16,2176]{1,0:T(8,128)(2,1)S(1)} %shard_map.142.refs_0_), channel_id=1, source_target_pairs={{0,12},{1,13},{2,14},{3,15},{4,8},{5,9},{6,10},{7,11},{8,4},{9,5},... | collective-permute-start | bytes 208904 | tf_op jit(solution)/shard_map/ppermute | solution.py:39
  50.1 5.2 %collective-permute-start.17 = (bf16[16,2176]{1,0:T(8,128)(2,1)S(1)}, bf16[16,2176]{1,0:T(8,128)(2,1)S(1)}, u32[]{:S(2)}, u32[]{:S(2)}) collective-permute-start(bf16[16,2176]{1,0:T(8,128)(2,1)S(1)} %shard_map.142.refs_0_), channel_id=1, source_target_pairs={{0,8},{1,9},{2,10},{3,11},{4,12},{5,13},{6,14},{7,15},{8,0},{9,1},... | collective-permute-start | bytes 208904 | tf_op jit(solution)/shard_map/ppermute | solution.py:39
  50.1 5.2 %collective-permute-start.16 = (bf16[16,2176]{1,0:T(8,128)(2,1)S(1)}, bf16[16,2176]{1,0:T(8,128)(2,1)S(1)}, u32[]{:S(2)}, u32[]{:S(2)}) collective-permute-start(bf16[16,2176]{1,0:T(8,128)(2,1)S(1)} %shard_map.142.refs_0_), channel_id=1, source_target_pairs={{0,4},{1,5},{2,6},{3,7},{4,0},{5,1},{6,2},{7,3},{8,12},{9,13},{10,... | collective-permute-start | bytes 208904 | tf_op jit(solution)/shard_map/ppermute | solution.py:39
  51.5 9.0 %collective-permute-start.19 = (bf16[16,2176]{1,0:T(8,128)(2,1)S(1)}, bf16[16,2176]{1,0:T(8,128)(2,1)S(1)}, u32[]{:S(2)}, u32[]{:S(2)}) collective-permute-start(bf16[16,2176]{1,0:T(8,128)(2,1)S(1)} %shard_map.142.refs_0_), channel_id=1, source_target_pairs={{0,1},{1,0},{2,3},{3,2},{4,5},{5,4},{6,7},{7,6},{8,9},{9,8},{10,11... | collective-permute-start | bytes 208904 | tf_op jit(solution)/shard_map/ppermute | solution.py:39
  53.3 7.3 %collective-permute-start.22 = (bf16[16,2176]{1,0:T(8,128)(2,1)S(1)}, bf16[16,2176]{1,0:T(8,128)(2,1)S(1)}, u32[]{:S(2)}, u32[]{:S(2)}) collective-permute-start(bf16[16,2176]{1,0:T(8,128)(2,1)S(1)} %collective-permute-done.18.refs_3_), channel_id=1, source_target_pairs={{0,1},{1,0},{2,3},{3,2},{4,5},{5,4},{6,7},{7,6},{8,9},{9,8},{10,11... | collective-permute-start | bytes 208904 | tf_op jit(solution)/shard_map/ppermute | solution.py:39
  55.3 5.2 %collective-permute-start.21 = (bf16[16,2176]{1,0:T(8,128)(2,1)S(1)}, bf16[16,2176]{1,0:T(8,128)(2,1)S(1)}, u32[]{:S(2)}, u32[]{:S(2)}) collective-permute-start(bf16[16,2176]{1,0:T(8,128)(2,1)S(1)} %collective-permute-done.17.refs_2_), channel_id=1, source_target_pairs={{0,1},{1,0},{2,3},{3,2},{4,5},{5,4},{6,7},{7,6},{8,9},{9,8},{10,11... | collective-permute-start | bytes 208904 | tf_op jit(solution)/shard_map/ppermute | solution.py:39
  55.3 5.3 %collective-permute-start.20 = (bf16[16,2176]{1,0:T(8,128)(2,1)S(1)}, bf16[16,2176]{1,0:T(8,128)(2,1)S(1)}, u32[]{:S(2)}, u32[]{:S(2)}) collective-permute-start(bf16[16,2176]{1,0:T(8,128)(2,1)S(1)} %collective-permute-done.16.refs_1_), channel_id=1, source_target_pairs={{0,1},{1,0},{2,3},{3,2},{4,5},{5,4},{6,7},{7,6},{8,9},{9,8},{10,11... | collective-permute-start | bytes 208904 | tf_op jit(solution)/shard_map/ppermute | solution.py:39
  62.8 1.6 %collective-permute-start.24 = (bf16[64,2304]{1,0:T(8,128)(2,1)S(1)}, bf16[64,2304]{1,0:T(8,128)(2,1)S(1)}, u32[]{:S(2)}, u32[]{:S(2)}) collective-permute-start(bf16[64,2304]{1,0:T(8,128)(2,1)S(1)} %get-tuple-element.55), channel_id=1, source_target_pairs={{0,1},{1,0},{2,3},{3,2},{4,5},{5,4},{6,7},{7,6},{8,9},{9,8},{10,11... | collective-permute-start | bytes 884744 | tf_op jit(solution)/shard_map/ppermute | solution.py:39
  62.8 3.3 %collective-permute-start.23 = (bf16[64,2304]{1,0:T(8,128)(2,1)S(1)}, bf16[64,2304]{1,0:T(8,128)(2,1)S(1)}, u32[]{:S(2)}, u32[]{:S(2)}) collective-permute-start(bf16[64,2304]{1,0:T(8,128)(2,1)S(1)} %get-tuple-element.53), channel_id=1, source_target_pairs={{0,1},{1,0},{2,3},{3,2},{4,5},{5,4},{6,7},{7,6},{8,9},{9,8},{10,11... | collective-permute-start | bytes 884744 | tf_op jit(solution)/shard_map/ppermute | solution.py:39
  64.5 9.1 %collective-permute-start.25 = (bf16[64,2304]{1,0:T(8,128)(2,1)S(1)}, bf16[64,2304]{1,0:T(8,128)(2,1)S(1)}, u32[]{:S(2)}, u32[]{:S(2)}) collective-permute-start(bf16[64,2304]{1,0:T(8,128)(2,1)S(1)} %shard_map.143), channel_id=1, source_target_pairs={{0,2},{1,3},{2,0},{3,1},{4,6},{5,7},{6,4},{7,5},{8,10},{9,11},{10,... | collective-permute-start | bytes 884744 | tf_op jit(solution)/shard_map/ppermute | solution.py:39
  73.7 5.0 %collective-permute-start.26 = (bf16[16,2560]{1,0:T(8,128)(2,1)S(1)}, bf16[16,2560]{1,0:T(8,128)(2,1)S(1)}, u32[]{:S(2)}, u32[]{:S(2)}) collective-permute-start(bf16[16,2560]{1,0:T(8,128)(2,1)S(1)} %get-tuple-element.57), channel_id=1, source_target_pairs={{0,4},{1,5},{2,6},{3,7},{4,0},{5,1},{6,2},{7,3},{8,12},{9,13},{10,... | collective-permute-start | bytes 245768 | tf_op jit(solution)/shard_map/ppermute | solution.py:39
  74.2 9.1 %collective-permute-start.27 = (bf16[16,2560]{1,0:T(8,128)(2,1)S(1)}, bf16[16,2560]{1,0:T(8,128)(2,1)S(1)}, u32[]{:S(2)}, u32[]{:S(2)}) collective-permute-start(bf16[16,2560]{1,0:T(8,128)(2,1)S(1)} %get-tuple-element.58), channel_id=1, source_target_pairs={{0,8},{1,9},{2,10},{3,11},{4,12},{5,13},{6,14},{7,15},{8,0},{9,1},... | collective-permute-start | bytes 245768 | tf_op jit(solution)/shard_map/ppermute | solution.py:39
  76.7 6.7 %collective-permute-start.28 = (bf16[16,2560]{1,0:T(8,128)(2,1)S(1)}, bf16[16,2560]{1,0:T(8,128)(2,1)S(1)}, u32[]{:S(2)}, u32[]{:S(2)}) collective-permute-start(bf16[16,2560]{1,0:T(8,128)(2,1)S(1)} %get-tuple-element.59), channel_id=1, source_target_pairs={{0,12},{1,13},{2,14},{3,15},{4,8},{5,9},{6,10},{7,11},{8,4},{9,5},... | collective-permute-start | bytes 245768 | tf_op jit(solution)/shard_map/ppermute | solution.py:39

commit v3 on v2

--- a/solution.py
+++ b/solution.py
@@ -37,6 +37,10 @@
 
 def hop(x, mask, width):
     return lax.ppermute(x, "ctx", [(i, i ^ mask) for i in range(width)])
+
+
+def sequence(nz):
+    return [nz - 1] + list(range(1, nz - 1)) + [0]
 
 
 def split3(x):
@@ -116,10 +120,10 @@
     table[...] = dot(picks[...], jnp.concatenate(seats, axis=0), NT).astype(BF)
     for kc in range(2):
         for ky in range(2):
-            for kz in range(width // 4):
+            for spot, kz in enumerate(sequence(width // 4)):
                 there = device ^ (kc + 2 * ky + 4 * kz)
                 there = pl.ds(pl.multiple_of(there * cap, cap), cap)
-                to = (kc * 2 + ky) * (width // 4) + kz
+                to = (kc * 2 + ky) * (width // 4) + spot
                 turn[to * cap : (to + 1) * cap, :] = table[there, :]
                 fill[to * cap : (to + 1) * cap, :] = own[there, :]
     chip_picks = [
@@ -203,7 +207,7 @@
 
 def attention_kernel(nz, lengths, *refs):
     pieces, (k_own, v_own, k_oth, v_oth) = refs[:nz], refs[nz : nz + 4]
-    outs, (rows, ready) = refs[nz + 4 : 2 * nz + 4], refs[2 * nz + 4 :]
+    outs, (rows, ready) = refs[nz + 4 : nz + 8], refs[nz + 8 :]
     device, core, chip, _ = place()
     per = pieces[0].shape[1]
     requests, span = k_own.shape[0], k_own.shape[1]
@@ -270,8 +274,10 @@
                         some_rows = slice(part * depth, (part + 1) * depth)
                         ready[dest, :depth, lo : lo + seat] = mixed[some_rows, mine]
                         ready[dest, depth:, lo : lo + seat] = stat[:, mine]
-    for kz in range(nz):
-        outs[kz][...] = ready[2 * kz : 2 * kz + 2]
+    order = sequence(nz)
+    for ky in range(2):
+        for spot, kz in enumerate(order):
+            outs[2 * ky + spot // (nz // 2)][spot % (nz // 2)] = ready[2 * kz + ky]
 
 
 def with_lse(lse):
@@ -285,14 +291,14 @@
     count = chips * per
     cols = HQ * HD // chips
     heads = max(1, cols // HD)
-    shape = (2, min(cols, HD) + STAT, heads * count)
+    shape = (nz // 2, min(cols, HD) + STAT, heads * count)
     work = 4 * k_own.size * (HQ // KVH) * 2 * count
     return pl.pallas_call(
         functools.partial(attention_kernel, nz),
-        out_shape=[jax.ShapeDtypeStruct(shape, BF)] * nz,
+        out_shape=[jax.ShapeDtypeStruct(shape, BF)] * 4,
         in_specs=[pl.BlockSpec(memory_space=pltpu.SMEM)]
         + [pl.BlockSpec(memory_space=pltpu.VMEM)] * (nz + 4),
-        out_specs=[pl.BlockSpec(memory_space=pltpu.VMEM)] * nz,
+        out_specs=[pl.BlockSpec(memory_space=pltpu.VMEM)] * 4,
         scratch_shapes=[
             pltpu.VMEM((count, HQ * HD), F32),
             pltpu.VMEM((chips,) + shape[1:], BF),
@@ -317,38 +323,37 @@
     return mixed * (1.0 / denom), best + jnp.log(denom)
 
 
-def fold_kernel(nz, *refs):
-    pieces, outs = refs[:nz], refs[nz:]
+def fold_kernel(near, far, *outs):
     depth = outs[0].shape[0] - STAT
-    for ky, out in enumerate(outs):
-        mixed, lse = merged([p[ky] for p in pieces])
+    for i, out in enumerate(outs):
+        mixed, lse = merged([near[i], far[i]])
         out[:depth, :] = mixed.astype(BF)
         out[depth:, :] = with_lse(lse)
 
 
-def fold(pieces):
-    nz = len(pieces)
-    shape = pieces[0].shape[1:]
-    return pl.pallas_call(
-        functools.partial(fold_kernel, nz),
-        out_shape=[jax.ShapeDtypeStruct(shape, BF)] * 2,
-        in_specs=[pl.BlockSpec(memory_space=pltpu.VMEM)] * nz,
-        out_specs=[pl.BlockSpec(memory_space=pltpu.VMEM)] * 2,
-        cost_estimate=pl.CostEstimate(
-            flops=4 * nz * pieces[0].size, bytes_accessed=4 * nz * pieces[0].size, transcendentals=0
+def fold(near, far):
+    count = near.shape[0]
+    return pl.pallas_call(
+        fold_kernel,
+        out_shape=[jax.ShapeDtypeStruct(near.shape[1:], BF)] * count,
+        in_specs=[pl.BlockSpec(memory_space=pltpu.VMEM)] * 2,
+        out_specs=[pl.BlockSpec(memory_space=pltpu.VMEM)] * count,
+        cost_estimate=pl.CostEstimate(
+            flops=8 * near.size, bytes_accessed=8 * near.size, transcendentals=0
         ),
         compiler_params=pltpu.CompilerParams(vmem_limit_bytes=16 * MIB),
         name="fold",
-    )(*pieces)
-
-
-def project_kernel(nz, near, far, w_own, w_oth, res_own, res_oth, home, *refs):
-    outs, attn, part = refs[:nz], refs[nz], refs[nz + 1]
+    )(near, far)
+
+
+def project_kernel(nz, *refs):
+    blocks, (w_own, w_oth, res_own, res_oth, home) = refs[:nz], refs[nz : nz + 5]
+    outs, attn, part = refs[nz + 5 : 2 * nz + 5], refs[2 * nz + 5], refs[2 * nz + 6]
     _, core, _, z = place()
-    depth = near.shape[0] - STAT
+    depth = blocks[0].shape[0] - STAT
     count = part.shape[0]
-    heads = near.shape[1] // count
-    mixed, _ = merged([near[...], far[...]])
+    heads = blocks[0].shape[1] // count
+    mixed, _ = merged([b[...] for b in blocks])
     mixed = mixed.T.astype(BF)
     if heads == 2:
         first, second = mixed[:count], mixed[count:]
@@ -371,7 +376,8 @@
         outs[kz][...] = part[pl.ds(spot, block), :].astype(BF)
 
 
-def project(near, far, w_own, w_oth, res_own, res_oth, home, nz):
+def project(blocks, w_own, w_oth, res_own, res_oth, home):
+    nz = len(blocks)
     count = home.shape[0]
     cols = D // (2 * nz)
     wide = res_own.shape[1]
@@ -379,7 +385,7 @@
         functools.partial(project_kernel, nz),
         out_shape=[jax.ShapeDtypeStruct((count // nz, wide), BF)] * nz
         + [jax.ShapeDtypeStruct((count, cols), BF)],
-        in_specs=[pl.BlockSpec(memory_space=pltpu.VMEM)] * 7,
+        in_specs=[pl.BlockSpec(memory_space=pltpu.VMEM)] * (nz + 5),
         out_specs=[pl.BlockSpec(memory_space=pltpu.VMEM)] * (nz + 1),
         scratch_shapes=[pltpu.VMEM((count, wide), F32)],
         cost_estimate=pl.CostEstimate(
@@ -387,15 +393,14 @@
         ),
         compiler_params=pltpu.CompilerParams(vmem_limit_bytes=12 * MIB),
         name="project",
-    )(near, far, w_own, w_oth, res_own, res_oth, home)
+    )(*blocks, w_own, w_oth, res_own, res_oth, home)
 
 
 def expert_kernel(nz, width, *refs):
     mine, theirs = refs[:nz], refs[nz : 2 * nz]
-    (gain, gate_up, down, turn, fill, mixed, keep0, keep1, send0, send1, stream_own) = refs[
-        2 * nz : 2 * nz + 11
-    ]
-    x, normed, hidden, scaled = refs[2 * nz + 11 :]
+    (gain, gate_up, down, turn, fill, mixed) = refs[2 * nz : 2 * nz + 6]
+    outs, stream_own = refs[2 * nz + 6 : 2 * nz + 12], refs[2 * nz + 12]
+    x, normed, hidden, scaled = refs[2 * nz + 13 :]
     device, core, _, z = place()
     block = mine[0].shape[0]
     half = block * nz
@@ -419,24 +424,26 @@
     for lo in range(0, D, tile):
         y = dot(hidden[...], down[0, :, lo : lo + tile], NN).astype(BF)
         scaled[:, lo : lo + tile] = (y.astype(F32) * weight).astype(BF)
-    for k, target in enumerate((keep0, keep1, send0, send1)):
-        size = target.shape[0]
-        some = slice(k * size, (k + 1) * size)
+    done = 0
+    for target in outs:
+        some = slice(done, done + target.shape[0])
         target[:, :D] = dot(turn[some, :], scaled[...], NN).astype(BF)
         target[:, D:] = dot(fill[some, :], mixed[...], NN).astype(BF)
-    stream_own[...] = dot(turn[:cap, :], x[:, :D], NN).astype(BF)
+        done = done + target.shape[0]
+    stream_own[...] = dot(turn[(nz - 1) * cap : nz * cap, :], x[:, :D], NN).astype(BF)
 
 
 def experts(mine, theirs, gain, gate_up, down, turn, fill, mixed, width, cap):
     nz = len(mine)
     block, wide = mine[0].shape
     total = 2 * nz * block
-    wide_out = jax.ShapeDtypeStruct((nz * cap, D + mixed.shape[1]), BF)
+    whole = jax.ShapeDtypeStruct((nz * cap, D + mixed.shape[1]), BF)
+    half = jax.ShapeDtypeStruct((nz // 2 * cap, D + mixed.shape[1]), BF)
     return pl.pallas_call(
         functools.partial(expert_kernel, nz, width),
-        out_shape=[wide_out] * 4 + [jax.ShapeDtypeStruct((cap, D), BF)],
+        out_shape=[whole, half, half] * 2 + [jax.ShapeDtypeStruct((cap, D), BF)],
         in_specs=[pl.BlockSpec(memory_space=pltpu.VMEM)] * (2 * nz + 6),
-        out_specs=[pl.BlockSpec(memory_space=pltpu.VMEM)] * 5,
+        out_specs=[pl.BlockSpec(memory_space=pltpu.VMEM)] * 7,
         scratch_shapes=[
             pltpu.VMEM((total, wide), BF),
             pltpu.VMEM((total, D), BF),
@@ -451,26 +458,26 @@
     )(*mine, *theirs, gain, gate_up, down, turn, fill, mixed)
 
 
-def mix_kernel(keep, near, far, *outs):
+def mix_kernel(first, keep, near, far, *outs):
     cap = outs[0].shape[0]
-    for kz, out in enumerate(outs):
-        some = slice(kz * cap, (kz + 1) * cap)
-        own = keep[some, :].astype(F32) + near[some, :].astype(F32)
-        other = far[some, :].astype(F32)
+    for i, out in enumerate(outs):
+        here = slice((first + i) * cap, (first + i + 1) * cap)
+        own = keep[here, :].astype(F32) + near[here, :].astype(F32)
+        other = far[i * cap : (i + 1) * cap, :].astype(F32)
         out[:, :D] = (own[:, :D] + other[:, :D]).astype(BF)
         out[:, D:] = jnp.concatenate([own[:, D:], other[:, D:]], axis=1).astype(BF)
 
 
-def mix(keep, near, far, nz):
-    cap = keep.shape[0] // nz
+def mix(keep, near, far, cap, first):
+    count = far.shape[0] // cap
     cols = keep.shape[1] - D
     return pl.pallas_call(
-        mix_kernel,
-        out_shape=[jax.ShapeDtypeStruct((cap, D + 2 * cols), BF)] * nz,
+        functools.partial(mix_kernel, first),
+        out_shape=[jax.ShapeDtypeStruct((cap, D + 2 * cols), BF)] * count,
         in_specs=[pl.BlockSpec(memory_space=pltpu.VMEM)] * 3,
-        out_specs=[pl.BlockSpec(memory_space=pltpu.VMEM)] * nz,
-        cost_estimate=pl.CostEstimate(
-            flops=3 * keep.size, bytes_accessed=8 * keep.size, transcendentals=0
+        out_specs=[pl.BlockSpec(memory_space=pltpu.VMEM)] * count,
+        cost_estimate=pl.CostEstimate(
+            flops=3 * far.size, bytes_accessed=8 * far.size, transcendentals=0
         ),
         compiler_params=pltpu.CompilerParams(vmem_limit_bytes=16 * MIB),
         name="mix",
@@ -546,6 +553,9 @@
             out.append(hop(terms[kz], 4 * kz, width))
         return out
 
+    def by_distance(blocks):
+        return [blocks[sequence(nz).index(kz)] for kz in range(nz)]
+
     def add(*terms):
         return small(total_kernel, terms[0].shape, *terms)
 
@@ -569,10 +579,15 @@
     )
     res_oth = hop(res_own, 1, width)
 
-    blocks = along_z(attention(pieces, k_own, v_own, k_oth, v_oth, lengths, chips))
-    mine, theirs = fold(blocks)
-    theirs = hop(theirs, 2, width)
-    *parts, mixed = project(mine, theirs, w_own, w_oth, res_own, res_oth, home, nz)
+    near_a, near_b, far_a, far_b = attention(
+        pieces, k_own, v_own, k_oth, v_oth, lengths, chips
+    )
+    far_a = hop(far_a, 2, width)
+    far_b = hop(far_b, 2, width)
+    first = fold(near_a, far_a)
+    second = fold(near_b, far_b)
+    blocks = along_z(by_distance(first + second))
+    *parts, mixed = project(blocks, w_own, w_oth, res_own, res_oth, home)
     chunk = add(*along_z(parts))
     (up,) = fetch(gate_up)
     other = hop(chunk, 2, width)
@@ -580,12 +595,18 @@
     mine = along_z([chunk] * nz)
     theirs = [hop(x, 1, width) for x in mine]
     (down,) = fetch(expert_down)
-    keep0, keep1, send0, send1, stream = experts(
+    keep, keep_a, keep_b, send, send_a, send_b, stream = experts(
         mine, theirs, gain, up, down, turn, fill, mixed, width, cap
     )
-    far = hop(add(keep1, hop(send1, 1, width)), 2, width)
-    sums = mix(keep0, hop(send0, 1, width), far, nz)
-    attn, layer_out = finish(stream, along_z(sums))
+    got_a = hop(send_a, 1, width)
+    got_b = hop(send_b, 1, width)
+    got = hop(send, 1, width)
+    far_a, far_b = add(keep_a, got_a), add(keep_b, got_b)
+    far_a = hop(far_a, 2, width)
+    far_b = hop(far_b, 2, width)
+    first = mix(keep, got, far_a, cap, 0)
+    second = mix(keep, got, far_b, cap, nz // 2)
+    attn, layer_out = finish(stream, along_z(by_distance(first + second)))
     return (attn, layer_out)
 
 

time: 84.3 us -> 82.6 us (0.980)
  waiting for transfers between devices: 36.7 us -> 33.2 us
  starting transfers between devices: 32.2 us -> 33.9 us
    ppermute x29 -> x32, waiting for transfers between devices: 36.7 us -> 33.2 us  [hop(): return lax.ppermute(x, 'ctx', [(i, i ^ mask) for i in range(width)])]
    ppermute x29 -> x32, starting transfers between devices: 32.2 us -> 33.9 us  [hop(): return lax.ppermute(x, 'ctx', [(i, i ^ mask) for i in range(width)])]
    pallas_call x3 -> x5, Pallas kernels: 2.4 us -> 2.55 us  [the longest x1 2.33 us: experts(): pl.pallas_call(functools.partial(expert_kernel, nz, width), out_shape=[wh...]
  transfers between devices with their start and end apart: 29 -> 32, of which waited for: 16 -> 17; matrix products, arithmetic and copies ran while one was open for 0% -> 0% of each run, Pallas kernels for 12% -> 12%
where the time goes in v3:
time: 82.6 us; the launch traced here: 82.4 us
  starting transfers between devices  33.9 us (41%)
  waiting for transfers between devices  33.2 us (40%)
  Pallas kernels  13.8 us (17%)
  between operations  1.44 us (2%)
    ppermute x32, starting transfers between devices, hop(): return lax.ppermute(x, 'ctx', [(i, i ^ mask) for i in range(width)])  33.9 us
    ppermute x32, waiting for transfers between devices, hop(): return lax.ppermute(x, 'ctx', [(i, i ^ mask) for i in range(width)])  33.2 us
    pallas_call x3, Pallas kernels, fetch(): pl.pallas_call(functools.partial(fetch_kernel, count), out_shape=[pltpu.V...  5.77 us
    pallas_call x1, Pallas kernels, experts(): pl.pallas_call(functools.partial(expert_kernel, nz, width), out_shape=[wh...  2.33 us
    pallas_call x1, Pallas kernels, attention(): pl.pallas_call(functools.partial(attention_kernel, nz), out_shape=[jax.Sh...  2.21 us
    pallas_call x1, Pallas kernels, prepare(): pl.pallas_call(functools.partial(prepare_kernel, per, width), out_shape=[...  1.98 us
  transfers between devices with their start and end apart: 32, of which 17 were waited for; matrix products, arithmetic and copies ran while one was open for 0% of the time, Pallas kernels for 12%

profile of v3, /device:TPU:0, one launch (start us, length us, event | category | flops | bytes accessed | tf_op | source)
XLA Modules:
  0.0 82.4 jit_solution(11284983407474462059)
XLA Ops:
  1.7 2.6 %collective-permute-start = (bf16[8,2048]{1,0:T(8,128)(2,1)}, bf16[8,2048]{1,0:T(8,128)(2,1)S(1)}, u32[]{:S(2)}, u32[]{:S(2)}) collective-permute-start(bf16[8,2048]{1,0:T(8,128)(2,1)} %refs_0_.3), channel_id=1, source_target_pairs={{0,2},{1,3},{2,0},{3,1},{4,6},{5,7},{6,4},{7,5},{8,10},{9,11},{10,... | collective-permute-start | bytes 98312 | tf_op jit(solution)/shard_map/ppermute | solution.py:39
  4.3 1.1 %fetch.3 = (bf16[8,2048]{1,0:T(8,128)(2,1)S(1)}, bf16[1,512,256]{2,1,0:T(8,128)(2,1)S(1)}, bf16[1,512,256]{2,1,0:T(8,128)(2,1)S(1)}) custom-call(bf16[8,2048]{1,0:T(8,128)(2,1)} %refs_0_.3, bf16[1,512,256]{2,1,0:T(8,128)(2,1)} %refs_1_.1, bf16[1,512,256]{2,1,0:T(8,128)(2,1)} %refs_2_.1), custom_call_target="tpu_custom_call" | custom-call | bytes 1114112 | tf_op jit(solution)/shard_map/fetch/pallas_call | solution.py:76
  5.4 1.1 %collective-permute-done.second = bf16[8,2048]{1,0:T(8,128)(2,1)S(1)} collective-permute-done((bf16[8,2048]{1,0:T(8,128)(2,1)}, bf16[8,2048]{1,0:T(8,128)(2,1)S(1)}, u32[]{:S(2)}, u32[]{:S(2)}) %collective-permute-start) | collective-permute-done | bytes 32800 | tf_op jit(solution)/shard_map/ppermute | solution.py:39
  6.5 4.0 %collective-permute-start.3 = (bf16[2,8,2048]{2,1,0:T(8,128)(2,1)S(1)}, bf16[2,8,2048]{2,1,0:T(8,128)(2,1)S(1)}, u32[]{:S(2)}, u32[]{:S(2)}) collective-permute-start(bf16[2,8,2048]{2,1,0:T(8,128)(2,1)S(1)} %shard_map.140.refs_0_), channel_id=1, source_target_pairs={{0,12},{1,13},{2,14},{3,15},{4,8},{5,9},{6,10},{7,11},{8,4},{9,5},... | collective-permute-start | bytes 196616 | tf_op jit(solution)/shard_map/ppermute | solution.py:39
  10.5 3.0 %collective-permute-done.3.refs_3_ = bf16[2,8,2048]{2,1,0:T(8,128)(2,1)S(1)} collective-permute-done((bf16[2,8,2048]{2,1,0:T(8,128)(2,1)S(1)}, bf16[2,8,2048]{2,1,0:T(8,128)(2,1)S(1)}, u32[]{:S(2)}, u32[]{:S(2)}) %collective-permute-start.3) | collective-permute-done | bytes 65568 | tf_op jit(solution)/shard_map/ppermute | solution.py:39
  15.7 2.1 %collective-permute-done.1.refs_1_ = bf16[2,8,2048]{2,1,0:T(8,128)(2,1)S(1)} collective-permute-done((bf16[2,8,2048]{2,1,0:T(8,128)(2,1)S(1)}, bf16[2,8,2048]{2,1,0:T(8,128)(2,1)S(1)}, u32[]{:S(2)}, u32[]{:S(2)}) %collective-permute-start.1) | collective-permute-done | bytes 65568 | tf_op jit(solution)/shard_map/ppermute | solution.py:39
  17.8 2.2 %attention.1 = (bf16[2,136,128]{2,1,0:T(8,128)(2,1)S(1)}, bf16[2,136,128]{2,1,0:T(8,128)(2,1)S(1)}, bf16[2,136,128]{2,1,0:T(8,128)(2,1)S(1)}, bf16[2,136,128]{2,1,0:T(8,128)(2,1)S(1)}) custom-call(s32[1]{0:T(128)S(6)} %copy.15.lengths, bf16[2,8,2048]{2,1,0:T(8,128)(2,1)S(1)} %shard_map.140.refs_0_, bf16[2,8,2048]{2,1,0:T(8,128)(2,1)S(1)} %collective-permute-done.1.refs_1_, ...), custom_call_target="tpu_custom_call" | custom-call | flops 536870912 | bytes 1048576 | tf_op jit(solution)/shard_map/attention/pallas_call | solution.py:296
  20.0 1.6 %collective-permute-start.6 = (bf16[2,136,128]{2,1,0:T(8,128)(2,1)S(1)}, bf16[2,136,128]{2,1,0:T(8,128)(2,1)S(1)}, u32[]{:S(2)}, u32[]{:S(2)}) collective-permute-start(bf16[2,136,128]{2,1,0:T(8,128)(2,1)S(1)} %get-tuple-element.39), channel_id=1, source_target_pairs={{0,2},{1,3},{2,0},{3,1},{4,6},{5,7},{6,4},{7,5},{8,10},{9,11},{10,... | collective-permute-start | bytes 208904 | tf_op jit(solution)/shard_map/ppermute | solution.py:39
  22.1 2.0 %prepare.1 = (bf16[16,2176]{1,0:T(8,128)(2,1)S(1)}, bf16[64,32]{1,0:T(8,128)(2,1)S(1)}, bf16[256,64]{1,0:T(8,128)(2,1)S(1)}, bf16[256,128]{1,0:T(8,128)(2,1)S(1)...) custom-call(s32[1,16]{1,0:T(1,128)} %bitcast.8, s32[1,128]{1,0:T(1,128)} %bitcast.9, s32[8,16]{1,0:T(8,128)} %bitcast.6, ...), custom_call_target="tpu_custom_call" | custom-call | flops 12582912 | bytes 131072 | tf_op jit(solution)/shard_map/prepare/pallas_call | solution.py:156
  24.4 2.3 %collective-permute-start.9 = (bf16[136,128]{1,0:T(8,128)(2,1)S(1)}, bf16[136,128]{1,0:T(8,128)(2,1)S(1)}, u32[]{:S(2)}, u32[]{:S(2)}) collective-permute-start(bf16[136,128]{1,0:T(8,128)(2,1)S(1)} %get-tuple-element.44), channel_id=1, source_target_pairs={{0,8},{1,9},{2,10},{3,11},{4,12},{5,13},{6,14},{7,15},{8,0},{9,1},... | collective-permute-start | bytes 104456 | tf_op jit(solution)/shard_map/ppermute | solution.py:39
  26.8 2.1 %collective-permute-start.8 = (bf16[136,128]{1,0:T(8,128)(2,1)S(1)}, bf16[136,128]{1,0:T(8,128)(2,1)S(1)}, u32[]{:S(2)}, u32[]{:S(2)}) collective-permute-start(bf16[136,128]{1,0:T(8,128)(2,1)S(1)} %get-tuple-element.43), channel_id=1, source_target_pairs={{0,4},{1,5},{2,6},{3,7},{4,0},{5,1},{6,2},{7,3},{8,12},{9,13},{10,... | collective-permute-start | bytes 104456 | tf_op jit(solution)/shard_map/ppermute | solution.py:39
  30.8 3.8 %collective-permute-done.10.refs_3_ = bf16[136,128]{1,0:T(8,128)(2,1)S(1)} collective-permute-done((bf16[136,128]{1,0:T(8,128)(2,1)S(1)}, bf16[136,128]{1,0:T(8,128)(2,1)S(1)}, u32[]{:S(2)}, u32[]{:S(2)}) %collective-permute-start.10) | collective-permute-done | bytes 34848 | tf_op jit(solution)/shard_map/ppermute | solution.py:39
  35.2 1.5 %collective-permute-start.14 = (bf16[16,2176]{1,0:T(8,128)(2,1)S(1)}, bf16[16,2176]{1,0:T(8,128)(2,1)S(1)}, u32[]{:S(2)}, u32[]{:S(2)}) collective-permute-start(bf16[16,2176]{1,0:T(8,128)(2,1)S(1)} %get-tuple-element.51), channel_id=1, source_target_pairs={{0,8},{1,9},{2,10},{3,11},{4,12},{5,13},{6,14},{7,15},{8,0},{9,1},... | collective-permute-start | bytes 208904 | tf_op jit(solution)/shard_map/ppermute | solution.py:39
  36.7 2.9 %collective-permute-start.15 = (bf16[16,2176]{1,0:T(8,128)(2,1)S(1)}, bf16[16,2176]{1,0:T(8,128)(2,1)S(1)}, u32[]{:S(2)}, u32[]{:S(2)}) collective-permute-start(bf16[16,2176]{1,0:T(8,128)(2,1)S(1)} %get-tuple-element.52), channel_id=1, source_target_pairs={{0,12},{1,13},{2,14},{3,15},{4,8},{5,9},{6,10},{7,11},{8,4},{9,5},... | collective-permute-start | bytes 208904 | tf_op jit(solution)/shard_map/ppermute | solution.py:39
  39.6 1.5 %collective-permute-done.14.refs_2_ = bf16[16,2176]{1,0:T(8,128)(2,1)S(1)} collective-permute-done((bf16[16,2176]{1,0:T(8,128)(2,1)S(1)}, bf16[16,2176]{1,0:T(8,128)(2,1)S(1)}, u32[]{:S(2)}, u32[]{:S(2)}) %collective-permute-start.14) | collective-permute-done | bytes 69664 | tf_op jit(solution)/shard_map/ppermute | solution.py:39
  41.1 1.8 %collective-permute-done.15.refs_3_ = bf16[16,2176]{1,0:T(8,128)(2,1)S(1)} collective-permute-done((bf16[16,2176]{1,0:T(8,128)(2,1)S(1)}, bf16[16,2176]{1,0:T(8,128)(2,1)S(1)}, u32[]{:S(2)}, u32[]{:S(2)}) %collective-permute-start.15) | collective-permute-done | bytes 69664 | tf_op jit(solution)/shard_map/ppermute | solution.py:39
  42.9 1.5 %collective-permute-start.16 = (bf16[16,2176]{1,0:T(8,128)(2,1)S(1)}, bf16[16,2176]{1,0:T(8,128)(2,1)S(1)}, u32[]{:S(2)}, u32[]{:S(2)}) collective-permute-start(bf16[16,2176]{1,0:T(8,128)(2,1)S(1)} %shard_map.141.refs_0_), channel_id=1, source_target_pairs={{0,2},{1,3},{2,0},{3,1},{4,6},{5,7},{6,4},{7,5},{8,10},{9,11},{10,... | collective-permute-start | bytes 208904 | tf_op jit(solution)/shard_map/ppermute | solution.py:39
  44.4 2.9 %collective-permute-done.16.refs_1_ = bf16[16,2176]{1,0:T(8,128)(2,1)S(1)} collective-permute-done((bf16[16,2176]{1,0:T(8,128)(2,1)S(1)}, bf16[16,2176]{1,0:T(8,128)(2,1)S(1)}, u32[]{:S(2)}, u32[]{:S(2)}) %collective-permute-start.16) | collective-permute-done | bytes 69664 | tf_op jit(solution)/shard_map/ppermute | solution.py:39
  47.3 2.9 %collective-permute-start.19 = (bf16[16,2176]{1,0:T(8,128)(2,1)S(1)}, bf16[16,2176]{1,0:T(8,128)(2,1)S(1)}, u32[]{:S(2)}, u32[]{:S(2)}) collective-permute-start(bf16[16,2176]{1,0:T(8,128)(2,1)S(1)} %shard_map.142.refs_0_), channel_id=1, source_target_pairs={{0,12},{1,13},{2,14},{3,15},{4,8},{5,9},{6,10},{7,11},{8,4},{9,5},... | collective-permute-start | bytes 208904 | tf_op jit(solution)/shard_map/ppermute | solution.py:39
  50.2 1.5 %collective-permute-start.17 = (bf16[16,2176]{1,0:T(8,128)(2,1)S(1)}, bf16[16,2176]{1,0:T(8,128)(2,1)S(1)}, u32[]{:S(2)}, u32[]{:S(2)}) collective-permute-start(bf16[16,2176]{1,0:T(8,128)(2,1)S(1)} %shard_map.142.refs_0_), channel_id=1, source_target_pairs={{0,4},{1,5},{2,6},{3,7},{4,0},{5,1},{6,2},{7,3},{8,12},{9,13},{10,... | collective-permute-start | bytes 208904 | tf_op jit(solution)/shard_map/ppermute | solution.py:39
  51.7 1.7 %collective-permute-done.19.refs_3_ = bf16[16,2176]{1,0:T(8,128)(2,1)S(1)} collective-permute-done((bf16[16,2176]{1,0:T(8,128)(2,1)S(1)}, bf16[16,2176]{1,0:T(8,128)(2,1)S(1)}, u32[]{:S(2)}, u32[]{:S(2)}) %collective-permute-start.19) | collective-permute-done | bytes 69664 | tf_op jit(solution)/shard_map/ppermute | solution.py:39
  53.5 2.0 %collective-permute-done.18.refs_2_ = bf16[16,2176]{1,0:T(8,128)(2,1)S(1)} collective-permute-done((bf16[16,2176]{1,0:T(8,128)(2,1)S(1)}, bf16[16,2176]{1,0:T(8,128)(2,1)S(1)}, u32[]{:S(2)}, u32[]{:S(2)}) %collective-permute-start.18) | collective-permute-done | bytes 69664 | tf_op jit(solution)/shard_map/ppermute | solution.py:39
  55.9 1.9 %fetch.5.refs_10_ = bf16[1,768,2048]{2,1,0:T(8,128)(2,1)S(1)} custom-call(bf16[1,768,2048]{2,1,0:T(8,128)(2,1)} %refs_0_.5), custom_call_target="tpu_custom_call" | custom-call | bytes 6291456 | tf_op jit(solution)/shard_map/fetch/pallas_call | solution.py:76
  57.8 2.8 %fetch.4.refs_9_ = bf16[1,2048,1536]{2,1,0:T(8,128)(2,1)S(1)} custom-call(bf16[1,2048,1536]{2,1,0:T(8,128)(2,1)} %refs_0_.4), custom_call_target="tpu_custom_call" | custom-call | bytes 12582912 | tf_op jit(solution)/shard_map/fetch/pallas_call | solution.py:76
  60.7 2.3 %experts.1 = (bf16[64,2304]{1,0:T(8,128)(2,1)S(1)}, bf16[32,2304]{1,0:T(8,128)(2,1)S(1)}, bf16[32,2304]{1,0:T(8,128)(2,1)S(1)}, bf16[64,2304]{1,0:T(8,128)(2,1)S...) custom-call(bf16[16,2176]{1,0:T(8,128)(2,1)S(1)} %shard_map.142.refs_0_, ...), custom_call_target="tpu_custom_call" | custom-call | flops 1207959552 | bytes 9437184 | tf_op jit(solution)/shard_map/experts/pallas_call | solution.py:442
  64.5 1.6 %collective-permute-start.28 = (bf16[32,2304]{1,0:T(8,128)(2,1)S(1)}, bf16[32,2304]{1,0:T(8,128)(2,1)S(1)}, u32[]{:S(2)}, u32[]{:S(2)}) collective-permute-start(bf16[32,2304]{1,0:T(8,128)(2,1)S(1)} %shard_map.144), channel_id=1, source_target_pairs={{0,2},{1,3},{2,0},{3,1},{4,6},{5,7},{6,4},{7,5},{8,10},{9,11},{10,... | collective-permute-start | bytes 442376 | tf_op jit(solution)/shard_map/ppermute | solution.py:39
  66.7 4.5 %collective-permute-done.28.far = bf16[32,2304]{1,0:T(8,128)(2,1)S(1)} collective-permute-done((bf16[32,2304]{1,0:T(8,128)(2,1)S(1)}, bf16[32,2304]{1,0:T(8,128)(2,1)S(1)}, u32[]{:S(2)}, u32[]{:S(2)}) %collective-permute-start.28) | collective-permute-done | bytes 147488 | tf_op jit(solution)/shard_map/ppermute | solution.py:39
  71.6 2.9 %collective-permute-start.31 = (bf16[16,2560]{1,0:T(8,128)(2,1)S(1)}, bf16[16,2560]{1,0:T(8,128)(2,1)S(1)}, u32[]{:S(2)}, u32[]{:S(2)}) collective-permute-start(bf16[16,2560]{1,0:T(8,128)(2,1)S(1)} %get-tuple-element.67), channel_id=1, source_target_pairs={{0,12},{1,13},{2,14},{3,15},{4,8},{5,9},{6,10},{7,11},{8,4},{9,5},... | collective-permute-start | bytes 245768 | tf_op jit(solution)/shard_map/ppermute | solution.py:39
  74.6 1.0 %collective-permute-start.30 = (bf16[16,2560]{1,0:T(8,128)(2,1)S(1)}, bf16[16,2560]{1,0:T(8,128)(2,1)S(1)}, u32[]{:S(2)}, u32[]{:S(2)}) collective-permute-start(bf16[16,2560]{1,0:T(8,128)(2,1)S(1)} %get-tuple-element.66), channel_id=1, source_target_pairs={{0,8},{1,9},{2,10},{3,11},{4,12},{5,13},{6,14},{7,15},{8,0},{9,1},... | collective-permute-start | bytes 245768 | tf_op jit(solution)/shard_map/ppermute | solution.py:39
  75.6 1.1 %collective-permute-done.29.refs_1_ = bf16[16,2560]{1,0:T(8,128)(2,1)S(1)} collective-permute-done((bf16[16,2560]{1,0:T(8,128)(2,1)S(1)}, bf16[16,2560]{1,0:T(8,128)(2,1)S(1)}, u32[]{:S(2)}, u32[]{:S(2)}) %collective-permute-start.29) | collective-permute-done | bytes 81952 | tf_op jit(solution)/shard_map/ppermute | solution.py:39
  76.7 2.1 %collective-permute-done.31.refs_3_ = bf16[16,2560]{1,0:T(8,128)(2,1)S(1)} collective-permute-done((bf16[16,2560]{1,0:T(8,128)(2,1)S(1)}, bf16[16,2560]{1,0:T(8,128)(2,1)S(1)}, u32[]{:S(2)}, u32[]{:S(2)}) %collective-permute-start.31) | collective-permute-done | bytes 81952 | tf_op jit(solution)/shard_map/ppermute | solution.py:39
  78.8 2.9 %collective-permute-done.30.refs_2_ = bf16[16,2560]{1,0:T(8,128)(2,1)S(1)} collective-permute-done((bf16[16,2560]{1,0:T(8,128)(2,1)S(1)}, bf16[16,2560]{1,0:T(8,128)(2,1)S(1)}, u32[]{:S(2)}, u32[]{:S(2)}) %collective-permute-start.30) | collective-permute-done | bytes 81952 | tf_op jit(solution)/shard_map/ppermute | solution.py:39
  (49 shorter events, 9.8 us)
Async XLA Ops:
  0.6 34.0 %collective-permute-start.11 = (bf16[128,2048]{1,0:T(8,128)(2,1)}, bf16[128,2048]{1,0:T(8,128)(2,1)S(1)}, u32[]{:S(2)}, u32[]{:S(2)}) collective-permute-start(bf16[128,2048]{1,0:T(8,128)(2,1)} %refs_5_.1), channel_id=1, source_target_pairs={{0,1},{1,0},{2,3},{3,2},{4,5},{5,4},{6,7},{7,6},{8,9},{9,8},{10,11... | collective-permute-start | bytes 1572872 | tf_op jit(solution)/shard_map/ppermute | solution.py:39
  1.2 16.6 %collective-permute-start.4 = (bf16[1,512,256]{2,1,0:T(8,128)(2,1)}, bf16[1,512,256]{2,1,0:T(8,128)(2,1)S(1)}, u32[]{:S(2)}, u32[]{:S(2)}) collective-permute-start(bf16[1,512,256]{2,1,0:T(8,128)(2,1)} %refs_1_.1), channel_id=1, source_target_pairs={{0,1},{1,0},{2,3},{3,2},{4,5},{5,4},{6,7},{7,6},{8,9},{9,8},{10,11... | collective-permute-start | bytes 786440 | tf_op jit(solution)/shard_map/ppermute | solution.py:39
  1.3 16.5 %collective-permute-start.5 = (bf16[1,512,256]{2,1,0:T(8,128)(2,1)}, bf16[1,512,256]{2,1,0:T(8,128)(2,1)S(1)}, u32[]{:S(2)}, u32[]{:S(2)}) collective-permute-start(bf16[1,512,256]{2,1,0:T(8,128)(2,1)} %refs_2_.1), channel_id=1, source_target_pairs={{0,1},{1,0},{2,3},{3,2},{4,5},{5,4},{6,7},{7,6},{8,9},{9,8},{10,11... | collective-permute-start | bytes 786440 | tf_op jit(solution)/shard_map/ppermute | solution.py:39
  1.7 4.8 %collective-permute-start = (bf16[8,2048]{1,0:T(8,128)(2,1)}, bf16[8,2048]{1,0:T(8,128)(2,1)S(1)}, u32[]{:S(2)}, u32[]{:S(2)}) collective-permute-start(bf16[8,2048]{1,0:T(8,128)(2,1)} %refs_0_.3), channel_id=1, source_target_pairs={{0,2},{1,3},{2,0},{3,1},{4,6},{5,7},{6,4},{7,5},{8,10},{9,11},{10,... | collective-permute-start | bytes 98312 | tf_op jit(solution)/shard_map/ppermute | solution.py:39
  6.5 7.0 %collective-permute-start.3 = (bf16[2,8,2048]{2,1,0:T(8,128)(2,1)S(1)}, bf16[2,8,2048]{2,1,0:T(8,128)(2,1)S(1)}, u32[]{:S(2)}, u32[]{:S(2)}) collective-permute-start(bf16[2,8,2048]{2,1,0:T(8,128)(2,1)S(1)} %shard_map.140.refs_0_), channel_id=1, source_target_pairs={{0,12},{1,13},{2,14},{3,15},{4,8},{5,9},{6,10},{7,11},{8,4},{9,5},... | collective-permute-start | bytes 196616 | tf_op jit(solution)/shard_map/ppermute | solution.py:39
  10.5 5.2 %collective-permute-start.2 = (bf16[2,8,2048]{2,1,0:T(8,128)(2,1)S(1)}, bf16[2,8,2048]{2,1,0:T(8,128)(2,1)S(1)}, u32[]{:S(2)}, u32[]{:S(2)}) collective-permute-start(bf16[2,8,2048]{2,1,0:T(8,128)(2,1)S(1)} %shard_map.140.refs_0_), channel_id=1, source_target_pairs={{0,8},{1,9},{2,10},{3,11},{4,12},{5,13},{6,14},{7,15},{8,0},{9,1},... | collective-permute-start | bytes 196616 | tf_op jit(solution)/shard_map/ppermute | solution.py:39
  13.5 4.3 %collective-permute-start.1 = (bf16[2,8,2048]{2,1,0:T(8,128)(2,1)S(1)}, bf16[2,8,2048]{2,1,0:T(8,128)(2,1)S(1)}, u32[]{:S(2)}, u32[]{:S(2)}) collective-permute-start(bf16[2,8,2048]{2,1,0:T(8,128)(2,1)S(1)} %shard_map.140.refs_0_), channel_id=1, source_target_pairs={{0,4},{1,5},{2,6},{3,7},{4,0},{5,1},{6,2},{7,3},{8,12},{9,13},{10,... | collective-permute-start | bytes 196616 | tf_op jit(solution)/shard_map/ppermute | solution.py:39
  20.0 4.4 %collective-permute-start.6 = (bf16[2,136,128]{2,1,0:T(8,128)(2,1)S(1)}, bf16[2,136,128]{2,1,0:T(8,128)(2,1)S(1)}, u32[]{:S(2)}, u32[]{:S(2)}) collective-permute-start(bf16[2,136,128]{2,1,0:T(8,128)(2,1)S(1)} %get-tuple-element.39), channel_id=1, source_target_pairs={{0,2},{1,3},{2,0},{3,1},{4,6},{5,7},{6,4},{7,5},{8,10},{9,11},{10,... | collective-permute-start | bytes 208904 | tf_op jit(solution)/shard_map/ppermute | solution.py:39
  21.6 5.2 %collective-permute-start.7 = (bf16[2,136,128]{2,1,0:T(8,128)(2,1)S(1)}, bf16[2,136,128]{2,1,0:T(8,128)(2,1)S(1)}, u32[]{:S(2)}, u32[]{:S(2)}) collective-permute-start(bf16[2,136,128]{2,1,0:T(8,128)(2,1)S(1)} %get-tuple-element.42), channel_id=1, source_target_pairs={{0,2},{1,3},{2,0},{3,1},{4,6},{5,7},{6,4},{7,5},{8,10},{9,11},{10,... | collective-permute-start | bytes 208904 | tf_op jit(solution)/shard_map/ppermute | solution.py:39
  24.1 5.8 %collective-permute-start.12 = (bf16[16,2176]{1,0:T(8,128)(2,1)S(1)}, bf16[16,2176]{1,0:T(8,128)(2,1)S(1)}, u32[]{:S(2)}, u32[]{:S(2)}) collective-permute-start(bf16[16,2176]{1,0:T(8,128)(2,1)S(1)} %get-tuple-element.47.refs_6_), channel_id=1, source_target_pairs={{0,1},{1,0},{2,3},{3,2},{4,5},{5,4},{6,7},{7,6},{8,9},{9,8},{10,11... | collective-permute-start | bytes 208904 | tf_op jit(solution)/shard_map/ppermute | solution.py:39
  24.4 5.4 %collective-permute-start.9 = (bf16[136,128]{1,0:T(8,128)(2,1)S(1)}, bf16[136,128]{1,0:T(8,128)(2,1)S(1)}, u32[]{:S(2)}, u32[]{:S(2)}) collective-permute-start(bf16[136,128]{1,0:T(8,128)(2,1)S(1)} %get-tuple-element.44), channel_id=1, source_target_pairs={{0,8},{1,9},{2,10},{3,11},{4,12},{5,13},{6,14},{7,15},{8,0},{9,1},... | collective-permute-start | bytes 104456 | tf_op jit(solution)/shard_map/ppermute | solution.py:39
  26.8 4.0 %collective-permute-start.8 = (bf16[136,128]{1,0:T(8,128)(2,1)S(1)}, bf16[136,128]{1,0:T(8,128)(2,1)S(1)}, u32[]{:S(2)}, u32[]{:S(2)}) collective-permute-start(bf16[136,128]{1,0:T(8,128)(2,1)S(1)} %get-tuple-element.43), channel_id=1, source_target_pairs={{0,4},{1,5},{2,6},{3,7},{4,0},{5,1},{6,2},{7,3},{8,12},{9,13},{10,... | collective-permute-start | bytes 104456 | tf_op jit(solution)/shard_map/ppermute | solution.py:39
  28.9 5.7 %collective-permute-start.10 = (bf16[136,128]{1,0:T(8,128)(2,1)S(1)}, bf16[136,128]{1,0:T(8,128)(2,1)S(1)}, u32[]{:S(2)}, u32[]{:S(2)}) collective-permute-start(bf16[136,128]{1,0:T(8,128)(2,1)S(1)} %get-tuple-element.45), channel_id=1, source_target_pairs={{0,12},{1,13},{2,14},{3,15},{4,8},{5,9},{6,10},{7,11},{8,4},{9,5},... | collective-permute-start | bytes 104456 | tf_op jit(solution)/shard_map/ppermute | solution.py:39
  35.1 4.5 %collective-permute-start.13 = (bf16[16,2176]{1,0:T(8,128)(2,1)S(1)}, bf16[16,2176]{1,0:T(8,128)(2,1)S(1)}, u32[]{:S(2)}, u32[]{:S(2)}) collective-permute-start(bf16[16,2176]{1,0:T(8,128)(2,1)S(1)} %get-tuple-element.50), channel_id=1, source_target_pairs={{0,4},{1,5},{2,6},{3,7},{4,0},{5,1},{6,2},{7,3},{8,12},{9,13},{10,... | collective-permute-start | bytes 208904 | tf_op jit(solution)/shard_map/ppermute | solution.py:39
  35.2 5.9 %collective-permute-start.14 = (bf16[16,2176]{1,0:T(8,128)(2,1)S(1)}, bf16[16,2176]{1,0:T(8,128)(2,1)S(1)}, u32[]{:S(2)}, u32[]{:S(2)}) collective-permute-start(bf16[16,2176]{1,0:T(8,128)(2,1)S(1)} %get-tuple-element.51), channel_id=1, source_target_pairs={{0,8},{1,9},{2,10},{3,11},{4,12},{5,13},{6,14},{7,15},{8,0},{9,1},... | collective-permute-start | bytes 208904 | tf_op jit(solution)/shard_map/ppermute | solution.py:39
  36.7 6.1 %collective-permute-start.15 = (bf16[16,2176]{1,0:T(8,128)(2,1)S(1)}, bf16[16,2176]{1,0:T(8,128)(2,1)S(1)}, u32[]{:S(2)}, u32[]{:S(2)}) collective-permute-start(bf16[16,2176]{1,0:T(8,128)(2,1)S(1)} %get-tuple-element.52), channel_id=1, source_target_pairs={{0,12},{1,13},{2,14},{3,15},{4,8},{5,9},{6,10},{7,11},{8,4},{9,5},... | collective-permute-start | bytes 208904 | tf_op jit(solution)/shard_map/ppermute | solution.py:39
  42.9 4.4 %collective-permute-start.16 = (bf16[16,2176]{1,0:T(8,128)(2,1)S(1)}, bf16[16,2176]{1,0:T(8,128)(2,1)S(1)}, u32[]{:S(2)}, u32[]{:S(2)}) collective-permute-start(bf16[16,2176]{1,0:T(8,128)(2,1)S(1)} %shard_map.141.refs_0_), channel_id=1, source_target_pairs={{0,2},{1,3},{2,0},{3,1},{4,6},{5,7},{6,4},{7,5},{8,10},{9,11},{10,... | collective-permute-start | bytes 208904 | tf_op jit(solution)/shard_map/ppermute | solution.py:39
  47.3 6.2 %collective-permute-start.19 = (bf16[16,2176]{1,0:T(8,128)(2,1)S(1)}, bf16[16,2176]{1,0:T(8,128)(2,1)S(1)}, u32[]{:S(2)}, u32[]{:S(2)}) collective-permute-start(bf16[16,2176]{1,0:T(8,128)(2,1)S(1)} %shard_map.142.refs_0_), channel_id=1, source_target_pairs={{0,12},{1,13},{2,14},{3,15},{4,8},{5,9},{6,10},{7,11},{8,4},{9,5},... | collective-permute-start | bytes 208904 | tf_op jit(solution)/shard_map/ppermute | solution.py:39
  50.2 5.2 %collective-permute-start.18 = (bf16[16,2176]{1,0:T(8,128)(2,1)S(1)}, bf16[16,2176]{1,0:T(8,128)(2,1)S(1)}, u32[]{:S(2)}, u32[]{:S(2)}) collective-permute-start(bf16[16,2176]{1,0:T(8,128)(2,1)S(1)} %shard_map.142.refs_0_), channel_id=1, source_target_pairs={{0,8},{1,9},{2,10},{3,11},{4,12},{5,13},{6,14},{7,15},{8,0},{9,1},... | collective-permute-start | bytes 208904 | tf_op jit(solution)/shard_map/ppermute | solution.py:39
  50.2 5.2 %collective-permute-start.17 = (bf16[16,2176]{1,0:T(8,128)(2,1)S(1)}, bf16[16,2176]{1,0:T(8,128)(2,1)S(1)}, u32[]{:S(2)}, u32[]{:S(2)}) collective-permute-start(bf16[16,2176]{1,0:T(8,128)(2,1)S(1)} %shard_map.142.refs_0_), channel_id=1, source_target_pairs={{0,4},{1,5},{2,6},{3,7},{4,0},{5,1},{6,2},{7,3},{8,12},{9,13},{10,... | collective-permute-start | bytes 208904 | tf_op jit(solution)/shard_map/ppermute | solution.py:39
  51.7 8.9 %collective-permute-start.20 = (bf16[16,2176]{1,0:T(8,128)(2,1)S(1)}, bf16[16,2176]{1,0:T(8,128)(2,1)S(1)}, u32[]{:S(2)}, u32[]{:S(2)}) collective-permute-start(bf16[16,2176]{1,0:T(8,128)(2,1)S(1)} %shard_map.142.refs_0_), channel_id=1, source_target_pairs={{0,1},{1,0},{2,3},{3,2},{4,5},{5,4},{6,7},{7,6},{8,9},{9,8},{10,11... | collective-permute-start | bytes 208904 | tf_op jit(solution)/shard_map/ppermute | solution.py:39
  53.5 7.2 %collective-permute-start.23 = (bf16[16,2176]{1,0:T(8,128)(2,1)S(1)}, bf16[16,2176]{1,0:T(8,128)(2,1)S(1)}, u32[]{:S(2)}, u32[]{:S(2)}) collective-permute-start(bf16[16,2176]{1,0:T(8,128)(2,1)S(1)} %collective-permute-done.19.refs_3_), channel_id=1, source_target_pairs={{0,1},{1,0},{2,3},{3,2},{4,5},{5,4},{6,7},{7,6},{8,9},{9,8},{10,11... | collective-permute-start | bytes 208904 | tf_op jit(solution)/shard_map/ppermute | solution.py:39
  55.4 5.2 %collective-permute-start.22 = (bf16[16,2176]{1,0:T(8,128)(2,1)S(1)}, bf16[16,2176]{1,0:T(8,128)(2,1)S(1)}, u32[]{:S(2)}, u32[]{:S(2)}) collective-permute-start(bf16[16,2176]{1,0:T(8,128)(2,1)S(1)} %collective-permute-done.18.refs_2_), channel_id=1, source_target_pairs={{0,1},{1,0},{2,3},{3,2},{4,5},{5,4},{6,7},{7,6},{8,9},{9,8},{10,11... | collective-permute-start | bytes 208904 | tf_op jit(solution)/shard_map/ppermute | solution.py:39
  55.4 5.3 %collective-permute-start.21 = (bf16[16,2176]{1,0:T(8,128)(2,1)S(1)}, bf16[16,2176]{1,0:T(8,128)(2,1)S(1)}, u32[]{:S(2)}, u32[]{:S(2)}) collective-permute-start(bf16[16,2176]{1,0:T(8,128)(2,1)S(1)} %collective-permute-done.17.refs_1_), channel_id=1, source_target_pairs={{0,1},{1,0},{2,3},{3,2},{4,5},{5,4},{6,7},{7,6},{8,9},{9,8},{10,11... | collective-permute-start | bytes 208904 | tf_op jit(solution)/shard_map/ppermute | solution.py:39
  63.0 1.4 %collective-permute-start.27 = (bf16[32,2304]{1,0:T(8,128)(2,1)S(1)}, bf16[32,2304]{1,0:T(8,128)(2,1)S(1)}, u32[]{:S(2)}, u32[]{:S(2)}) collective-permute-start(bf16[32,2304]{1,0:T(8,128)(2,1)S(1)} %get-tuple-element.64), channel_id=1, source_target_pairs={{0,1},{1,0},{2,3},{3,2},{4,5},{5,4},{6,7},{7,6},{8,9},{9,8},{10,11... | collective-permute-start | bytes 442376 | tf_op jit(solution)/shard_map/ppermute | solution.py:39
  63.1 8.2 %collective-permute-start.24 = (bf16[64,2304]{1,0:T(8,128)(2,1)S(1)}, bf16[64,2304]{1,0:T(8,128)(2,1)S(1)}, u32[]{:S(2)}, u32[]{:S(2)}) collective-permute-start(bf16[64,2304]{1,0:T(8,128)(2,1)S(1)} %get-tuple-element.59), channel_id=1, source_target_pairs={{0,1},{1,0},{2,3},{3,2},{4,5},{5,4},{6,7},{7,6},{8,9},{9,8},{10,11... | collective-permute-start | bytes 884744 | tf_op jit(solution)/shard_map/ppermute | solution.py:39
  63.6 2.5 %collective-permute-start.25 = (bf16[32,2304]{1,0:T(8,128)(2,1)S(1)}, bf16[32,2304]{1,0:T(8,128)(2,1)S(1)}, u32[]{:S(2)}, u32[]{:S(2)}) collective-permute-start(bf16[32,2304]{1,0:T(8,128)(2,1)S(1)} %get-tuple-element.61), channel_id=1, source_target_pairs={{0,1},{1,0},{2,3},{3,2},{4,5},{5,4},{6,7},{7,6},{8,9},{9,8},{10,11... | collective-permute-start | bytes 442376 | tf_op jit(solution)/shard_map/ppermute | solution.py:39
  64.5 6.8 %collective-permute-start.28 = (bf16[32,2304]{1,0:T(8,128)(2,1)S(1)}, bf16[32,2304]{1,0:T(8,128)(2,1)S(1)}, u32[]{:S(2)}, u32[]{:S(2)}) collective-permute-start(bf16[32,2304]{1,0:T(8,128)(2,1)S(1)} %shard_map.144), channel_id=1, source_target_pairs={{0,2},{1,3},{2,0},{3,1},{4,6},{5,7},{6,4},{7,5},{8,10},{9,11},{10,... | collective-permute-start | bytes 442376 | tf_op jit(solution)/shard_map/ppermute | solution.py:39
  66.1 8.4 %collective-permute-start.26 = (bf16[32,2304]{1,0:T(8,128)(2,1)S(1)}, bf16[32,2304]{1,0:T(8,128)(2,1)S(1)}, u32[]{:S(2)}, u32[]{:S(2)}) collective-permute-start(bf16[32,2304]{1,0:T(8,128)(2,1)S(1)} %shard_map.143), channel_id=1, source_target_pairs={{0,2},{1,3},{2,0},{3,1},{4,6},{5,7},{6,4},{7,5},{8,10},{9,11},{10,... | collective-permute-start | bytes 442376 | tf_op jit(solution)/shard_map/ppermute | solution.py:39
  71.3 5.4 %collective-permute-start.29 = (bf16[16,2560]{1,0:T(8,128)(2,1)S(1)}, bf16[16,2560]{1,0:T(8,128)(2,1)S(1)}, u32[]{:S(2)}, u32[]{:S(2)}) collective-permute-start(bf16[16,2560]{1,0:T(8,128)(2,1)S(1)} %get-tuple-element.65), channel_id=1, source_target_pairs={{0,4},{1,5},{2,6},{3,7},{4,0},{5,1},{6,2},{7,3},{8,12},{9,13},{10,... | collective-permute-start | bytes 245768 | tf_op jit(solution)/shard_map/ppermute | solution.py:39
  71.6 7.1 %collective-permute-start.31 = (bf16[16,2560]{1,0:T(8,128)(2,1)S(1)}, bf16[16,2560]{1,0:T(8,128)(2,1)S(1)}, u32[]{:S(2)}, u32[]{:S(2)}) collective-permute-start(bf16[16,2560]{1,0:T(8,128)(2,1)S(1)} %get-tuple-element.67), channel_id=1, source_target_pairs={{0,12},{1,13},{2,14},{3,15},{4,8},{5,9},{6,10},{7,11},{8,4},{9,5},... | collective-permute-start | bytes 245768 | tf_op jit(solution)/shard_map/ppermute | solution.py:39
  74.6 7.1 %collective-permute-start.30 = (bf16[16,2560]{1,0:T(8,128)(2,1)S(1)}, bf16[16,2560]{1,0:T(8,128)(2,1)S(1)}, u32[]{:S(2)}, u32[]{:S(2)}) collective-permute-start(bf16[16,2560]{1,0:T(8,128)(2,1)S(1)} %get-tuple-element.66), channel_id=1, source_target_pairs={{0,8},{1,9},{2,10},{3,11},{4,12},{5,13},{6,14},{7,15},{8,0},{9,1},... | collective-permute-start | bytes 245768 | tf_op jit(solution)/shard_map/ppermute | solution.py:39

commit v4 on v3

--- a/solution.py
+++ b/solution.py
@@ -40,7 +40,11 @@
 
 
 def sequence(nz):
-    return [nz - 1] + list(range(1, nz - 1)) + [0]
+    return list(range(nz - 1, -1, -1))
+
+
+def portions(nz):
+    return [1, 1, nz - 2]
 
 
 def split3(x):
@@ -399,8 +403,7 @@
 def expert_kernel(nz, width, *refs):
     mine, theirs = refs[:nz], refs[nz : 2 * nz]
     (gain, gate_up, down, turn, fill, mixed) = refs[2 * nz : 2 * nz + 6]
-    outs, stream_own = refs[2 * nz + 6 : 2 * nz + 12], refs[2 * nz + 12]
-    x, normed, hidden, scaled = refs[2 * nz + 13 :]
+    *outs, stream_own, x, normed, hidden, scaled = refs[2 * nz + 6 :]
     device, core, _, z = place()
     block = mine[0].shape[0]
     half = block * nz
@@ -437,13 +440,15 @@
     nz = len(mine)
     block, wide = mine[0].shape
     total = 2 * nz * block
-    whole = jax.ShapeDtypeStruct((nz * cap, D + mixed.shape[1]), BF)
-    half = jax.ShapeDtypeStruct((nz // 2 * cap, D + mixed.shape[1]), BF)
+    shapes = [
+        jax.ShapeDtypeStruct((blocks * cap, D + mixed.shape[1]), BF)
+        for blocks in [nz] + portions(nz)
+    ]
     return pl.pallas_call(
         functools.partial(expert_kernel, nz, width),
-        out_shape=[whole, half, half] * 2 + [jax.ShapeDtypeStruct((cap, D), BF)],
+        out_shape=shapes * 2 + [jax.ShapeDtypeStruct((cap, D), BF)],
         in_specs=[pl.BlockSpec(memory_space=pltpu.VMEM)] * (2 * nz + 6),
-        out_specs=[pl.BlockSpec(memory_space=pltpu.VMEM)] * 7,
+        out_specs=[pl.BlockSpec(memory_space=pltpu.VMEM)] * (2 * len(shapes) + 1),
         scratch_shapes=[
             pltpu.VMEM((total, wide), BF),
             pltpu.VMEM((total, D), BF),
@@ -595,18 +600,22 @@
     mine = along_z([chunk] * nz)
     theirs = [hop(x, 1, width) for x in mine]
     (down,) = fetch(expert_down)
-    keep, keep_a, keep_b, send, send_a, send_b, stream = experts(
+    *halves, stream = experts(
         mine, theirs, gain, up, down, turn, fill, mixed, width, cap
     )
-    got_a = hop(send_a, 1, width)
-    got_b = hop(send_b, 1, width)
+    count = len(portions(nz))
+    keep, *keeps = halves[: count + 1]
+    send, *sends = halves[count + 1 :]
+    gots, fars, blocks = [], [], []
+    for i in range(count):
+        gots.append(hop(sends[i], 1, width))
     got = hop(send, 1, width)
-    far_a, far_b = add(keep_a, got_a), add(keep_b, got_b)
-    far_a = hop(far_a, 2, width)
-    far_b = hop(far_b, 2, width)
-    first = mix(keep, got, far_a, cap, 0)
-    second = mix(keep, got, far_b, cap, nz // 2)
-    attn, layer_out = finish(stream, along_z(by_distance(first + second)))
+    for i in range(count):
+        term = add(keeps[i], gots[i])
+        fars.append(hop(term, 2, width))
+    for i in range(count):
+        blocks += mix(keep, got, fars[i], cap, len(blocks))
+    attn, layer_out = finish(stream, along_z(by_distance(blocks)))
     return (attn, layer_out)
 
 

time: 82.6 us -> 82.4 us (level)
  waiting for transfers between devices: 33.2 us -> 31.4 us
  starting transfers between devices: 33.9 us -> 35.3 us
    ppermute x32 -> x34, waiting for transfers between devices: 33.2 us -> 31.4 us  [hop(): return lax.ppermute(x, 'ctx', [(i, i ^ mask) for i in range(width)])]
    ppermute x32 -> x34, starting transfers between devices: 33.9 us -> 35.3 us  [hop(): return lax.ppermute(x, 'ctx', [(i, i ^ mask) for i in range(width)])]
  transfers between devices with their start and end apart: 32 -> 34, of which waited for: 17 -> 18; matrix products, arithmetic and copies ran while one was open for 0% -> 0% of each run, Pallas kernels for 12% -> 13%
where the time goes in v4:
time: 82.4 us; the launch traced here: 82.1 us
  starting transfers between devices  35.3 us (43%)
  waiting for transfers between devices  31.4 us (38%)
  Pallas kernels  14 us (17%)
  between operations  1.45 us (2%)
    ppermute x34, starting transfers between devices, hop(): return lax.ppermute(x, 'ctx', [(i, i ^ mask) for i in range(width)])  35.3 us
    ppermute x34, waiting for transfers between devices, hop(): return lax.ppermute(x, 'ctx', [(i, i ^ mask) for i in range(width)])  31.4 us
    pallas_call x3, Pallas kernels, fetch(): pl.pallas_call(functools.partial(fetch_kernel, count), out_shape=[pltpu.V...  5.77 us
    pallas_call x1, Pallas kernels, experts(): pl.pallas_call(functools.partial(expert_kernel, nz, width), out_shape=sha...  2.46 us
    pallas_call x1, Pallas kernels, attention(): pl.pallas_call(functools.partial(attention_kernel, nz), out_shape=[jax.Sh...  2.21 us
    pallas_call x1, Pallas kernels, prepare(): pl.pallas_call(functools.partial(prepare_kernel, per, width), out_shape=[...  1.98 us
  transfers between devices with their start and end apart: 34, of which 18 were waited for; matrix products, arithmetic and copies ran while one was open for 0% of the time, Pallas kernels for 13%

profile of v4, /device:TPU:0, one launch (start us, length us, event | category | flops | bytes accessed | tf_op | source)
XLA Modules:
  0.0 82.1 jit_solution(83421820499384029)
XLA Ops:
  1.7 2.6 %collective-permute-start = (bf16[8,2048]{1,0:T(8,128)(2,1)}, bf16[8,2048]{1,0:T(8,128)(2,1)S(1)}, u32[]{:S(2)}, u32[]{:S(2)}) collective-permute-start(bf16[8,2048]{1,0:T(8,128)(2,1)} %refs_0_.3), channel_id=1, source_target_pairs={{0,2},{1,3},{2,0},{3,1},{4,6},{5,7},{6,4},{7,5},{8,10},{9,11},{10,... | collective-permute-start | bytes 98312 | tf_op jit(solution)/shard_map/ppermute | solution.py:39
  4.3 1.1 %fetch.3 = (bf16[8,2048]{1,0:T(8,128)(2,1)S(1)}, bf16[1,512,256]{2,1,0:T(8,128)(2,1)S(1)}, bf16[1,512,256]{2,1,0:T(8,128)(2,1)S(1)}) custom-call(bf16[8,2048]{1,0:T(8,128)(2,1)} %refs_0_.3, bf16[1,512,256]{2,1,0:T(8,128)(2,1)} %refs_1_.1, bf16[1,512,256]{2,1,0:T(8,128)(2,1)} %refs_2_.1), custom_call_target="tpu_custom_call" | custom-call | bytes 1114112 | tf_op jit(solution)/shard_map/fetch/pallas_call | solution.py:80
  5.4 1.1 %collective-permute-done.second = bf16[8,2048]{1,0:T(8,128)(2,1)S(1)} collective-permute-done((bf16[8,2048]{1,0:T(8,128)(2,1)}, bf16[8,2048]{1,0:T(8,128)(2,1)S(1)}, u32[]{:S(2)}, u32[]{:S(2)}) %collective-permute-start) | collective-permute-done | bytes 32800 | tf_op jit(solution)/shard_map/ppermute | solution.py:39
  6.5 4.0 %collective-permute-start.3 = (bf16[2,8,2048]{2,1,0:T(8,128)(2,1)S(1)}, bf16[2,8,2048]{2,1,0:T(8,128)(2,1)S(1)}, u32[]{:S(2)}, u32[]{:S(2)}) collective-permute-start(bf16[2,8,2048]{2,1,0:T(8,128)(2,1)S(1)} %shard_map.140.refs_0_), channel_id=1, source_target_pairs={{0,12},{1,13},{2,14},{3,15},{4,8},{5,9},{6,10},{7,11},{8,4},{9,5},... | collective-permute-start | bytes 196616 | tf_op jit(solution)/shard_map/ppermute | solution.py:39
  10.5 3.0 %collective-permute-done.3.refs_3_ = bf16[2,8,2048]{2,1,0:T(8,128)(2,1)S(1)} collective-permute-done((bf16[2,8,2048]{2,1,0:T(8,128)(2,1)S(1)}, bf16[2,8,2048]{2,1,0:T(8,128)(2,1)S(1)}, u32[]{:S(2)}, u32[]{:S(2)}) %collective-permute-start.3) | collective-permute-done | bytes 65568 | tf_op jit(solution)/shard_map/ppermute | solution.py:39
  15.7 2.1 %collective-permute-done.1.refs_1_ = bf16[2,8,2048]{2,1,0:T(8,128)(2,1)S(1)} collective-permute-done((bf16[2,8,2048]{2,1,0:T(8,128)(2,1)S(1)}, bf16[2,8,2048]{2,1,0:T(8,128)(2,1)S(1)}, u32[]{:S(2)}, u32[]{:S(2)}) %collective-permute-start.1) | collective-permute-done | bytes 65568 | tf_op jit(solution)/shard_map/ppermute | solution.py:39
  17.8 2.2 %attention.1 = (bf16[2,136,128]{2,1,0:T(8,128)(2,1)S(1)}, bf16[2,136,128]{2,1,0:T(8,128)(2,1)S(1)}, bf16[2,136,128]{2,1,0:T(8,128)(2,1)S(1)}, bf16[2,136,128]{2,1,0:T(8,128)(2,1)S(1)}) custom-call(s32[1]{0:T(128)S(6)} %copy.15.lengths, bf16[2,8,2048]{2,1,0:T(8,128)(2,1)S(1)} %shard_map.140.refs_0_, bf16[2,8,2048]{2,1,0:T(8,128)(2,1)S(1)} %collective-permute-done.1.refs_1_, ...), custom_call_target="tpu_custom_call" | custom-call | flops 536870912 | bytes 1048576 | tf_op jit(solution)/shard_map/attention/pallas_call | solution.py:300
  20.0 1.6 %collective-permute-start.6 = (bf16[2,136,128]{2,1,0:T(8,128)(2,1)S(1)}, bf16[2,136,128]{2,1,0:T(8,128)(2,1)S(1)}, u32[]{:S(2)}, u32[]{:S(2)}) collective-permute-start(bf16[2,136,128]{2,1,0:T(8,128)(2,1)S(1)} %get-tuple-element.39), channel_id=1, source_target_pairs={{0,2},{1,3},{2,0},{3,1},{4,6},{5,7},{6,4},{7,5},{8,10},{9,11},{10,... | collective-permute-start | bytes 208904 | tf_op jit(solution)/shard_map/ppermute | solution.py:39
  22.1 2.0 %prepare.1 = (bf16[16,2176]{1,0:T(8,128)(2,1)S(1)}, bf16[64,32]{1,0:T(8,128)(2,1)S(1)}, bf16[256,64]{1,0:T(8,128)(2,1)S(1)}, bf16[256,128]{1,0:T(8,128)(2,1)S(1)...) custom-call(s32[1,16]{1,0:T(1,128)} %bitcast.8, s32[1,128]{1,0:T(1,128)} %bitcast.9, s32[8,16]{1,0:T(8,128)} %bitcast.6, ...), custom_call_target="tpu_custom_call" | custom-call | flops 12582912 | bytes 131072 | tf_op jit(solution)/shard_map/prepare/pallas_call | solution.py:160
  25.9 3.0 %collective-permute-start.9 = (bf16[136,128]{1,0:T(8,128)(2,1)S(1)}, bf16[136,128]{1,0:T(8,128)(2,1)S(1)}, u32[]{:S(2)}, u32[]{:S(2)}) collective-permute-start(bf16[136,128]{1,0:T(8,128)(2,1)S(1)} %get-tuple-element.44), channel_id=1, source_target_pairs={{0,8},{1,9},{2,10},{3,11},{4,12},{5,13},{6,14},{7,15},{8,0},{9,1},... | collective-permute-start | bytes 104456 | tf_op jit(solution)/shard_map/ppermute | solution.py:39
  28.9 0.9 %collective-permute-start.10 = (bf16[136,128]{1,0:T(8,128)(2,1)S(1)}, bf16[136,128]{1,0:T(8,128)(2,1)S(1)}, u32[]{:S(2)}, u32[]{:S(2)}) collective-permute-start(bf16[136,128]{1,0:T(8,128)(2,1)S(1)} %get-tuple-element.45), channel_id=1, source_target_pairs={{0,12},{1,13},{2,14},{3,15},{4,8},{5,9},{6,10},{7,11},{8,4},{9,5},... | collective-permute-start | bytes 104456 | tf_op jit(solution)/shard_map/ppermute | solution.py:39
  29.8 1.0 %collective-permute-done.9.refs_2_ = bf16[136,128]{1,0:T(8,128)(2,1)S(1)} collective-permute-done((bf16[136,128]{1,0:T(8,128)(2,1)S(1)}, bf16[136,128]{1,0:T(8,128)(2,1)S(1)}, u32[]{:S(2)}, u32[]{:S(2)}) %collective-permute-start.9) | collective-permute-done | bytes 34848 | tf_op jit(solution)/shard_map/ppermute | solution.py:39
  30.8 3.8 %collective-permute-done.10.refs_3_ = bf16[136,128]{1,0:T(8,128)(2,1)S(1)} collective-permute-done((bf16[136,128]{1,0:T(8,128)(2,1)S(1)}, bf16[136,128]{1,0:T(8,128)(2,1)S(1)}, u32[]{:S(2)}, u32[]{:S(2)}) %collective-permute-start.10) | collective-permute-done | bytes 34848 | tf_op jit(solution)/shard_map/ppermute | solution.py:39
  35.2 1.6 %collective-permute-start.14 = (bf16[16,2176]{1,0:T(8,128)(2,1)S(1)}, bf16[16,2176]{1,0:T(8,128)(2,1)S(1)}, u32[]{:S(2)}, u32[]{:S(2)}) collective-permute-start(bf16[16,2176]{1,0:T(8,128)(2,1)S(1)} %get-tuple-element.51), channel_id=1, source_target_pairs={{0,8},{1,9},{2,10},{3,11},{4,12},{5,13},{6,14},{7,15},{8,0},{9,1},... | collective-permute-start | bytes 208904 | tf_op jit(solution)/shard_map/ppermute | solution.py:39
  36.8 2.8 %collective-permute-start.15 = (bf16[16,2176]{1,0:T(8,128)(2,1)S(1)}, bf16[16,2176]{1,0:T(8,128)(2,1)S(1)}, u32[]{:S(2)}, u32[]{:S(2)}) collective-permute-start(bf16[16,2176]{1,0:T(8,128)(2,1)S(1)} %get-tuple-element.52), channel_id=1, source_target_pairs={{0,12},{1,13},{2,14},{3,15},{4,8},{5,9},{6,10},{7,11},{8,4},{9,5},... | collective-permute-start | bytes 208904 | tf_op jit(solution)/shard_map/ppermute | solution.py:39
  39.6 2.5 %collective-permute-done.14.refs_2_ = bf16[16,2176]{1,0:T(8,128)(2,1)S(1)} collective-permute-done((bf16[16,2176]{1,0:T(8,128)(2,1)S(1)}, bf16[16,2176]{1,0:T(8,128)(2,1)S(1)}, u32[]{:S(2)}, u32[]{:S(2)}) %collective-permute-start.14) | collective-permute-done | bytes 69664 | tf_op jit(solution)/shard_map/ppermute | solution.py:39
  43.0 1.4 %collective-permute-start.16 = (bf16[16,2176]{1,0:T(8,128)(2,1)S(1)}, bf16[16,2176]{1,0:T(8,128)(2,1)S(1)}, u32[]{:S(2)}, u32[]{:S(2)}) collective-permute-start(bf16[16,2176]{1,0:T(8,128)(2,1)S(1)} %shard_map.141.refs_0_), channel_id=1, source_target_pairs={{0,2},{1,3},{2,0},{3,1},{4,6},{5,7},{6,4},{7,5},{8,10},{9,11},{10,... | collective-permute-start | bytes 208904 | tf_op jit(solution)/shard_map/ppermute | solution.py:39
  44.4 3.0 %collective-permute-done.16.refs_1_ = bf16[16,2176]{1,0:T(8,128)(2,1)S(1)} collective-permute-done((bf16[16,2176]{1,0:T(8,128)(2,1)S(1)}, bf16[16,2176]{1,0:T(8,128)(2,1)S(1)}, u32[]{:S(2)}, u32[]{:S(2)}) %collective-permute-start.16) | collective-permute-done | bytes 69664 | tf_op jit(solution)/shard_map/ppermute | solution.py:39
  47.4 2.8 %collective-permute-start.19 = (bf16[16,2176]{1,0:T(8,128)(2,1)S(1)}, bf16[16,2176]{1,0:T(8,128)(2,1)S(1)}, u32[]{:S(2)}, u32[]{:S(2)}) collective-permute-start(bf16[16,2176]{1,0:T(8,128)(2,1)S(1)} %shard_map.142.refs_0_), channel_id=1, source_target_pairs={{0,12},{1,13},{2,14},{3,15},{4,8},{5,9},{6,10},{7,11},{8,4},{9,5},... | collective-permute-start | bytes 208904 | tf_op jit(solution)/shard_map/ppermute | solution.py:39
  50.2 1.6 %collective-permute-start.17 = (bf16[16,2176]{1,0:T(8,128)(2,1)S(1)}, bf16[16,2176]{1,0:T(8,128)(2,1)S(1)}, u32[]{:S(2)}, u32[]{:S(2)}) collective-permute-start(bf16[16,2176]{1,0:T(8,128)(2,1)S(1)} %shard_map.142.refs_0_), channel_id=1, source_target_pairs={{0,4},{1,5},{2,6},{3,7},{4,0},{5,1},{6,2},{7,3},{8,12},{9,13},{10,... | collective-permute-start | bytes 208904 | tf_op jit(solution)/shard_map/ppermute | solution.py:39
  51.8 1.7 %collective-permute-done.19.refs_3_ = bf16[16,2176]{1,0:T(8,128)(2,1)S(1)} collective-permute-done((bf16[16,2176]{1,0:T(8,128)(2,1)S(1)}, bf16[16,2176]{1,0:T(8,128)(2,1)S(1)}, u32[]{:S(2)}, u32[]{:S(2)}) %collective-permute-start.19) | collective-permute-done | bytes 69664 | tf_op jit(solution)/shard_map/ppermute | solution.py:39
  53.6 1.9 %collective-permute-done.18.refs_2_ = bf16[16,2176]{1,0:T(8,128)(2,1)S(1)} collective-permute-done((bf16[16,2176]{1,0:T(8,128)(2,1)S(1)}, bf16[16,2176]{1,0:T(8,128)(2,1)S(1)}, u32[]{:S(2)}, u32[]{:S(2)}) %collective-permute-start.18) | collective-permute-done | bytes 69664 | tf_op jit(solution)/shard_map/ppermute | solution.py:39
  55.9 1.9 %fetch.5.refs_10_ = bf16[1,768,2048]{2,1,0:T(8,128)(2,1)S(1)} custom-call(bf16[1,768,2048]{2,1,0:T(8,128)(2,1)} %refs_0_.5), custom_call_target="tpu_custom_call" | custom-call | bytes 6291456 | tf_op jit(solution)/shard_map/fetch/pallas_call | solution.py:80
  57.8 2.8 %fetch.4.refs_9_ = bf16[1,2048,1536]{2,1,0:T(8,128)(2,1)S(1)} custom-call(bf16[1,2048,1536]{2,1,0:T(8,128)(2,1)} %refs_0_.4), custom_call_target="tpu_custom_call" | custom-call | bytes 12582912 | tf_op jit(solution)/shard_map/fetch/pallas_call | solution.py:80
  60.7 2.5 %experts.1 = (bf16[64,2304]{1,0:T(8,128)(2,1)S(1)}, bf16[16,2304]{1,0:T(8,128)(2,1)S(1)}, bf16[16,2304]{1,0:T(8,128)(2,1)S(1)}, bf16[32,2304]{1,0:T(8,128)(2,1)S...) custom-call(bf16[16,2176]{1,0:T(8,128)(2,1)S(1)} %shard_map.142.refs, ...), custom_call_target="tpu_custom_call" | custom-call | flops 1207959552 | bytes 9437184 | tf_op jit(solution)/shard_map/experts/pallas_call | solution.py:447
  64.6 1.6 %collective-permute-start.26 = (bf16[32,2304]{1,0:T(8,128)(2,1)S(1)}, bf16[32,2304]{1,0:T(8,128)(2,1)S(1)}, u32[]{:S(2)}, u32[]{:S(2)}) collective-permute-start(bf16[32,2304]{1,0:T(8,128)(2,1)S(1)} %shard_map.143), channel_id=1, source_target_pairs={{0,2},{1,3},{2,0},{3,1},{4,6},{5,7},{6,4},{7,5},{8,10},{9,11},{10,... | collective-permute-start | bytes 442376 | tf_op jit(solution)/shard_map/ppermute | solution.py:39
  68.1 1.6 %collective-permute-start.32 = (bf16[16,2304]{1,0:T(8,128)(2,1)S(1)}, bf16[16,2304]{1,0:T(8,128)(2,1)S(1)}, u32[]{:S(2)}, u32[]{:S(2)}) collective-permute-start(bf16[16,2304]{1,0:T(8,128)(2,1)S(1)} %shard_map.145), channel_id=1, source_target_pairs={{0,2},{1,3},{2,0},{3,1},{4,6},{5,7},{6,4},{7,5},{8,10},{9,11},{10,... | collective-permute-start | bytes 221192 | tf_op jit(solution)/shard_map/ppermute | solution.py:39
  69.7 1.1 %collective-permute-done.26.far = bf16[32,2304]{1,0:T(8,128)(2,1)S(1)} collective-permute-done((bf16[32,2304]{1,0:T(8,128)(2,1)S(1)}, bf16[32,2304]{1,0:T(8,128)(2,1)S(1)}, u32[]{:S(2)}, u32[]{:S(2)}) %collective-permute-start.26) | collective-permute-done | bytes 147488 | tf_op jit(solution)/shard_map/ppermute | solution.py:39
  70.9 1.0 %collective-permute-start.27 = (bf16[16,2560]{1,0:T(8,128)(2,1)S(1)}, bf16[16,2560]{1,0:T(8,128)(2,1)S(1)}, u32[]{:S(2)}, u32[]{:S(2)}) collective-permute-start(bf16[16,2560]{1,0:T(8,128)(2,1)S(1)} %get-tuple-element.63), channel_id=1, source_target_pairs={{0,4},{1,5},{2,6},{3,7},{4,0},{5,1},{6,2},{7,3},{8,12},{9,13},{10,... | collective-permute-start | bytes 245768 | tf_op jit(solution)/shard_map/ppermute | solution.py:39
  72.8 1.8 %collective-permute-start.30 = (bf16[16,2560]{1,0:T(8,128)(2,1)S(1)}, bf16[16,2560]{1,0:T(8,128)(2,1)S(1)}, u32[]{:S(2)}, u32[]{:S(2)}) collective-permute-start(bf16[16,2560]{1,0:T(8,128)(2,1)S(1)} %mix.4), channel_id=1, source_target_pairs={{0,8},{1,9},{2,10},{3,11},{4,12},{5,13},{6,14},{7,15},{8,0},{9,1},... | collective-permute-start | bytes 245768 | tf_op jit(solution)/shard_map/ppermute | solution.py:39
  74.6 1.6 %collective-permute-start.33 = (bf16[16,2560]{1,0:T(8,128)(2,1)S(1)}, bf16[16,2560]{1,0:T(8,128)(2,1)S(1)}, u32[]{:S(2)}, u32[]{:S(2)}) collective-permute-start(bf16[16,2560]{1,0:T(8,128)(2,1)S(1)} %mix.5), channel_id=1, source_target_pairs={{0,12},{1,13},{2,14},{3,15},{4,8},{5,9},{6,10},{7,11},{8,4},{9,5},... | collective-permute-start | bytes 245768 | tf_op jit(solution)/shard_map/ppermute | solution.py:39
  76.2 5.2 %collective-permute-done.30.refs_2_ = bf16[16,2560]{1,0:T(8,128)(2,1)S(1)} collective-permute-done((bf16[16,2560]{1,0:T(8,128)(2,1)S(1)}, bf16[16,2560]{1,0:T(8,128)(2,1)S(1)}, u32[]{:S(2)}, u32[]{:S(2)}) %collective-permute-start.30) | collective-permute-done | bytes 81952 | tf_op jit(solution)/shard_map/ppermute | solution.py:39
  (55 shorter events, 12.0 us)
Async XLA Ops:
  0.6 34.0 %collective-permute-start.11 = (bf16[128,2048]{1,0:T(8,128)(2,1)}, bf16[128,2048]{1,0:T(8,128)(2,1)S(1)}, u32[]{:S(2)}, u32[]{:S(2)}) collective-permute-start(bf16[128,2048]{1,0:T(8,128)(2,1)} %refs_5_.1), channel_id=1, source_target_pairs={{0,1},{1,0},{2,3},{3,2},{4,5},{5,4},{6,7},{7,6},{8,9},{9,8},{10,11... | collective-permute-start | bytes 1572872 | tf_op jit(solution)/shard_map/ppermute | solution.py:39
  1.2 16.6 %collective-permute-start.4 = (bf16[1,512,256]{2,1,0:T(8,128)(2,1)}, bf16[1,512,256]{2,1,0:T(8,128)(2,1)S(1)}, u32[]{:S(2)}, u32[]{:S(2)}) collective-permute-start(bf16[1,512,256]{2,1,0:T(8,128)(2,1)} %refs_1_.1), channel_id=1, source_target_pairs={{0,1},{1,0},{2,3},{3,2},{4,5},{5,4},{6,7},{7,6},{8,9},{9,8},{10,11... | collective-permute-start | bytes 786440 | tf_op jit(solution)/shard_map/ppermute | solution.py:39
  1.3 16.5 %collective-permute-start.5 = (bf16[1,512,256]{2,1,0:T(8,128)(2,1)}, bf16[1,512,256]{2,1,0:T(8,128)(2,1)S(1)}, u32[]{:S(2)}, u32[]{:S(2)}) collective-permute-start(bf16[1,512,256]{2,1,0:T(8,128)(2,1)} %refs_2_.1), channel_id=1, source_target_pairs={{0,1},{1,0},{2,3},{3,2},{4,5},{5,4},{6,7},{7,6},{8,9},{9,8},{10,11... | collective-permute-start | bytes 786440 | tf_op jit(solution)/shard_map/ppermute | solution.py:39
  1.7 4.8 %collective-permute-start = (bf16[8,2048]{1,0:T(8,128)(2,1)}, bf16[8,2048]{1,0:T(8,128)(2,1)S(1)}, u32[]{:S(2)}, u32[]{:S(2)}) collective-permute-start(bf16[8,2048]{1,0:T(8,128)(2,1)} %refs_0_.3), channel_id=1, source_target_pairs={{0,2},{1,3},{2,0},{3,1},{4,6},{5,7},{6,4},{7,5},{8,10},{9,11},{10,... | collective-permute-start | bytes 98312 | tf_op jit(solution)/shard_map/ppermute | solution.py:39
  6.5 7.0 %collective-permute-start.3 = (bf16[2,8,2048]{2,1,0:T(8,128)(2,1)S(1)}, bf16[2,8,2048]{2,1,0:T(8,128)(2,1)S(1)}, u32[]{:S(2)}, u32[]{:S(2)}) collective-permute-start(bf16[2,8,2048]{2,1,0:T(8,128)(2,1)S(1)} %shard_map.140.refs_0_), channel_id=1, source_target_pairs={{0,12},{1,13},{2,14},{3,15},{4,8},{5,9},{6,10},{7,11},{8,4},{9,5},... | collective-permute-start | bytes 196616 | tf_op jit(solution)/shard_map/ppermute | solution.py:39
  10.5 5.2 %collective-permute-start.2 = (bf16[2,8,2048]{2,1,0:T(8,128)(2,1)S(1)}, bf16[2,8,2048]{2,1,0:T(8,128)(2,1)S(1)}, u32[]{:S(2)}, u32[]{:S(2)}) collective-permute-start(bf16[2,8,2048]{2,1,0:T(8,128)(2,1)S(1)} %shard_map.140.refs_0_), channel_id=1, source_target_pairs={{0,8},{1,9},{2,10},{3,11},{4,12},{5,13},{6,14},{7,15},{8,0},{9,1},... | collective-permute-start | bytes 196616 | tf_op jit(solution)/shard_map/ppermute | solution.py:39
  13.5 4.3 %collective-permute-start.1 = (bf16[2,8,2048]{2,1,0:T(8,128)(2,1)S(1)}, bf16[2,8,2048]{2,1,0:T(8,128)(2,1)S(1)}, u32[]{:S(2)}, u32[]{:S(2)}) collective-permute-start(bf16[2,8,2048]{2,1,0:T(8,128)(2,1)S(1)} %shard_map.140.refs_0_), channel_id=1, source_target_pairs={{0,4},{1,5},{2,6},{3,7},{4,0},{5,1},{6,2},{7,3},{8,12},{9,13},{10,... | collective-permute-start | bytes 196616 | tf_op jit(solution)/shard_map/ppermute | solution.py:39
  20.0 4.4 %collective-permute-start.6 = (bf16[2,136,128]{2,1,0:T(8,128)(2,1)S(1)}, bf16[2,136,128]{2,1,0:T(8,128)(2,1)S(1)}, u32[]{:S(2)}, u32[]{:S(2)}) collective-permute-start(bf16[2,136,128]{2,1,0:T(8,128)(2,1)S(1)} %get-tuple-element.39), channel_id=1, source_target_pairs={{0,2},{1,3},{2,0},{3,1},{4,6},{5,7},{6,4},{7,5},{8,10},{9,11},{10,... | collective-permute-start | bytes 208904 | tf_op jit(solution)/shard_map/ppermute | solution.py:39
  21.6 4.3 %collective-permute-start.8 = (bf16[2,136,128]{2,1,0:T(8,128)(2,1)S(1)}, bf16[2,136,128]{2,1,0:T(8,128)(2,1)S(1)}, u32[]{:S(2)}, u32[]{:S(2)}) collective-permute-start(bf16[2,136,128]{2,1,0:T(8,128)(2,1)S(1)} %get-tuple-element.43), channel_id=1, source_target_pairs={{0,2},{1,3},{2,0},{3,1},{4,6},{5,7},{6,4},{7,5},{8,10},{9,11},{10,... | collective-permute-start | bytes 208904 | tf_op jit(solution)/shard_map/ppermute | solution.py:39
  24.1 5.8 %collective-permute-start.12 = (bf16[16,2176]{1,0:T(8,128)(2,1)S(1)}, bf16[16,2176]{1,0:T(8,128)(2,1)S(1)}, u32[]{:S(2)}, u32[]{:S(2)}) collective-permute-start(bf16[16,2176]{1,0:T(8,128)(2,1)S(1)} %get-tuple-element.47.refs_6_), channel_id=1, source_target_pairs={{0,1},{1,0},{2,3},{3,2},{4,5},{5,4},{6,7},{7,6},{8,9},{9,8},{10,11... | collective-permute-start | bytes 208904 | tf_op jit(solution)/shard_map/ppermute | solution.py:39
  24.4 5.4 %collective-permute-start.7 = (bf16[136,128]{1,0:T(8,128)(2,1)S(1)}, bf16[136,128]{1,0:T(8,128)(2,1)S(1)}, u32[]{:S(2)}, u32[]{:S(2)}) collective-permute-start(bf16[136,128]{1,0:T(8,128)(2,1)S(1)} %get-tuple-element.41), channel_id=1, source_target_pairs={{0,4},{1,5},{2,6},{3,7},{4,0},{5,1},{6,2},{7,3},{8,12},{9,13},{10,... | collective-permute-start | bytes 104456 | tf_op jit(solution)/shard_map/ppermute | solution.py:39
  25.9 4.9 %collective-permute-start.9 = (bf16[136,128]{1,0:T(8,128)(2,1)S(1)}, bf16[136,128]{1,0:T(8,128)(2,1)S(1)}, u32[]{:S(2)}, u32[]{:S(2)}) collective-permute-start(bf16[136,128]{1,0:T(8,128)(2,1)S(1)} %get-tuple-element.44), channel_id=1, source_target_pairs={{0,8},{1,9},{2,10},{3,11},{4,12},{5,13},{6,14},{7,15},{8,0},{9,1},... | collective-permute-start | bytes 104456 | tf_op jit(solution)/shard_map/ppermute | solution.py:39
  28.9 5.7 %collective-permute-start.10 = (bf16[136,128]{1,0:T(8,128)(2,1)S(1)}, bf16[136,128]{1,0:T(8,128)(2,1)S(1)}, u32[]{:S(2)}, u32[]{:S(2)}) collective-permute-start(bf16[136,128]{1,0:T(8,128)(2,1)S(1)} %get-tuple-element.45), channel_id=1, source_target_pairs={{0,12},{1,13},{2,14},{3,15},{4,8},{5,9},{6,10},{7,11},{8,4},{9,5},... | collective-permute-start | bytes 104456 | tf_op jit(solution)/shard_map/ppermute | solution.py:39
  35.1 4.5 %collective-permute-start.13 = (bf16[16,2176]{1,0:T(8,128)(2,1)S(1)}, bf16[16,2176]{1,0:T(8,128)(2,1)S(1)}, u32[]{:S(2)}, u32[]{:S(2)}) collective-permute-start(bf16[16,2176]{1,0:T(8,128)(2,1)S(1)} %get-tuple-element.50), channel_id=1, source_target_pairs={{0,4},{1,5},{2,6},{3,7},{4,0},{5,1},{6,2},{7,3},{8,12},{9,13},{10,... | collective-permute-start | bytes 208904 | tf_op jit(solution)/shard_map/ppermute | solution.py:39
  35.2 6.9 %collective-permute-start.14 = (bf16[16,2176]{1,0:T(8,128)(2,1)S(1)}, bf16[16,2176]{1,0:T(8,128)(2,1)S(1)}, u32[]{:S(2)}, u32[]{:S(2)}) collective-permute-start(bf16[16,2176]{1,0:T(8,128)(2,1)S(1)} %get-tuple-element.51), channel_id=1, source_target_pairs={{0,8},{1,9},{2,10},{3,11},{4,12},{5,13},{6,14},{7,15},{8,0},{9,1},... | collective-permute-start | bytes 208904 | tf_op jit(solution)/shard_map/ppermute | solution.py:39
  36.8 6.1 %collective-permute-start.15 = (bf16[16,2176]{1,0:T(8,128)(2,1)S(1)}, bf16[16,2176]{1,0:T(8,128)(2,1)S(1)}, u32[]{:S(2)}, u32[]{:S(2)}) collective-permute-start(bf16[16,2176]{1,0:T(8,128)(2,1)S(1)} %get-tuple-element.52), channel_id=1, source_target_pairs={{0,12},{1,13},{2,14},{3,15},{4,8},{5,9},{6,10},{7,11},{8,4},{9,5},... | collective-permute-start | bytes 208904 | tf_op jit(solution)/shard_map/ppermute | solution.py:39
  43.0 4.4 %collective-permute-start.16 = (bf16[16,2176]{1,0:T(8,128)(2,1)S(1)}, bf16[16,2176]{1,0:T(8,128)(2,1)S(1)}, u32[]{:S(2)}, u32[]{:S(2)}) collective-permute-start(bf16[16,2176]{1,0:T(8,128)(2,1)S(1)} %shard_map.141.refs_0_), channel_id=1, source_target_pairs={{0,2},{1,3},{2,0},{3,1},{4,6},{5,7},{6,4},{7,5},{8,10},{9,11},{10,... | collective-permute-start | bytes 208904 | tf_op jit(solution)/shard_map/ppermute | solution.py:39
  47.4 6.2 %collective-permute-start.19 = (bf16[16,2176]{1,0:T(8,128)(2,1)S(1)}, bf16[16,2176]{1,0:T(8,128)(2,1)S(1)}, u32[]{:S(2)}, u32[]{:S(2)}) collective-permute-start(bf16[16,2176]{1,0:T(8,128)(2,1)S(1)} %shard_map.142.refs_0_), channel_id=1, source_target_pairs={{0,12},{1,13},{2,14},{3,15},{4,8},{5,9},{6,10},{7,11},{8,4},{9,5},... | collective-permute-start | bytes 208904 | tf_op jit(solution)/shard_map/ppermute | solution.py:39
  50.2 5.2 %collective-permute-start.18 = (bf16[16,2176]{1,0:T(8,128)(2,1)S(1)}, bf16[16,2176]{1,0:T(8,128)(2,1)S(1)}, u32[]{:S(2)}, u32[]{:S(2)}) collective-permute-start(bf16[16,2176]{1,0:T(8,128)(2,1)S(1)} %shard_map.142.refs_0_), channel_id=1, source_target_pairs={{0,8},{1,9},{2,10},{3,11},{4,12},{5,13},{6,14},{7,15},{8,0},{9,1},... | collective-permute-start | bytes 208904 | tf_op jit(solution)/shard_map/ppermute | solution.py:39
  50.2 5.2 %collective-permute-start.17 = (bf16[16,2176]{1,0:T(8,128)(2,1)S(1)}, bf16[16,2176]{1,0:T(8,128)(2,1)S(1)}, u32[]{:S(2)}, u32[]{:S(2)}) collective-permute-start(bf16[16,2176]{1,0:T(8,128)(2,1)S(1)} %shard_map.142.refs_0_), channel_id=1, source_target_pairs={{0,4},{1,5},{2,6},{3,7},{4,0},{5,1},{6,2},{7,3},{8,12},{9,13},{10,... | collective-permute-start | bytes 208904 | tf_op jit(solution)/shard_map/ppermute | solution.py:39
  51.8 8.8 %collective-permute-start.20 = (bf16[16,2176]{1,0:T(8,128)(2,1)S(1)}, bf16[16,2176]{1,0:T(8,128)(2,1)S(1)}, u32[]{:S(2)}, u32[]{:S(2)}) collective-permute-start(bf16[16,2176]{1,0:T(8,128)(2,1)S(1)} %shard_map.142.refs_0_), channel_id=1, source_target_pairs={{0,1},{1,0},{2,3},{3,2},{4,5},{5,4},{6,7},{7,6},{8,9},{9,8},{10,11... | collective-permute-start | bytes 208904 | tf_op jit(solution)/shard_map/ppermute | solution.py:39
  53.6 7.1 %collective-permute-start.23 = (bf16[16,2176]{1,0:T(8,128)(2,1)S(1)}, bf16[16,2176]{1,0:T(8,128)(2,1)S(1)}, u32[]{:S(2)}, u32[]{:S(2)}) collective-permute-start(bf16[16,2176]{1,0:T(8,128)(2,1)S(1)} %collective-permute-done.19.refs_3_), channel_id=1, source_target_pairs={{0,1},{1,0},{2,3},{3,2},{4,5},{5,4},{6,7},{7,6},{8,9},{9,8},{10,11... | collective-permute-start | bytes 208904 | tf_op jit(solution)/shard_map/ppermute | solution.py:39
  55.4 5.2 %collective-permute-start.22 = (bf16[16,2176]{1,0:T(8,128)(2,1)S(1)}, bf16[16,2176]{1,0:T(8,128)(2,1)S(1)}, u32[]{:S(2)}, u32[]{:S(2)}) collective-permute-start(bf16[16,2176]{1,0:T(8,128)(2,1)S(1)} %collective-permute-done.18.refs_2_), channel_id=1, source_target_pairs={{0,1},{1,0},{2,3},{3,2},{4,5},{5,4},{6,7},{7,6},{8,9},{9,8},{10,11... | collective-permute-start | bytes 208904 | tf_op jit(solution)/shard_map/ppermute | solution.py:39
  55.4 5.3 %collective-permute-start.21 = (bf16[16,2176]{1,0:T(8,128)(2,1)S(1)}, bf16[16,2176]{1,0:T(8,128)(2,1)S(1)}, u32[]{:S(2)}, u32[]{:S(2)}) collective-permute-start(bf16[16,2176]{1,0:T(8,128)(2,1)S(1)} %collective-permute-done.17.refs_1_), channel_id=1, source_target_pairs={{0,1},{1,0},{2,3},{3,2},{4,5},{5,4},{6,7},{7,6},{8,9},{9,8},{10,11... | collective-permute-start | bytes 208904 | tf_op jit(solution)/shard_map/ppermute | solution.py:39
  63.2 7.6 %collective-permute-start.24 = (bf16[64,2304]{1,0:T(8,128)(2,1)S(1)}, bf16[64,2304]{1,0:T(8,128)(2,1)S(1)}, u32[]{:S(2)}, u32[]{:S(2)}) collective-permute-start(bf16[64,2304]{1,0:T(8,128)(2,1)S(1)} %get-tuple-element.59), channel_id=1, source_target_pairs={{0,1},{1,0},{2,3},{3,2},{4,5},{5,4},{6,7},{7,6},{8,9},{9,8},{10,11... | collective-permute-start | bytes 884744 | tf_op jit(solution)/shard_map/ppermute | solution.py:39
  64.6 6.2 %collective-permute-start.26 = (bf16[32,2304]{1,0:T(8,128)(2,1)S(1)}, bf16[32,2304]{1,0:T(8,128)(2,1)S(1)}, u32[]{:S(2)}, u32[]{:S(2)}) collective-permute-start(bf16[32,2304]{1,0:T(8,128)(2,1)S(1)} %shard_map.143), channel_id=1, source_target_pairs={{0,2},{1,3},{2,0},{3,1},{4,6},{5,7},{6,4},{7,5},{8,10},{9,11},{10,... | collective-permute-start | bytes 442376 | tf_op jit(solution)/shard_map/ppermute | solution.py:39
  66.2 1.8 %collective-permute-start.31 = (bf16[16,2304]{1,0:T(8,128)(2,1)S(1)}, bf16[16,2304]{1,0:T(8,128)(2,1)S(1)}, u32[]{:S(2)}, u32[]{:S(2)}) collective-permute-start(bf16[16,2304]{1,0:T(8,128)(2,1)S(1)} %get-tuple-element.67), channel_id=1, source_target_pairs={{0,1},{1,0},{2,3},{3,2},{4,5},{5,4},{6,7},{7,6},{8,9},{9,8},{10,11... | collective-permute-start | bytes 221192 | tf_op jit(solution)/shard_map/ppermute | solution.py:39
  67.5 5.2 %collective-permute-start.29 = (bf16[16,2304]{1,0:T(8,128)(2,1)S(1)}, bf16[16,2304]{1,0:T(8,128)(2,1)S(1)}, u32[]{:S(2)}, u32[]{:S(2)}) collective-permute-start(bf16[16,2304]{1,0:T(8,128)(2,1)S(1)} %shard_map.144), channel_id=1, source_target_pairs={{0,2},{1,3},{2,0},{3,1},{4,6},{5,7},{6,4},{7,5},{8,10},{9,11},{10,... | collective-permute-start | bytes 221192 | tf_op jit(solution)/shard_map/ppermute | solution.py:39
  68.1 6.5 %collective-permute-start.32 = (bf16[16,2304]{1,0:T(8,128)(2,1)S(1)}, bf16[16,2304]{1,0:T(8,128)(2,1)S(1)}, u32[]{:S(2)}, u32[]{:S(2)}) collective-permute-start(bf16[16,2304]{1,0:T(8,128)(2,1)S(1)} %shard_map.145), channel_id=1, source_target_pairs={{0,2},{1,3},{2,0},{3,1},{4,6},{5,7},{6,4},{7,5},{8,10},{9,11},{10,... | collective-permute-start | bytes 221192 | tf_op jit(solution)/shard_map/ppermute | solution.py:39
  70.9 5.4 %collective-permute-start.27 = (bf16[16,2560]{1,0:T(8,128)(2,1)S(1)}, bf16[16,2560]{1,0:T(8,128)(2,1)S(1)}, u32[]{:S(2)}, u32[]{:S(2)}) collective-permute-start(bf16[16,2560]{1,0:T(8,128)(2,1)S(1)} %get-tuple-element.63), channel_id=1, source_target_pairs={{0,4},{1,5},{2,6},{3,7},{4,0},{5,1},{6,2},{7,3},{8,12},{9,13},{10,... | collective-permute-start | bytes 245768 | tf_op jit(solution)/shard_map/ppermute | solution.py:39
  72.8 8.7 %collective-permute-start.30 = (bf16[16,2560]{1,0:T(8,128)(2,1)S(1)}, bf16[16,2560]{1,0:T(8,128)(2,1)S(1)}, u32[]{:S(2)}, u32[]{:S(2)}) collective-permute-start(bf16[16,2560]{1,0:T(8,128)(2,1)S(1)} %mix.4), channel_id=1, source_target_pairs={{0,8},{1,9},{2,10},{3,11},{4,12},{5,13},{6,14},{7,15},{8,0},{9,1},... | collective-permute-start | bytes 245768 | tf_op jit(solution)/shard_map/ppermute | solution.py:39
  74.6 6.8 %collective-permute-start.33 = (bf16[16,2560]{1,0:T(8,128)(2,1)S(1)}, bf16[16,2560]{1,0:T(8,128)(2,1)S(1)}, u32[]{:S(2)}, u32[]{:S(2)}) collective-permute-start(bf16[16,2560]{1,0:T(8,128)(2,1)S(1)} %mix.5), channel_id=1, source_target_pairs={{0,12},{1,13},{2,14},{3,15},{4,8},{5,9},{6,10},{7,11},{8,4},{9,5},... | collective-permute-start | bytes 245768 | tf_op jit(solution)/shard_map/ppermute | solution.py:39
  (2 other events, 2.7 us)

commit v5 on v4

--- a/solution.py
+++ b/solution.py
@@ -44,7 +44,7 @@
 
 
 def portions(nz):
-    return [1, 1, nz - 2]
+    return [1, nz // 2 - 1, nz // 2]
 
 
 def split3(x):
@@ -209,10 +209,10 @@
     )(*terms)
 
 
-def attention_kernel(nz, lengths, *refs):
+def attention_kernel(nz, far, lengths, *refs):
     pieces, (k_own, v_own, k_oth, v_oth) = refs[:nz], refs[nz : nz + 4]
-    outs, (rows, ready) = refs[nz + 4 : nz + 8], refs[nz + 8 :]
-    device, core, chip, _ = place()
+    *outs, rows, ready = refs[nz + 4 :]
+    device, core, chip, z = place()
     per = pieces[0].shape[1]
     requests, span = k_own.shape[0], k_own.shape[1]
     count = rows.shape[0]
@@ -234,12 +234,17 @@
     for q in range(requests):
         last = lengths[q] + ahead
         see_own, see_oth = key <= last - first_own, key <= last - first_oth
-        for v in range(KVH):
-            kv = slice(v * HD, (v + 1) * HD)
+        for near_head in range(KVH // 2):
+            half = z // (nz // 2) ^ far
+            v = half * (KVH // 2) + near_head
+            kv = pl.ds(pl.multiple_of(v * HD, HD), HD)
             asked = jnp.concatenate(
                 [
-                    rows[q * seat : (q + 1) * seat, h * HD : (h + 1) * HD]
-                    for h in range(v * group, (v + 1) * group)
+                    rows[
+                        q * seat : (q + 1) * seat,
+                        pl.ds(pl.multiple_of((v * group + e) * HD, HD), HD),
+                    ]
+                    for e in range(group)
                 ],
                 axis=0,
             ).astype(BF)
@@ -264,7 +269,7 @@
             stat = with_lse(lse)
             if heads == 2 and requests == 1:
                 for g in range(group // 2):
-                    dest = (v * group // 2 + g) ^ chip
+                    dest = (v * (group // 2) + g) ^ chip
                     mine = slice(2 * g * seat, 2 * (g + 1) * seat)
                     ready[dest, :depth, :] = mixed[:, mine]
                     ready[dest, depth:, :] = stat[:, mine]
@@ -272,16 +277,21 @@
                 for e in range(group):
                     mine = slice(e * seat, (e + 1) * seat)
                     head = v * group + e
-                    lo = (head % heads) * count + q * seat
+                    lo = (e % heads) * count + q * seat
                     for part in range(HD // depth):
                         dest = ((head * HD + part * depth) // cols) ^ chip
                         some_rows = slice(part * depth, (part + 1) * depth)
                         ready[dest, :depth, lo : lo + seat] = mixed[some_rows, mine]
                         ready[dest, depth:, lo : lo + seat] = stat[:, mine]
     order = sequence(nz)
+    outs = iter(outs)
     for ky in range(2):
-        for spot, kz in enumerate(order):
-            outs[2 * ky + spot // (nz // 2)][spot % (nz // 2)] = ready[2 * kz + ky]
+        taken = 0 if far else nz // 2
+        for blocks in portions(nz)[:2] if far else portions(nz)[2:]:
+            out = next(outs)
+            for i in range(blocks):
+                out[i] = ready[2 * order[taken + i] + ky]
+            taken = taken + blocks
 
 
 def with_lse(lse):
@@ -289,23 +299,24 @@
     return jnp.concatenate(parts + [jnp.zeros((STAT - 3, lse.shape[1]), F32)], axis=0).astype(BF)
 
 
-def attention(pieces, k_own, v_own, k_oth, v_oth, lengths, chips):
+def attention(pieces, k_own, v_own, k_oth, v_oth, lengths, chips, far):
     nz = len(pieces)
     per = pieces[0].shape[1]
     count = chips * per
     cols = HQ * HD // chips
     heads = max(1, cols // HD)
-    shape = (nz // 2, min(cols, HD) + STAT, heads * count)
-    work = 4 * k_own.size * (HQ // KVH) * 2 * count
-    return pl.pallas_call(
-        functools.partial(attention_kernel, nz),
-        out_shape=[jax.ShapeDtypeStruct(shape, BF)] * 4,
+    shape = (min(cols, HD) + STAT, heads * count)
+    work = 2 * k_own.size * (HQ // KVH) * 2 * count
+    parts = portions(nz)[:2] if far else portions(nz)[2:]
+    return pl.pallas_call(
+        functools.partial(attention_kernel, nz, far),
+        out_shape=[jax.ShapeDtypeStruct((blocks,) + shape, BF) for blocks in parts] * 2,
         in_specs=[pl.BlockSpec(memory_space=pltpu.SMEM)]
         + [pl.BlockSpec(memory_space=pltpu.VMEM)] * (nz + 4),
-        out_specs=[pl.BlockSpec(memory_space=pltpu.VMEM)] * 4,
+        out_specs=[pl.BlockSpec(memory_space=pltpu.VMEM)] * (2 * len(parts)),
         scratch_shapes=[
             pltpu.VMEM((count, HQ * HD), F32),
-            pltpu.VMEM((chips,) + shape[1:], BF),
+            pltpu.VMEM((chips,) + shape, BF),
         ],
         cost_estimate=pl.CostEstimate(
             flops=work, bytes_accessed=8 * k_own.size, transcendentals=work // (4 * HD)
@@ -584,14 +595,16 @@
     )
     res_oth = hop(res_own, 1, width)
 
-    near_a, near_b, far_a, far_b = attention(
-        pieces, k_own, v_own, k_oth, v_oth, lengths, chips
-    )
-    far_a = hop(far_a, 2, width)
-    far_b = hop(far_b, 2, width)
-    first = fold(near_a, far_a)
-    second = fold(near_b, far_b)
-    blocks = along_z(by_distance(first + second))
+    asked = (pieces, k_own, v_own, k_oth, v_oth, lengths, chips)
+    one, two, send_one, send_two = attention(*asked, 1)
+    three, send_three = attention(*asked, 0)
+    count = len(portions(nz))
+    fars, blocks = [], []
+    for send in (send_one, send_two, send_three):
+        fars.append(hop(send, 2, width))
+    for i, near in enumerate((one, two, three)):
+        blocks += fold(near, fars[i])
+    blocks = along_z(by_distance(blocks))
     *parts, mixed = project(blocks, w_own, w_oth, res_own, res_oth, home)
     chunk = add(*along_z(parts))
     (up,) = fetch(gate_up)
@@ -603,7 +616,6 @@
     *halves, stream = experts(
         mine, theirs, gain, up, down, turn, fill, mixed, width, cap
     )
-    count = len(portions(nz))
     keep, *keeps = halves[: count + 1]
     send, *sends = halves[count + 1 :]
     gots, fars, blocks = [], [], []

time: 82.4 us -> 82.8 us (level)
    ppermute x34 -> x35, waiting for transfers between devices: 31.4 us -> 32.2 us  [hop(): return lax.ppermute(x, 'ctx', [(i, i ^ mask) for i in range(width)])]
    ppermute x34 -> x35, starting transfers between devices: 35.3 us -> 34.7 us  [hop(): return lax.ppermute(x, 'ctx', [(i, i ^ mask) for i in range(width)])]
    pallas_call x1 -> x2, Pallas kernels: 2.21 us -> 2.32 us  [attention(): pl.pallas_call(functools.partial(attention_kernel, nz, far), out_shape=[j...]
  transfers between devices with their start and end apart: 34 -> 35, of which waited for: 18 -> 18; matrix products, arithmetic and copies ran while one was open for 0% -> 0% of each run, Pallas kernels for 13% -> 13%
where the time goes in v5:
time: 82.8 us; the launch traced here: 82.5 us
  starting transfers between devices  34.7 us (42%)
  waiting for transfers between devices  32.2 us (39%)
  Pallas kernels  14.1 us (17%)
  between operations  1.46 us (2%)
    ppermute x35, starting transfers between devices, hop(): return lax.ppermute(x, 'ctx', [(i, i ^ mask) for i in range(width)])  34.7 us
    ppermute x35, waiting for transfers between devices, hop(): return lax.ppermute(x, 'ctx', [(i, i ^ mask) for i in range(width)])  32.2 us
    pallas_call x3, Pallas kernels, fetch(): pl.pallas_call(functools.partial(fetch_kernel, count), out_shape=[pltpu.V...  5.77 us
    pallas_call x1, Pallas kernels, experts(): pl.pallas_call(functools.partial(expert_kernel, nz, width), out_shape=sha...  2.45 us
    pallas_call x2, Pallas kernels, attention(): pl.pallas_call(functools.partial(attention_kernel, nz, far), out_shape=[j...  2.32 us
    pallas_call x1, Pallas kernels, prepare(): pl.pallas_call(functools.partial(prepare_kernel, per, width), out_shape=[...  1.98 us
  transfers between devices with their start and end apart: 35, of which 18 were waited for; matrix products, arithmetic and copies ran while one was open for 0% of the time, Pallas kernels for 13%

profile of v5, /device:TPU:0, one launch (start us, length us, event | category | flops | bytes accessed | tf_op | source)
XLA Modules:
  0.0 82.5 jit_solution(1365335880249326461)
XLA Ops:
  1.7 2.6 %collective-permute-start = (bf16[8,2048]{1,0:T(8,128)(2,1)}, bf16[8,2048]{1,0:T(8,128)(2,1)S(1)}, u32[]{:S(2)}, u32[]{:S(2)}) collective-permute-start(bf16[8,2048]{1,0:T(8,128)(2,1)} %refs_0_.3), channel_id=1, source_target_pairs={{0,2},{1,3},{2,0},{3,1},{4,6},{5,7},{6,4},{7,5},{8,10},{9,11},{10,... | collective-permute-start | bytes 98312 | tf_op jit(solution)/shard_map/ppermute | solution.py:39
  4.3 1.1 %fetch.3 = (bf16[8,2048]{1,0:T(8,128)(2,1)S(1)}, bf16[1,512,256]{2,1,0:T(8,128)(2,1)S(1)}, bf16[1,512,256]{2,1,0:T(8,128)(2,1)S(1)}) custom-call(bf16[8,2048]{1,0:T(8,128)(2,1)} %refs_0_.3, bf16[1,512,256]{2,1,0:T(8,128)(2,1)} %refs_1_.1, bf16[1,512,256]{2,1,0:T(8,128)(2,1)} %refs_2_.1), custom_call_target="tpu_custom_call" | custom-call | bytes 1114112 | tf_op jit(solution)/shard_map/fetch/pallas_call | solution.py:80
  5.4 1.1 %collective-permute-done.second = bf16[8,2048]{1,0:T(8,128)(2,1)S(1)} collective-permute-done((bf16[8,2048]{1,0:T(8,128)(2,1)}, bf16[8,2048]{1,0:T(8,128)(2,1)S(1)}, u32[]{:S(2)}, u32[]{:S(2)}) %collective-permute-start) | collective-permute-done | bytes 32800 | tf_op jit(solution)/shard_map/ppermute | solution.py:39
  6.5 4.0 %collective-permute-start.3 = (bf16[2,8,2048]{2,1,0:T(8,128)(2,1)S(1)}, bf16[2,8,2048]{2,1,0:T(8,128)(2,1)S(1)}, u32[]{:S(2)}, u32[]{:S(2)}) collective-permute-start(bf16[2,8,2048]{2,1,0:T(8,128)(2,1)S(1)} %shard_map.140.refs_0_), channel_id=1, source_target_pairs={{0,12},{1,13},{2,14},{3,15},{4,8},{5,9},{6,10},{7,11},{8,4},{9,5},... | collective-permute-start | bytes 196616 | tf_op jit(solution)/shard_map/ppermute | solution.py:39
  10.5 3.0 %collective-permute-done.3.refs_3_ = bf16[2,8,2048]{2,1,0:T(8,128)(2,1)S(1)} collective-permute-done((bf16[2,8,2048]{2,1,0:T(8,128)(2,1)S(1)}, bf16[2,8,2048]{2,1,0:T(8,128)(2,1)S(1)}, u32[]{:S(2)}, u32[]{:S(2)}) %collective-permute-start.3) | collective-permute-done | bytes 65568 | tf_op jit(solution)/shard_map/ppermute | solution.py:39
  15.7 2.1 %collective-permute-done.1.refs_1_ = bf16[2,8,2048]{2,1,0:T(8,128)(2,1)S(1)} collective-permute-done((bf16[2,8,2048]{2,1,0:T(8,128)(2,1)S(1)}, bf16[2,8,2048]{2,1,0:T(8,128)(2,1)S(1)}, u32[]{:S(2)}, u32[]{:S(2)}) %collective-permute-start.1) | collective-permute-done | bytes 65568 | tf_op jit(solution)/shard_map/ppermute | solution.py:39
  17.8 1.2 %attention.2 = (bf16[2,136,128]{2,1,0:T(8,128)(2,1)S(1)}, bf16[2,136,128]{2,1,0:T(8,128)(2,1)S(1)}) custom-call(s32[1]{0:T(128)S(6)} %copy.15.lengths, bf16[2,8,2048]{2,1,0:T(8,128)(2,1)S(1)} %shard_map.140.refs_0_, bf16[2,8,2048]{2,1,0:T(8,128)(2,1)S(1)} %collective-permute-done.1.refs_1_, bf16[2,8,2048]{2,1,0:T(8,128)(2,1)S(1)} %collective-permute-done.2.refs_2_, ...), custom_call_target="tpu_custom_call" | custom-call | flops 268435456 | bytes 1048576 | tf_op jit(solution)/shard_map/attention/pallas_call | solution.py:311
  18.9 1.6 %collective-permute-start.6 = (bf16[2,136,128]{2,1,0:T(8,128)(2,1)S(1)}, bf16[2,136,128]{2,1,0:T(8,128)(2,1)S(1)}, u32[]{:S(2)}, u32[]{:S(2)}) collective-permute-start(bf16[2,136,128]{2,1,0:T(8,128)(2,1)S(1)} %get-tuple-element.39), channel_id=1, source_target_pairs={{0,2},{1,3},{2,0},{3,1},{4,6},{5,7},{6,4},{7,5},{8,10},{9,11},{10,... | collective-permute-start | bytes 208904 | tf_op jit(solution)/shard_map/ppermute | solution.py:39
  20.5 1.2 %attention.3 = (bf16[1,136,128]{2,1,0:T(8,128)(2,1)S(1)}, bf16[1,136,128]{2,1,0:T(8,128)(2,1)S(1)}, bf16[1,136,128]{2,1,0:T(8,128)(2,1)S(1)}, bf16[1,136,128]{2,1,0:T(8,128)(2,1)S(1)}) custom-call(s32[1]{0:T(128)S(6)} %copy.15.lengths, bf16[2,8,2048]{2,1,0:T(8,128)(2,1)S(1)} %shard_map.140.refs_0_, bf16[2,8,2048]{2,1,0:T(8,128)(2,1)S(1)} %collective-permute-done.1.refs_1_, ...), custom_call_target="tpu_custom_call" | custom-call | flops 268435456 | bytes 1048576 | tf_op jit(solution)/shard_map/attention/pallas_call | solution.py:311
  22.3 1.5 %collective-permute-start.10 = (bf16[1,136,128]{2,1,0:T(8,128)(2,1)S(1)}, bf16[1,136,128]{2,1,0:T(8,128)(2,1)S(1)}, u32[]{:S(2)}, u32[]{:S(2)}) collective-permute-start(bf16[1,136,128]{2,1,0:T(8,128)(2,1)S(1)} %get-tuple-element.45), channel_id=1, source_target_pairs={{0,2},{1,3},{2,0},{3,1},{4,6},{5,7},{6,4},{7,5},{8,10},{9,11},{10,... | collective-permute-start | bytes 104456 | tf_op jit(solution)/shard_map/ppermute | solution.py:39
  23.8 2.0 %prepare.1 = (bf16[16,2176]{1,0:T(8,128)(2,1)S(1)}, bf16[64,32]{1,0:T(8,128)(2,1)S(1)}, bf16[256,64]{1,0:T(8,128)(2,1)S(1)}, bf16[256,128]{1,0:T(8,128)(2,1)S(1)...) custom-call(s32[1,16]{1,0:T(1,128)} %bitcast.8, s32[1,128]{1,0:T(1,128)} %bitcast.9, s32[8,16]{1,0:T(8,128)} %bitcast.6, ...), custom_call_target="tpu_custom_call" | custom-call | flops 12582912 | bytes 131072 | tf_op jit(solution)/shard_map/prepare/pallas_call | solution.py:160
  25.9 2.4 %collective-permute-start.9 = (bf16[136,128]{1,0:T(8,128)(2,1)S(1)}, bf16[136,128]{1,0:T(8,128)(2,1)S(1)}, u32[]{:S(2)}, u32[]{:S(2)}) collective-permute-start(bf16[136,128]{1,0:T(8,128)(2,1)S(1)} %fold.4), channel_id=1, source_target_pairs={{0,8},{1,9},{2,10},{3,11},{4,12},{5,13},{6,14},{7,15},{8,0},{9,1},... | collective-permute-start | bytes 104456 | tf_op jit(solution)/shard_map/ppermute | solution.py:39
  28.3 1.7 %collective-permute-start.11 = (bf16[136,128]{1,0:T(8,128)(2,1)S(1)}, bf16[136,128]{1,0:T(8,128)(2,1)S(1)}, u32[]{:S(2)}, u32[]{:S(2)}) collective-permute-start(bf16[136,128]{1,0:T(8,128)(2,1)S(1)} %fold.5), channel_id=1, source_target_pairs={{0,12},{1,13},{2,14},{3,15},{4,8},{5,9},{6,10},{7,11},{8,4},{9,5},... | collective-permute-start | bytes 104456 | tf_op jit(solution)/shard_map/ppermute | solution.py:39
  30.8 3.5 %collective-permute-done.11.refs_3_ = bf16[136,128]{1,0:T(8,128)(2,1)S(1)} collective-permute-done((bf16[136,128]{1,0:T(8,128)(2,1)S(1)}, bf16[136,128]{1,0:T(8,128)(2,1)S(1)}, u32[]{:S(2)}, u32[]{:S(2)}) %collective-permute-start.11) | collective-permute-done | bytes 34848 | tf_op jit(solution)/shard_map/ppermute | solution.py:39
  35.1 2.4 %collective-permute-start.15 = (bf16[16,2176]{1,0:T(8,128)(2,1)S(1)}, bf16[16,2176]{1,0:T(8,128)(2,1)S(1)}, u32[]{:S(2)}, u32[]{:S(2)}) collective-permute-start(bf16[16,2176]{1,0:T(8,128)(2,1)S(1)} %get-tuple-element.51), channel_id=1, source_target_pairs={{0,8},{1,9},{2,10},{3,11},{4,12},{5,13},{6,14},{7,15},{8,0},{9,1},... | collective-permute-start | bytes 208904 | tf_op jit(solution)/shard_map/ppermute | solution.py:39
  37.5 1.9 %collective-permute-start.16 = (bf16[16,2176]{1,0:T(8,128)(2,1)S(1)}, bf16[16,2176]{1,0:T(8,128)(2,1)S(1)}, u32[]{:S(2)}, u32[]{:S(2)}) collective-permute-start(bf16[16,2176]{1,0:T(8,128)(2,1)S(1)} %get-tuple-element.52), channel_id=1, source_target_pairs={{0,12},{1,13},{2,14},{3,15},{4,8},{5,9},{6,10},{7,11},{8,4},{9,5},... | collective-permute-start | bytes 208904 | tf_op jit(solution)/shard_map/ppermute | solution.py:39
  39.4 3.2 %collective-permute-done.15.refs_2_ = bf16[16,2176]{1,0:T(8,128)(2,1)S(1)} collective-permute-done((bf16[16,2176]{1,0:T(8,128)(2,1)S(1)}, bf16[16,2176]{1,0:T(8,128)(2,1)S(1)}, u32[]{:S(2)}, u32[]{:S(2)}) %collective-permute-start.15) | collective-permute-done | bytes 69664 | tf_op jit(solution)/shard_map/ppermute | solution.py:39
  43.7 1.1 %collective-permute-start.17 = (bf16[16,2176]{1,0:T(8,128)(2,1)S(1)}, bf16[16,2176]{1,0:T(8,128)(2,1)S(1)}, u32[]{:S(2)}, u32[]{:S(2)}) collective-permute-start(bf16[16,2176]{1,0:T(8,128)(2,1)S(1)} %shard_map.141.refs_0_), channel_id=1, source_target_pairs={{0,2},{1,3},{2,0},{3,1},{4,6},{5,7},{6,4},{7,5},{8,10},{9,11},{10,... | collective-permute-start | bytes 208904 | tf_op jit(solution)/shard_map/ppermute | solution.py:39
  44.7 3.3 %collective-permute-done.17.refs_1_ = bf16[16,2176]{1,0:T(8,128)(2,1)S(1)} collective-permute-done((bf16[16,2176]{1,0:T(8,128)(2,1)S(1)}, bf16[16,2176]{1,0:T(8,128)(2,1)S(1)}, u32[]{:S(2)}, u32[]{:S(2)}) %collective-permute-start.17) | collective-permute-done | bytes 69664 | tf_op jit(solution)/shard_map/ppermute | solution.py:39
  48.1 2.2 %collective-permute-start.20 = (bf16[16,2176]{1,0:T(8,128)(2,1)S(1)}, bf16[16,2176]{1,0:T(8,128)(2,1)S(1)}, u32[]{:S(2)}, u32[]{:S(2)}) collective-permute-start(bf16[16,2176]{1,0:T(8,128)(2,1)S(1)} %shard_map.142.refs_0_), channel_id=1, source_target_pairs={{0,12},{1,13},{2,14},{3,15},{4,8},{5,9},{6,10},{7,11},{8,4},{9,5},... | collective-permute-start | bytes 208904 | tf_op jit(solution)/shard_map/ppermute | solution.py:39
  50.7 1.9 %collective-permute-start.18 = (bf16[16,2176]{1,0:T(8,128)(2,1)S(1)}, bf16[16,2176]{1,0:T(8,128)(2,1)S(1)}, u32[]{:S(2)}, u32[]{:S(2)}) collective-permute-start(bf16[16,2176]{1,0:T(8,128)(2,1)S(1)} %shard_map.142.refs_0_), channel_id=1, source_target_pairs={{0,4},{1,5},{2,6},{3,7},{4,0},{5,1},{6,2},{7,3},{8,12},{9,13},{10,... | collective-permute-start | bytes 208904 | tf_op jit(solution)/shard_map/ppermute | solution.py:39
  52.5 1.7 %collective-permute-done.20.refs_3_ = bf16[16,2176]{1,0:T(8,128)(2,1)S(1)} collective-permute-done((bf16[16,2176]{1,0:T(8,128)(2,1)S(1)}, bf16[16,2176]{1,0:T(8,128)(2,1)S(1)}, u32[]{:S(2)}, u32[]{:S(2)}) %collective-permute-start.20) | collective-permute-done | bytes 69664 | tf_op jit(solution)/shard_map/ppermute | solution.py:39
  54.3 1.8 %collective-permute-done.19.refs_2_ = bf16[16,2176]{1,0:T(8,128)(2,1)S(1)} collective-permute-done((bf16[16,2176]{1,0:T(8,128)(2,1)S(1)}, bf16[16,2176]{1,0:T(8,128)(2,1)S(1)}, u32[]{:S(2)}, u32[]{:S(2)}) %collective-permute-start.19) | collective-permute-done | bytes 69664 | tf_op jit(solution)/shard_map/ppermute | solution.py:39
  56.6 1.9 %fetch.5.refs_10_ = bf16[1,768,2048]{2,1,0:T(8,128)(2,1)S(1)} custom-call(bf16[1,768,2048]{2,1,0:T(8,128)(2,1)} %refs_0_.5), custom_call_target="tpu_custom_call" | custom-call | bytes 6291456 | tf_op jit(solution)/shard_map/fetch/pallas_call | solution.py:80
  58.5 2.8 %fetch.4.refs_9_ = bf16[1,2048,1536]{2,1,0:T(8,128)(2,1)S(1)} custom-call(bf16[1,2048,1536]{2,1,0:T(8,128)(2,1)} %refs_0_.4), custom_call_target="tpu_custom_call" | custom-call | bytes 12582912 | tf_op jit(solution)/shard_map/fetch/pallas_call | solution.py:80
  61.3 2.5 %experts.1 = (bf16[64,2304]{1,0:T(8,128)(2,1)S(1)}, bf16[16,2304]{1,0:T(8,128)(2,1)S(1)}, bf16[16,2304]{1,0:T(8,128)(2,1)S(1)}, bf16[32,2304]{1,0:T(8,128)(2,1)S...) custom-call(bf16[16,2176]{1,0:T(8,128)(2,1)S(1)} %shard_map.142.refs, ...), custom_call_target="tpu_custom_call" | custom-call | flops 1207959552 | bytes 9437184 | tf_op jit(solution)/shard_map/experts/pallas_call | solution.py:458
  67.3 1.4 %collective-permute-start.30 = (bf16[16,2304]{1,0:T(8,128)(2,1)S(1)}, bf16[16,2304]{1,0:T(8,128)(2,1)S(1)}, u32[]{:S(2)}, u32[]{:S(2)}) collective-permute-start(bf16[16,2304]{1,0:T(8,128)(2,1)S(1)} %shard_map.144), channel_id=1, source_target_pairs={{0,2},{1,3},{2,0},{3,1},{4,6},{5,7},{6,4},{7,5},{8,10},{9,11},{10,... | collective-permute-start | bytes 221192 | tf_op jit(solution)/shard_map/ppermute | solution.py:39
  69.5 2.6 %collective-permute-done.27.far = bf16[32,2304]{1,0:T(8,128)(2,1)S(1)} collective-permute-done((bf16[32,2304]{1,0:T(8,128)(2,1)S(1)}, bf16[32,2304]{1,0:T(8,128)(2,1)S(1)}, u32[]{:S(2)}, u32[]{:S(2)}) %collective-permute-start.27) | collective-permute-done | bytes 147488 | tf_op jit(solution)/shard_map/ppermute | solution.py:39
  72.6 1.0 %collective-permute-done.30.far = bf16[16,2304]{1,0:T(8,128)(2,1)S(1)} collective-permute-done((bf16[16,2304]{1,0:T(8,128)(2,1)S(1)}, bf16[16,2304]{1,0:T(8,128)(2,1)S(1)}, u32[]{:S(2)}, u32[]{:S(2)}) %collective-permute-start.30) | collective-permute-done | bytes 73760 | tf_op jit(solution)/shard_map/ppermute | solution.py:39
  73.6 1.2 %collective-permute-start.31 = (bf16[16,2560]{1,0:T(8,128)(2,1)S(1)}, bf16[16,2560]{1,0:T(8,128)(2,1)S(1)}, u32[]{:S(2)}, u32[]{:S(2)}) collective-permute-start(bf16[16,2560]{1,0:T(8,128)(2,1)S(1)} %mix.4), channel_id=1, source_target_pairs={{0,8},{1,9},{2,10},{3,11},{4,12},{5,13},{6,14},{7,15},{8,0},{9,1},... | collective-permute-start | bytes 245768 | tf_op jit(solution)/shard_map/ppermute | solution.py:39
  74.8 1.9 %collective-permute-start.34 = (bf16[16,2560]{1,0:T(8,128)(2,1)S(1)}, bf16[16,2560]{1,0:T(8,128)(2,1)S(1)}, u32[]{:S(2)}, u32[]{:S(2)}) collective-permute-start(bf16[16,2560]{1,0:T(8,128)(2,1)S(1)} %mix.5), channel_id=1, source_target_pairs={{0,12},{1,13},{2,14},{3,15},{4,8},{5,9},{6,10},{7,11},{8,4},{9,5},... | collective-permute-start | bytes 245768 | tf_op jit(solution)/shard_map/ppermute | solution.py:39
  77.4 4.4 %collective-permute-done.31.refs_2_ = bf16[16,2560]{1,0:T(8,128)(2,1)S(1)} collective-permute-done((bf16[16,2560]{1,0:T(8,128)(2,1)S(1)}, bf16[16,2560]{1,0:T(8,128)(2,1)S(1)}, u32[]{:S(2)}, u32[]{:S(2)}) %collective-permute-start.31) | collective-permute-done | bytes 81952 | tf_op jit(solution)/shard_map/ppermute | solution.py:39
  (59 shorter events, 13.2 us)
Async XLA Ops:
  0.6 33.8 %collective-permute-start.12 = (bf16[128,2048]{1,0:T(8,128)(2,1)}, bf16[128,2048]{1,0:T(8,128)(2,1)S(1)}, u32[]{:S(2)}, u32[]{:S(2)}) collective-permute-start(bf16[128,2048]{1,0:T(8,128)(2,1)} %refs_5_.1), channel_id=1, source_target_pairs={{0,1},{1,0},{2,3},{3,2},{4,5},{5,4},{6,7},{7,6},{8,9},{9,8},{10,11... | collective-permute-start | bytes 1572872 | tf_op jit(solution)/shard_map/ppermute | solution.py:39
  1.2 16.6 %collective-permute-start.4 = (bf16[1,512,256]{2,1,0:T(8,128)(2,1)}, bf16[1,512,256]{2,1,0:T(8,128)(2,1)S(1)}, u32[]{:S(2)}, u32[]{:S(2)}) collective-permute-start(bf16[1,512,256]{2,1,0:T(8,128)(2,1)} %refs_1_.1), channel_id=1, source_target_pairs={{0,1},{1,0},{2,3},{3,2},{4,5},{5,4},{6,7},{7,6},{8,9},{9,8},{10,11... | collective-permute-start | bytes 786440 | tf_op jit(solution)/shard_map/ppermute | solution.py:39
  1.3 16.5 %collective-permute-start.5 = (bf16[1,512,256]{2,1,0:T(8,128)(2,1)}, bf16[1,512,256]{2,1,0:T(8,128)(2,1)S(1)}, u32[]{:S(2)}, u32[]{:S(2)}) collective-permute-start(bf16[1,512,256]{2,1,0:T(8,128)(2,1)} %refs_2_.1), channel_id=1, source_target_pairs={{0,1},{1,0},{2,3},{3,2},{4,5},{5,4},{6,7},{7,6},{8,9},{9,8},{10,11... | collective-permute-start | bytes 786440 | tf_op jit(solution)/shard_map/ppermute | solution.py:39
  1.7 4.8 %collective-permute-start = (bf16[8,2048]{1,0:T(8,128)(2,1)}, bf16[8,2048]{1,0:T(8,128)(2,1)S(1)}, u32[]{:S(2)}, u32[]{:S(2)}) collective-permute-start(bf16[8,2048]{1,0:T(8,128)(2,1)} %refs_0_.3), channel_id=1, source_target_pairs={{0,2},{1,3},{2,0},{3,1},{4,6},{5,7},{6,4},{7,5},{8,10},{9,11},{10,... | collective-permute-start | bytes 98312 | tf_op jit(solution)/shard_map/ppermute | solution.py:39
  6.5 7.0 %collective-permute-start.3 = (bf16[2,8,2048]{2,1,0:T(8,128)(2,1)S(1)}, bf16[2,8,2048]{2,1,0:T(8,128)(2,1)S(1)}, u32[]{:S(2)}, u32[]{:S(2)}) collective-permute-start(bf16[2,8,2048]{2,1,0:T(8,128)(2,1)S(1)} %shard_map.140.refs_0_), channel_id=1, source_target_pairs={{0,12},{1,13},{2,14},{3,15},{4,8},{5,9},{6,10},{7,11},{8,4},{9,5},... | collective-permute-start | bytes 196616 | tf_op jit(solution)/shard_map/ppermute | solution.py:39
  10.5 5.2 %collective-permute-start.2 = (bf16[2,8,2048]{2,1,0:T(8,128)(2,1)S(1)}, bf16[2,8,2048]{2,1,0:T(8,128)(2,1)S(1)}, u32[]{:S(2)}, u32[]{:S(2)}) collective-permute-start(bf16[2,8,2048]{2,1,0:T(8,128)(2,1)S(1)} %shard_map.140.refs_0_), channel_id=1, source_target_pairs={{0,8},{1,9},{2,10},{3,11},{4,12},{5,13},{6,14},{7,15},{8,0},{9,1},... | collective-permute-start | bytes 196616 | tf_op jit(solution)/shard_map/ppermute | solution.py:39
  13.5 4.3 %collective-permute-start.1 = (bf16[2,8,2048]{2,1,0:T(8,128)(2,1)S(1)}, bf16[2,8,2048]{2,1,0:T(8,128)(2,1)S(1)}, u32[]{:S(2)}, u32[]{:S(2)}) collective-permute-start(bf16[2,8,2048]{2,1,0:T(8,128)(2,1)S(1)} %shard_map.140.refs_0_), channel_id=1, source_target_pairs={{0,4},{1,5},{2,6},{3,7},{4,0},{5,1},{6,2},{7,3},{8,12},{9,13},{10,... | collective-permute-start | bytes 196616 | tf_op jit(solution)/shard_map/ppermute | solution.py:39
  18.9 11.1 %collective-permute-start.6 = (bf16[2,136,128]{2,1,0:T(8,128)(2,1)S(1)}, bf16[2,136,128]{2,1,0:T(8,128)(2,1)S(1)}, u32[]{:S(2)}, u32[]{:S(2)}) collective-permute-start(bf16[2,136,128]{2,1,0:T(8,128)(2,1)S(1)} %get-tuple-element.39), channel_id=1, source_target_pairs={{0,2},{1,3},{2,0},{3,1},{4,6},{5,7},{6,4},{7,5},{8,10},{9,11},{10,... | collective-permute-start | bytes 208904 | tf_op jit(solution)/shard_map/ppermute | solution.py:39
  21.7 4.2 %collective-permute-start.8 = (bf16[1,136,128]{2,1,0:T(8,128)(2,1)S(1)}, bf16[1,136,128]{2,1,0:T(8,128)(2,1)S(1)}, u32[]{:S(2)}, u32[]{:S(2)}) collective-permute-start(bf16[1,136,128]{2,1,0:T(8,128)(2,1)S(1)} %get-tuple-element.43), channel_id=1, source_target_pairs={{0,2},{1,3},{2,0},{3,1},{4,6},{5,7},{6,4},{7,5},{8,10},{9,11},{10,... | collective-permute-start | bytes 104456 | tf_op jit(solution)/shard_map/ppermute | solution.py:39
  22.3 6.0 %collective-permute-start.10 = (bf16[1,136,128]{2,1,0:T(8,128)(2,1)S(1)}, bf16[1,136,128]{2,1,0:T(8,128)(2,1)S(1)}, u32[]{:S(2)}, u32[]{:S(2)}) collective-permute-start(bf16[1,136,128]{2,1,0:T(8,128)(2,1)S(1)} %get-tuple-element.45), channel_id=1, source_target_pairs={{0,2},{1,3},{2,0},{3,1},{4,6},{5,7},{6,4},{7,5},{8,10},{9,11},{10,... | collective-permute-start | bytes 104456 | tf_op jit(solution)/shard_map/ppermute | solution.py:39
  25.8 4.8 %collective-permute-start.13 = (bf16[16,2176]{1,0:T(8,128)(2,1)S(1)}, bf16[16,2176]{1,0:T(8,128)(2,1)S(1)}, u32[]{:S(2)}, u32[]{:S(2)}) collective-permute-start(bf16[16,2176]{1,0:T(8,128)(2,1)S(1)} %get-tuple-element.47.refs_6_), channel_id=1, source_target_pairs={{0,1},{1,0},{2,3},{3,2},{4,5},{5,4},{6,7},{7,6},{8,9},{9,8},{10,11... | collective-permute-start | bytes 208904 | tf_op jit(solution)/shard_map/ppermute | solution.py:39
  25.9 4.9 %collective-permute-start.9 = (bf16[136,128]{1,0:T(8,128)(2,1)S(1)}, bf16[136,128]{1,0:T(8,128)(2,1)S(1)}, u32[]{:S(2)}, u32[]{:S(2)}) collective-permute-start(bf16[136,128]{1,0:T(8,128)(2,1)S(1)} %fold.4), channel_id=1, source_target_pairs={{0,8},{1,9},{2,10},{3,11},{4,12},{5,13},{6,14},{7,15},{8,0},{9,1},... | collective-permute-start | bytes 104456 | tf_op jit(solution)/shard_map/ppermute | solution.py:39
  28.3 6.0 %collective-permute-start.11 = (bf16[136,128]{1,0:T(8,128)(2,1)S(1)}, bf16[136,128]{1,0:T(8,128)(2,1)S(1)}, u32[]{:S(2)}, u32[]{:S(2)}) collective-permute-start(bf16[136,128]{1,0:T(8,128)(2,1)S(1)} %fold.5), channel_id=1, source_target_pairs={{0,12},{1,13},{2,14},{3,15},{4,8},{5,9},{6,10},{7,11},{8,4},{9,5},... | collective-permute-start | bytes 104456 | tf_op jit(solution)/shard_map/ppermute | solution.py:39
  30.1 4.4 %collective-permute-start.7 = (bf16[136,128]{1,0:T(8,128)(2,1)S(1)}, bf16[136,128]{1,0:T(8,128)(2,1)S(1)}, u32[]{:S(2)}, u32[]{:S(2)}) collective-permute-start(bf16[136,128]{1,0:T(8,128)(2,1)S(1)} %get-tuple-element.41), channel_id=1, source_target_pairs={{0,4},{1,5},{2,6},{3,7},{4,0},{5,1},{6,2},{7,3},{8,12},{9,13},{10,... | collective-permute-start | bytes 104456 | tf_op jit(solution)/shard_map/ppermute | solution.py:39
  35.0 4.5 %collective-permute-start.14 = (bf16[16,2176]{1,0:T(8,128)(2,1)S(1)}, bf16[16,2176]{1,0:T(8,128)(2,1)S(1)}, u32[]{:S(2)}, u32[]{:S(2)}) collective-permute-start(bf16[16,2176]{1,0:T(8,128)(2,1)S(1)} %get-tuple-element.50), channel_id=1, source_target_pairs={{0,4},{1,5},{2,6},{3,7},{4,0},{5,1},{6,2},{7,3},{8,12},{9,13},{10,... | collective-permute-start | bytes 208904 | tf_op jit(solution)/shard_map/ppermute | solution.py:39
  35.1 7.5 %collective-permute-start.15 = (bf16[16,2176]{1,0:T(8,128)(2,1)S(1)}, bf16[16,2176]{1,0:T(8,128)(2,1)S(1)}, u32[]{:S(2)}, u32[]{:S(2)}) collective-permute-start(bf16[16,2176]{1,0:T(8,128)(2,1)S(1)} %get-tuple-element.51), channel_id=1, source_target_pairs={{0,8},{1,9},{2,10},{3,11},{4,12},{5,13},{6,14},{7,15},{8,0},{9,1},... | collective-permute-start | bytes 208904 | tf_op jit(solution)/shard_map/ppermute | solution.py:39
  37.5 6.1 %collective-permute-start.16 = (bf16[16,2176]{1,0:T(8,128)(2,1)S(1)}, bf16[16,2176]{1,0:T(8,128)(2,1)S(1)}, u32[]{:S(2)}, u32[]{:S(2)}) collective-permute-start(bf16[16,2176]{1,0:T(8,128)(2,1)S(1)} %get-tuple-element.52), channel_id=1, source_target_pairs={{0,12},{1,13},{2,14},{3,15},{4,8},{5,9},{6,10},{7,11},{8,4},{9,5},... | collective-permute-start | bytes 208904 | tf_op jit(solution)/shard_map/ppermute | solution.py:39
  43.7 4.4 %collective-permute-start.17 = (bf16[16,2176]{1,0:T(8,128)(2,1)S(1)}, bf16[16,2176]{1,0:T(8,128)(2,1)S(1)}, u32[]{:S(2)}, u32[]{:S(2)}) collective-permute-start(bf16[16,2176]{1,0:T(8,128)(2,1)S(1)} %shard_map.141.refs_0_), channel_id=1, source_target_pairs={{0,2},{1,3},{2,0},{3,1},{4,6},{5,7},{6,4},{7,5},{8,10},{9,11},{10,... | collective-permute-start | bytes 208904 | tf_op jit(solution)/shard_map/ppermute | solution.py:39
  48.1 6.2 %collective-permute-start.20 = (bf16[16,2176]{1,0:T(8,128)(2,1)S(1)}, bf16[16,2176]{1,0:T(8,128)(2,1)S(1)}, u32[]{:S(2)}, u32[]{:S(2)}) collective-permute-start(bf16[16,2176]{1,0:T(8,128)(2,1)S(1)} %shard_map.142.refs_0_), channel_id=1, source_target_pairs={{0,12},{1,13},{2,14},{3,15},{4,8},{5,9},{6,10},{7,11},{8,4},{9,5},... | collective-permute-start | bytes 208904 | tf_op jit(solution)/shard_map/ppermute | solution.py:39
  50.3 5.8 %collective-permute-start.19 = (bf16[16,2176]{1,0:T(8,128)(2,1)S(1)}, bf16[16,2176]{1,0:T(8,128)(2,1)S(1)}, u32[]{:S(2)}, u32[]{:S(2)}) collective-permute-start(bf16[16,2176]{1,0:T(8,128)(2,1)S(1)} %shard_map.142.refs_0_), channel_id=1, source_target_pairs={{0,8},{1,9},{2,10},{3,11},{4,12},{5,13},{6,14},{7,15},{8,0},{9,1},... | collective-permute-start | bytes 208904 | tf_op jit(solution)/shard_map/ppermute | solution.py:39
  50.7 5.4 %collective-permute-start.18 = (bf16[16,2176]{1,0:T(8,128)(2,1)S(1)}, bf16[16,2176]{1,0:T(8,128)(2,1)S(1)}, u32[]{:S(2)}, u32[]{:S(2)}) collective-permute-start(bf16[16,2176]{1,0:T(8,128)(2,1)S(1)} %shard_map.142.refs_0_), channel_id=1, source_target_pairs={{0,4},{1,5},{2,6},{3,7},{4,0},{5,1},{6,2},{7,3},{8,12},{9,13},{10,... | collective-permute-start | bytes 208904 | tf_op jit(solution)/shard_map/ppermute | solution.py:39
  52.5 8.8 %collective-permute-start.21 = (bf16[16,2176]{1,0:T(8,128)(2,1)S(1)}, bf16[16,2176]{1,0:T(8,128)(2,1)S(1)}, u32[]{:S(2)}, u32[]{:S(2)}) collective-permute-start(bf16[16,2176]{1,0:T(8,128)(2,1)S(1)} %shard_map.142.refs_0_), channel_id=1, source_target_pairs={{0,1},{1,0},{2,3},{3,2},{4,5},{5,4},{6,7},{7,6},{8,9},{9,8},{10,11... | collective-permute-start | bytes 208904 | tf_op jit(solution)/shard_map/ppermute | solution.py:39
  54.3 7.1 %collective-permute-start.24 = (bf16[16,2176]{1,0:T(8,128)(2,1)S(1)}, bf16[16,2176]{1,0:T(8,128)(2,1)S(1)}, u32[]{:S(2)}, u32[]{:S(2)}) collective-permute-start(bf16[16,2176]{1,0:T(8,128)(2,1)S(1)} %collective-permute-done.20.refs_3_), channel_id=1, source_target_pairs={{0,1},{1,0},{2,3},{3,2},{4,5},{5,4},{6,7},{7,6},{8,9},{9,8},{10,11... | collective-permute-start | bytes 208904 | tf_op jit(solution)/shard_map/ppermute | solution.py:39
  56.1 5.2 %collective-permute-start.23 = (bf16[16,2176]{1,0:T(8,128)(2,1)S(1)}, bf16[16,2176]{1,0:T(8,128)(2,1)S(1)}, u32[]{:S(2)}, u32[]{:S(2)}) collective-permute-start(bf16[16,2176]{1,0:T(8,128)(2,1)S(1)} %collective-permute-done.19.refs_2_), channel_id=1, source_target_pairs={{0,1},{1,0},{2,3},{3,2},{4,5},{5,4},{6,7},{7,6},{8,9},{9,8},{10,11... | collective-permute-start | bytes 208904 | tf_op jit(solution)/shard_map/ppermute | solution.py:39
  56.1 5.3 %collective-permute-start.22 = (bf16[16,2176]{1,0:T(8,128)(2,1)S(1)}, bf16[16,2176]{1,0:T(8,128)(2,1)S(1)}, u32[]{:S(2)}, u32[]{:S(2)}) collective-permute-start(bf16[16,2176]{1,0:T(8,128)(2,1)S(1)} %collective-permute-done.18.refs_1_), channel_id=1, source_target_pairs={{0,1},{1,0},{2,3},{3,2},{4,5},{5,4},{6,7},{7,6},{8,9},{9,8},{10,11... | collective-permute-start | bytes 208904 | tf_op jit(solution)/shard_map/ppermute | solution.py:39
  63.9 8.2 %collective-permute-start.25 = (bf16[64,2304]{1,0:T(8,128)(2,1)S(1)}, bf16[64,2304]{1,0:T(8,128)(2,1)S(1)}, u32[]{:S(2)}, u32[]{:S(2)}) collective-permute-start(bf16[64,2304]{1,0:T(8,128)(2,1)S(1)} %get-tuple-element.59), channel_id=1, source_target_pairs={{0,1},{1,0},{2,3},{3,2},{4,5},{5,4},{6,7},{7,6},{8,9},{9,8},{10,11... | collective-permute-start | bytes 884744 | tf_op jit(solution)/shard_map/ppermute | solution.py:39
  65.2 6.8 %collective-permute-start.27 = (bf16[32,2304]{1,0:T(8,128)(2,1)S(1)}, bf16[32,2304]{1,0:T(8,128)(2,1)S(1)}, u32[]{:S(2)}, u32[]{:S(2)}) collective-permute-start(bf16[32,2304]{1,0:T(8,128)(2,1)S(1)} %shard_map.143), channel_id=1, source_target_pairs={{0,2},{1,3},{2,0},{3,1},{4,6},{5,7},{6,4},{7,5},{8,10},{9,11},{10,... | collective-permute-start | bytes 442376 | tf_op jit(solution)/shard_map/ppermute | solution.py:39
  67.3 6.3 %collective-permute-start.30 = (bf16[16,2304]{1,0:T(8,128)(2,1)S(1)}, bf16[16,2304]{1,0:T(8,128)(2,1)S(1)}, u32[]{:S(2)}, u32[]{:S(2)}) collective-permute-start(bf16[16,2304]{1,0:T(8,128)(2,1)S(1)} %shard_map.144), channel_id=1, source_target_pairs={{0,2},{1,3},{2,0},{3,1},{4,6},{5,7},{6,4},{7,5},{8,10},{9,11},{10,... | collective-permute-start | bytes 221192 | tf_op jit(solution)/shard_map/ppermute | solution.py:39
  68.7 6.1 %collective-permute-start.33 = (bf16[16,2304]{1,0:T(8,128)(2,1)S(1)}, bf16[16,2304]{1,0:T(8,128)(2,1)S(1)}, u32[]{:S(2)}, u32[]{:S(2)}) collective-permute-start(bf16[16,2304]{1,0:T(8,128)(2,1)S(1)} %shard_map.145), channel_id=1, source_target_pairs={{0,2},{1,3},{2,0},{3,1},{4,6},{5,7},{6,4},{7,5},{8,10},{9,11},{10,... | collective-permute-start | bytes 221192 | tf_op jit(solution)/shard_map/ppermute | solution.py:39
  72.1 5.3 %collective-permute-start.28 = (bf16[16,2560]{1,0:T(8,128)(2,1)S(1)}, bf16[16,2560]{1,0:T(8,128)(2,1)S(1)}, u32[]{:S(2)}, u32[]{:S(2)}) collective-permute-start(bf16[16,2560]{1,0:T(8,128)(2,1)S(1)} %get-tuple-element.63), channel_id=1, source_target_pairs={{0,4},{1,5},{2,6},{3,7},{4,0},{5,1},{6,2},{7,3},{8,12},{9,13},{10,... | collective-permute-start | bytes 245768 | tf_op jit(solution)/shard_map/ppermute | solution.py:39
  73.6 8.2 %collective-permute-start.31 = (bf16[16,2560]{1,0:T(8,128)(2,1)S(1)}, bf16[16,2560]{1,0:T(8,128)(2,1)S(1)}, u32[]{:S(2)}, u32[]{:S(2)}) collective-permute-start(bf16[16,2560]{1,0:T(8,128)(2,1)S(1)} %mix.4), channel_id=1, source_target_pairs={{0,8},{1,9},{2,10},{3,11},{4,12},{5,13},{6,14},{7,15},{8,0},{9,1},... | collective-permute-start | bytes 245768 | tf_op jit(solution)/shard_map/ppermute | solution.py:39
  74.8 7.0 %collective-permute-start.34 = (bf16[16,2560]{1,0:T(8,128)(2,1)S(1)}, bf16[16,2560]{1,0:T(8,128)(2,1)S(1)}, u32[]{:S(2)}, u32[]{:S(2)}) collective-permute-start(bf16[16,2560]{1,0:T(8,128)(2,1)S(1)} %mix.5), channel_id=1, source_target_pairs={{0,12},{1,13},{2,14},{3,15},{4,8},{5,9},{6,10},{7,11},{8,4},{9,5},... | collective-permute-start | bytes 245768 | tf_op jit(solution)/shard_map/ppermute | solution.py:39
  (3 other events, 5.4 us)

commit v6 on v5

--- a/solution.py
+++ b/solution.py
@@ -414,11 +414,11 @@
 def expert_kernel(nz, width, *refs):
     mine, theirs = refs[:nz], refs[nz : 2 * nz]
     (gain, gate_up, down, turn, fill, mixed) = refs[2 * nz : 2 * nz + 6]
-    *outs, stream_own, x, normed, hidden, scaled = refs[2 * nz + 6 :]
+    *outs, scaled, x, normed, hidden = refs[2 * nz + 6 :]
     device, core, _, z = place()
     block = mine[0].shape[0]
     half = block * nz
-    cap = stream_own.shape[0]
+    cap = fill.shape[0] // width
     for kz in range(nz):
         spot = (z ^ kz) * block
         x[pl.ds(pl.multiple_of(core * half + spot, block), block), :] = mine[kz][...]
@@ -438,13 +438,38 @@
     for lo in range(0, D, tile):
         y = dot(hidden[...], down[0, :, lo : lo + tile], NN).astype(BF)
         scaled[:, lo : lo + tile] = (y.astype(F32) * weight).astype(BF)
-    done = 0
+    done = nz * cap
     for target in outs:
         some = slice(done, done + target.shape[0])
         target[:, :D] = dot(turn[some, :], scaled[...], NN).astype(BF)
         target[:, D:] = dot(fill[some, :], mixed[...], NN).astype(BF)
         done = done + target.shape[0]
-    stream_own[...] = dot(turn[(nz - 1) * cap : nz * cap, :], x[:, :D], NN).astype(BF)
+
+
+def stay_kernel(scaled, x, turn, fill, mixed, keep, stream_own):
+    cap = stream_own.shape[0]
+    size = keep.shape[0]
+    keep[:, :D] = dot(turn[:size, :], scaled[...], NN).astype(BF)
+    keep[:, D:] = dot(fill[:size, :], mixed[...], NN).astype(BF)
+    stream_own[...] = dot(turn[size - cap : size, :], x[:, :D], NN).astype(BF)
+
+
+def stay(scaled, x, turn, fill, mixed, cap):
+    size = turn.shape[0] // 4
+    return pl.pallas_call(
+        stay_kernel,
+        out_shape=[
+            jax.ShapeDtypeStruct((size, D + mixed.shape[1]), BF),
+            jax.ShapeDtypeStruct((cap, D), BF),
+        ],
+        in_specs=[pl.BlockSpec(memory_space=pltpu.VMEM)] * 5,
+        out_specs=[pl.BlockSpec(memory_space=pltpu.VMEM)] * 2,
+        cost_estimate=pl.CostEstimate(
+            flops=2 * size * scaled.size, bytes_accessed=6 * scaled.size, transcendentals=0
+        ),
+        compiler_params=pltpu.CompilerParams(vmem_limit_bytes=16 * MIB),
+        name="stay",
+    )(scaled, x, turn, fill, mixed)
 
 
 def experts(mine, theirs, gain, gate_up, down, turn, fill, mixed, width, cap):
@@ -457,15 +482,12 @@
     ]
     return pl.pallas_call(
         functools.partial(expert_kernel, nz, width),
-        out_shape=shapes * 2 + [jax.ShapeDtypeStruct((cap, D), BF)],
+        out_shape=shapes[1:]
+        + shapes
+        + [jax.ShapeDtypeStruct((total, D), BF), jax.ShapeDtypeStruct((total, wide), BF)],
         in_specs=[pl.BlockSpec(memory_space=pltpu.VMEM)] * (2 * nz + 6),
         out_specs=[pl.BlockSpec(memory_space=pltpu.VMEM)] * (2 * len(shapes) + 1),
-        scratch_shapes=[
-            pltpu.VMEM((total, wide), BF),
-            pltpu.VMEM((total, D), BF),
-            pltpu.VMEM((total, EFF), BF),
-            pltpu.VMEM((total, D), BF),
-        ],
+        scratch_shapes=[pltpu.VMEM((total, D), BF), pltpu.VMEM((total, EFF), BF)],
         cost_estimate=pl.CostEstimate(
             flops=6 * total * D * EFF, bytes_accessed=6 * D * EFF, transcendentals=total * EFF
         ),
@@ -613,11 +635,11 @@
     mine = along_z([chunk] * nz)
     theirs = [hop(x, 1, width) for x in mine]
     (down,) = fetch(expert_down)
-    *halves, stream = experts(
+    *halves, scaled, rows = experts(
         mine, theirs, gain, up, down, turn, fill, mixed, width, cap
     )
-    keep, *keeps = halves[: count + 1]
-    send, *sends = halves[count + 1 :]
+    keeps, (send, *sends) = halves[:count], halves[count:]
+    keep, stream = stay(scaled, rows, turn, fill, mixed, cap)
     gots, fars, blocks = [], [], []
     for i in range(count):
         gots.append(hop(sends[i], 1, width))

time: 82.8 us -> 82.7 us (level)
  no operation moved by 1% of the time
where the time goes in v6:
time: 82.7 us; the launch traced here: 82.4 us
  starting transfers between devices  34.7 us (42%)
  waiting for transfers between devices  31.9 us (39%)
  Pallas kernels  14.3 us (17%)
  between operations  1.47 us (2%)
    ppermute x35, starting transfers between devices, hop(): return lax.ppermute(x, 'ctx', [(i, i ^ mask) for i in range(width)])  34.7 us
    ppermute x35, waiting for transfers between devices, hop(): return lax.ppermute(x, 'ctx', [(i, i ^ mask) for i in range(width)])  31.9 us
    pallas_call x3, Pallas kernels, fetch(): pl.pallas_call(functools.partial(fetch_kernel, count), out_shape=[pltpu.V...  5.77 us
    pallas_call x1, Pallas kernels, experts(): pl.pallas_call(functools.partial(expert_kernel, nz, width), out_shape=sha...  2.33 us
    pallas_call x2, Pallas kernels, attention(): pl.pallas_call(functools.partial(attention_kernel, nz, far), out_shape=[j...  2.32 us
    pallas_call x1, Pallas kernels, prepare(): pl.pallas_call(functools.partial(prepare_kernel, per, width), out_shape=[...  1.98 us
  transfers between devices with their start and end apart: 35, of which 18 were waited for; matrix products, arithmetic and copies ran while one was open for 0% of the time, Pallas kernels for 13%

profile of v6, /device:TPU:0, one launch (start us, length us, event | category | flops | bytes accessed | tf_op | source)
XLA Modules:
  0.0 82.4 jit_solution(1586245402556103839)
XLA Ops:
  1.7 2.6 %collective-permute-start = (bf16[8,2048]{1,0:T(8,128)(2,1)}, bf16[8,2048]{1,0:T(8,128)(2,1)S(1)}, u32[]{:S(2)}, u32[]{:S(2)}) collective-permute-start(bf16[8,2048]{1,0:T(8,128)(2,1)} %refs_0_.3), channel_id=1, source_target_pairs={{0,2},{1,3},{2,0},{3,1},{4,6},{5,7},{6,4},{7,5},{8,10},{9,11},{10,... | collective-permute-start | bytes 98312 | tf_op jit(solution)/shard_map/ppermute | solution.py:39
  4.3 1.1 %fetch.3 = (bf16[8,2048]{1,0:T(8,128)(2,1)S(1)}, bf16[1,512,256]{2,1,0:T(8,128)(2,1)S(1)}, bf16[1,512,256]{2,1,0:T(8,128)(2,1)S(1)}) custom-call(bf16[8,2048]{1,0:T(8,128)(2,1)} %refs_0_.3, bf16[1,512,256]{2,1,0:T(8,128)(2,1)} %refs_1_.1, bf16[1,512,256]{2,1,0:T(8,128)(2,1)} %refs_2_.1), custom_call_target="tpu_custom_call" | custom-call | bytes 1114112 | tf_op jit(solution)/shard_map/fetch/pallas_call | solution.py:80
  5.4 1.1 %collective-permute-done.second = bf16[8,2048]{1,0:T(8,128)(2,1)S(1)} collective-permute-done((bf16[8,2048]{1,0:T(8,128)(2,1)}, bf16[8,2048]{1,0:T(8,128)(2,1)S(1)}, u32[]{:S(2)}, u32[]{:S(2)}) %collective-permute-start) | collective-permute-done | bytes 32800 | tf_op jit(solution)/shard_map/ppermute | solution.py:39
  6.5 4.0 %collective-permute-start.3 = (bf16[2,8,2048]{2,1,0:T(8,128)(2,1)S(1)}, bf16[2,8,2048]{2,1,0:T(8,128)(2,1)S(1)}, u32[]{:S(2)}, u32[]{:S(2)}) collective-permute-start(bf16[2,8,2048]{2,1,0:T(8,128)(2,1)S(1)} %shard_map.140.refs_0_), channel_id=1, source_target_pairs={{0,12},{1,13},{2,14},{3,15},{4,8},{5,9},{6,10},{7,11},{8,4},{9,5},... | collective-permute-start | bytes 196616 | tf_op jit(solution)/shard_map/ppermute | solution.py:39
  10.5 3.0 %collective-permute-done.3.refs_3_ = bf16[2,8,2048]{2,1,0:T(8,128)(2,1)S(1)} collective-permute-done((bf16[2,8,2048]{2,1,0:T(8,128)(2,1)S(1)}, bf16[2,8,2048]{2,1,0:T(8,128)(2,1)S(1)}, u32[]{:S(2)}, u32[]{:S(2)}) %collective-permute-start.3) | collective-permute-done | bytes 65568 | tf_op jit(solution)/shard_map/ppermute | solution.py:39
  15.7 2.1 %collective-permute-done.1.refs_1_ = bf16[2,8,2048]{2,1,0:T(8,128)(2,1)S(1)} collective-permute-done((bf16[2,8,2048]{2,1,0:T(8,128)(2,1)S(1)}, bf16[2,8,2048]{2,1,0:T(8,128)(2,1)S(1)}, u32[]{:S(2)}, u32[]{:S(2)}) %collective-permute-start.1) | collective-permute-done | bytes 65568 | tf_op jit(solution)/shard_map/ppermute | solution.py:39
  17.8 1.2 %attention.2 = (bf16[2,136,128]{2,1,0:T(8,128)(2,1)S(1)}, bf16[2,136,128]{2,1,0:T(8,128)(2,1)S(1)}) custom-call(s32[1]{0:T(128)S(6)} %copy.15.lengths, bf16[2,8,2048]{2,1,0:T(8,128)(2,1)S(1)} %shard_map.140.refs_0_, bf16[2,8,2048]{2,1,0:T(8,128)(2,1)S(1)} %collective-permute-done.1.refs_1_, bf16[2,8,2048]{2,1,0:T(8,128)(2,1)S(1)} %collective-permute-done.2.refs_2_, ...), custom_call_target="tpu_custom_call" | custom-call | flops 268435456 | bytes 1048576 | tf_op jit(solution)/shard_map/attention/pallas_call | solution.py:311
  18.9 1.6 %collective-permute-start.6 = (bf16[2,136,128]{2,1,0:T(8,128)(2,1)S(1)}, bf16[2,136,128]{2,1,0:T(8,128)(2,1)S(1)}, u32[]{:S(2)}, u32[]{:S(2)}) collective-permute-start(bf16[2,136,128]{2,1,0:T(8,128)(2,1)S(1)} %get-tuple-element.41), channel_id=1, source_target_pairs={{0,2},{1,3},{2,0},{3,1},{4,6},{5,7},{6,4},{7,5},{8,10},{9,11},{10,... | collective-permute-start | bytes 208904 | tf_op jit(solution)/shard_map/ppermute | solution.py:39
  20.5 1.2 %attention.3 = (bf16[1,136,128]{2,1,0:T(8,128)(2,1)S(1)}, bf16[1,136,128]{2,1,0:T(8,128)(2,1)S(1)}, bf16[1,136,128]{2,1,0:T(8,128)(2,1)S(1)}, bf16[1,136,128]{2,1,0:T(8,128)(2,1)S(1)}) custom-call(s32[1]{0:T(128)S(6)} %copy.15.lengths, bf16[2,8,2048]{2,1,0:T(8,128)(2,1)S(1)} %shard_map.140.refs_0_, bf16[2,8,2048]{2,1,0:T(8,128)(2,1)S(1)} %collective-permute-done.1.refs_1_, ...), custom_call_target="tpu_custom_call" | custom-call | flops 268435456 | bytes 1048576 | tf_op jit(solution)/shard_map/attention/pallas_call | solution.py:311
  22.3 1.5 %collective-permute-start.10 = (bf16[1,136,128]{2,1,0:T(8,128)(2,1)S(1)}, bf16[1,136,128]{2,1,0:T(8,128)(2,1)S(1)}, u32[]{:S(2)}, u32[]{:S(2)}) collective-permute-start(bf16[1,136,128]{2,1,0:T(8,128)(2,1)S(1)} %get-tuple-element.47), channel_id=1, source_target_pairs={{0,2},{1,3},{2,0},{3,1},{4,6},{5,7},{6,4},{7,5},{8,10},{9,11},{10,... | collective-permute-start | bytes 104456 | tf_op jit(solution)/shard_map/ppermute | solution.py:39
  23.8 2.0 %prepare.1 = (bf16[16,2176]{1,0:T(8,128)(2,1)S(1)}, bf16[64,32]{1,0:T(8,128)(2,1)S(1)}, bf16[256,64]{1,0:T(8,128)(2,1)S(1)}, bf16[256,128]{1,0:T(8,128)(2,1)S(1)...) custom-call(s32[1,16]{1,0:T(1,128)} %bitcast.8, s32[1,128]{1,0:T(1,128)} %bitcast.9, s32[8,16]{1,0:T(8,128)} %bitcast.6, ...), custom_call_target="tpu_custom_call" | custom-call | flops 12582912 | bytes 131072 | tf_op jit(solution)/shard_map/prepare/pallas_call | solution.py:160
  25.9 2.4 %collective-permute-start.9 = (bf16[136,128]{1,0:T(8,128)(2,1)S(1)}, bf16[136,128]{1,0:T(8,128)(2,1)S(1)}, u32[]{:S(2)}, u32[]{:S(2)}) collective-permute-start(bf16[136,128]{1,0:T(8,128)(2,1)S(1)} %fold.4), channel_id=1, source_target_pairs={{0,8},{1,9},{2,10},{3,11},{4,12},{5,13},{6,14},{7,15},{8,0},{9,1},... | collective-permute-start | bytes 104456 | tf_op jit(solution)/shard_map/ppermute | solution.py:39
  28.3 1.7 %collective-permute-start.11 = (bf16[136,128]{1,0:T(8,128)(2,1)S(1)}, bf16[136,128]{1,0:T(8,128)(2,1)S(1)}, u32[]{:S(2)}, u32[]{:S(2)}) collective-permute-start(bf16[136,128]{1,0:T(8,128)(2,1)S(1)} %fold.5), channel_id=1, source_target_pairs={{0,12},{1,13},{2,14},{3,15},{4,8},{5,9},{6,10},{7,11},{8,4},{9,5},... | collective-permute-start | bytes 104456 | tf_op jit(solution)/shard_map/ppermute | solution.py:39
  30.8 3.5 %collective-permute-done.11.refs_3_ = bf16[136,128]{1,0:T(8,128)(2,1)S(1)} collective-permute-done((bf16[136,128]{1,0:T(8,128)(2,1)S(1)}, bf16[136,128]{1,0:T(8,128)(2,1)S(1)}, u32[]{:S(2)}, u32[]{:S(2)}) %collective-permute-start.11) | collective-permute-done | bytes 34848 | tf_op jit(solution)/shard_map/ppermute | solution.py:39
  35.1 2.4 %collective-permute-start.15 = (bf16[16,2176]{1,0:T(8,128)(2,1)S(1)}, bf16[16,2176]{1,0:T(8,128)(2,1)S(1)}, u32[]{:S(2)}, u32[]{:S(2)}) collective-permute-start(bf16[16,2176]{1,0:T(8,128)(2,1)S(1)} %get-tuple-element.53), channel_id=1, source_target_pairs={{0,8},{1,9},{2,10},{3,11},{4,12},{5,13},{6,14},{7,15},{8,0},{9,1},... | collective-permute-start | bytes 208904 | tf_op jit(solution)/shard_map/ppermute | solution.py:39
  37.5 1.9 %collective-permute-start.16 = (bf16[16,2176]{1,0:T(8,128)(2,1)S(1)}, bf16[16,2176]{1,0:T(8,128)(2,1)S(1)}, u32[]{:S(2)}, u32[]{:S(2)}) collective-permute-start(bf16[16,2176]{1,0:T(8,128)(2,1)S(1)} %get-tuple-element.54), channel_id=1, source_target_pairs={{0,12},{1,13},{2,14},{3,15},{4,8},{5,9},{6,10},{7,11},{8,4},{9,5},... | collective-permute-start | bytes 208904 | tf_op jit(solution)/shard_map/ppermute | solution.py:39
  39.4 3.2 %collective-permute-done.15.refs_2_ = bf16[16,2176]{1,0:T(8,128)(2,1)S(1)} collective-permute-done((bf16[16,2176]{1,0:T(8,128)(2,1)S(1)}, bf16[16,2176]{1,0:T(8,128)(2,1)S(1)}, u32[]{:S(2)}, u32[]{:S(2)}) %collective-permute-start.15) | collective-permute-done | bytes 69664 | tf_op jit(solution)/shard_map/ppermute | solution.py:39
  43.7 1.1 %collective-permute-start.17 = (bf16[16,2176]{1,0:T(8,128)(2,1)S(1)}, bf16[16,2176]{1,0:T(8,128)(2,1)S(1)}, u32[]{:S(2)}, u32[]{:S(2)}) collective-permute-start(bf16[16,2176]{1,0:T(8,128)(2,1)S(1)} %shard_map.141.refs_0_), channel_id=1, source_target_pairs={{0,2},{1,3},{2,0},{3,1},{4,6},{5,7},{6,4},{7,5},{8,10},{9,11},{10,... | collective-permute-start | bytes 208904 | tf_op jit(solution)/shard_map/ppermute | solution.py:39
  44.7 3.3 %collective-permute-done.17.refs_1_ = bf16[16,2176]{1,0:T(8,128)(2,1)S(1)} collective-permute-done((bf16[16,2176]{1,0:T(8,128)(2,1)S(1)}, bf16[16,2176]{1,0:T(8,128)(2,1)S(1)}, u32[]{:S(2)}, u32[]{:S(2)}) %collective-permute-start.17) | collective-permute-done | bytes 69664 | tf_op jit(solution)/shard_map/ppermute | solution.py:39
  48.1 2.2 %collective-permute-start.20 = (bf16[16,2176]{1,0:T(8,128)(2,1)S(1)}, bf16[16,2176]{1,0:T(8,128)(2,1)S(1)}, u32[]{:S(2)}, u32[]{:S(2)}) collective-permute-start(bf16[16,2176]{1,0:T(8,128)(2,1)S(1)} %shard_map.142.refs_0_), channel_id=1, source_target_pairs={{0,12},{1,13},{2,14},{3,15},{4,8},{5,9},{6,10},{7,11},{8,4},{9,5},... | collective-permute-start | bytes 208904 | tf_op jit(solution)/shard_map/ppermute | solution.py:39
  50.7 1.9 %collective-permute-start.18 = (bf16[16,2176]{1,0:T(8,128)(2,1)S(1)}, bf16[16,2176]{1,0:T(8,128)(2,1)S(1)}, u32[]{:S(2)}, u32[]{:S(2)}) collective-permute-start(bf16[16,2176]{1,0:T(8,128)(2,1)S(1)} %shard_map.142.refs_0_), channel_id=1, source_target_pairs={{0,4},{1,5},{2,6},{3,7},{4,0},{5,1},{6,2},{7,3},{8,12},{9,13},{10,... | collective-permute-start | bytes 208904 | tf_op jit(solution)/shard_map/ppermute | solution.py:39
  52.5 1.7 %collective-permute-done.20.refs_3_ = bf16[16,2176]{1,0:T(8,128)(2,1)S(1)} collective-permute-done((bf16[16,2176]{1,0:T(8,128)(2,1)S(1)}, bf16[16,2176]{1,0:T(8,128)(2,1)S(1)}, u32[]{:S(2)}, u32[]{:S(2)}) %collective-permute-start.20) | collective-permute-done | bytes 69664 | tf_op jit(solution)/shard_map/ppermute | solution.py:39
  54.3 1.8 %collective-permute-done.19.refs_2_ = bf16[16,2176]{1,0:T(8,128)(2,1)S(1)} collective-permute-done((bf16[16,2176]{1,0:T(8,128)(2,1)S(1)}, bf16[16,2176]{1,0:T(8,128)(2,1)S(1)}, u32[]{:S(2)}, u32[]{:S(2)}) %collective-permute-start.19) | collective-permute-done | bytes 69664 | tf_op jit(solution)/shard_map/ppermute | solution.py:39
  56.6 1.9 %fetch.5.refs_10_ = bf16[1,768,2048]{2,1,0:T(8,128)(2,1)S(1)} custom-call(bf16[1,768,2048]{2,1,0:T(8,128)(2,1)} %refs_0_.5), custom_call_target="tpu_custom_call" | custom-call | bytes 6291456 | tf_op jit(solution)/shard_map/fetch/pallas_call | solution.py:80
  58.5 2.8 %fetch.4.refs_9_ = bf16[1,2048,1536]{2,1,0:T(8,128)(2,1)S(1)} custom-call(bf16[1,2048,1536]{2,1,0:T(8,128)(2,1)} %refs_0_.4), custom_call_target="tpu_custom_call" | custom-call | bytes 12582912 | tf_op jit(solution)/shard_map/fetch/pallas_call | solution.py:80
  61.3 2.3 %experts.1 = (bf16[16,2304]{1,0:T(8,128)(2,1)S(1)}, bf16[16,2304]{1,0:T(8,128)(2,1)S(1)}, bf16[32,2304]{1,0:T(8,128)(2,1)S(1)}, bf16[64,2304]{1,0:T(8,128)(2,1)S...) custom-call(bf16[16,2176]{1,0:T(8,128)(2,1)S(1)} %shard_map.142.refs, ...), custom_call_target="tpu_custom_call" | custom-call | flops 1207959552 | bytes 9437184 | tf_op jit(solution)/shard_map/experts/pallas_call | solution.py:483
  67.2 1.4 %collective-permute-start.30 = (bf16[16,2304]{1,0:T(8,128)(2,1)S(1)}, bf16[16,2304]{1,0:T(8,128)(2,1)S(1)}, u32[]{:S(2)}, u32[]{:S(2)}) collective-permute-start(bf16[16,2304]{1,0:T(8,128)(2,1)S(1)} %shard_map.144), channel_id=1, source_target_pairs={{0,2},{1,3},{2,0},{3,1},{4,6},{5,7},{6,4},{7,5},{8,10},{9,11},{10,... | collective-permute-start | bytes 221192 | tf_op jit(solution)/shard_map/ppermute | solution.py:39
  69.7 2.3 %collective-permute-done.27.far = bf16[32,2304]{1,0:T(8,128)(2,1)S(1)} collective-permute-done((bf16[32,2304]{1,0:T(8,128)(2,1)S(1)}, bf16[32,2304]{1,0:T(8,128)(2,1)S(1)}, u32[]{:S(2)}, u32[]{:S(2)}) %collective-permute-start.27) | collective-permute-done | bytes 147488 | tf_op jit(solution)/shard_map/ppermute | solution.py:39
  72.5 1.0 %collective-permute-done.30.far = bf16[16,2304]{1,0:T(8,128)(2,1)S(1)} collective-permute-done((bf16[16,2304]{1,0:T(8,128)(2,1)S(1)}, bf16[16,2304]{1,0:T(8,128)(2,1)S(1)}, u32[]{:S(2)}, u32[]{:S(2)}) %collective-permute-start.30) | collective-permute-done | bytes 73760 | tf_op jit(solution)/shard_map/ppermute | solution.py:39
  73.5 1.2 %collective-permute-start.31 = (bf16[16,2560]{1,0:T(8,128)(2,1)S(1)}, bf16[16,2560]{1,0:T(8,128)(2,1)S(1)}, u32[]{:S(2)}, u32[]{:S(2)}) collective-permute-start(bf16[16,2560]{1,0:T(8,128)(2,1)S(1)} %mix.4), channel_id=1, source_target_pairs={{0,8},{1,9},{2,10},{3,11},{4,12},{5,13},{6,14},{7,15},{8,0},{9,1},... | collective-permute-start | bytes 245768 | tf_op jit(solution)/shard_map/ppermute | solution.py:39
  74.7 1.9 %collective-permute-start.34 = (bf16[16,2560]{1,0:T(8,128)(2,1)S(1)}, bf16[16,2560]{1,0:T(8,128)(2,1)S(1)}, u32[]{:S(2)}, u32[]{:S(2)}) collective-permute-start(bf16[16,2560]{1,0:T(8,128)(2,1)S(1)} %mix.5), channel_id=1, source_target_pairs={{0,12},{1,13},{2,14},{3,15},{4,8},{5,9},{6,10},{7,11},{8,4},{9,5},... | collective-permute-start | bytes 245768 | tf_op jit(solution)/shard_map/ppermute | solution.py:39
  77.3 4.4 %collective-permute-done.31.refs_2_ = bf16[16,2560]{1,0:T(8,128)(2,1)S(1)} collective-permute-done((bf16[16,2560]{1,0:T(8,128)(2,1)S(1)}, bf16[16,2560]{1,0:T(8,128)(2,1)S(1)}, u32[]{:S(2)}, u32[]{:S(2)}) %collective-permute-start.31) | collective-permute-done | bytes 81952 | tf_op jit(solution)/shard_map/ppermute | solution.py:39
  (60 shorter events, 13.5 us)
Async XLA Ops:
  0.6 33.8 %collective-permute-start.12 = (bf16[128,2048]{1,0:T(8,128)(2,1)}, bf16[128,2048]{1,0:T(8,128)(2,1)S(1)}, u32[]{:S(2)}, u32[]{:S(2)}) collective-permute-start(bf16[128,2048]{1,0:T(8,128)(2,1)} %refs_5_.1), channel_id=1, source_target_pairs={{0,1},{1,0},{2,3},{3,2},{4,5},{5,4},{6,7},{7,6},{8,9},{9,8},{10,11... | collective-permute-start | bytes 1572872 | tf_op jit(solution)/shard_map/ppermute | solution.py:39
  1.2 16.6 %collective-permute-start.4 = (bf16[1,512,256]{2,1,0:T(8,128)(2,1)}, bf16[1,512,256]{2,1,0:T(8,128)(2,1)S(1)}, u32[]{:S(2)}, u32[]{:S(2)}) collective-permute-start(bf16[1,512,256]{2,1,0:T(8,128)(2,1)} %refs_1_.1), channel_id=1, source_target_pairs={{0,1},{1,0},{2,3},{3,2},{4,5},{5,4},{6,7},{7,6},{8,9},{9,8},{10,11... | collective-permute-start | bytes 786440 | tf_op jit(solution)/shard_map/ppermute | solution.py:39
  1.3 16.5 %collective-permute-start.5 = (bf16[1,512,256]{2,1,0:T(8,128)(2,1)}, bf16[1,512,256]{2,1,0:T(8,128)(2,1)S(1)}, u32[]{:S(2)}, u32[]{:S(2)}) collective-permute-start(bf16[1,512,256]{2,1,0:T(8,128)(2,1)} %refs_2_.1), channel_id=1, source_target_pairs={{0,1},{1,0},{2,3},{3,2},{4,5},{5,4},{6,7},{7,6},{8,9},{9,8},{10,11... | collective-permute-start | bytes 786440 | tf_op jit(solution)/shard_map/ppermute | solution.py:39
  1.7 4.8 %collective-permute-start = (bf16[8,2048]{1,0:T(8,128)(2,1)}, bf16[8,2048]{1,0:T(8,128)(2,1)S(1)}, u32[]{:S(2)}, u32[]{:S(2)}) collective-permute-start(bf16[8,2048]{1,0:T(8,128)(2,1)} %refs_0_.3), channel_id=1, source_target_pairs={{0,2},{1,3},{2,0},{3,1},{4,6},{5,7},{6,4},{7,5},{8,10},{9,11},{10,... | collective-permute-start | bytes 98312 | tf_op jit(solution)/shard_map/ppermute | solution.py:39
  6.5 7.0 %collective-permute-start.3 = (bf16[2,8,2048]{2,1,0:T(8,128)(2,1)S(1)}, bf16[2,8,2048]{2,1,0:T(8,128)(2,1)S(1)}, u32[]{:S(2)}, u32[]{:S(2)}) collective-permute-start(bf16[2,8,2048]{2,1,0:T(8,128)(2,1)S(1)} %shard_map.140.refs_0_), channel_id=1, source_target_pairs={{0,12},{1,13},{2,14},{3,15},{4,8},{5,9},{6,10},{7,11},{8,4},{9,5},... | collective-permute-start | bytes 196616 | tf_op jit(solution)/shard_map/ppermute | solution.py:39
  10.5 5.2 %collective-permute-start.2 = (bf16[2,8,2048]{2,1,0:T(8,128)(2,1)S(1)}, bf16[2,8,2048]{2,1,0:T(8,128)(2,1)S(1)}, u32[]{:S(2)}, u32[]{:S(2)}) collective-permute-start(bf16[2,8,2048]{2,1,0:T(8,128)(2,1)S(1)} %shard_map.140.refs_0_), channel_id=1, source_target_pairs={{0,8},{1,9},{2,10},{3,11},{4,12},{5,13},{6,14},{7,15},{8,0},{9,1},... | collective-permute-start | bytes 196616 | tf_op jit(solution)/shard_map/ppermute | solution.py:39
  13.5 4.3 %collective-permute-start.1 = (bf16[2,8,2048]{2,1,0:T(8,128)(2,1)S(1)}, bf16[2,8,2048]{2,1,0:T(8,128)(2,1)S(1)}, u32[]{:S(2)}, u32[]{:S(2)}) collective-permute-start(bf16[2,8,2048]{2,1,0:T(8,128)(2,1)S(1)} %shard_map.140.refs_0_), channel_id=1, source_target_pairs={{0,4},{1,5},{2,6},{3,7},{4,0},{5,1},{6,2},{7,3},{8,12},{9,13},{10,... | collective-permute-start | bytes 196616 | tf_op jit(solution)/shard_map/ppermute | solution.py:39
  18.9 11.1 %collective-permute-start.6 = (bf16[2,136,128]{2,1,0:T(8,128)(2,1)S(1)}, bf16[2,136,128]{2,1,0:T(8,128)(2,1)S(1)}, u32[]{:S(2)}, u32[]{:S(2)}) collective-permute-start(bf16[2,136,128]{2,1,0:T(8,128)(2,1)S(1)} %get-tuple-element.41), channel_id=1, source_target_pairs={{0,2},{1,3},{2,0},{3,1},{4,6},{5,7},{6,4},{7,5},{8,10},{9,11},{10,... | collective-permute-start | bytes 208904 | tf_op jit(solution)/shard_map/ppermute | solution.py:39
  21.7 4.2 %collective-permute-start.8 = (bf16[1,136,128]{2,1,0:T(8,128)(2,1)S(1)}, bf16[1,136,128]{2,1,0:T(8,128)(2,1)S(1)}, u32[]{:S(2)}, u32[]{:S(2)}) collective-permute-start(bf16[1,136,128]{2,1,0:T(8,128)(2,1)S(1)} %get-tuple-element.45), channel_id=1, source_target_pairs={{0,2},{1,3},{2,0},{3,1},{4,6},{5,7},{6,4},{7,5},{8,10},{9,11},{10,... | collective-permute-start | bytes 104456 | tf_op jit(solution)/shard_map/ppermute | solution.py:39
  22.3 6.0 %collective-permute-start.10 = (bf16[1,136,128]{2,1,0:T(8,128)(2,1)S(1)}, bf16[1,136,128]{2,1,0:T(8,128)(2,1)S(1)}, u32[]{:S(2)}, u32[]{:S(2)}) collective-permute-start(bf16[1,136,128]{2,1,0:T(8,128)(2,1)S(1)} %get-tuple-element.47), channel_id=1, source_target_pairs={{0,2},{1,3},{2,0},{3,1},{4,6},{5,7},{6,4},{7,5},{8,10},{9,11},{10,... | collective-permute-start | bytes 104456 | tf_op jit(solution)/shard_map/ppermute | solution.py:39
  25.8 4.8 %collective-permute-start.13 = (bf16[16,2176]{1,0:T(8,128)(2,1)S(1)}, bf16[16,2176]{1,0:T(8,128)(2,1)S(1)}, u32[]{:S(2)}, u32[]{:S(2)}) collective-permute-start(bf16[16,2176]{1,0:T(8,128)(2,1)S(1)} %get-tuple-element.49.refs_6_), channel_id=1, source_target_pairs={{0,1},{1,0},{2,3},{3,2},{4,5},{5,4},{6,7},{7,6},{8,9},{9,8},{10,11... | collective-permute-start | bytes 208904 | tf_op jit(solution)/shard_map/ppermute | solution.py:39
  25.9 4.9 %collective-permute-start.9 = (bf16[136,128]{1,0:T(8,128)(2,1)S(1)}, bf16[136,128]{1,0:T(8,128)(2,1)S(1)}, u32[]{:S(2)}, u32[]{:S(2)}) collective-permute-start(bf16[136,128]{1,0:T(8,128)(2,1)S(1)} %fold.4), channel_id=1, source_target_pairs={{0,8},{1,9},{2,10},{3,11},{4,12},{5,13},{6,14},{7,15},{8,0},{9,1},... | collective-permute-start | bytes 104456 | tf_op jit(solution)/shard_map/ppermute | solution.py:39
  28.3 6.0 %collective-permute-start.11 = (bf16[136,128]{1,0:T(8,128)(2,1)S(1)}, bf16[136,128]{1,0:T(8,128)(2,1)S(1)}, u32[]{:S(2)}, u32[]{:S(2)}) collective-permute-start(bf16[136,128]{1,0:T(8,128)(2,1)S(1)} %fold.5), channel_id=1, source_target_pairs={{0,12},{1,13},{2,14},{3,15},{4,8},{5,9},{6,10},{7,11},{8,4},{9,5},... | collective-permute-start | bytes 104456 | tf_op jit(solution)/shard_map/ppermute | solution.py:39
  30.1 4.4 %collective-permute-start.7 = (bf16[136,128]{1,0:T(8,128)(2,1)S(1)}, bf16[136,128]{1,0:T(8,128)(2,1)S(1)}, u32[]{:S(2)}, u32[]{:S(2)}) collective-permute-start(bf16[136,128]{1,0:T(8,128)(2,1)S(1)} %get-tuple-element.43), channel_id=1, source_target_pairs={{0,4},{1,5},{2,6},{3,7},{4,0},{5,1},{6,2},{7,3},{8,12},{9,13},{10,... | collective-permute-start | bytes 104456 | tf_op jit(solution)/shard_map/ppermute | solution.py:39
  35.0 4.5 %collective-permute-start.14 = (bf16[16,2176]{1,0:T(8,128)(2,1)S(1)}, bf16[16,2176]{1,0:T(8,128)(2,1)S(1)}, u32[]{:S(2)}, u32[]{:S(2)}) collective-permute-start(bf16[16,2176]{1,0:T(8,128)(2,1)S(1)} %get-tuple-element.52), channel_id=1, source_target_pairs={{0,4},{1,5},{2,6},{3,7},{4,0},{5,1},{6,2},{7,3},{8,12},{9,13},{10,... | collective-permute-start | bytes 208904 | tf_op jit(solution)/shard_map/ppermute | solution.py:39
  35.1 7.5 %collective-permute-start.15 = (bf16[16,2176]{1,0:T(8,128)(2,1)S(1)}, bf16[16,2176]{1,0:T(8,128)(2,1)S(1)}, u32[]{:S(2)}, u32[]{:S(2)}) collective-permute-start(bf16[16,2176]{1,0:T(8,128)(2,1)S(1)} %get-tuple-element.53), channel_id=1, source_target_pairs={{0,8},{1,9},{2,10},{3,11},{4,12},{5,13},{6,14},{7,15},{8,0},{9,1},... | collective-permute-start | bytes 208904 | tf_op jit(solution)/shard_map/ppermute | solution.py:39
  37.5 6.1 %collective-permute-start.16 = (bf16[16,2176]{1,0:T(8,128)(2,1)S(1)}, bf16[16,2176]{1,0:T(8,128)(2,1)S(1)}, u32[]{:S(2)}, u32[]{:S(2)}) collective-permute-start(bf16[16,2176]{1,0:T(8,128)(2,1)S(1)} %get-tuple-element.54), channel_id=1, source_target_pairs={{0,12},{1,13},{2,14},{3,15},{4,8},{5,9},{6,10},{7,11},{8,4},{9,5},... | collective-permute-start | bytes 208904 | tf_op jit(solution)/shard_map/ppermute | solution.py:39
  43.7 4.4 %collective-permute-start.17 = (bf16[16,2176]{1,0:T(8,128)(2,1)S(1)}, bf16[16,2176]{1,0:T(8,128)(2,1)S(1)}, u32[]{:S(2)}, u32[]{:S(2)}) collective-permute-start(bf16[16,2176]{1,0:T(8,128)(2,1)S(1)} %shard_map.141.refs_0_), channel_id=1, source_target_pairs={{0,2},{1,3},{2,0},{3,1},{4,6},{5,7},{6,4},{7,5},{8,10},{9,11},{10,... | collective-permute-start | bytes 208904 | tf_op jit(solution)/shard_map/ppermute | solution.py:39
  48.1 6.2 %collective-permute-start.20 = (bf16[16,2176]{1,0:T(8,128)(2,1)S(1)}, bf16[16,2176]{1,0:T(8,128)(2,1)S(1)}, u32[]{:S(2)}, u32[]{:S(2)}) collective-permute-start(bf16[16,2176]{1,0:T(8,128)(2,1)S(1)} %shard_map.142.refs_0_), channel_id=1, source_target_pairs={{0,12},{1,13},{2,14},{3,15},{4,8},{5,9},{6,10},{7,11},{8,4},{9,5},... | collective-permute-start | bytes 208904 | tf_op jit(solution)/shard_map/ppermute | solution.py:39
  50.3 5.8 %collective-permute-start.19 = (bf16[16,2176]{1,0:T(8,128)(2,1)S(1)}, bf16[16,2176]{1,0:T(8,128)(2,1)S(1)}, u32[]{:S(2)}, u32[]{:S(2)}) collective-permute-start(bf16[16,2176]{1,0:T(8,128)(2,1)S(1)} %shard_map.142.refs_0_), channel_id=1, source_target_pairs={{0,8},{1,9},{2,10},{3,11},{4,12},{5,13},{6,14},{7,15},{8,0},{9,1},... | collective-permute-start | bytes 208904 | tf_op jit(solution)/shard_map/ppermute | solution.py:39
  50.7 5.4 %collective-permute-start.18 = (bf16[16,2176]{1,0:T(8,128)(2,1)S(1)}, bf16[16,2176]{1,0:T(8,128)(2,1)S(1)}, u32[]{:S(2)}, u32[]{:S(2)}) collective-permute-start(bf16[16,2176]{1,0:T(8,128)(2,1)S(1)} %shard_map.142.refs_0_), channel_id=1, source_target_pairs={{0,4},{1,5},{2,6},{3,7},{4,0},{5,1},{6,2},{7,3},{8,12},{9,13},{10,... | collective-permute-start | bytes 208904 | tf_op jit(solution)/shard_map/ppermute | solution.py:39
  52.5 8.8 %collective-permute-start.21 = (bf16[16,2176]{1,0:T(8,128)(2,1)S(1)}, bf16[16,2176]{1,0:T(8,128)(2,1)S(1)}, u32[]{:S(2)}, u32[]{:S(2)}) collective-permute-start(bf16[16,2176]{1,0:T(8,128)(2,1)S(1)} %shard_map.142.refs_0_), channel_id=1, source_target_pairs={{0,1},{1,0},{2,3},{3,2},{4,5},{5,4},{6,7},{7,6},{8,9},{9,8},{10,11... | collective-permute-start | bytes 208904 | tf_op jit(solution)/shard_map/ppermute | solution.py:39
  54.3 7.1 %collective-permute-start.24 = (bf16[16,2176]{1,0:T(8,128)(2,1)S(1)}, bf16[16,2176]{1,0:T(8,128)(2,1)S(1)}, u32[]{:S(2)}, u32[]{:S(2)}) collective-permute-start(bf16[16,2176]{1,0:T(8,128)(2,1)S(1)} %collective-permute-done.20.refs_3_), channel_id=1, source_target_pairs={{0,1},{1,0},{2,3},{3,2},{4,5},{5,4},{6,7},{7,6},{8,9},{9,8},{10,11... | collective-permute-start | bytes 208904 | tf_op jit(solution)/shard_map/ppermute | solution.py:39
  56.1 5.2 %collective-permute-start.23 = (bf16[16,2176]{1,0:T(8,128)(2,1)S(1)}, bf16[16,2176]{1,0:T(8,128)(2,1)S(1)}, u32[]{:S(2)}, u32[]{:S(2)}) collective-permute-start(bf16[16,2176]{1,0:T(8,128)(2,1)S(1)} %collective-permute-done.19.refs_2_), channel_id=1, source_target_pairs={{0,1},{1,0},{2,3},{3,2},{4,5},{5,4},{6,7},{7,6},{8,9},{9,8},{10,11... | collective-permute-start | bytes 208904 | tf_op jit(solution)/shard_map/ppermute | solution.py:39
  56.1 5.3 %collective-permute-start.22 = (bf16[16,2176]{1,0:T(8,128)(2,1)S(1)}, bf16[16,2176]{1,0:T(8,128)(2,1)S(1)}, u32[]{:S(2)}, u32[]{:S(2)}) collective-permute-start(bf16[16,2176]{1,0:T(8,128)(2,1)S(1)} %collective-permute-done.18.refs_1_), channel_id=1, source_target_pairs={{0,1},{1,0},{2,3},{3,2},{4,5},{5,4},{6,7},{7,6},{8,9},{9,8},{10,11... | collective-permute-start | bytes 208904 | tf_op jit(solution)/shard_map/ppermute | solution.py:39
  63.8 8.2 %collective-permute-start.25 = (bf16[64,2304]{1,0:T(8,128)(2,1)S(1)}, bf16[64,2304]{1,0:T(8,128)(2,1)S(1)}, u32[]{:S(2)}, u32[]{:S(2)}) collective-permute-start(bf16[64,2304]{1,0:T(8,128)(2,1)S(1)} %get-tuple-element.63), channel_id=1, source_target_pairs={{0,1},{1,0},{2,3},{3,2},{4,5},{5,4},{6,7},{7,6},{8,9},{9,8},{10,11... | collective-permute-start | bytes 884744 | tf_op jit(solution)/shard_map/ppermute | solution.py:39
  65.1 6.8 %collective-permute-start.27 = (bf16[32,2304]{1,0:T(8,128)(2,1)S(1)}, bf16[32,2304]{1,0:T(8,128)(2,1)S(1)}, u32[]{:S(2)}, u32[]{:S(2)}) collective-permute-start(bf16[32,2304]{1,0:T(8,128)(2,1)S(1)} %shard_map.143), channel_id=1, source_target_pairs={{0,2},{1,3},{2,0},{3,1},{4,6},{5,7},{6,4},{7,5},{8,10},{9,11},{10,... | collective-permute-start | bytes 442376 | tf_op jit(solution)/shard_map/ppermute | solution.py:39
  67.2 6.3 %collective-permute-start.30 = (bf16[16,2304]{1,0:T(8,128)(2,1)S(1)}, bf16[16,2304]{1,0:T(8,128)(2,1)S(1)}, u32[]{:S(2)}, u32[]{:S(2)}) collective-permute-start(bf16[16,2304]{1,0:T(8,128)(2,1)S(1)} %shard_map.144), channel_id=1, source_target_pairs={{0,2},{1,3},{2,0},{3,1},{4,6},{5,7},{6,4},{7,5},{8,10},{9,11},{10,... | collective-permute-start | bytes 221192 | tf_op jit(solution)/shard_map/ppermute | solution.py:39
  68.6 6.1 %collective-permute-start.33 = (bf16[16,2304]{1,0:T(8,128)(2,1)S(1)}, bf16[16,2304]{1,0:T(8,128)(2,1)S(1)}, u32[]{:S(2)}, u32[]{:S(2)}) collective-permute-start(bf16[16,2304]{1,0:T(8,128)(2,1)S(1)} %shard_map.145), channel_id=1, source_target_pairs={{0,2},{1,3},{2,0},{3,1},{4,6},{5,7},{6,4},{7,5},{8,10},{9,11},{10,... | collective-permute-start | bytes 221192 | tf_op jit(solution)/shard_map/ppermute | solution.py:39
  72.0 5.3 %collective-permute-start.28 = (bf16[16,2560]{1,0:T(8,128)(2,1)S(1)}, bf16[16,2560]{1,0:T(8,128)(2,1)S(1)}, u32[]{:S(2)}, u32[]{:S(2)}) collective-permute-start(bf16[16,2560]{1,0:T(8,128)(2,1)S(1)} %get-tuple-element.67), channel_id=1, source_target_pairs={{0,4},{1,5},{2,6},{3,7},{4,0},{5,1},{6,2},{7,3},{8,12},{9,13},{10,... | collective-permute-start | bytes 245768 | tf_op jit(solution)/shard_map/ppermute | solution.py:39
  73.5 8.2 %collective-permute-start.31 = (bf16[16,2560]{1,0:T(8,128)(2,1)S(1)}, bf16[16,2560]{1,0:T(8,128)(2,1)S(1)}, u32[]{:S(2)}, u32[]{:S(2)}) collective-permute-start(bf16[16,2560]{1,0:T(8,128)(2,1)S(1)} %mix.4), channel_id=1, source_target_pairs={{0,8},{1,9},{2,10},{3,11},{4,12},{5,13},{6,14},{7,15},{8,0},{9,1},... | collective-permute-start | bytes 245768 | tf_op jit(solution)/shard_map/ppermute | solution.py:39
  74.7 7.0 %collective-permute-start.34 = (bf16[16,2560]{1,0:T(8,128)(2,1)S(1)}, bf16[16,2560]{1,0:T(8,128)(2,1)S(1)}, u32[]{:S(2)}, u32[]{:S(2)}) collective-permute-start(bf16[16,2560]{1,0:T(8,128)(2,1)S(1)} %mix.5), channel_id=1, source_target_pairs={{0,12},{1,13},{2,14},{3,15},{4,8},{5,9},{6,10},{7,11},{8,4},{9,5},... | collective-permute-start | bytes 245768 | tf_op jit(solution)/shard_map/ppermute | solution.py:39
  (3 other events, 5.4 us)

commit v7 on v6

--- a/solution.py
+++ b/solution.py
@@ -45,6 +45,10 @@
 
 def portions(nz):
     return [1, nz // 2 - 1, nz // 2]
+
+
+def shares(nz):
+    return [1, 1, nz // 2 - 1, nz // 2 - 1]
 
 
 def split3(x):
@@ -478,7 +482,7 @@
     total = 2 * nz * block
     shapes = [
         jax.ShapeDtypeStruct((blocks * cap, D + mixed.shape[1]), BF)
-        for blocks in [nz] + portions(nz)
+        for blocks in [nz] + shares(nz)
     ]
     return pl.pallas_call(
         functools.partial(expert_kernel, nz, width),
@@ -638,6 +642,7 @@
     *halves, scaled, rows = experts(
         mine, theirs, gain, up, down, turn, fill, mixed, width, cap
     )
+    count = len(shares(nz))
     keeps, (send, *sends) = halves[:count], halves[count:]
     keep, stream = stay(scaled, rows, turn, fill, mixed, cap)
     gots, fars, blocks = [], [], []

time: 82.7 us -> 81.5 us (0.985)
  waiting for transfers between devices: 31.9 us -> 29.7 us
  starting transfers between devices: 34.7 us -> 35.7 us
    ppermute x35 -> x37, waiting for transfers between devices: 31.9 us -> 29.7 us  [hop(): return lax.ppermute(x, 'ctx', [(i, i ^ mask) for i in range(width)])]
    ppermute x35 -> x37, starting transfers between devices: 34.7 us -> 35.7 us  [hop(): return lax.ppermute(x, 'ctx', [(i, i ^ mask) for i in range(width)])]
  transfers between devices with their start and end apart: 35 -> 37, of which waited for: 18 -> 17; matrix products, arithmetic and copies ran while one was open for 0% -> 0% of each run, Pallas kernels for 13% -> 13%
where the time goes in v7:
time: 81.5 us; the launch traced here: 81.2 us
  starting transfers between devices  35.7 us (44%)
  waiting for transfers between devices  29.7 us (36%)
  Pallas kernels  14.4 us (18%)
  between operations  1.49 us (2%)
    ppermute x37, starting transfers between devices, hop(): return lax.ppermute(x, 'ctx', [(i, i ^ mask) for i in range(width)])  35.7 us
    ppermute x37, waiting for transfers between devices, hop(): return lax.ppermute(x, 'ctx', [(i, i ^ mask) for i in range(width)])  29.7 us
    pallas_call x3, Pallas kernels, fetch(): pl.pallas_call(functools.partial(fetch_kernel, count), out_shape=[pltpu.V...  5.77 us
    pallas_call x1, Pallas kernels, experts(): pl.pallas_call(functools.partial(expert_kernel, nz, width), out_shape=sha...  2.47 us
    pallas_call x2, Pallas kernels, attention(): pl.pallas_call(functools.partial(attention_kernel, nz, far), out_shape=[j...  2.32 us
    pallas_call x1, Pallas kernels, prepare(): pl.pallas_call(functools.partial(prepare_kernel, per, width), out_shape=[...  1.98 us
  transfers between devices with their start and end apart: 37, of which 17 were waited for; matrix products, arithmetic and copies ran while one was open for 0% of the time, Pallas kernels for 13%

profile of v7, /device:TPU:0, one launch (start us, length us, event | category | flops | bytes accessed | tf_op | source)
XLA Modules:
  0.0 81.2 jit_solution(12735839355800108109)
XLA Ops:
  1.7 2.6 %collective-permute-start = (bf16[8,2048]{1,0:T(8,128)(2,1)}, bf16[8,2048]{1,0:T(8,128)(2,1)S(1)}, u32[]{:S(2)}, u32[]{:S(2)}) collective-permute-start(bf16[8,2048]{1,0:T(8,128)(2,1)} %refs_0_.3), channel_id=1, source_target_pairs={{0,2},{1,3},{2,0},{3,1},{4,6},{5,7},{6,4},{7,5},{8,10},{9,11},{10,... | collective-permute-start | bytes 98312 | tf_op jit(solution)/shard_map/ppermute | solution.py:39
  4.3 1.1 %fetch.3 = (bf16[8,2048]{1,0:T(8,128)(2,1)S(1)}, bf16[1,512,256]{2,1,0:T(8,128)(2,1)S(1)}, bf16[1,512,256]{2,1,0:T(8,128)(2,1)S(1)}) custom-call(bf16[8,2048]{1,0:T(8,128)(2,1)} %refs_0_.3, bf16[1,512,256]{2,1,0:T(8,128)(2,1)} %refs_1_.1, bf16[1,512,256]{2,1,0:T(8,128)(2,1)} %refs_2_.1), custom_call_target="tpu_custom_call" | custom-call | bytes 1114112 | tf_op jit(solution)/shard_map/fetch/pallas_call | solution.py:84
  5.4 1.1 %collective-permute-done.second = bf16[8,2048]{1,0:T(8,128)(2,1)S(1)} collective-permute-done((bf16[8,2048]{1,0:T(8,128)(2,1)}, bf16[8,2048]{1,0:T(8,128)(2,1)S(1)}, u32[]{:S(2)}, u32[]{:S(2)}) %collective-permute-start) | collective-permute-done | bytes 32800 | tf_op jit(solution)/shard_map/ppermute | solution.py:39
  6.5 4.0 %collective-permute-start.3 = (bf16[2,8,2048]{2,1,0:T(8,128)(2,1)S(1)}, bf16[2,8,2048]{2,1,0:T(8,128)(2,1)S(1)}, u32[]{:S(2)}, u32[]{:S(2)}) collective-permute-start(bf16[2,8,2048]{2,1,0:T(8,128)(2,1)S(1)} %shard_map.140.refs_0_), channel_id=1, source_target_pairs={{0,12},{1,13},{2,14},{3,15},{4,8},{5,9},{6,10},{7,11},{8,4},{9,5},... | collective-permute-start | bytes 196616 | tf_op jit(solution)/shard_map/ppermute | solution.py:39
  10.5 3.0 %collective-permute-done.3.refs_3_ = bf16[2,8,2048]{2,1,0:T(8,128)(2,1)S(1)} collective-permute-done((bf16[2,8,2048]{2,1,0:T(8,128)(2,1)S(1)}, bf16[2,8,2048]{2,1,0:T(8,128)(2,1)S(1)}, u32[]{:S(2)}, u32[]{:S(2)}) %collective-permute-start.3) | collective-permute-done | bytes 65568 | tf_op jit(solution)/shard_map/ppermute | solution.py:39
  15.7 2.1 %collective-permute-done.1.refs_1_ = bf16[2,8,2048]{2,1,0:T(8,128)(2,1)S(1)} collective-permute-done((bf16[2,8,2048]{2,1,0:T(8,128)(2,1)S(1)}, bf16[2,8,2048]{2,1,0:T(8,128)(2,1)S(1)}, u32[]{:S(2)}, u32[]{:S(2)}) %collective-permute-start.1) | collective-permute-done | bytes 65568 | tf_op jit(solution)/shard_map/ppermute | solution.py:39
  17.8 1.2 %attention.2 = (bf16[2,136,128]{2,1,0:T(8,128)(2,1)S(1)}, bf16[2,136,128]{2,1,0:T(8,128)(2,1)S(1)}) custom-call(s32[1]{0:T(128)S(6)} %copy.15.lengths, bf16[2,8,2048]{2,1,0:T(8,128)(2,1)S(1)} %shard_map.140.refs_0_, bf16[2,8,2048]{2,1,0:T(8,128)(2,1)S(1)} %collective-permute-done.1.refs_1_, bf16[2,8,2048]{2,1,0:T(8,128)(2,1)S(1)} %collective-permute-done.2.refs_2_, ...), custom_call_target="tpu_custom_call" | custom-call | flops 268435456 | bytes 1048576 | tf_op jit(solution)/shard_map/attention/pallas_call | solution.py:315
  18.9 1.6 %collective-permute-start.6 = (bf16[2,136,128]{2,1,0:T(8,128)(2,1)S(1)}, bf16[2,136,128]{2,1,0:T(8,128)(2,1)S(1)}, u32[]{:S(2)}, u32[]{:S(2)}) collective-permute-start(bf16[2,136,128]{2,1,0:T(8,128)(2,1)S(1)} %get-tuple-element.41), channel_id=1, source_target_pairs={{0,2},{1,3},{2,0},{3,1},{4,6},{5,7},{6,4},{7,5},{8,10},{9,11},{10,... | collective-permute-start | bytes 208904 | tf_op jit(solution)/shard_map/ppermute | solution.py:39
  20.5 1.2 %attention.3 = (bf16[1,136,128]{2,1,0:T(8,128)(2,1)S(1)}, bf16[1,136,128]{2,1,0:T(8,128)(2,1)S(1)}, bf16[1,136,128]{2,1,0:T(8,128)(2,1)S(1)}, bf16[1,136,128]{2,1,0:T(8,128)(2,1)S(1)}) custom-call(s32[1]{0:T(128)S(6)} %copy.15.lengths, bf16[2,8,2048]{2,1,0:T(8,128)(2,1)S(1)} %shard_map.140.refs_0_, bf16[2,8,2048]{2,1,0:T(8,128)(2,1)S(1)} %collective-permute-done.1.refs_1_, ...), custom_call_target="tpu_custom_call" | custom-call | flops 268435456 | bytes 1048576 | tf_op jit(solution)/shard_map/attention/pallas_call | solution.py:315
  22.3 1.5 %collective-permute-start.10 = (bf16[1,136,128]{2,1,0:T(8,128)(2,1)S(1)}, bf16[1,136,128]{2,1,0:T(8,128)(2,1)S(1)}, u32[]{:S(2)}, u32[]{:S(2)}) collective-permute-start(bf16[1,136,128]{2,1,0:T(8,128)(2,1)S(1)} %get-tuple-element.47), channel_id=1, source_target_pairs={{0,2},{1,3},{2,0},{3,1},{4,6},{5,7},{6,4},{7,5},{8,10},{9,11},{10,... | collective-permute-start | bytes 104456 | tf_op jit(solution)/shard_map/ppermute | solution.py:39
  23.8 2.0 %prepare.1 = (bf16[16,2176]{1,0:T(8,128)(2,1)S(1)}, bf16[64,32]{1,0:T(8,128)(2,1)S(1)}, bf16[256,64]{1,0:T(8,128)(2,1)S(1)}, bf16[256,128]{1,0:T(8,128)(2,1)S(1)...) custom-call(s32[1,16]{1,0:T(1,128)} %bitcast.8, s32[1,128]{1,0:T(1,128)} %bitcast.9, s32[8,16]{1,0:T(8,128)} %bitcast.6, ...), custom_call_target="tpu_custom_call" | custom-call | flops 12582912 | bytes 131072 | tf_op jit(solution)/shard_map/prepare/pallas_call | solution.py:164
  25.9 2.4 %collective-permute-start.9 = (bf16[136,128]{1,0:T(8,128)(2,1)S(1)}, bf16[136,128]{1,0:T(8,128)(2,1)S(1)}, u32[]{:S(2)}, u32[]{:S(2)}) collective-permute-start(bf16[136,128]{1,0:T(8,128)(2,1)S(1)} %fold.4), channel_id=1, source_target_pairs={{0,8},{1,9},{2,10},{3,11},{4,12},{5,13},{6,14},{7,15},{8,0},{9,1},... | collective-permute-start | bytes 104456 | tf_op jit(solution)/shard_map/ppermute | solution.py:39
  28.3 1.7 %collective-permute-start.11 = (bf16[136,128]{1,0:T(8,128)(2,1)S(1)}, bf16[136,128]{1,0:T(8,128)(2,1)S(1)}, u32[]{:S(2)}, u32[]{:S(2)}) collective-permute-start(bf16[136,128]{1,0:T(8,128)(2,1)S(1)} %fold.5), channel_id=1, source_target_pairs={{0,12},{1,13},{2,14},{3,15},{4,8},{5,9},{6,10},{7,11},{8,4},{9,5},... | collective-permute-start | bytes 104456 | tf_op jit(solution)/shard_map/ppermute | solution.py:39
  30.8 3.5 %collective-permute-done.11.refs_3_ = bf16[136,128]{1,0:T(8,128)(2,1)S(1)} collective-permute-done((bf16[136,128]{1,0:T(8,128)(2,1)S(1)}, bf16[136,128]{1,0:T(8,128)(2,1)S(1)}, u32[]{:S(2)}, u32[]{:S(2)}) %collective-permute-start.11) | collective-permute-done | bytes 34848 | tf_op jit(solution)/shard_map/ppermute | solution.py:39
  35.1 2.4 %collective-permute-start.15 = (bf16[16,2176]{1,0:T(8,128)(2,1)S(1)}, bf16[16,2176]{1,0:T(8,128)(2,1)S(1)}, u32[]{:S(2)}, u32[]{:S(2)}) collective-permute-start(bf16[16,2176]{1,0:T(8,128)(2,1)S(1)} %get-tuple-element.53), channel_id=1, source_target_pairs={{0,8},{1,9},{2,10},{3,11},{4,12},{5,13},{6,14},{7,15},{8,0},{9,1},... | collective-permute-start | bytes 208904 | tf_op jit(solution)/shard_map/ppermute | solution.py:39
  37.5 1.9 %collective-permute-start.16 = (bf16[16,2176]{1,0:T(8,128)(2,1)S(1)}, bf16[16,2176]{1,0:T(8,128)(2,1)S(1)}, u32[]{:S(2)}, u32[]{:S(2)}) collective-permute-start(bf16[16,2176]{1,0:T(8,128)(2,1)S(1)} %get-tuple-element.54), channel_id=1, source_target_pairs={{0,12},{1,13},{2,14},{3,15},{4,8},{5,9},{6,10},{7,11},{8,4},{9,5},... | collective-permute-start | bytes 208904 | tf_op jit(solution)/shard_map/ppermute | solution.py:39
  39.4 3.2 %collective-permute-done.15.refs_2_ = bf16[16,2176]{1,0:T(8,128)(2,1)S(1)} collective-permute-done((bf16[16,2176]{1,0:T(8,128)(2,1)S(1)}, bf16[16,2176]{1,0:T(8,128)(2,1)S(1)}, u32[]{:S(2)}, u32[]{:S(2)}) %collective-permute-start.15) | collective-permute-done | bytes 69664 | tf_op jit(solution)/shard_map/ppermute | solution.py:39
  43.7 1.1 %collective-permute-start.17 = (bf16[16,2176]{1,0:T(8,128)(2,1)S(1)}, bf16[16,2176]{1,0:T(8,128)(2,1)S(1)}, u32[]{:S(2)}, u32[]{:S(2)}) collective-permute-start(bf16[16,2176]{1,0:T(8,128)(2,1)S(1)} %shard_map.141.refs_0_), channel_id=1, source_target_pairs={{0,2},{1,3},{2,0},{3,1},{4,6},{5,7},{6,4},{7,5},{8,10},{9,11},{10,... | collective-permute-start | bytes 208904 | tf_op jit(solution)/shard_map/ppermute | solution.py:39
  44.7 3.3 %collective-permute-done.17.refs_1_ = bf16[16,2176]{1,0:T(8,128)(2,1)S(1)} collective-permute-done((bf16[16,2176]{1,0:T(8,128)(2,1)S(1)}, bf16[16,2176]{1,0:T(8,128)(2,1)S(1)}, u32[]{:S(2)}, u32[]{:S(2)}) %collective-permute-start.17) | collective-permute-done | bytes 69664 | tf_op jit(solution)/shard_map/ppermute | solution.py:39
  48.1 2.2 %collective-permute-start.20 = (bf16[16,2176]{1,0:T(8,128)(2,1)S(1)}, bf16[16,2176]{1,0:T(8,128)(2,1)S(1)}, u32[]{:S(2)}, u32[]{:S(2)}) collective-permute-start(bf16[16,2176]{1,0:T(8,128)(2,1)S(1)} %shard_map.142.refs_0_), channel_id=1, source_target_pairs={{0,12},{1,13},{2,14},{3,15},{4,8},{5,9},{6,10},{7,11},{8,4},{9,5},... | collective-permute-start | bytes 208904 | tf_op jit(solution)/shard_map/ppermute | solution.py:39
  50.7 1.9 %collective-permute-start.18 = (bf16[16,2176]{1,0:T(8,128)(2,1)S(1)}, bf16[16,2176]{1,0:T(8,128)(2,1)S(1)}, u32[]{:S(2)}, u32[]{:S(2)}) collective-permute-start(bf16[16,2176]{1,0:T(8,128)(2,1)S(1)} %shard_map.142.refs_0_), channel_id=1, source_target_pairs={{0,4},{1,5},{2,6},{3,7},{4,0},{5,1},{6,2},{7,3},{8,12},{9,13},{10,... | collective-permute-start | bytes 208904 | tf_op jit(solution)/shard_map/ppermute | solution.py:39
  52.5 1.7 %collective-permute-done.20.refs_3_ = bf16[16,2176]{1,0:T(8,128)(2,1)S(1)} collective-permute-done((bf16[16,2176]{1,0:T(8,128)(2,1)S(1)}, bf16[16,2176]{1,0:T(8,128)(2,1)S(1)}, u32[]{:S(2)}, u32[]{:S(2)}) %collective-permute-start.20) | collective-permute-done | bytes 69664 | tf_op jit(solution)/shard_map/ppermute | solution.py:39
  54.3 1.8 %collective-permute-done.19.refs_2_ = bf16[16,2176]{1,0:T(8,128)(2,1)S(1)} collective-permute-done((bf16[16,2176]{1,0:T(8,128)(2,1)S(1)}, bf16[16,2176]{1,0:T(8,128)(2,1)S(1)}, u32[]{:S(2)}, u32[]{:S(2)}) %collective-permute-start.19) | collective-permute-done | bytes 69664 | tf_op jit(solution)/shard_map/ppermute | solution.py:39
  56.6 1.9 %fetch.5.refs_10_ = bf16[1,768,2048]{2,1,0:T(8,128)(2,1)S(1)} custom-call(bf16[1,768,2048]{2,1,0:T(8,128)(2,1)} %refs_0_.5), custom_call_target="tpu_custom_call" | custom-call | bytes 6291456 | tf_op jit(solution)/shard_map/fetch/pallas_call | solution.py:84
  58.5 2.8 %fetch.4.refs_9_ = bf16[1,2048,1536]{2,1,0:T(8,128)(2,1)S(1)} custom-call(bf16[1,2048,1536]{2,1,0:T(8,128)(2,1)} %refs_0_.4), custom_call_target="tpu_custom_call" | custom-call | bytes 12582912 | tf_op jit(solution)/shard_map/fetch/pallas_call | solution.py:84
  61.3 2.5 %experts.1 = (bf16[16,2304]{1,0:T(8,128)(2,1)S(1)}, bf16[16,2304]{1,0:T(8,128)(2,1)S(1)}, bf16[16,2304]{1,0:T(8,128)(2,1)S(1)}, bf16[16,2304]{1,0:T(8,128)(2,1)S...) custom-call(bf16[16,2176]{1,0:T(8,128)(2,1)S(1)} %shard_map.142.refs, ...), custom_call_target="tpu_custom_call" | custom-call | flops 1207959552 | bytes 9437184 | tf_op jit(solution)/shard_map/experts/pallas_call | solution.py:487
  66.4 1.4 %collective-permute-start.32 = (bf16[16,2304]{1,0:T(8,128)(2,1)S(1)}, bf16[16,2304]{1,0:T(8,128)(2,1)S(1)}, u32[]{:S(2)}, u32[]{:S(2)}) collective-permute-start(bf16[16,2304]{1,0:T(8,128)(2,1)S(1)} %shard_map.145), channel_id=1, source_target_pairs={{0,2},{1,3},{2,0},{3,1},{4,6},{5,7},{6,4},{7,5},{8,10},{9,11},{10,... | collective-permute-start | bytes 221192 | tf_op jit(solution)/shard_map/ppermute | solution.py:39
  68.8 1.9 %collective-permute-done.29.far = bf16[16,2304]{1,0:T(8,128)(2,1)S(1)} collective-permute-done((bf16[16,2304]{1,0:T(8,128)(2,1)S(1)}, bf16[16,2304]{1,0:T(8,128)(2,1)S(1)}, u32[]{:S(2)}, u32[]{:S(2)}) %collective-permute-start.29) | collective-permute-done | bytes 73760 | tf_op jit(solution)/shard_map/ppermute | solution.py:39
  71.3 1.0 %collective-permute-done.32.far = bf16[16,2304]{1,0:T(8,128)(2,1)S(1)} collective-permute-done((bf16[16,2304]{1,0:T(8,128)(2,1)S(1)}, bf16[16,2304]{1,0:T(8,128)(2,1)S(1)}, u32[]{:S(2)}, u32[]{:S(2)}) %collective-permute-start.32) | collective-permute-done | bytes 73760 | tf_op jit(solution)/shard_map/ppermute | solution.py:39
  72.4 1.2 %collective-permute-start.33 = (bf16[16,2560]{1,0:T(8,128)(2,1)S(1)}, bf16[16,2560]{1,0:T(8,128)(2,1)S(1)}, u32[]{:S(2)}, u32[]{:S(2)}) collective-permute-start(bf16[16,2560]{1,0:T(8,128)(2,1)S(1)} %mix.6), channel_id=1, source_target_pairs={{0,8},{1,9},{2,10},{3,11},{4,12},{5,13},{6,14},{7,15},{8,0},{9,1},... | collective-permute-start | bytes 245768 | tf_op jit(solution)/shard_map/ppermute | solution.py:39
  73.6 1.9 %collective-permute-start.36 = (bf16[16,2560]{1,0:T(8,128)(2,1)S(1)}, bf16[16,2560]{1,0:T(8,128)(2,1)S(1)}, u32[]{:S(2)}, u32[]{:S(2)}) collective-permute-start(bf16[16,2560]{1,0:T(8,128)(2,1)S(1)} %mix.7), channel_id=1, source_target_pairs={{0,12},{1,13},{2,14},{3,15},{4,8},{5,9},{6,10},{7,11},{8,4},{9,5},... | collective-permute-start | bytes 245768 | tf_op jit(solution)/shard_map/ppermute | solution.py:39
  76.4 3.5 %collective-permute-done.27.far = bf16[16,2304]{1,0:T(8,128)(2,1)S(1)} collective-permute-done((bf16[16,2304]{1,0:T(8,128)(2,1)S(1)}, bf16[16,2304]{1,0:T(8,128)(2,1)S(1)}, u32[]{:S(2)}, u32[]{:S(2)}) %collective-permute-start.27) | collective-permute-done | bytes 73760 | tf_op jit(solution)/shard_map/ppermute | solution.py:39
  (66 shorter events, 13.4 us)
Async XLA Ops:
  0.6 33.8 %collective-permute-start.12 = (bf16[128,2048]{1,0:T(8,128)(2,1)}, bf16[128,2048]{1,0:T(8,128)(2,1)S(1)}, u32[]{:S(2)}, u32[]{:S(2)}) collective-permute-start(bf16[128,2048]{1,0:T(8,128)(2,1)} %refs_5_.1), channel_id=1, source_target_pairs={{0,1},{1,0},{2,3},{3,2},{4,5},{5,4},{6,7},{7,6},{8,9},{9,8},{10,11... | collective-permute-start | bytes 1572872 | tf_op jit(solution)/shard_map/ppermute | solution.py:39
  1.2 16.6 %collective-permute-start.4 = (bf16[1,512,256]{2,1,0:T(8,128)(2,1)}, bf16[1,512,256]{2,1,0:T(8,128)(2,1)S(1)}, u32[]{:S(2)}, u32[]{:S(2)}) collective-permute-start(bf16[1,512,256]{2,1,0:T(8,128)(2,1)} %refs_1_.1), channel_id=1, source_target_pairs={{0,1},{1,0},{2,3},{3,2},{4,5},{5,4},{6,7},{7,6},{8,9},{9,8},{10,11... | collective-permute-start | bytes 786440 | tf_op jit(solution)/shard_map/ppermute | solution.py:39
  1.3 16.5 %collective-permute-start.5 = (bf16[1,512,256]{2,1,0:T(8,128)(2,1)}, bf16[1,512,256]{2,1,0:T(8,128)(2,1)S(1)}, u32[]{:S(2)}, u32[]{:S(2)}) collective-permute-start(bf16[1,512,256]{2,1,0:T(8,128)(2,1)} %refs_2_.1), channel_id=1, source_target_pairs={{0,1},{1,0},{2,3},{3,2},{4,5},{5,4},{6,7},{7,6},{8,9},{9,8},{10,11... | collective-permute-start | bytes 786440 | tf_op jit(solution)/shard_map/ppermute | solution.py:39
  1.7 4.8 %collective-permute-start = (bf16[8,2048]{1,0:T(8,128)(2,1)}, bf16[8,2048]{1,0:T(8,128)(2,1)S(1)}, u32[]{:S(2)}, u32[]{:S(2)}) collective-permute-start(bf16[8,2048]{1,0:T(8,128)(2,1)} %refs_0_.3), channel_id=1, source_target_pairs={{0,2},{1,3},{2,0},{3,1},{4,6},{5,7},{6,4},{7,5},{8,10},{9,11},{10,... | collective-permute-start | bytes 98312 | tf_op jit(solution)/shard_map/ppermute | solution.py:39
  6.5 7.0 %collective-permute-start.3 = (bf16[2,8,2048]{2,1,0:T(8,128)(2,1)S(1)}, bf16[2,8,2048]{2,1,0:T(8,128)(2,1)S(1)}, u32[]{:S(2)}, u32[]{:S(2)}) collective-permute-start(bf16[2,8,2048]{2,1,0:T(8,128)(2,1)S(1)} %shard_map.140.refs_0_), channel_id=1, source_target_pairs={{0,12},{1,13},{2,14},{3,15},{4,8},{5,9},{6,10},{7,11},{8,4},{9,5},... | collective-permute-start | bytes 196616 | tf_op jit(solution)/shard_map/ppermute | solution.py:39
  10.5 5.2 %collective-permute-start.2 = (bf16[2,8,2048]{2,1,0:T(8,128)(2,1)S(1)}, bf16[2,8,2048]{2,1,0:T(8,128)(2,1)S(1)}, u32[]{:S(2)}, u32[]{:S(2)}) collective-permute-start(bf16[2,8,2048]{2,1,0:T(8,128)(2,1)S(1)} %shard_map.140.refs_0_), channel_id=1, source_target_pairs={{0,8},{1,9},{2,10},{3,11},{4,12},{5,13},{6,14},{7,15},{8,0},{9,1},... | collective-permute-start | bytes 196616 | tf_op jit(solution)/shard_map/ppermute | solution.py:39
  18.9 11.1 %collective-permute-start.6 = (bf16[2,136,128]{2,1,0:T(8,128)(2,1)S(1)}, bf16[2,136,128]{2,1,0:T(8,128)(2,1)S(1)}, u32[]{:S(2)}, u32[]{:S(2)}) collective-permute-start(bf16[2,136,128]{2,1,0:T(8,128)(2,1)S(1)} %get-tuple-element.41), channel_id=1, source_target_pairs={{0,2},{1,3},{2,0},{3,1},{4,6},{5,7},{6,4},{7,5},{8,10},{9,11},{10,... | collective-permute-start | bytes 208904 | tf_op jit(solution)/shard_map/ppermute | solution.py:39
  22.3 6.0 %collective-permute-start.10 = (bf16[1,136,128]{2,1,0:T(8,128)(2,1)S(1)}, bf16[1,136,128]{2,1,0:T(8,128)(2,1)S(1)}, u32[]{:S(2)}, u32[]{:S(2)}) collective-permute-start(bf16[1,136,128]{2,1,0:T(8,128)(2,1)S(1)} %get-tuple-element.47), channel_id=1, source_target_pairs={{0,2},{1,3},{2,0},{3,1},{4,6},{5,7},{6,4},{7,5},{8,10},{9,11},{10,... | collective-permute-start | bytes 104456 | tf_op jit(solution)/shard_map/ppermute | solution.py:39
  25.8 4.8 %collective-permute-start.13 = (bf16[16,2176]{1,0:T(8,128)(2,1)S(1)}, bf16[16,2176]{1,0:T(8,128)(2,1)S(1)}, u32[]{:S(2)}, u32[]{:S(2)}) collective-permute-start(bf16[16,2176]{1,0:T(8,128)(2,1)S(1)} %get-tuple-element.49.refs_6_), channel_id=1, source_target_pairs={{0,1},{1,0},{2,3},{3,2},{4,5},{5,4},{6,7},{7,6},{8,9},{9,8},{10,11... | collective-permute-start | bytes 208904 | tf_op jit(solution)/shard_map/ppermute | solution.py:39
  25.9 4.9 %collective-permute-start.9 = (bf16[136,128]{1,0:T(8,128)(2,1)S(1)}, bf16[136,128]{1,0:T(8,128)(2,1)S(1)}, u32[]{:S(2)}, u32[]{:S(2)}) collective-permute-start(bf16[136,128]{1,0:T(8,128)(2,1)S(1)} %fold.4), channel_id=1, source_target_pairs={{0,8},{1,9},{2,10},{3,11},{4,12},{5,13},{6,14},{7,15},{8,0},{9,1},... | collective-permute-start | bytes 104456 | tf_op jit(solution)/shard_map/ppermute | solution.py:39
  28.3 6.0 %collective-permute-start.11 = (bf16[136,128]{1,0:T(8,128)(2,1)S(1)}, bf16[136,128]{1,0:T(8,128)(2,1)S(1)}, u32[]{:S(2)}, u32[]{:S(2)}) collective-permute-start(bf16[136,128]{1,0:T(8,128)(2,1)S(1)} %fold.5), channel_id=1, source_target_pairs={{0,12},{1,13},{2,14},{3,15},{4,8},{5,9},{6,10},{7,11},{8,4},{9,5},... | collective-permute-start | bytes 104456 | tf_op jit(solution)/shard_map/ppermute | solution.py:39
  30.1 4.4 %collective-permute-start.7 = (bf16[136,128]{1,0:T(8,128)(2,1)S(1)}, bf16[136,128]{1,0:T(8,128)(2,1)S(1)}, u32[]{:S(2)}, u32[]{:S(2)}) collective-permute-start(bf16[136,128]{1,0:T(8,128)(2,1)S(1)} %get-tuple-element.43), channel_id=1, source_target_pairs={{0,4},{1,5},{2,6},{3,7},{4,0},{5,1},{6,2},{7,3},{8,12},{9,13},{10,... | collective-permute-start | bytes 104456 | tf_op jit(solution)/shard_map/ppermute | solution.py:39
  35.0 4.5 %collective-permute-start.14 = (bf16[16,2176]{1,0:T(8,128)(2,1)S(1)}, bf16[16,2176]{1,0:T(8,128)(2,1)S(1)}, u32[]{:S(2)}, u32[]{:S(2)}) collective-permute-start(bf16[16,2176]{1,0:T(8,128)(2,1)S(1)} %get-tuple-element.52), channel_id=1, source_target_pairs={{0,4},{1,5},{2,6},{3,7},{4,0},{5,1},{6,2},{7,3},{8,12},{9,13},{10,... | collective-permute-start | bytes 208904 | tf_op jit(solution)/shard_map/ppermute | solution.py:39
  35.1 7.5 %collective-permute-start.15 = (bf16[16,2176]{1,0:T(8,128)(2,1)S(1)}, bf16[16,2176]{1,0:T(8,128)(2,1)S(1)}, u32[]{:S(2)}, u32[]{:S(2)}) collective-permute-start(bf16[16,2176]{1,0:T(8,128)(2,1)S(1)} %get-tuple-element.53), channel_id=1, source_target_pairs={{0,8},{1,9},{2,10},{3,11},{4,12},{5,13},{6,14},{7,15},{8,0},{9,1},... | collective-permute-start | bytes 208904 | tf_op jit(solution)/shard_map/ppermute | solution.py:39
  37.5 6.1 %collective-permute-start.16 = (bf16[16,2176]{1,0:T(8,128)(2,1)S(1)}, bf16[16,2176]{1,0:T(8,128)(2,1)S(1)}, u32[]{:S(2)}, u32[]{:S(2)}) collective-permute-start(bf16[16,2176]{1,0:T(8,128)(2,1)S(1)} %get-tuple-element.54), channel_id=1, source_target_pairs={{0,12},{1,13},{2,14},{3,15},{4,8},{5,9},{6,10},{7,11},{8,4},{9,5},... | collective-permute-start | bytes 208904 | tf_op jit(solution)/shard_map/ppermute | solution.py:39
  43.7 4.4 %collective-permute-start.17 = (bf16[16,2176]{1,0:T(8,128)(2,1)S(1)}, bf16[16,2176]{1,0:T(8,128)(2,1)S(1)}, u32[]{:S(2)}, u32[]{:S(2)}) collective-permute-start(bf16[16,2176]{1,0:T(8,128)(2,1)S(1)} %shard_map.141.refs_0_), channel_id=1, source_target_pairs={{0,2},{1,3},{2,0},{3,1},{4,6},{5,7},{6,4},{7,5},{8,10},{9,11},{10,... | collective-permute-start | bytes 208904 | tf_op jit(solution)/shard_map/ppermute | solution.py:39
  48.1 6.2 %collective-permute-start.20 = (bf16[16,2176]{1,0:T(8,128)(2,1)S(1)}, bf16[16,2176]{1,0:T(8,128)(2,1)S(1)}, u32[]{:S(2)}, u32[]{:S(2)}) collective-permute-start(bf16[16,2176]{1,0:T(8,128)(2,1)S(1)} %shard_map.142.refs_0_), channel_id=1, source_target_pairs={{0,12},{1,13},{2,14},{3,15},{4,8},{5,9},{6,10},{7,11},{8,4},{9,5},... | collective-permute-start | bytes 208904 | tf_op jit(solution)/shard_map/ppermute | solution.py:39
  50.3 5.8 %collective-permute-start.19 = (bf16[16,2176]{1,0:T(8,128)(2,1)S(1)}, bf16[16,2176]{1,0:T(8,128)(2,1)S(1)}, u32[]{:S(2)}, u32[]{:S(2)}) collective-permute-start(bf16[16,2176]{1,0:T(8,128)(2,1)S(1)} %shard_map.142.refs_0_), channel_id=1, source_target_pairs={{0,8},{1,9},{2,10},{3,11},{4,12},{5,13},{6,14},{7,15},{8,0},{9,1},... | collective-permute-start | bytes 208904 | tf_op jit(solution)/shard_map/ppermute | solution.py:39
  50.7 5.4 %collective-permute-start.18 = (bf16[16,2176]{1,0:T(8,128)(2,1)S(1)}, bf16[16,2176]{1,0:T(8,128)(2,1)S(1)}, u32[]{:S(2)}, u32[]{:S(2)}) collective-permute-start(bf16[16,2176]{1,0:T(8,128)(2,1)S(1)} %shard_map.142.refs_0_), channel_id=1, source_target_pairs={{0,4},{1,5},{2,6},{3,7},{4,0},{5,1},{6,2},{7,3},{8,12},{9,13},{10,... | collective-permute-start | bytes 208904 | tf_op jit(solution)/shard_map/ppermute | solution.py:39
  52.5 8.8 %collective-permute-start.21 = (bf16[16,2176]{1,0:T(8,128)(2,1)S(1)}, bf16[16,2176]{1,0:T(8,128)(2,1)S(1)}, u32[]{:S(2)}, u32[]{:S(2)}) collective-permute-start(bf16[16,2176]{1,0:T(8,128)(2,1)S(1)} %shard_map.142.refs_0_), channel_id=1, source_target_pairs={{0,1},{1,0},{2,3},{3,2},{4,5},{5,4},{6,7},{7,6},{8,9},{9,8},{10,11... | collective-permute-start | bytes 208904 | tf_op jit(solution)/shard_map/ppermute | solution.py:39
  54.3 7.1 %collective-permute-start.24 = (bf16[16,2176]{1,0:T(8,128)(2,1)S(1)}, bf16[16,2176]{1,0:T(8,128)(2,1)S(1)}, u32[]{:S(2)}, u32[]{:S(2)}) collective-permute-start(bf16[16,2176]{1,0:T(8,128)(2,1)S(1)} %collective-permute-done.20.refs_3_), channel_id=1, source_target_pairs={{0,1},{1,0},{2,3},{3,2},{4,5},{5,4},{6,7},{7,6},{8,9},{9,8},{10,11... | collective-permute-start | bytes 208904 | tf_op jit(solution)/shard_map/ppermute | solution.py:39
  56.1 5.2 %collective-permute-start.23 = (bf16[16,2176]{1,0:T(8,128)(2,1)S(1)}, bf16[16,2176]{1,0:T(8,128)(2,1)S(1)}, u32[]{:S(2)}, u32[]{:S(2)}) collective-permute-start(bf16[16,2176]{1,0:T(8,128)(2,1)S(1)} %collective-permute-done.19.refs_2_), channel_id=1, source_target_pairs={{0,1},{1,0},{2,3},{3,2},{4,5},{5,4},{6,7},{7,6},{8,9},{9,8},{10,11... | collective-permute-start | bytes 208904 | tf_op jit(solution)/shard_map/ppermute | solution.py:39
  56.1 5.3 %collective-permute-start.22 = (bf16[16,2176]{1,0:T(8,128)(2,1)S(1)}, bf16[16,2176]{1,0:T(8,128)(2,1)S(1)}, u32[]{:S(2)}, u32[]{:S(2)}) collective-permute-start(bf16[16,2176]{1,0:T(8,128)(2,1)S(1)} %collective-permute-done.18.refs_1_), channel_id=1, source_target_pairs={{0,1},{1,0},{2,3},{3,2},{4,5},{5,4},{6,7},{7,6},{8,9},{9,8},{10,11... | collective-permute-start | bytes 208904 | tf_op jit(solution)/shard_map/ppermute | solution.py:39
  63.8 7.0 %collective-permute-start.25 = (bf16[64,2304]{1,0:T(8,128)(2,1)S(1)}, bf16[64,2304]{1,0:T(8,128)(2,1)S(1)}, u32[]{:S(2)}, u32[]{:S(2)}) collective-permute-start(bf16[64,2304]{1,0:T(8,128)(2,1)S(1)} %get-tuple-element.63), channel_id=1, source_target_pairs={{0,1},{1,0},{2,3},{3,2},{4,5},{5,4},{6,7},{7,6},{8,9},{9,8},{10,11... | collective-permute-start | bytes 884744 | tf_op jit(solution)/shard_map/ppermute | solution.py:39
  65.6 5.2 %collective-permute-start.29 = (bf16[16,2304]{1,0:T(8,128)(2,1)S(1)}, bf16[16,2304]{1,0:T(8,128)(2,1)S(1)}, u32[]{:S(2)}, u32[]{:S(2)}) collective-permute-start(bf16[16,2304]{1,0:T(8,128)(2,1)S(1)} %shard_map.144), channel_id=1, source_target_pairs={{0,2},{1,3},{2,0},{3,1},{4,6},{5,7},{6,4},{7,5},{8,10},{9,11},{10,... | collective-permute-start | bytes 221192 | tf_op jit(solution)/shard_map/ppermute | solution.py:39
  66.4 6.0 %collective-permute-start.32 = (bf16[16,2304]{1,0:T(8,128)(2,1)S(1)}, bf16[16,2304]{1,0:T(8,128)(2,1)S(1)}, u32[]{:S(2)}, u32[]{:S(2)}) collective-permute-start(bf16[16,2304]{1,0:T(8,128)(2,1)S(1)} %shard_map.145), channel_id=1, source_target_pairs={{0,2},{1,3},{2,0},{3,1},{4,6},{5,7},{6,4},{7,5},{8,10},{9,11},{10,... | collective-permute-start | bytes 221192 | tf_op jit(solution)/shard_map/ppermute | solution.py:39
  67.8 5.7 %collective-permute-start.35 = (bf16[16,2304]{1,0:T(8,128)(2,1)S(1)}, bf16[16,2304]{1,0:T(8,128)(2,1)S(1)}, u32[]{:S(2)}, u32[]{:S(2)}) collective-permute-start(bf16[16,2304]{1,0:T(8,128)(2,1)S(1)} %shard_map.146), channel_id=1, source_target_pairs={{0,2},{1,3},{2,0},{3,1},{4,6},{5,7},{6,4},{7,5},{8,10},{9,11},{10,... | collective-permute-start | bytes 221192 | tf_op jit(solution)/shard_map/ppermute | solution.py:39
  68.6 6.9 %collective-permute-start.26 = (bf16[16,2304]{1,0:T(8,128)(2,1)S(1)}, bf16[16,2304]{1,0:T(8,128)(2,1)S(1)}, u32[]{:S(2)}, u32[]{:S(2)}) collective-permute-start(bf16[16,2304]{1,0:T(8,128)(2,1)S(1)} %get-tuple-element.65), channel_id=1, source_target_pairs={{0,1},{1,0},{2,3},{3,2},{4,5},{5,4},{6,7},{7,6},{8,9},{9,8},{10,11... | collective-permute-start | bytes 221192 | tf_op jit(solution)/shard_map/ppermute | solution.py:39
  70.8 9.1 %collective-permute-start.30 = (bf16[16,2560]{1,0:T(8,128)(2,1)S(1)}, bf16[16,2560]{1,0:T(8,128)(2,1)S(1)}, u32[]{:S(2)}, u32[]{:S(2)}) collective-permute-start(bf16[16,2560]{1,0:T(8,128)(2,1)S(1)} %mix.5), channel_id=1, source_target_pairs={{0,4},{1,5},{2,6},{3,7},{4,0},{5,1},{6,2},{7,3},{8,12},{9,13},{10,... | collective-permute-start | bytes 245768 | tf_op jit(solution)/shard_map/ppermute | solution.py:39
  72.4 8.2 %collective-permute-start.33 = (bf16[16,2560]{1,0:T(8,128)(2,1)S(1)}, bf16[16,2560]{1,0:T(8,128)(2,1)S(1)}, u32[]{:S(2)}, u32[]{:S(2)}) collective-permute-start(bf16[16,2560]{1,0:T(8,128)(2,1)S(1)} %mix.6), channel_id=1, source_target_pairs={{0,8},{1,9},{2,10},{3,11},{4,12},{5,13},{6,14},{7,15},{8,0},{9,1},... | collective-permute-start | bytes 245768 | tf_op jit(solution)/shard_map/ppermute | solution.py:39
  73.6 7.0 %collective-permute-start.36 = (bf16[16,2560]{1,0:T(8,128)(2,1)S(1)}, bf16[16,2560]{1,0:T(8,128)(2,1)S(1)}, u32[]{:S(2)}, u32[]{:S(2)}) collective-permute-start(bf16[16,2560]{1,0:T(8,128)(2,1)S(1)} %mix.7), channel_id=1, source_target_pairs={{0,12},{1,13},{2,14},{3,15},{4,8},{5,9},{6,10},{7,11},{8,4},{9,5},... | collective-permute-start | bytes 245768 | tf_op jit(solution)/shard_map/ppermute | solution.py:39
  75.5 4.4 %collective-permute-start.27 = (bf16[16,2304]{1,0:T(8,128)(2,1)S(1)}, bf16[16,2304]{1,0:T(8,128)(2,1)S(1)}, u32[]{:S(2)}, u32[]{:S(2)}) collective-permute-start(bf16[16,2304]{1,0:T(8,128)(2,1)S(1)} %shard_map.143), channel_id=1, source_target_pairs={{0,2},{1,3},{2,0},{3,1},{4,6},{5,7},{6,4},{7,5},{8,10},{9,11},{10,... | collective-permute-start | bytes 221192 | tf_op jit(solution)/shard_map/ppermute | solution.py:39
  (5 other events, 15.4 us)
